TPU v7x, 768 devices: a whole 4x8x12 slice. The times are simulated.
768 devices in a mesh: dp: 48 (over x_hi, z, core), fsdp: 16 (over x_lo, y).
Axes of the slice: x: 4 (x_hi: 2, x_lo: 2; x = x_hi * 2 + x_lo), y: 8, z: 12, core: 2. Of those that a mesh axis runs over, the one named last changes fastest.
Arguments:
- features: bfloat16 [384, 512, 640], P('dp', 'fsdp'), may hold values from -6 to 6
- skip_input: bfloat16 [384, 512, 640], P('dp', 'fsdp'), may hold values from -6 to 6
- cotangent: bfloat16 [384, 512, 640], P('dp', 'fsdp'), may hold values from -6 to 6
- temporal_weight: bfloat16 [640, 1920], P('fsdp'), may hold values from -0.125 to 0.125
- clip_lengths: int32 [48], replicated, may hold values from 1 to 16, 384 in all
- cycle_start: int32 [1], replicated, may hold values from 0 to 383
Outputs:
- block_out: bfloat16 [384, 512, 640], P('dp', 'fsdp')
- grad_features: bfloat16 [384, 512, 640], P('dp', 'fsdp')
- grad_weight: float32 [640, 1920], P('fsdp')
Inputs may be any that keep to these rules, and one draw needn't show every extreme that they name: `clip_lengths`: the lengths sum to 384; the longest clip has exactly 16 frames.
All inputs are finite; a program needn't handle non-finite values.
Results may differ from a plain program's by a relative error of at most 0.001.
Values may be sent and summed in bfloat16 or wider, within the bound.
No kernel may reach another device: no remote copies, remote signals or barrier semaphores. Data moves between devices by JAX's collectives and lax.ppermute only.
A program may use at most 128 MiB of HBM per device.

v0:
```python
import jax
import jax.numpy as jnp
from jax import lax
from jax.sharding import PartitionSpec as P


def padded(block, sides, width):
    for axis, dim in sides:
        count = lax.axis_size(axis)
        forward = [(i, i + 1) for i in range(count - 1)]
        forward.append((count - 1, 0))
        backward = [(target, source) for source, target in forward]
        low = lax.ppermute(
            lax.slice_in_dim(block, block.shape[dim] - width, None, axis=dim), axis, forward
        )
        high = lax.ppermute(lax.slice_in_dim(block, 0, width, axis=dim), axis, backward)
        block = jnp.concatenate([low, block, high], axis=dim)
    return block


def border_flags(clip_lengths, cycle_start, frame_index, total):
    starts = jnp.cumsum(clip_lengths) - clip_lengths
    position = jnp.mod(frame_index - cycle_start[0], total)
    following = jnp.mod(frame_index + 1 - cycle_start[0], total)
    first_here = jnp.any(position[:, None] == starts[None, :], axis=1)
    first_next = jnp.any(following[:, None] == starts[None, :], axis=1)
    return (1 - first_here.astype(jnp.int32), 1 - first_next.astype(jnp.int32))


def shards(features, skip_input, cotangent, temporal_weight, clip_lengths, cycle_start):
    frames, strip, width = features.shape
    tile_index = lax.axis_index("dp")
    total_frames = frames * lax.axis_size("dp")
    frame_index = tile_index * frames + jnp.arange(frames, dtype=jnp.int32)
    prev_ok, next_ok = border_flags(clip_lengths, cycle_start, frame_index, total_frames)
    prev_scale = prev_ok.astype(jnp.bfloat16)[:, None, None]
    next_scale = next_ok.astype(jnp.bfloat16)[:, None, None]
    joined = jnp.concatenate([features, cotangent], axis=2)
    widened = padded(joined, (("dp", 0),), 1)
    features_prev = prev_scale * widened[:-2, :, :width]
    features_next = next_scale * widened[2:, :, :width]
    cot_prev = prev_scale * widened[:-2, :, width:]
    cot_next = next_scale * widened[2:, :, width:]
    tokens = frames * strip
    stacked_in = jnp.stack([features_prev, features, features_next], axis=2).reshape(
        tokens, 3, width
    )
    stacked_back = jnp.stack([cot_next, cotangent, cot_prev], axis=2).reshape(tokens, 3, width)
    cot_flat = cotangent.reshape(tokens, width)
    piece = lax.all_gather(temporal_weight, "fsdp", axis=0, tiled=True)
    count = piece.shape[0]
    kernel_rows = piece.reshape(count, 3, width)
    columns = stacked_in
    mixed = jnp.einsum("nkr,rkc->nc", columns, kernel_rows, preferred_element_type=jnp.float32)
    block = jnp.einsum("nkc,rkc->nr", stacked_back, kernel_rows, preferred_element_type=jnp.float32)
    back = block
    mixed, back = (mixed, back)
    block_out = (skip_input.astype(jnp.float32) + mixed.reshape(frames, strip, width)).astype(
        jnp.bfloat16
    )
    grad_features = back.reshape(frames, strip, width).astype(jnp.bfloat16)
    local_rows = temporal_weight.shape[0]
    columns = stacked_in
    term = jnp.einsum("nkr,nc->rkc", columns, cot_flat, preferred_element_type=jnp.float32)
    strip_sum = lax.psum_scatter(
        term.reshape(local_rows * lax.axis_size("fsdp"), 3 * width),
        "fsdp",
        scatter_dimension=0,
        tiled=True,
    )
    summed = lax.psum(strip_sum, "dp")
    grad_weight = summed / jnp.sqrt(jnp.float32(total_frames * strip * lax.axis_size("fsdp")))
    return (block_out, grad_features, grad_weight)


def solution(mesh):
    in_specs = (
        P("dp", "fsdp", None),
        P("dp", "fsdp", None),
        P("dp", "fsdp", None),
        P("fsdp", None),
        P(),
        P(),
    )
    out_specs = (P("dp", "fsdp", None), P("dp", "fsdp", None), P("fsdp", None))
    return jax.shard_map(shards, mesh=mesh, in_specs=in_specs, out_specs=out_specs, check_vma=False)
```

profile of v0, /device:TPU:1, one launch (start us, length us, event | category | flops | bytes accessed | tf_op | source)
XLA Modules:
  0.0 576.2 jit_solution(3427802692180480060)
XLA Ops:
  7.2 0.0 all-gather.2.cloned.1.call-start
  7.2 0.7 all-gather.2.cloned.1.call-update
  7.9 0.0 reduce-scatter.5.cloned.1.call-start
  8.0 1.0 constant_dynamic-update-slice_fusion.1
  9.0 1.0 constant_dynamic-update-slice_fusion
  10.0 5.4 collective-permute-start
  15.4 9.0 %collective-permute-start.1 = (bf16[1,32,1280]{2,1,0:T(8,128)(2,1)S(1)}, bf16[1,32,1280]{2,1,0:T(8,128)(2,1)S(1)}, u32[]{:S(2)}, u32[]{:S(2)}) collective-permute-start(bf16[1,32,1280]{2,1,0:T(8,128)(2,1)S(1)} %get-tuple-element.12), channel_id=1, source_target_pairs={{16,0},{32,16},{48,32},{64,48},{80,64},{96,80},{112,96},{128,112},... | collective-permute-start | bytes 245768 | tf_op jit(solution)/shard_map/ppermute | solution.py:16
  25.0 0.7 copy.27
  25.8 0.1 reduce-window.9
  25.9 0.1 reduce
  26.0 0.7 sub.37
  26.6 0.2 compare_reduce_fusion.1
  26.9 0.4 fusion.5
  27.4 3.2 fusion.3
  30.6 5.8 %copy.32 = f32[640,1920]{1,0:T(8,128)} copy(f32[640,1920]{0,1:T(8,128)} %bitcast.47) | data formatting | bytes 9830400 | tf_op jit(solution)/shard_map/reshape | solution.py:66
  36.4 0.0 all-reduce.3.cloned.1.call-start
  36.5 0.1 pad_maximum_fusion.1
  36.6 50.2 %all-gather.2.cloned.1.call-done = bf16[640,1920]{1,0:T(8,128)(2,1)} async-done(((bf16[40,1920]{1,0:T(8,128)(2,1)}), bf16[640,1920]{1,0:T(8,128)(2,1)}) %all-gather.2.cloned.1.call-update) | async-done | bytes 2457616 | tf_op jit(solution)/shard_map/all_gather | solution.py:50
  86.8 3.5 copy.29
  90.3 3.0 fusion.1
  93.3 81.2 %reduce-scatter.5.cloned.1.call-done = f32[40,1920]{1,0:T(8,128)} async-done(((f32[640,1920]{1,0:T(8,128)}), f32[40,1920]{1,0:T(8,128)}) %reduce-scatter.5.cloned.1.call-update) | async-done | bytes 307216
  174.5 1.7 fusion.2
  176.2 391.8 %all-reduce.3.cloned.1.call-done = f32[40,1920]{1,0:T(8,128)} async-done(((f32[40,1920]{1,0:T(8,128)}), f32[40,1920]{1,0:T(8,128)}) %all-reduce.3.cloned.1.call-update) | async-done | bytes 307216 | tf_op jit(solution)/shard_map/psum | solution.py:71
  568.0 1.7 broadcast_multiply_fusion
  (16 shorter events, 0.1 us)
Async XLA Ops:
  7.2 20.2 %copy-start.1 = (bf16[8,32,640]{2,1,0:T(8,128)(2,1)S(1)}, bf16[8,32,640]{2,1,0:T(8,128)(2,1)}, u32[]{:S(2)}) copy-start(bf16[8,32,640]{2,1,0:T(8,128)(2,1)} %param.6) | copy-start | bytes 983044
  7.2 20.2 %copy-start = (bf16[8,32,640]{2,1,0:T(8,128)(2,1)S(1)}, bf16[8,32,640]{2,1,0:T(8,128)(2,1)}, u32[]{:S(2)}) copy-start(bf16[8,32,640]{2,1,0:T(8,128)(2,1)} %param.8) | copy-start | bytes 983044
  7.2 79.6 %all-gather.2.cloned.1.call-start = ((), (), s32[]{:S(2)}) async-start(), calls=%async_computation.1 | async-start | bytes 2611200 | tf_op jit(solution)/shard_map/all_gather | solution.py:50
  7.9 166.6 %reduce-scatter.5.cloned.1.call-start = ((), (), s32[]{:S(2)}) async-start(), calls=%async_computation.3 | async-start | bytes 5222400
  10.0 16.9 %collective-permute-start = (bf16[1,32,1280]{2,1,0:T(8,128)(2,1)S(1)}, bf16[1,32,1280]{2,1,0:T(8,128)(2,1)S(1)}, u32[]{:S(2)}, u32[]{:S(2)}) collective-permute-start(bf16[1,32,1280]{2,1,0:T(8,128)(2,1)S(1)} %get-tuple-element.11), channel_id=1, source_target_pairs={{0,16},{16,32},{32,48},{48,64},{64,80},{80,96},{96,112},{112,128},... | collective-permute-start | bytes 245768 | tf_op jit(solution)/shard_map/ppermute | solution.py:13
  15.4 11.5 %collective-permute-start.1 = (bf16[1,32,1280]{2,1,0:T(8,128)(2,1)S(1)}, bf16[1,32,1280]{2,1,0:T(8,128)(2,1)S(1)}, u32[]{:S(2)}, u32[]{:S(2)}) collective-permute-start(bf16[1,32,1280]{2,1,0:T(8,128)(2,1)S(1)} %get-tuple-element.12), channel_id=1, source_target_pairs={{16,0},{32,16},{48,32},{64,48},{80,64},{96,80},{112,96},{128,112},... | collective-permute-start | bytes 245768 | tf_op jit(solution)/shard_map/ppermute | solution.py:16
  27.4 3.2 copy-start.2
  27.4 3.2 copy-start.3
  36.4 531.5 %all-reduce.3.cloned.1.call-start = ((), (), s32[]{:S(2)}) async-start(), calls=%async_computation.2 | async-start | bytes 614400 | tf_op jit(solution)/shard_map/psum | solution.py:71
Sparse Core Ops, SparseCore 0:
  10.4 76.3 all-gather.1
  90.0 84.4 reduce-scatter.4
  178.0 389.8 all-reduce.2
where the time goes:
time: 577 us; the launch traced here: 576 us
  waiting for transfers between devices  524 us (91%)
  starting transfers between devices  14.5 us (3%)
  between operations  14.5 us (3%)
  local copies, waits for them, and re-layouts  12.1 us (2%)
  matrix products  7.88 us (1%)
    psum x1, waiting for transfers between devices, shards(): summed = lax.psum(strip_sum, 'dp')  392 us
    unnamed x4, waiting for transfers between devices  81.9 us
    all_gather x1, waiting for transfers between devices, shards(): piece = lax.all_gather(temporal_weight, 'fsdp', axis=0, tiled=True)  50.2 us
  transfers between devices with their start and end apart: 5, of which 3 were waited for; matrix products, arithmetic and copies ran while one was open for 4% of the time, Pallas kernels for 0%

commit v1 on v0

v1 whole, which is shorter than its diff:
```python
import jax
import jax.numpy as jnp
from jax import lax
from jax.experimental import pallas as pl
from jax.experimental.pallas import tpu as pltpu
from jax.sharding import Mesh, PartitionSpec as P

DP = ("xh", "z", "c")
FSDP = ("xl", "y")
X = ("xh", "xl")


def border_flags(clip_lengths, cycle_start, frame_index, total):
    starts = jnp.cumsum(clip_lengths) - clip_lengths
    position = jnp.mod(frame_index - cycle_start[0], total)
    following = jnp.mod(frame_index + 1 - cycle_start[0], total)
    first_here = jnp.any(position[:, None] == starts[None, :], axis=1)
    first_next = jnp.any(following[:, None] == starts[None, :], axis=1)
    return (1 - first_here.astype(jnp.int32), 1 - first_next.astype(jnp.int32))


def term_kernel(core_ref, prev_ref, next_ref, f_ref, sf_ref, g_ref, sg_ref, halo_ref, out_ref, fa, fc, gg):
    frames, strip, width = f_ref.shape
    half = frames * strip
    core = core_ref[0]

    def put(slot, value, ok):
        fa[pl.ds(slot * strip, strip), :] = jnp.where(ok != 0, value, jnp.zeros_like(value))

    for ref, offset, dst in ((f_ref, 0, fc), (sf_ref, half, fc), (g_ref, 0, gg), (sg_ref, half, gg)):
        dst[pl.ds(offset, half), :] = ref[...].reshape(half, width)

    @pl.when(core == 0)
    def _():
        for j in range(frames):
            put(j, halo_ref[...] if j == 0 else f_ref[j - 1], prev_ref[j])
            put(frames + j, f_ref[frames - 1] if j == 0 else sf_ref[j - 1], prev_ref[frames + j])

    @pl.when(core != 0)
    def _():
        for j in range(frames):
            put(j, halo_ref[...] if j == frames - 1 else f_ref[j + 1], next_ref[frames + j])
            put(frames + j, f_ref[0] if j == frames - 1 else sf_ref[j + 1], next_ref[j])

    def dot(a, b):
        return lax.dot_general(a, b, (((0,), (0,)), ((), ())), preferred_element_type=jnp.float32)

    rows = width // 2
    wide = out_ref.shape[3]
    rest = width - wide
    first = dot(fa[...], gg[...])
    for xl in range(2):
        out_ref[0, xl] = first[xl * rows:(xl + 1) * rows, :wide]
        out_ref[1, xl, :, :rest] = first[xl * rows:(xl + 1) * rows, wide:]

    @pl.when(core == 0)
    def _():
        second = dot(fc[...], gg[:, :384])
        for xl in range(2):
            out_ref[1, xl, :, rest:] = second[xl * rows:(xl + 1) * rows]

    @pl.when(core != 0)
    def _():
        second = dot(fc[...], gg[:, 384:])
        for xl in range(2):
            out_ref[1, xl, :, rest:rest + 256] = second[xl * rows:(xl + 1) * rows]
            out_ref[1, xl, :, rest + 256:] = jnp.zeros((rows, 128), jnp.float32)


def chip_term(core, prev_ok, next_ok, features, sib_features, cotangent, sib_cotangent, halo):
    frames, strip, width = features.shape
    smem = pl.BlockSpec(memory_space=pltpu.SMEM)
    vmem = pl.BlockSpec(memory_space=pltpu.VMEM)
    buf = pltpu.VMEM((2 * frames * strip, width), jnp.bfloat16)
    return pl.pallas_call(
        term_kernel,
        out_shape=jax.ShapeDtypeStruct((2, 2, width // 2, 512), jnp.float32),
        in_specs=[smem] * 3 + [vmem] * 5,
        out_specs=vmem,
        scratch_shapes=[buf, buf, buf],
        compiler_params=pltpu.CompilerParams(vmem_limit_bytes=48 << 20),
        name="chip_term",
    )(core, prev_ok, next_ok, features, sib_features, cotangent, sib_cotangent, halo)


def shards(features, skip_input, cotangent, temporal_weight, clip_lengths, cycle_start):
    frames, strip, width = features.shape
    core = lax.axis_index("c")
    chip = lax.axis_index("xh") * lax.axis_size("z") + lax.axis_index("z")
    n_dp = lax.axis_size(DP)
    total_frames = frames * n_dp
    tokens = frames * strip

    weight_all = lax.all_gather(temporal_weight, FSDP, axis=0, tiled=True)

    both = [(0, 1), (1, 0)]
    sib_features = lax.ppermute(features, "c", both)
    sib_cotangent = lax.ppermute(cotangent, "c", both)
    edge_f = jnp.where(core == 0, features[0], features[-1])
    edge_g = jnp.where(core == 0, cotangent[0], cotangent[-1])
    across = [(d, (d - 1) % n_dp if d % 2 == 0 else (d + 1) % n_dp) for d in range(n_dp)]
    halo = lax.ppermute(jnp.concatenate([edge_f, edge_g], axis=1), DP, across)
    halo_f, halo_g = halo[:, :width], halo[:, width:]

    chip_frames = chip * (2 * frames) + jnp.arange(2 * frames, dtype=jnp.int32)
    prev_all, next_all = border_flags(clip_lengths, cycle_start, chip_frames, total_frames)

    term = chip_term(
        core.astype(jnp.int32).reshape(1), prev_all, next_all,
        features, sib_features, cotangent, sib_cotangent, halo_f,
    )
    n_x, n_y, n_z = lax.axis_size(X), lax.axis_size("y"), lax.axis_size("z")
    part = lax.all_to_all(term.reshape(n_x, width // 2, 512), X, 0, 0, tiled=True).sum(0)
    part = lax.all_to_all(part.reshape(n_y, width // 2 // n_y, 512), "y", 0, 0, tiled=True).sum(0)
    part, weight_all = lax.optimization_barrier((part, weight_all))
    local_rows = part.shape[0]
    blocks = jnp.pad(part, ((0, 48 - local_rows), (0, 0))).reshape(6, 8, 2, 256).transpose(0, 2, 1, 3)
    mine = lax.all_to_all(blocks.reshape(n_z, 8, 256), "z", 0, 0, tiled=True).sum(0)
    mine = mine / jnp.sqrt(jnp.float32(total_frames * strip * lax.axis_size(FSDP)))
    n_xz = 2 * n_z
    gathered = lax.all_to_all(jnp.broadcast_to(mine[None], (n_xz, 8, 256)), ("xh", "z"), 0, 0, tiled=True)
    other = lax.ppermute(gathered, "c", both)

    def flat(a):
        a = a.reshape(2, 6, 2, 8, 256).transpose(1, 3, 0, 2, 4)
        return a.reshape(48, 1024)[:local_rows]

    low = flat(jnp.where(core == 0, gathered, other))
    high = flat(jnp.where(core == 0, other, gathered))
    grad_weight = jnp.concatenate([low, high[:, 640:896], high[:, :640]], axis=1)

    own = core * frames
    prev_scale = lax.dynamic_slice_in_dim(prev_all, own, frames).astype(jnp.bfloat16)[:, None, None]
    next_scale = lax.dynamic_slice_in_dim(next_all, own, frames).astype(jnp.bfloat16)[:, None, None]

    def around(x, sib, edge):
        before = jnp.where(core == 0, edge, sib[-1])[None]
        after = jnp.where(core == 0, sib[0], edge)[None]
        wide = jnp.concatenate([before, x, after], axis=0)
        return prev_scale * wide[:-2], next_scale * wide[2:]

    features_prev, features_next = around(features, sib_features, halo_f)
    cot_prev, cot_next = around(cotangent, sib_cotangent, halo_g)
    kernel_rows = weight_all.reshape(width, 3, width)
    stacked_in = jnp.stack([features_prev, features, features_next], axis=2).reshape(tokens, 3, width)
    stacked_back = jnp.stack([cot_next, cotangent, cot_prev], axis=2).reshape(tokens, 3, width)
    mixed = jnp.einsum("nkr,rkc->nc", stacked_in, kernel_rows, preferred_element_type=jnp.float32)
    back = jnp.einsum("nkc,rkc->nr", stacked_back, kernel_rows, preferred_element_type=jnp.float32)
    block_out = (skip_input.astype(jnp.float32) + mixed.reshape(frames, strip, width)).astype(jnp.bfloat16)
    grad_features = back.reshape(frames, strip, width).astype(jnp.bfloat16)
    return (block_out, grad_features, grad_weight)


def solution(mesh):
    split = Mesh(mesh.devices.reshape(2, 12, 2, 2, 8), DP + FSDP)
    tokens = P(DP, FSDP, None)
    in_specs = (tokens, tokens, tokens, P(FSDP, None), P(), P())
    out_specs = (tokens, tokens, P(FSDP, None))
    return jax.shard_map(shards, mesh=split, in_specs=in_specs, out_specs=out_specs, check_vma=False)
```

time: 577 us -> 170 us (0.29)
  waiting for transfers between devices: 524 us -> 15.7 us
  blocking collectives: 0 us -> 68.6 us
  starting transfers between devices: 14.5 us -> 47.6 us
    psum x1 -> x0, waiting for transfers between devices: 392 us -> none  [shards(): summed = lax.psum(strip_sum, 'dp')]
    unnamed x4 -> x1, waiting for transfers between devices: 81.9 us -> 0.02 us
    all_to_all x0 -> x2, blocking collectives: none -> 68.6 us  [the longest x1 51.6 us: shards(): lax.all_to_all(term.reshape(n_x, width // 2, 512), X, 0, 0, tiled=True)]
    all_gather x1, waiting for transfers between devices: 50.2 us -> 0.02 us  [shards(): weight_all = lax.all_gather(temporal_weight, FSDP, axis=0, tiled=True)]
    all_to_all x0 -> x2, starting transfers between devices: none -> 25.3 us  [the longest x1 21.4 us: shards(): lax.all_to_all(blocks.reshape(n_z, 8, 256), 'z', 0, 0, tiled=True).sum(0)]
    all_to_all x0 -> x2, waiting for transfers between devices: none -> 14.3 us  [the longest x1 9.95 us: shards(): lax.all_to_all(blocks.reshape(n_z, 8, 256), 'z', 0, 0, tiled=True).sum(0)]
    ppermute x2 -> x4, starting transfers between devices: 14.3 us -> 22.3 us  [the longest x1 12.4 us: shards(): sib_features = lax.ppermute(features, 'c', both)]
    reshape x1 -> x0, local copies, waits for them, and re-layouts: 5.82 us -> none  [shards(): term.reshape(local_rows * lax.axis_size('fsdp'), 3 * width)]
  transfers between devices with their start and end apart: 5 -> 7, of which waited for: 3 -> 3; matrix products, arithmetic and copies ran while one was open for 4% -> 10% of each run, Pallas kernels for 0% -> 1%
where the time goes in v1:
time: 170 us
  blocking collectives  68.6 us (40%)
  starting transfers between devices  47.6 us (28%)
  waiting for transfers between devices  15.7 us (9%)
  between operations  14.9 us (9%)
  local copies, waits for them, and re-layouts  7.1 us (4%)
  other arithmetic  7.01 us (4%)
  matrix products  6.69 us (4%)
  Pallas kernels  1.82 us (1%)
    all_to_all x1, blocking collectives, shards(): lax.all_to_all(term.reshape(n_x, width // 2, 512), X, 0, 0, tiled=True)  51.6 us
    all_to_all x1, starting transfers between devices, shards(): lax.all_to_all(blocks.reshape(n_z, 8, 256), 'z', 0, 0, tiled=True).sum(0)  21.4 us
    all_to_all x1, blocking collectives, shards(): lax.all_to_all(part.reshape(n_y, width // 2 // n_y, 512), 'y', 0, 0, tile...  17 us
    ppermute x1, starting transfers between devices, shards(): sib_features = lax.ppermute(features, 'c', both)  12.4 us
    all_to_all x1, waiting for transfers between devices, shards(): lax.all_to_all(blocks.reshape(n_z, 8, 256), 'z', 0, 0, tiled=True).sum(0)  9.95 us
    ppermute x1, starting transfers between devices, shards(): other = lax.ppermute(gathered, 'c', both)  6.07 us
    all_to_all x1, waiting for transfers between devices, shards(): lax.all_to_all(jnp.broadcast_to(mine[None], (n_xz, 8, 256)), ('xh', 'z'),...  4.38 us
    all_to_all x1, starting transfers between devices, shards(): lax.all_to_all(jnp.broadcast_to(mine[None], (n_xz, 8, 256)), ('xh', 'z'),...  3.83 us
  transfers between devices with their start and end apart: 7, of which 3 were waited for; matrix products, arithmetic and copies ran while one was open for 10% of the time, Pallas kernels for 1%

profile of v1, /device:TPU:1, one launch (start us, length us, event | category | flops | bytes accessed | tf_op | source)
XLA Modules:
  0.0 169.5 jit_solution(699131355263564955)
XLA Ops:
  7.2 12.4 %collective-permute-start.1 = (bf16[8,32,640]{2,1,0:T(8,128)(2,1)}, bf16[8,32,640]{2,1,0:T(8,128)(2,1)S(1)}, u32[]{:S(2)}, u32[]{:S(2)}) collective-permute-start(bf16[8,32,640]{2,1,0:T(8,128)(2,1)} %f_ref.1), channel_id=1, source_target_pairs={{0,16},{16,0},{1,17},{17,1},{2,18},{18,2},{3,19},{19,3},{4,20},{20... | collective-permute-start | bytes 983048 | tf_op jit(solution)/shard_map/ppermute | solution.py:97
  19.6 1.9 %collective-permute-start.2 = (bf16[8,32,640]{2,1,0:T(8,128)(2,1)}, bf16[8,32,640]{2,1,0:T(8,128)(2,1)S(1)}, u32[]{:S(2)}, u32[]{:S(2)}) collective-permute-start(bf16[8,32,640]{2,1,0:T(8,128)(2,1)} %g_ref.1), channel_id=1, source_target_pairs={{0,16},{16,0},{1,17},{17,1},{2,18},{18,2},{3,19},{19,3},{4,20},{20... | collective-permute-start | bytes 983048 | tf_op jit(solution)/shard_map/ppermute | solution.py:98
  21.6 0.8 select_bitcast_fusion
  22.4 0.8 select_bitcast_fusion.1
  23.2 1.9 %collective-permute-start = (bf16[32,1280]{1,0:T(8,128)(2,1)S(1)}, bf16[32,1280]{1,0:T(8,128)(2,1)S(1)}, u32[]{:S(2)}, u32[]{:S(2)}) collective-permute-start(bf16[32,1280]{1,0:T(8,128)(2,1)S(1)} %pad_maximum_fusion.6), channel_id=1, source_target_pairs={{0,752},{16,32},{32,16},{48,64},{64,48},{80,96},{96,80},{112,128},... | collective-permute-start | bytes 245768 | tf_op jit(solution)/shard_map/ppermute | solution.py:102
  25.2 0.7 copy.29
  27.7 1.3 collective-permute-done
  29.0 1.0 copy-done
  30.0 1.0 copy-done.2
  31.0 1.8 %chip_term.1 = f32[2,2,320,512]{3,2,1,0:T(8,128)S(1)} custom-call(s32[1]{0:T(128)} %bitcast.11.core_ref, s32[16]{0:T(128)S(1)} %convert_subtract_fusion.1.prev_ref, s32[16]{0:T(128)S(1)} %convert_subtract_fusion.next_ref, bf16[8,32,640]{2,1,0:T(8,128)(2,1)S(1)} %copy-done.2, bf16[8,32,640]{2,1,0:T(8,128)(2,1)S(1)} %collective-permute-done.1.sf_ref, ...), custom_call_target="tpu_custom_call" | custom-call | tf_op jit(solution)/shard_map/chip_term/pallas_call | solution.py:75
  32.8 51.6 %all_to_all.20 = f32[4,320,512]{2,1,0:T(8,128)S(1)} all-to-all(f32[4,320,512]{2,1,0:T(8,128)S(1)} %bitcast.84), channel_id=1, replica_groups=mesh['xh'=2,'z'=12,'c'=2,'xl'=2,'y'=8] {'xh','xl'}, dimensions={0} | all-to-all | bytes 5242880 | tf_op jit(solution)/shard_map/all_to_all | solution.py:113
  84.4 1.2 reduce_sum.27
  85.6 17.0 %all_to_all.21 = f32[8,40,512]{2,1,0:T(8,128)S(1)} all-to-all(f32[8,40,512]{2,1,0:T(8,128)} %bitcast.87), channel_id=1, replica_groups=mesh['xh'=2,'z'=12,'c'=2,'xl'=2,'y'=8] {'y'}, dimensions={0} | all-to-all | bytes 1310720 | tf_op jit(solution)/shard_map/all_to_all | solution.py:114
  103.3 21.4 %all-to-all-start.2 = ((f32[12,8,256]{2,1,0:T(8,128)}), f32[12,8,256]{2,1,0:T(8,128)S(1)}, u32[]{:S(2)}, u32[]{:S(2)}) async-start(f32[12,8,256]{2,1,0:T(8,128)} %bitcast.31), calls=%async_computation.2 | async-start | bytes 196608 | tf_op jit(solution)/shard_map/all_to_all | solution.py:118
  124.9 9.9 %all-to-all-done.2 = f32[12,8,256]{2,1,0:T(8,128)S(1)} async-done(((f32[12,8,256]{2,1,0:T(8,128)}), f32[12,8,256]{2,1,0:T(8,128)S(1)}, u32[]{:S(2)}, u32[]{:S(2)}) %all-to-all-start.2) | async-done | bytes 98336 | tf_op jit(solution)/shard_map/all_to_all | solution.py:118
  135.6 3.8 %all-to-all-start.3 = ((f32[24,8,256]{2,1,0:T(8,128)}), f32[24,8,256]{2,1,0:T(8,128)S(1)}, u32[]{:S(2)}, u32[]{:S(2)}) async-start(f32[24,8,256]{2,1,0:T(8,128)} %broadcast_in_dim.28), calls=%async_computation.3 | async-start | bytes 393216 | tf_op jit(solution)/shard_map/all_to_all | solution.py:121
  139.5 1.1 fusion.13
  140.5 1.1 pad_maximum_fusion
  141.6 2.6 %copy.30 = bf16[640,1920]{0,1:T(8,128)(2,1)} copy(bf16[640,1920]{1,0:T(8,128)(2,1)S(1)} %copy-done.4) | data formatting | bytes 4915200 | tf_op jit(solution)/shard_map/optimization_barrier | solution.py:115
  144.2 3.8 %fusion.1 = bf16[8,32,640]{2,1,0:T(8,128)(2,1)} fusion(bf16[640,3,640,1]{0,2,1,3:T(8,128)(2,1)} %bitcast.88, bf16[8,32,1,640]{3,1,2,0:T(8,128)(2,1)} %get-tuple-element.18, bf16[8,32,1,640]{3,1,2,0:T(8,128)(2,1)S(1)} %bitcast.86, bf16[8,32,1,640]{3,1,2,0:T(8,128)(2,1)} %get-tuple-element.17, bf16[8,32,640]{2,1,0:T(8,128)(2,1)} %param.7), kind=kOutput, calls=%fused_computation.3 | convolution fusion | flops 630620160 | bytes 4096000 | tf_op jit(solution)/shard_map/nkr,rkc->nc/dot_general | solution.py:147
  148.0 4.4 %all-to-all-done.3 = f32[24,8,256]{2,1,0:T(8,128)S(1)} async-done(((f32[24,8,256]{2,1,0:T(8,128)}), f32[24,8,256]{2,1,0:T(8,128)S(1)}, u32[]{:S(2)}, u32[]{:S(2)}) %all-to-all-start.3) | async-done | bytes 196640 | tf_op jit(solution)/shard_map/all_to_all | solution.py:121
  152.4 6.1 %collective-permute-start.3 = (f32[24,8,256]{2,1,0:T(8,128)S(1)}, f32[24,8,256]{2,1,0:T(8,128)S(1)}, u32[]{:S(2)}, u32[]{:S(2)}) collective-permute-start(f32[24,8,256]{2,1,0:T(8,128)S(1)} %all-to-all-done.3), channel_id=1, source_target_pairs={{0,16},{16,0},{1,17},{17,1},{2,18},{18,2},{3,19},{19,3},{4,20},{20... | collective-permute-start | bytes 589832 | tf_op jit(solution)/shard_map/ppermute | solution.py:122
  158.5 2.9 %fusion.2 = bf16[8,32,640]{2,1,0:T(8,128)(2,1)} fusion(bf16[8,32,640,3]{2,1,0,3:T(8,128)(2,1)} %bitcast.92, bf16[640,3,640,1]{0,2,3,1:T(8,128)(2,1)S(1)} %bitcast.89), kind=kOutput, calls=%fused_computation.4 | convolution fusion | flops 629309440 | bytes 3768320 | tf_op jit(solution)/shard_map/nkc,rkc->nr/dot_general | solution.py:148
  161.9 0.7 pad_maximum_fusion.5
  (41 shorter events, 3.3 us)
Async XLA Ops:
  7.2 95.5 %all-gather.2.cloned.1.call-start = ((), (), s32[]{:S(2)}) async-start(), calls=%async_computation.4 | async-start | bytes 2611200 | tf_op jit(solution)/shard_map/all_gather | solution.py:94
  7.2 21.8 %collective-permute-start.1 = (bf16[8,32,640]{2,1,0:T(8,128)(2,1)}, bf16[8,32,640]{2,1,0:T(8,128)(2,1)S(1)}, u32[]{:S(2)}, u32[]{:S(2)}) collective-permute-start(bf16[8,32,640]{2,1,0:T(8,128)(2,1)} %f_ref.1), channel_id=1, source_target_pairs={{0,16},{16,0},{1,17},{17,1},{2,18},{18,2},{3,19},{19,3},{4,20},{20... | collective-permute-start | bytes 983048 | tf_op jit(solution)/shard_map/ppermute | solution.py:97
  19.6 9.4 %collective-permute-start.2 = (bf16[8,32,640]{2,1,0:T(8,128)(2,1)}, bf16[8,32,640]{2,1,0:T(8,128)(2,1)S(1)}, u32[]{:S(2)}, u32[]{:S(2)}) collective-permute-start(bf16[8,32,640]{2,1,0:T(8,128)(2,1)} %g_ref.1), channel_id=1, source_target_pairs={{0,16},{16,0},{1,17},{17,1},{2,18},{18,2},{3,19},{19,3},{4,20},{20... | collective-permute-start | bytes 983048 | tf_op jit(solution)/shard_map/ppermute | solution.py:98
  23.2 5.8 %collective-permute-start = (bf16[32,1280]{1,0:T(8,128)(2,1)S(1)}, bf16[32,1280]{1,0:T(8,128)(2,1)S(1)}, u32[]{:S(2)}, u32[]{:S(2)}) collective-permute-start(bf16[32,1280]{1,0:T(8,128)(2,1)S(1)} %pad_maximum_fusion.6), channel_id=1, source_target_pairs={{0,752},{16,32},{32,16},{48,64},{64,48},{80,96},{96,80},{112,128},... | collective-permute-start | bytes 245768 | tf_op jit(solution)/shard_map/ppermute | solution.py:102
  29.0 1.0 copy-start
  30.0 1.0 copy-start.2
  84.4 55.1 %copy-start.1 = (bf16[8,32,640]{2,1,0:T(8,128)(2,1)S(1)}, bf16[8,32,640]{2,1,0:T(8,128)(2,1)}, u32[]{:S(2)}) copy-start(bf16[8,32,640]{2,1,0:T(8,128)(2,1)} %g_ref.1) | copy-start | bytes 983044
  84.4 55.1 %copy-start.3 = (bf16[8,32,640]{2,1,0:T(8,128)(2,1)S(1)}, bf16[8,32,640]{2,1,0:T(8,128)(2,1)}, u32[]{:S(2)}) copy-start(bf16[8,32,640]{2,1,0:T(8,128)(2,1)} %f_ref.1) | copy-start | bytes 983044
  103.3 31.5 %all-to-all-start.2 = ((f32[12,8,256]{2,1,0:T(8,128)}), f32[12,8,256]{2,1,0:T(8,128)S(1)}, u32[]{:S(2)}, u32[]{:S(2)}) async-start(f32[12,8,256]{2,1,0:T(8,128)} %bitcast.31), calls=%async_computation.2 | async-start | bytes 196608 | tf_op jit(solution)/shard_map/all_to_all | solution.py:118
  124.8 16.8 %copy-start.4 = (bf16[640,1920]{1,0:T(8,128)(2,1)S(1)}, bf16[640,1920]{1,0:T(8,128)(2,1)}, u32[]{:S(2)}) copy-start(bf16[640,1920]{1,0:T(8,128)(2,1)} %all-gather.2.cloned.1.call-done) | copy-start | bytes 7372804
  135.6 16.8 %all-to-all-start.3 = ((f32[24,8,256]{2,1,0:T(8,128)}), f32[24,8,256]{2,1,0:T(8,128)S(1)}, u32[]{:S(2)}, u32[]{:S(2)}) async-start(f32[24,8,256]{2,1,0:T(8,128)} %broadcast_in_dim.28), calls=%async_computation.3 | async-start | bytes 393216 | tf_op jit(solution)/shard_map/all_to_all | solution.py:121
  144.2 14.3 %copy-start.5 = (bf16[640,1920]{0,1:T(8,128)(2,1)S(1)}, bf16[640,1920]{0,1:T(8,128)(2,1)}, u32[]{:S(2)}) copy-start(bf16[640,1920]{0,1:T(8,128)(2,1)} %copy.30) | copy-start | bytes 7372804
  152.4 9.0 %collective-permute-start.3 = (f32[24,8,256]{2,1,0:T(8,128)S(1)}, f32[24,8,256]{2,1,0:T(8,128)S(1)}, u32[]{:S(2)}, u32[]{:S(2)}) collective-permute-start(f32[24,8,256]{2,1,0:T(8,128)S(1)} %all-to-all-done.3), channel_id=1, source_target_pairs={{0,16},{16,0},{1,17},{17,1},{2,18},{18,2},{3,19},{19,3},{4,20},{20... | collective-permute-start | bytes 589832 | tf_op jit(solution)/shard_map/ppermute | solution.py:122
Sparse Core Ops, SparseCore 0:
  21.7 66.6 all-gather.1

commit v2 on v1

v2 whole, which is shorter than its diff:
```python
import jax
import jax.numpy as jnp
from jax import lax
from jax.experimental import pallas as pl
from jax.experimental.pallas import tpu as pltpu
from jax.sharding import Mesh, PartitionSpec as P

DP = ("xh", "z", "c")
FSDP = ("xl", "y")
X = ("xh", "xl")


def border_flags(clip_lengths, cycle_start, frame_index, total):
    starts = jnp.cumsum(clip_lengths) - clip_lengths
    position = jnp.mod(frame_index - cycle_start[0], total)
    following = jnp.mod(frame_index + 1 - cycle_start[0], total)
    first_here = jnp.any(position[:, None] == starts[None, :], axis=1)
    first_next = jnp.any(following[:, None] == starts[None, :], axis=1)
    return (1 - first_here.astype(jnp.int32), 1 - first_next.astype(jnp.int32))


def pack_kernel(f_ref, g_ref, out_ref):
    frames, strip, width = f_ref.shape
    f = f_ref[...].reshape(frames * strip, width)
    g = g_ref[...].reshape(frames * strip, width)
    f_mid, g_mid = f[:, 256:384], g[:, 256:384]
    f_rolled, g_rolled = [pltpu.roll(m.astype(jnp.float32), 64, 1).astype(jnp.bfloat16) for m in (f_mid, g_mid)]
    left = lax.broadcasted_iota(jnp.int32, f_mid.shape, 1) < 64
    for xh in range(2):
        for xl in range(2):
            j = 2 * xh + xl
            out_ref[j, :, :256] = f[:, 384 * xl:384 * xl + 256]
            out_ref[j, :, 256:384] = jnp.where(left, f_rolled if xl else f_mid, g_mid if xh else g_rolled)
            out_ref[j, :, 384:] = g[:, 384 * xh:384 * xh + 256]


def pack(features, cotangent):
    frames, strip, width = features.shape
    vmem = pl.BlockSpec(memory_space=pltpu.VMEM)
    return pl.pallas_call(
        pack_kernel,
        out_shape=jax.ShapeDtypeStruct((4, frames * strip, width), jnp.bfloat16),
        in_specs=[vmem] * 2,
        out_specs=vmem,
        compiler_params=pltpu.CompilerParams(vmem_limit_bytes=48 << 20),
        name="pack",
    )(features, cotangent)


def term_kernel(place_ref, prev_ref, next_ref, own_ref, sib_ref, halo_ref, out_ref, fa_own, fa_sib):
    chips, frames, strip, _ = own_ref.shape
    core, xl, wrapped = place_ref[0], place_ref[1], place_ref[2]

    def put(dst, chip, slot, value, ok):
        dst[pl.ds((chip * frames + slot) * strip, strip), :] = jnp.where(ok != 0, value, jnp.zeros_like(value))

    def halo(chip):
        return halo_ref[(chip // 2 + wrapped) % 2 * 2 + chip % 2]

    @pl.when(core == 0)
    def _():
        for chip in range(chips):
            at = chip // 2 * 2 * frames
            for j in range(frames):
                mine = halo(chip) if j == 0 else own_ref[chip, j - 1, :, :384]
                its = own_ref[chip, frames - 1, :, :384] if j == 0 else sib_ref[chip, j - 1, :, :384]
                put(fa_own, chip, j, mine, prev_ref[at + j])
                put(fa_sib, chip, j, its, prev_ref[at + frames + j])

    @pl.when(core != 0)
    def _():
        for chip in range(chips):
            at = chip // 2 * 2 * frames
            for j in range(frames):
                mine = halo(chip) if j == frames - 1 else own_ref[chip, j + 1, :, :384]
                its = own_ref[chip, 0, :, :384] if j == frames - 1 else sib_ref[chip, j + 1, :, :384]
                put(fa_own, chip, j, mine, next_ref[at + frames + j])
                put(fa_sib, chip, j, its, next_ref[at + j])

    def flat(ref, start, stop):
        return ref[:, :, :, start:stop].reshape(chips * frames * strip, stop - start)

    def dot(a, b):
        return lax.dot_general(a, b, (((0,), (0,)), ((), ())), preferred_element_type=jnp.float32)

    def center(start, stop):
        return dot(flat(own_ref, 0, 384), flat(own_ref, start, stop)) + dot(flat(sib_ref, 0, 384), flat(sib_ref, start, stop))

    outer = dot(fa_own[...], flat(own_ref, 256, 640)) + dot(fa_sib[...], flat(sib_ref, 256, 640))
    left = lax.broadcasted_iota(jnp.int32, (384, 128), 1) < 64
    rolled = pltpu.roll(outer[:, :128], 64, 1)

    def store(start, stop, value):
        @pl.when(xl == 0)
        def _():
            out_ref[:, start:stop] = value[:320]

        @pl.when(xl != 0)
        def _():
            out_ref[64:, start:stop] = value[:256]
            out_ref[:64, start:stop] = value[256:320]

    store(0, 256, outer[:, 128:])

    @pl.when(core == 0)
    def _():
        mid = center(256, 512)
        store(256, 384, jnp.where(left, rolled, mid[:, :128]))
        store(384, 512, mid[:, 128:])

    @pl.when(core != 0)
    def _():
        store(256, 384, jnp.where(left, rolled, jnp.zeros_like(rolled)))
        store(384, 512, center(512, 640))


def x_term(place, prev_ok, next_ok, own, sib, halo):
    smem = pl.BlockSpec(memory_space=pltpu.SMEM)
    vmem = pl.BlockSpec(memory_space=pltpu.VMEM)
    chips, frames, strip, _ = own.shape
    buf = pltpu.VMEM((chips * frames * strip, 384), jnp.bfloat16)
    return pl.pallas_call(
        term_kernel,
        out_shape=jax.ShapeDtypeStruct((320, 512), jnp.float32),
        in_specs=[smem] * 3 + [vmem] * 3,
        out_specs=vmem,
        scratch_shapes=[buf, buf],
        compiler_params=pltpu.CompilerParams(vmem_limit_bytes=48 << 20),
        name="x_term",
    )(place, prev_ok, next_ok, own, sib, halo)


def shards(features, skip_input, cotangent, temporal_weight, clip_lengths, cycle_start):
    frames, strip, width = features.shape
    core, xl, xh, z = [lax.axis_index(a) for a in ("c", "xl", "xh", "z")]
    n_x, n_y, n_z = lax.axis_size(X), lax.axis_size("y"), lax.axis_size("z")
    n_dp = lax.axis_size(DP)
    total_frames = frames * n_dp
    tokens = frames * strip

    weight_all = lax.all_gather(temporal_weight, FSDP, axis=0, tiled=True)

    both = [(0, 1), (1, 0)]
    own = lax.all_to_all(pack(features, cotangent), X, 0, 0, tiled=True).reshape(n_x, frames, strip, width)
    sib = lax.ppermute(own, "c", both)
    z_next = [(2 * i, (2 * i - 1) % (2 * n_z)) for i in range(n_z)] + [(2 * i + 1, (2 * i + 2) % (2 * n_z)) for i in range(n_z)]
    edge = jnp.where(core == 0, own[:, 0, :, :384], own[:, -1, :, :384])
    halo_x = lax.ppermute(edge, ("z", "c"), z_next)

    first = (jnp.arange(2, dtype=jnp.int32) * n_z + z)[:, None] * (2 * frames)
    chip_frames = (first + jnp.arange(2 * frames, dtype=jnp.int32)).reshape(-1)
    prev_all, next_all = border_flags(clip_lengths, cycle_start, chip_frames, total_frames)
    wrapped = jnp.where(core == 0, z == 0, z == n_z - 1)
    place = jnp.stack([core, xl, wrapped.astype(jnp.int32)]).astype(jnp.int32)
    term = x_term(place, prev_all, next_all, own, sib, halo_x)

    part = lax.all_to_all(term.reshape(n_y, 320 // n_y, 512), "y", 0, 0, tiled=True).sum(0)
    part, weight_all = lax.optimization_barrier((part, weight_all))
    local_rows = part.shape[0]
    blocks = jnp.pad(part, ((0, 48 - local_rows), (0, 0))).reshape(6, 8, 2, 256).transpose(0, 2, 1, 3)
    mine = lax.all_to_all(blocks.reshape(n_z, 8, 256), "z", 0, 0, tiled=True).sum(0)
    mine = mine / jnp.sqrt(jnp.float32(total_frames * strip * lax.axis_size(FSDP)))
    n_xz = 2 * n_z
    gathered = lax.all_to_all(jnp.broadcast_to(mine[None], (n_xz, 8, 256)), ("xh", "z"), 0, 0, tiled=True)
    other = lax.ppermute(gathered, "c", both)

    def flat(a):
        a = a.reshape(2, 6, 2, 8, 256).transpose(0, 1, 3, 2, 4)
        return a.reshape(2, 48, 512)[:, :local_rows]

    low = flat(jnp.where(core == 0, gathered, other))
    high = flat(jnp.where(core == 0, other, gathered))

    def outer_tap(b):
        return [b[0, :, :320], b[1, :, 256:320], b[1, :, :256]]

    tap_1 = [low[0, :, 384:], high[0, :, 384:], low[0, :, 320:384], low[1, :, 320:], high[1, :, 384:]]
    grad_weight = jnp.concatenate(outer_tap(low) + tap_1 + outer_tap(high), axis=1)

    ends = [jnp.concatenate([features[i], cotangent[i]], axis=1) for i in (0, -1)]
    sib_edge = lax.ppermute(jnp.where(core == 0, ends[1], ends[0]), "c", both)
    across = [(d, (d - 1) % n_dp if d % 2 == 0 else (d + 1) % n_dp) for d in range(n_dp)]
    halo = lax.ppermute(jnp.where(core == 0, ends[0], ends[1]), DP, across)
    before = jnp.where(core == 0, halo, sib_edge)[None]
    after = jnp.where(core == 0, sib_edge, halo)[None]
    at = xh * (2 * frames) + core * frames
    prev_scale = lax.dynamic_slice_in_dim(prev_all, at, frames).astype(jnp.bfloat16)[:, None, None]
    next_scale = lax.dynamic_slice_in_dim(next_all, at, frames).astype(jnp.bfloat16)[:, None, None]

    def around(x, lanes):
        wide = jnp.concatenate([before[:, :, lanes], x, after[:, :, lanes]], axis=0)
        return prev_scale * wide[:-2], next_scale * wide[2:]

    features_prev, features_next = around(features, slice(0, width))
    cot_prev, cot_next = around(cotangent, slice(width, 2 * width))
    kernel_rows = weight_all.reshape(width, 3, width)
    stacked_in = jnp.stack([features_prev, features, features_next], axis=2).reshape(tokens, 3, width)
    stacked_back = jnp.stack([cot_next, cotangent, cot_prev], axis=2).reshape(tokens, 3, width)
    mixed = jnp.einsum("nkr,rkc->nc", stacked_in, kernel_rows, preferred_element_type=jnp.float32)
    back = jnp.einsum("nkc,rkc->nr", stacked_back, kernel_rows, preferred_element_type=jnp.float32)
    block_out = (skip_input.astype(jnp.float32) + mixed.reshape(frames, strip, width)).astype(jnp.bfloat16)
    grad_features = back.reshape(frames, strip, width).astype(jnp.bfloat16)
    return (block_out, grad_features, grad_weight)


def solution(mesh):
    split = Mesh(mesh.devices.reshape(2, 12, 2, 2, 8), DP + FSDP)
    tokens = P(DP, FSDP, None)
    in_specs = (tokens, tokens, tokens, P(FSDP, None), P(), P())
    out_specs = (tokens, tokens, P(FSDP, None))
    return jax.shard_map(shards, mesh=split, in_specs=in_specs, out_specs=out_specs, check_vma=False)
```

time: 170 us -> 158 us (0.929)
  blocking collectives: 68.6 us -> 0 us
  waiting for transfers between devices: 15.7 us -> 49.7 us
  starting transfers between devices: 47.6 us -> 71.5 us
  other arithmetic: 7.01 us -> 3.01 us
  Pallas kernels: 1.82 us -> 4.54 us
    all_to_all x2 -> x0, blocking collectives: 68.6 us -> none  [the longest x1 51.6 us: shards(): lax.all_to_all(term.reshape(n_x, width // 2, 512), X, 0, 0, tiled=True)]
    all_gather x1, waiting for transfers between devices: 0.02 us -> 19.2 us  [shards(): weight_all = lax.all_gather(temporal_weight, FSDP, axis=0, tiled=True)]
    ppermute x3 -> x4, starting transfers between devices: 16.3 us -> 32.1 us  [the longest x1 14.4 us: shards(): sib_edge = lax.ppermute(jnp.where(core == 0, ends[1], ends[0]), 'c', both)]
    all_to_all x0 -> x2, waiting for transfers between devices: none -> 10.2 us  [the longest x1 10.2 us: shards(): lax.all_to_all(pack(features, cotangent), X, 0, 0, tiled=True)]
    all_to_all x0 -> x2, starting transfers between devices: none -> 9.31 us  [the longest x1 4.84 us: shards(): lax.all_to_all(pack(features, cotangent), X, 0, 0, tiled=True)]
    all_to_all x1, starting transfers between devices: 21.4 us -> 12.2 us  [shards(): lax.all_to_all(blocks.reshape(n_z, 8, 256), 'z', 0, 0, tiled=True).sum(0)]
    ppermute x1, starting transfers between devices: 6.07 us -> 13.2 us  [shards(): other = lax.ppermute(gathered, 'c', both)]
    ppermute x3 -> x4, waiting for transfers between devices: 1.35 us -> 5.07 us  [the longest x1 4.33 us: shards(): halo_x = lax.ppermute(edge, ('z', 'c'), z_next)]
  transfers between devices with their start and end apart: 7 -> 10, of which waited for: 3 -> 6; matrix products, arithmetic and copies ran while one was open for 10% -> 8% of each run, Pallas kernels for 1% -> 3%
where the time goes in v2:
time: 158 us
  starting transfers between devices  71.5 us (45%)
  waiting for transfers between devices  49.7 us (31%)
  between operations  15 us (9%)
  local copies, waits for them, and re-layouts  7.19 us (5%)
  matrix products  6.6 us (4%)
  Pallas kernels  4.54 us (3%)
  other arithmetic  3.01 us (2%)
    all_gather x1, waiting for transfers between devices, shards(): weight_all = lax.all_gather(temporal_weight, FSDP, axis=0, tiled=True)  19.2 us
    ppermute x1, starting transfers between devices, shards(): sib_edge = lax.ppermute(jnp.where(core == 0, ends[1], ends[0]), 'c', both)  14.4 us
    ppermute x1, starting transfers between devices, shards(): other = lax.ppermute(gathered, 'c', both)  13.2 us
    ppermute x1, starting transfers between devices, shards(): sib = lax.ppermute(own, 'c', both)  12.2 us
    all_to_all x1, starting transfers between devices, shards(): lax.all_to_all(blocks.reshape(n_z, 8, 256), 'z', 0, 0, tiled=True).sum(0)  12.2 us
    all_to_all x1, waiting for transfers between devices, shards(): lax.all_to_all(pack(features, cotangent), X, 0, 0, tiled=True)  10.2 us
    all_to_all x1, waiting for transfers between devices, shards(): lax.all_to_all(blocks.reshape(n_z, 8, 256), 'z', 0, 0, tiled=True).sum(0)  10.1 us
    all_to_all x1, starting transfers between devices, shards(): lax.all_to_all(pack(features, cotangent), X, 0, 0, tiled=True)  4.84 us
  transfers between devices with their start and end apart: 10, of which 6 were waited for; matrix products, arithmetic and copies ran while one was open for 8% of the time, Pallas kernels for 3%

profile of v2, /device:TPU:1, one launch (start us, length us, event | category | flops | bytes accessed | tf_op | source)
XLA Modules:
  0.0 157.5 jit_solution(17866514548685135906)
XLA Ops:
  7.9 1.0 copy-done
  8.9 1.0 copy-done.2
  9.9 1.2 pack.1
  11.0 4.8 %all-to-all-start = ((bf16[4,256,640]{2,1,0:T(8,128)(2,1)}), bf16[4,256,640]{2,1,0:T(8,128)(2,1)S(1)}, u32[]{:S(2)}, u32[]{:S(2)}) async-start(bf16[4,256,640]{2,1,0:T(8,128)(2,1)} %pack.1), calls=%async_computation | async-start | bytes 2621440 | tf_op jit(solution)/shard_map/all_to_all | solution.py:144
  16.8 10.2 %all-to-all-done = bf16[4,256,640]{2,1,0:T(8,128)(2,1)S(1)} async-done(((bf16[4,256,640]{2,1,0:T(8,128)(2,1)}), bf16[4,256,640]{2,1,0:T(8,128)(2,1)S(1)}, u32[]{:S(2)}, u32[]{:S(2)}) %all-to-all-start) | async-done | bytes 1310752 | tf_op jit(solution)/shard_map/all_to_all | solution.py:144
  27.0 12.2 %collective-permute-start.2 = (bf16[4,8,32,640]{3,2,1,0:T(8,128)(2,1)S(1)}, bf16[4,8,32,640]{3,2,1,0:T(8,128)(2,1)S(1)}, u32[]{:S(2)}, u32[]{:S(2)}) collective-permute-start(bf16[4,8,32,640]{3,2,1,0:T(8,128)(2,1)S(1)} %bitcast.100), channel_id=1, source_target_pairs={{0,16},{16,0},{1,17},{17,1},{2,18},{18,2},{3,19},{19,3},{4,20},{20... | collective-permute-start | bytes 3932168 | tf_op jit(solution)/shard_map/ppermute | solution.py:145
  39.8 2.1 %collective-permute-start.3 = (bf16[4,32,384]{2,1,0:T(8,128)(2,1)S(1)}, bf16[4,32,384]{2,1,0:T(8,128)(2,1)S(1)}, u32[]{:S(2)}, u32[]{:S(2)}) collective-permute-start(bf16[4,32,384]{2,1,0:T(8,128)(2,1)S(1)} %fusion.15), channel_id=1, source_target_pairs={{0,368},{32,16},{64,48},{96,80},{128,112},{160,144},{192,176},{224... | collective-permute-start | bytes 294920 | tf_op jit(solution)/shard_map/ppermute | solution.py:148
  41.9 4.3 %collective-permute-done.3.halo_ref = bf16[4,32,384]{2,1,0:T(8,128)(2,1)S(1)} collective-permute-done((bf16[4,32,384]{2,1,0:T(8,128)(2,1)S(1)}, bf16[4,32,384]{2,1,0:T(8,128)(2,1)S(1)}, u32[]{:S(2)}, u32[]{:S(2)}) %collective-permute-start.3) | collective-permute-done | bytes 98336 | tf_op jit(solution)/shard_map/ppermute | solution.py:148
  46.2 3.4 %x_term.1 = f32[320,512]{1,0:T(8,128)} custom-call(s32[3]{0:T(128)S(1)} %pad_add_fusion.place_ref, s32[32]{0:T(128)S(1)} %get-tuple-element.36.prev_ref, s32[32]{0:T(128)S(1)} %get-tuple-element.35.next_ref, bf16[4,8,32,640]{3,2,1,0:T(8,128)(2,1)S(1)} %bitcast.102, bf16[4,8,32,640]{3,2,1,0:T(8,128)(2,1)S(1)} %collective-permute-done.2.sib_ref, ...), custom_call_target="tpu_custom_call" | custom-call | tf_op jit(solution)/shard_map/x_term/pallas_call | solution.py:122
  49.6 4.5 %all-to-all-start.1 = ((f32[8,40,512]{2,1,0:T(8,128)}), f32[8,40,512]{2,1,0:T(8,128)S(1)}, u32[]{:S(2)}, u32[]{:S(2)}) async-start(f32[8,40,512]{2,1,0:T(8,128)} %bitcast.16), calls=%async_computation.1 | async-start | bytes 1310720 | tf_op jit(solution)/shard_map/all_to_all | solution.py:157
  54.1 3.5 %collective-permute-start = (bf16[32,1280]{1,0:T(8,128)(2,1)S(1)}, bf16[32,1280]{1,0:T(8,128)(2,1)S(1)}, u32[]{:S(2)}, u32[]{:S(2)}) collective-permute-start(bf16[32,1280]{1,0:T(8,128)(2,1)S(1)} %get-tuple-element.25), channel_id=1, source_target_pairs={{0,752},{16,32},{32,16},{48,64},{64,48},{80,96},{96,80},{112,128},... | collective-permute-start | bytes 245768 | tf_op jit(solution)/shard_map/ppermute | solution.py:183
  57.7 14.4 %collective-permute-start.1 = (bf16[32,1280]{1,0:T(8,128)(2,1)S(1)}, bf16[32,1280]{1,0:T(8,128)(2,1)S(1)}, u32[]{:S(2)}, u32[]{:S(2)}) collective-permute-start(bf16[32,1280]{1,0:T(8,128)(2,1)S(1)} %get-tuple-element.26), channel_id=1, source_target_pairs={{0,16},{16,0},{1,17},{17,1},{2,18},{18,2},{3,19},{19,3},{4,20},{20... | collective-permute-start | bytes 245768 | tf_op jit(solution)/shard_map/ppermute | solution.py:181
  73.0 19.2 %all-gather.2.cloned.1.call-done = bf16[640,1920]{1,0:T(8,128)(2,1)} async-done(((bf16[40,1920]{1,0:T(8,128)(2,1)}), bf16[640,1920]{1,0:T(8,128)(2,1)}) %all-gather.2.cloned.1.call-update) | async-done | bytes 2457616 | tf_op jit(solution)/shard_map/all_gather | solution.py:141
  92.9 12.2 %all-to-all-start.2 = ((f32[12,8,256]{2,1,0:T(8,128)}), f32[12,8,256]{2,1,0:T(8,128)S(1)}, u32[]{:S(2)}, u32[]{:S(2)}) async-start(f32[12,8,256]{2,1,0:T(8,128)} %bitcast.30), calls=%async_computation.2 | async-start | bytes 196608 | tf_op jit(solution)/shard_map/all_to_all | solution.py:161
  105.1 10.1 %all-to-all-done.2 = f32[12,8,256]{2,1,0:T(8,128)S(1)} async-done(((f32[12,8,256]{2,1,0:T(8,128)}), f32[12,8,256]{2,1,0:T(8,128)S(1)}, u32[]{:S(2)}, u32[]{:S(2)}) %all-to-all-start.2) | async-done | bytes 98336 | tf_op jit(solution)/shard_map/all_to_all | solution.py:161
  115.9 4.7 %all-to-all-start.3 = ((f32[24,8,256]{2,1,0:T(8,128)}), f32[24,8,256]{2,1,0:T(8,128)S(1)}, u32[]{:S(2)}, u32[]{:S(2)}) async-start(f32[24,8,256]{2,1,0:T(8,128)} %broadcast_in_dim.8), calls=%async_computation.3 | async-start | bytes 393216 | tf_op jit(solution)/shard_map/all_to_all | solution.py:164
  120.6 1.1 fusion.13
  121.6 1.1 pad_maximum_fusion
  122.7 2.6 %copy.30 = bf16[640,1920]{0,1:T(8,128)(2,1)} copy(bf16[640,1920]{1,0:T(8,128)(2,1)S(1)} %copy-done.4) | data formatting | bytes 4915200 | tf_op jit(solution)/shard_map/optimization_barrier | solution.py:158
  125.3 3.7 %fusion.1 = bf16[8,32,640]{2,1,0:T(8,128)(2,1)} fusion(bf16[640,3,640,1]{0,2,1,3:T(8,128)(2,1)} %bitcast.105, bf16[8,32,1,640]{3,1,2,0:T(8,128)(2,1)} %get-tuple-element.14, bf16[8,32,1,640]{3,1,2,0:T(8,128)(2,1)S(1)} %bitcast.104, bf16[8,32,1,640]{3,1,2,0:T(8,128)(2,1)S(1)} %copy-done.6, bf16[8,32,640]{2,1,0:T(8,128)(2,1)} %param.7), kind=kOutput, calls=%fused_computation.3 | convolution fusion | flops 630620160 | bytes 4096000 | tf_op jit(solution)/shard_map/nkr,rkc->nc/dot_general | solution.py:199
  129.0 4.5 %all-to-all-done.3 = f32[24,8,256]{2,1,0:T(8,128)S(1)} async-done(((f32[24,8,256]{2,1,0:T(8,128)}), f32[24,8,256]{2,1,0:T(8,128)S(1)}, u32[]{:S(2)}, u32[]{:S(2)}) %all-to-all-start.3) | async-done | bytes 196640 | tf_op jit(solution)/shard_map/all_to_all | solution.py:164
  133.5 13.2 %collective-permute-start.4 = (f32[24,8,256]{2,1,0:T(8,128)S(1)}, f32[24,8,256]{2,1,0:T(8,128)S(1)}, u32[]{:S(2)}, u32[]{:S(2)}) collective-permute-start(f32[24,8,256]{2,1,0:T(8,128)S(1)} %all-to-all-done.3), channel_id=1, source_target_pairs={{0,16},{16,0},{1,17},{17,1},{2,18},{18,2},{3,19},{19,3},{4,20},{20... | collective-permute-start | bytes 589832 | tf_op jit(solution)/shard_map/ppermute | solution.py:165
  146.7 2.9 %fusion.2 = bf16[8,32,640]{2,1,0:T(8,128)(2,1)} fusion(bf16[8,32,640,3]{2,1,0,3:T(8,128)(2,1)} %bitcast.109, bf16[640,3,640,1]{0,2,3,1:T(8,128)(2,1)S(1)} %bitcast.106), kind=kOutput, calls=%fused_computation.4 | convolution fusion | flops 629309440 | bytes 3768320 | tf_op jit(solution)/shard_map/nkc,rkc->nr/dot_general | solution.py:200
  149.9 0.8 concatenate.32
  (57 shorter events, 4.2 us)
Async XLA Ops:
  7.2 8.7 %copy-start.7 = (s32[48]{0:T(128)S(1)}, s32[48]{0:T(128)}, u32[]{:S(2)}) copy-start(s32[48]{0:T(128)} %param.10) | copy-start | bytes 580
  7.2 85.1 %all-gather.2.cloned.1.call-start = ((), (), s32[]{:S(2)}) async-start(), calls=%async_computation.4 | async-start | bytes 2611200 | tf_op jit(solution)/shard_map/all_gather | solution.py:141
  7.9 1.0 copy-start
  8.9 1.0 copy-start.2
  11.0 16.0 %all-to-all-start = ((bf16[4,256,640]{2,1,0:T(8,128)(2,1)}), bf16[4,256,640]{2,1,0:T(8,128)(2,1)S(1)}, u32[]{:S(2)}, u32[]{:S(2)}) async-start(bf16[4,256,640]{2,1,0:T(8,128)(2,1)} %pack.1), calls=%async_computation | async-start | bytes 2621440 | tf_op jit(solution)/shard_map/all_to_all | solution.py:144
  27.0 19.2 %collective-permute-start.2 = (bf16[4,8,32,640]{3,2,1,0:T(8,128)(2,1)S(1)}, bf16[4,8,32,640]{3,2,1,0:T(8,128)(2,1)S(1)}, u32[]{:S(2)}, u32[]{:S(2)}) collective-permute-start(bf16[4,8,32,640]{3,2,1,0:T(8,128)(2,1)S(1)} %bitcast.100), channel_id=1, source_target_pairs={{0,16},{16,0},{1,17},{17,1},{2,18},{18,2},{3,19},{19,3},{4,20},{20... | collective-permute-start | bytes 3932168 | tf_op jit(solution)/shard_map/ppermute | solution.py:145
  39.7 14.3 %copy-start.1 = (bf16[8,32,640]{2,1,0:T(8,128)(2,1)S(1)}, bf16[8,32,640]{2,1,0:T(8,128)(2,1)}, u32[]{:S(2)}) copy-start(bf16[8,32,640]{2,1,0:T(8,128)(2,1)} %g_ref.1) | copy-start | bytes 983044
  39.7 14.3 %copy-start.3 = (bf16[8,32,640]{2,1,0:T(8,128)(2,1)S(1)}, bf16[8,32,640]{2,1,0:T(8,128)(2,1)}, u32[]{:S(2)}) copy-start(bf16[8,32,640]{2,1,0:T(8,128)(2,1)} %f_ref.1) | copy-start | bytes 983044
  39.8 6.5 %collective-permute-start.3 = (bf16[4,32,384]{2,1,0:T(8,128)(2,1)S(1)}, bf16[4,32,384]{2,1,0:T(8,128)(2,1)S(1)}, u32[]{:S(2)}, u32[]{:S(2)}) collective-permute-start(bf16[4,32,384]{2,1,0:T(8,128)(2,1)S(1)} %fusion.15), channel_id=1, source_target_pairs={{0,368},{32,16},{64,48},{96,80},{128,112},{160,144},{192,176},{224... | collective-permute-start | bytes 294920 | tf_op jit(solution)/shard_map/ppermute | solution.py:148
  49.6 23.3 %all-to-all-start.1 = ((f32[8,40,512]{2,1,0:T(8,128)}), f32[8,40,512]{2,1,0:T(8,128)S(1)}, u32[]{:S(2)}, u32[]{:S(2)}) async-start(f32[8,40,512]{2,1,0:T(8,128)} %bitcast.16), calls=%async_computation.1 | async-start | bytes 1310720 | tf_op jit(solution)/shard_map/all_to_all | solution.py:157
  54.1 18.0 %collective-permute-start = (bf16[32,1280]{1,0:T(8,128)(2,1)S(1)}, bf16[32,1280]{1,0:T(8,128)(2,1)S(1)}, u32[]{:S(2)}, u32[]{:S(2)}) collective-permute-start(bf16[32,1280]{1,0:T(8,128)(2,1)S(1)} %get-tuple-element.25), channel_id=1, source_target_pairs={{0,752},{16,32},{32,16},{48,64},{64,48},{80,96},{96,80},{112,128},... | collective-permute-start | bytes 245768 | tf_op jit(solution)/shard_map/ppermute | solution.py:183
  57.7 15.3 %collective-permute-start.1 = (bf16[32,1280]{1,0:T(8,128)(2,1)S(1)}, bf16[32,1280]{1,0:T(8,128)(2,1)S(1)}, u32[]{:S(2)}, u32[]{:S(2)}) collective-permute-start(bf16[32,1280]{1,0:T(8,128)(2,1)S(1)} %get-tuple-element.26), channel_id=1, source_target_pairs={{0,16},{16,0},{1,17},{17,1},{2,18},{18,2},{3,19},{19,3},{4,20},{20... | collective-permute-start | bytes 245768 | tf_op jit(solution)/shard_map/ppermute | solution.py:181
  92.9 22.3 %all-to-all-start.2 = ((f32[12,8,256]{2,1,0:T(8,128)}), f32[12,8,256]{2,1,0:T(8,128)S(1)}, u32[]{:S(2)}, u32[]{:S(2)}) async-start(f32[12,8,256]{2,1,0:T(8,128)} %bitcast.30), calls=%async_computation.2 | async-start | bytes 196608 | tf_op jit(solution)/shard_map/all_to_all | solution.py:161
  105.1 17.6 %copy-start.4 = (bf16[640,1920]{1,0:T(8,128)(2,1)S(1)}, bf16[640,1920]{1,0:T(8,128)(2,1)}, u32[]{:S(2)}) copy-start(bf16[640,1920]{1,0:T(8,128)(2,1)} %all-gather.2.cloned.1.call-done) | copy-start | bytes 7372804
  115.9 17.6 %all-to-all-start.3 = ((f32[24,8,256]{2,1,0:T(8,128)}), f32[24,8,256]{2,1,0:T(8,128)S(1)}, u32[]{:S(2)}, u32[]{:S(2)}) async-start(f32[24,8,256]{2,1,0:T(8,128)} %broadcast_in_dim.8), calls=%async_computation.3 | async-start | bytes 393216 | tf_op jit(solution)/shard_map/all_to_all | solution.py:164
  122.7 2.6 %copy-start.6 = (bf16[8,32,1,640]{3,1,2,0:T(8,128)(2,1)S(1)}, bf16[8,32,1,640]{3,1,2,0:T(8,128)(2,1)}, u32[]{:S(2)}) copy-start(bf16[8,32,1,640]{3,1,2,0:T(8,128)(2,1)} %get-tuple-element.13) | copy-start | bytes 983044
  125.3 21.4 %copy-start.5 = (bf16[640,1920]{0,1:T(8,128)(2,1)S(1)}, bf16[640,1920]{0,1:T(8,128)(2,1)}, u32[]{:S(2)}) copy-start(bf16[640,1920]{0,1:T(8,128)(2,1)} %copy.30) | copy-start | bytes 7372804
  133.5 16.1 %collective-permute-start.4 = (f32[24,8,256]{2,1,0:T(8,128)S(1)}, f32[24,8,256]{2,1,0:T(8,128)S(1)}, u32[]{:S(2)}, u32[]{:S(2)}) collective-permute-start(f32[24,8,256]{2,1,0:T(8,128)S(1)} %all-to-all-done.3), channel_id=1, source_target_pairs={{0,16},{16,0},{1,17},{17,1},{2,18},{18,2},{3,19},{19,3},{4,20},{20... | collective-permute-start | bytes 589832 | tf_op jit(solution)/shard_map/ppermute | solution.py:165
Sparse Core Ops, SparseCore 0:
  10.4 81.8 all-gather.1

commit v3 on v2

--- a/solution.py
+++ b/solution.py
@@ -130,18 +130,81 @@
     )(place, prev_ok, next_ok, own, sib, halo)
 
 
+def out_kernel(place_ref, prev_ref, next_ref, f_ref, g_ref, skip_ref, halo_ref, edge_ref, own_ref, sib_ref, out_ref, back_ref, f_lo, f_hi, g_lo, g_hi):
+    frames, strip, width = f_ref.shape
+    tokens = frames * strip
+    core, at = place_ref[0], place_ref[1]
+
+    def put(dst, j, value, ok):
+        dst[pl.ds(j * strip, strip), :] = jnp.where(ok != 0, value, jnp.zeros_like(value))
+
+    for src, lo, hi, lanes in ((f_ref, f_lo, f_hi, slice(0, width)), (g_ref, g_lo, g_hi, slice(width, 2 * width))):
+        halo, edge = halo_ref[:, lanes], edge_ref[:, lanes]
+        for j in range(frames):
+            put(lo, j, jnp.where(core == 0, halo, edge) if j == 0 else src[j - 1], prev_ref[at + j])
+            put(hi, j, jnp.where(core == 0, edge, halo) if j == frames - 1 else src[j + 1], next_ref[at + j])
+
+    def run(low, high):
+        def dot(a, b):
+            return jnp.dot(a, b, preferred_element_type=jnp.float32)
+
+        def dot_t(a, b):
+            return lax.dot_general(a, b, (((1,), (1,)), ((), ())), preferred_element_type=jnp.float32)
+
+        f = f_ref[...].reshape(tokens, width)
+        g = g_ref[...].reshape(tokens, width)
+        for lanes, center in ((slice(0, 384), low[:, 640:1024]), (slice(384, 640), high[:, 128:384])):
+            outer = slice(384 + lanes.start, 384 + lanes.stop)
+            mixed = dot(f_lo[...], low[:, lanes]) + dot(f, center) + dot(f_hi[...], high[:, outer])
+            mixed = mixed.reshape(frames, strip, -1) + skip_ref[:, :, lanes].astype(jnp.float32)
+            out_ref[:, :, lanes] = mixed.astype(jnp.bfloat16)
+        back = dot_t(g_hi[...], low[:, :640]) + dot_t(g[:, :384], low[:, 640:1024])
+        back = back + dot_t(g[:, 384:], high[:, 128:384]) + dot_t(g_lo[...], high[:, 384:])
+        back_ref[...] = back.reshape(frames, strip, width).astype(jnp.bfloat16)
+
+    @pl.when(core == 0)
+    def _():
+        run(own_ref, sib_ref)
+
+    @pl.when(core != 0)
+    def _():
+        run(sib_ref, own_ref)
+
+
+def outputs(place, prev_ok, next_ok, features, cotangent, skip_input, halo, edge, weight_own, weight_sib):
+    frames, strip, width = features.shape
+    smem = pl.BlockSpec(memory_space=pltpu.SMEM)
+    vmem = pl.BlockSpec(memory_space=pltpu.VMEM)
+    buf = pltpu.VMEM((frames * strip, width), jnp.bfloat16)
+    out = jax.ShapeDtypeStruct(features.shape, jnp.bfloat16)
+    return pl.pallas_call(
+        out_kernel,
+        out_shape=(out, out),
+        in_specs=[smem] * 3 + [vmem] * 7,
+        out_specs=(vmem, vmem),
+        scratch_shapes=[buf] * 4,
+        compiler_params=pltpu.CompilerParams(vmem_limit_bytes=48 << 20),
+        name="outputs",
+    )(place, prev_ok, next_ok, features, cotangent, skip_input, halo, edge, weight_own, weight_sib)
+
+
 def shards(features, skip_input, cotangent, temporal_weight, clip_lengths, cycle_start):
     frames, strip, width = features.shape
     core, xl, xh, z = [lax.axis_index(a) for a in ("c", "xl", "xh", "z")]
     n_x, n_y, n_z = lax.axis_size(X), lax.axis_size("y"), lax.axis_size("z")
     n_dp = lax.axis_size(DP)
     total_frames = frames * n_dp
-    tokens = frames * strip
-
-    weight_all = lax.all_gather(temporal_weight, FSDP, axis=0, tiled=True)
+
+    weight_half = lax.dynamic_slice_in_dim(temporal_weight, core * 896, 1024, axis=1)
+    weight_half = lax.all_gather(weight_half, FSDP, axis=0, tiled=True)
 
     both = [(0, 1), (1, 0)]
     own = lax.all_to_all(pack(features, cotangent), X, 0, 0, tiled=True).reshape(n_x, frames, strip, width)
+    ends = [jnp.concatenate([features[i], cotangent[i]], axis=1) for i in (0, -1)]
+    sib_edge = lax.ppermute(jnp.where(core == 0, ends[1], ends[0]), "c", both)
+    across = [(d, (d - 1) % n_dp if d % 2 == 0 else (d + 1) % n_dp) for d in range(n_dp)]
+    halo = lax.ppermute(jnp.where(core == 0, ends[0], ends[1]), DP, across)
+    own, halo, sib_edge = lax.optimization_barrier((own, halo, sib_edge))
     sib = lax.ppermute(own, "c", both)
     z_next = [(2 * i, (2 * i - 1) % (2 * n_z)) for i in range(n_z)] + [(2 * i + 1, (2 * i + 2) % (2 * n_z)) for i in range(n_z)]
     edge = jnp.where(core == 0, own[:, 0, :, :384], own[:, -1, :, :384])
@@ -155,13 +218,19 @@
     term = x_term(place, prev_all, next_all, own, sib, halo_x)
 
     part = lax.all_to_all(term.reshape(n_y, 320 // n_y, 512), "y", 0, 0, tiled=True).sum(0)
-    part, weight_all = lax.optimization_barrier((part, weight_all))
     local_rows = part.shape[0]
     blocks = jnp.pad(part, ((0, 48 - local_rows), (0, 0))).reshape(6, 8, 2, 256).transpose(0, 2, 1, 3)
     mine = lax.all_to_all(blocks.reshape(n_z, 8, 256), "z", 0, 0, tiled=True).sum(0)
     mine = mine / jnp.sqrt(jnp.float32(total_frames * strip * lax.axis_size(FSDP)))
+    mine, weight_half = lax.optimization_barrier((mine, weight_half))
+    weight_sib = lax.ppermute(weight_half, "c", both)
     n_xz = 2 * n_z
     gathered = lax.all_to_all(jnp.broadcast_to(mine[None], (n_xz, 8, 256)), ("xh", "z"), 0, 0, tiled=True)
+    place_out = jnp.stack([core, xh * (2 * frames) + core * frames]).astype(jnp.int32)
+    block_out, grad_features = outputs(
+        place_out, prev_all, next_all, features, cotangent, skip_input, halo, sib_edge, weight_half, weight_sib
+    )
+    gathered, block_out, grad_features = lax.optimization_barrier((gathered, block_out, grad_features))
     other = lax.ppermute(gathered, "c", both)
 
     def flat(a):
@@ -177,29 +246,6 @@
     tap_1 = [low[0, :, 384:], high[0, :, 384:], low[0, :, 320:384], low[1, :, 320:], high[1, :, 384:]]
     grad_weight = jnp.concatenate(outer_tap(low) + tap_1 + outer_tap(high), axis=1)
 
-    ends = [jnp.concatenate([features[i], cotangent[i]], axis=1) for i in (0, -1)]
-    sib_edge = lax.ppermute(jnp.where(core == 0, ends[1], ends[0]), "c", both)
-    across = [(d, (d - 1) % n_dp if d % 2 == 0 else (d + 1) % n_dp) for d in range(n_dp)]
-    halo = lax.ppermute(jnp.where(core == 0, ends[0], ends[1]), DP, across)
-    before = jnp.where(core == 0, halo, sib_edge)[None]
-    after = jnp.where(core == 0, sib_edge, halo)[None]
-    at = xh * (2 * frames) + core * frames
-    prev_scale = lax.dynamic_slice_in_dim(prev_all, at, frames).astype(jnp.bfloat16)[:, None, None]
-    next_scale = lax.dynamic_slice_in_dim(next_all, at, frames).astype(jnp.bfloat16)[:, None, None]
-
-    def around(x, lanes):
-        wide = jnp.concatenate([before[:, :, lanes], x, after[:, :, lanes]], axis=0)
-        return prev_scale * wide[:-2], next_scale * wide[2:]
-
-    features_prev, features_next = around(features, slice(0, width))
-    cot_prev, cot_next = around(cotangent, slice(width, 2 * width))
-    kernel_rows = weight_all.reshape(width, 3, width)
-    stacked_in = jnp.stack([features_prev, features, features_next], axis=2).reshape(tokens, 3, width)
-    stacked_back = jnp.stack([cot_next, cotangent, cot_prev], axis=2).reshape(tokens, 3, width)
-    mixed = jnp.einsum("nkr,rkc->nc", stacked_in, kernel_rows, preferred_element_type=jnp.float32)
-    back = jnp.einsum("nkc,rkc->nr", stacked_back, kernel_rows, preferred_element_type=jnp.float32)
-    block_out = (skip_input.astype(jnp.float32) + mixed.reshape(frames, strip, width)).astype(jnp.bfloat16)
-    grad_features = back.reshape(frames, strip, width).astype(jnp.bfloat16)
     return (block_out, grad_features, grad_weight)
 
 

time: 158 us -> 152 us (0.962)
  blocking collectives: 0 us -> 52.7 us
  waiting for transfers between devices: 49.7 us -> 14.6 us
  starting transfers between devices: 71.5 us -> 53.2 us
  matrix products: 6.6 us -> 0 us
  Pallas kernels: 4.54 us -> 7.16 us
    all_to_all x0 -> x2, blocking collectives: none -> 52.7 us  [the longest x1 30.8 us: shards(): lax.all_to_all(blocks.reshape(n_z, 8, 256), 'z', 0, 0, tiled=True).sum(0)]
    all_gather x1, waiting for transfers between devices: 19.2 us -> 0.02 us  [shards(): weight_half = lax.all_gather(weight_half, FSDP, axis=0, tiled=True)]
    all_to_all x2 -> x0, starting transfers between devices: 16.6 us -> none  [the longest x1 12.2 us: shards(): lax.all_to_all(blocks.reshape(n_z, 8, 256), 'z', 0, 0, tiled=True).sum(0)]
    all_to_all x1, waiting for transfers between devices: 10.2 us -> 0.01 us  [shards(): lax.all_to_all(pack(features, cotangent), X, 0, 0, tiled=True)]
    all_to_all x2 -> x0, waiting for transfers between devices: 10.1 us -> none  [the longest x1 10.1 us: shards(): lax.all_to_all(blocks.reshape(n_z, 8, 256), 'z', 0, 0, tiled=True).sum(0)]
    ppermute x1, starting transfers between devices: 12.2 us -> 2.84 us  [shards(): sib = lax.ppermute(own, 'c', both)]
    all_to_all x1, starting transfers between devices: 4.69 us -> 14.1 us  [shards(): lax.all_to_all(jnp.broadcast_to(mine[None], (n_xz, 8, 256)), ('xh', 'z'),...]
    ppermute x1, starting transfers between devices: 13.2 us -> 4.09 us  [shards(): other = lax.ppermute(gathered, 'c', both)]
  transfers between devices with their start and end apart: 10 -> 9, of which waited for: 6 -> 3; matrix products, arithmetic and copies ran while one was open for 8% -> 2% of each run, Pallas kernels for 3% -> 4%
where the time goes in v3:
time: 152 us; the launch traced here: 151 us
  starting transfers between devices  53.2 us (35%)
  blocking collectives  52.7 us (35%)
  between operations  15 us (10%)
  waiting for transfers between devices  14.6 us (10%)
  local copies, waits for them, and re-layouts  7.18 us (5%)
  Pallas kernels  7.16 us (5%)
  other arithmetic  1.52 us (1%)
    all_to_all x1, blocking collectives, shards(): lax.all_to_all(blocks.reshape(n_z, 8, 256), 'z', 0, 0, tiled=True).sum(0)  30.8 us
    all_to_all x1, blocking collectives, shards(): lax.all_to_all(term.reshape(n_y, 320 // n_y, 512), 'y', 0, 0, tiled=True)  21.9 us
    ppermute x1, starting transfers between devices, shards(): sib_edge = lax.ppermute(jnp.where(core == 0, ends[1], ends[0]), 'c', both)  14.5 us
    all_to_all x1, starting transfers between devices, shards(): lax.all_to_all(jnp.broadcast_to(mine[None], (n_xz, 8, 256)), ('xh', 'z'),...  14.1 us
    all_to_all x1, waiting for transfers between devices, shards(): lax.all_to_all(jnp.broadcast_to(mine[None], (n_xz, 8, 256)), ('xh', 'z'),...  9.52 us
    ppermute x1, starting transfers between devices, shards(): weight_sib = lax.ppermute(weight_half, 'c', both)  6.03 us
    all_to_all x1, starting transfers between devices, shards(): lax.all_to_all(pack(features, cotangent), X, 0, 0, tiled=True)  4.97 us
    ppermute x1, starting transfers between devices, shards(): halo = lax.ppermute(jnp.where(core == 0, ends[0], ends[1]), DP, across)  4.84 us
  transfers between devices with their start and end apart: 9, of which 3 were waited for; matrix products, arithmetic and copies ran while one was open for 2% of the time, Pallas kernels for 4%

profile of v3, /device:TPU:1, one launch (start us, length us, event | category | flops | bytes accessed | tf_op | source)
XLA Modules:
  0.0 151.3 jit_solution(18074796714181711281)
XLA Ops:
  7.2 1.0 copy-done.1
  8.2 1.0 copy-done.3
  9.2 1.2 pack.1
  10.3 5.0 %all-to-all-start = ((bf16[4,256,640]{2,1,0:T(8,128)(2,1)}), bf16[4,256,640]{2,1,0:T(8,128)(2,1)S(1)}, u32[]{:S(2)}, u32[]{:S(2)}) async-start(bf16[4,256,640]{2,1,0:T(8,128)(2,1)} %pack.1), calls=%async_computation | async-start | bytes 2621440 | tf_op jit(solution)/shard_map/all_to_all | solution.py:202
  15.4 4.8 %collective-permute-start = (bf16[32,1280]{1,0:T(8,128)(2,1)S(1)}, bf16[32,1280]{1,0:T(8,128)(2,1)S(1)}, u32[]{:S(2)}, u32[]{:S(2)}) collective-permute-start(bf16[32,1280]{1,0:T(8,128)(2,1)S(1)} %get-tuple-element.36), channel_id=1, source_target_pairs={{0,752},{16,32},{32,16},{48,64},{64,48},{80,96},{96,80},{112,128},... | collective-permute-start | bytes 245768 | tf_op jit(solution)/shard_map/ppermute | solution.py:206
  20.2 14.5 %collective-permute-start.1 = (bf16[32,1280]{1,0:T(8,128)(2,1)S(1)}, bf16[32,1280]{1,0:T(8,128)(2,1)S(1)}, u32[]{:S(2)}, u32[]{:S(2)}) collective-permute-start(bf16[32,1280]{1,0:T(8,128)(2,1)S(1)} %get-tuple-element.35), channel_id=1, source_target_pairs={{0,16},{16,0},{1,17},{17,1},{2,18},{18,2},{3,19},{19,3},{4,20},{20... | collective-permute-start | bytes 245768 | tf_op jit(solution)/shard_map/ppermute | solution.py:204
  34.7 0.6 constant_dynamic-slice_fusion
  36.7 2.8 %collective-permute-start.2 = (bf16[4,8,32,640]{3,2,1,0:T(8,128)(2,1)S(1)}, bf16[4,8,32,640]{3,2,1,0:T(8,128)(2,1)S(1)}, u32[]{:S(2)}, u32[]{:S(2)}) collective-permute-start(bf16[4,8,32,640]{3,2,1,0:T(8,128)(2,1)S(1)} %bitcast.56), channel_id=1, source_target_pairs={{0,16},{16,0},{1,17},{17,1},{2,18},{18,2},{3,19},{19,3},{4,20},{20... | collective-permute-start | bytes 3932168 | tf_op jit(solution)/shard_map/ppermute | solution.py:208
  39.8 0.7 copy.15
  40.5 0.8 reduce-window.9
  41.7 1.9 %collective-permute-start.3 = (bf16[4,32,384]{2,1,0:T(8,128)(2,1)S(1)}, bf16[4,32,384]{2,1,0:T(8,128)(2,1)S(1)}, u32[]{:S(2)}, u32[]{:S(2)}) collective-permute-start(bf16[4,32,384]{2,1,0:T(8,128)(2,1)S(1)} %fusion), channel_id=1, source_target_pairs={{0,368},{32,16},{64,48},{96,80},{128,112},{160,144},{192,176},{224... | collective-permute-start | bytes 294920 | tf_op jit(solution)/shard_map/ppermute | solution.py:211
  43.7 3.9 %collective-permute-done.3.halo_ref = bf16[4,32,384]{2,1,0:T(8,128)(2,1)S(1)} collective-permute-done((bf16[4,32,384]{2,1,0:T(8,128)(2,1)S(1)}, bf16[4,32,384]{2,1,0:T(8,128)(2,1)S(1)}, u32[]{:S(2)}, u32[]{:S(2)}) %collective-permute-start.3) | collective-permute-done | bytes 98336 | tf_op jit(solution)/shard_map/ppermute | solution.py:211
  47.7 2.5 %x_term.1 = f32[320,512]{1,0:T(8,128)S(1)} custom-call(s32[3]{0:T(128)S(1)} %pad_add_fusion.place_ref, s32[32]{0:T(128)S(1)} %get-tuple-element.40.prev_ref, s32[32]{0:T(128)S(1)} %get-tuple-element.39.next_ref, bf16[4,8,32,640]{3,2,1,0:T(8,128)(2,1)S(1)} %bitcast.58, bf16[4,8,32,640]{3,2,1,0:T(8,128)(2,1)S(1)} %collective-permute-done.2.sib_ref, ...), custom_call_target="tpu_custom_call" | custom-call | tf_op jit(solution)/shard_map/x_term/pallas_call | solution.py:122
  50.2 21.9 %all_to_all.20 = f32[8,40,512]{2,1,0:T(8,128)S(1)} all-to-all(f32[8,40,512]{2,1,0:T(8,128)S(1)} %bitcast.59), channel_id=1, replica_groups=mesh['xh'=2,'z'=12,'c'=2,'xl'=2,'y'=8] {'y'}, dimensions={0} | all-to-all | bytes 1310720 | tf_op jit(solution)/shard_map/all_to_all | solution.py:220
  72.2 30.8 %all_to_all.21 = f32[12,8,256]{2,1,0:T(8,128)S(1)} all-to-all(f32[12,8,256]{2,1,0:T(8,128)S(1)} %bitcast.69), channel_id=1, replica_groups=mesh['xh'=2,'z'=12,'c'=2,'xl'=2,'y'=8] {'z'}, dimensions={0} | all-to-all | bytes 196608 | tf_op jit(solution)/shard_map/all_to_all | solution.py:223
  103.1 6.0 %collective-permute-start.4 = (bf16[640,1024]{1,0:T(8,128)(2,1)}, bf16[640,1024]{1,0:T(8,128)(2,1)S(1)}, u32[]{:S(2)}, u32[]{:S(2)}) collective-permute-start(bf16[640,1024]{1,0:T(8,128)(2,1)} %all-gather.2.cloned.1.call-done.own_ref), channel_id=1, source_target_pairs={{0,16},{16,0},{1,17},{17,1},{2,18},{18,2},{3,19},{19,3},{4,20},{20... | collective-permute-start | bytes 3932168 | tf_op jit(solution)/shard_map/ppermute | solution.py:226
  109.1 0.7 broadcast_in_dim.2
  109.8 14.1 %all-to-all-start.3 = ((f32[24,8,256]{2,1,0:T(8,128)}), f32[24,8,256]{2,1,0:T(8,128)S(1)}, u32[]{:S(2)}, u32[]{:S(2)}) async-start(f32[24,8,256]{2,1,0:T(8,128)} %broadcast_in_dim.2), calls=%async_computation.3 | async-start | bytes 393216 | tf_op jit(solution)/shard_map/all_to_all | solution.py:228
  124.0 1.3 copy-done.5
  125.3 3.5 %outputs.1 = (bf16[8,32,640]{2,1,0:T(8,128)(2,1)}, bf16[8,32,640]{2,1,0:T(8,128)(2,1)}) custom-call(s32[2]{0:T(128)S(1)} %pad_add_fusion.1.place_ref, s32[32]{0:T(128)S(1)} %get-tuple-element.40.prev_ref, s32[32]{0:T(128)S(1)} %get-tuple-element.39.next_ref, bf16[8,32,640]{2,1,0:T(8,128)(2,1)S(1)} %copy-done.2, bf16[8,32,640]{2,1,0:T(8,128)(2,1)S(1)} %copy-done.4, ...), custom_call_target="tpu_custom_call" | custom-call | tf_op jit(solution)/shard_map/outputs/pallas_call | solution.py:180
  128.8 9.5 %all-to-all-done.3 = f32[24,8,256]{2,1,0:T(8,128)S(1)} async-done(((f32[24,8,256]{2,1,0:T(8,128)}), f32[24,8,256]{2,1,0:T(8,128)S(1)}, u32[]{:S(2)}, u32[]{:S(2)}) %all-to-all-start.3) | async-done | bytes 196640 | tf_op jit(solution)/shard_map/all_to_all | solution.py:228
  138.3 4.1 %collective-permute-start.5 = (f32[24,8,256]{2,1,0:T(8,128)S(1)}, f32[24,8,256]{2,1,0:T(8,128)S(1)}, u32[]{:S(2)}, u32[]{:S(2)}) collective-permute-start(f32[24,8,256]{2,1,0:T(8,128)S(1)} %all-to-all-done.3), channel_id=1, source_target_pairs={{0,16},{16,0},{1,17},{17,1},{2,18},{18,2},{3,19},{19,3},{4,20},{20... | collective-permute-start | bytes 589832 | tf_op jit(solution)/shard_map/ppermute | solution.py:234
  142.4 1.0 collective-permute-done.5
  143.7 0.8 concatenate.11
  (54 shorter events, 1.8 us)
Async XLA Ops:
  7.2 27.5 %copy-start = (bf16[40,1920]{1,0:T(8,128)(2,1)S(1)}, bf16[40,1920]{1,0:T(8,128)(2,1)}, u32[]{:S(2)}) copy-start(bf16[40,1920]{1,0:T(8,128)(2,1)} %param.9) | copy-start | bytes 460804
  7.2 1.0 copy-start.1
  8.2 1.0 copy-start.3
  10.3 5.0 %copy-start.2 = (bf16[8,32,640]{2,1,0:T(8,128)(2,1)S(1)}, bf16[8,32,640]{2,1,0:T(8,128)(2,1)}, u32[]{:S(2)}) copy-start(bf16[8,32,640]{2,1,0:T(8,128)(2,1)} %f_ref.3) | copy-start | bytes 983044
  10.3 5.0 %copy-start.4 = (bf16[8,32,640]{2,1,0:T(8,128)(2,1)S(1)}, bf16[8,32,640]{2,1,0:T(8,128)(2,1)}, u32[]{:S(2)}) copy-start(bf16[8,32,640]{2,1,0:T(8,128)(2,1)} %g_ref.3) | copy-start | bytes 983044
  10.3 29.5 %copy-start.9 = (s32[48]{0:T(128)S(1)}, s32[48]{0:T(128)}, u32[]{:S(2)}) copy-start(s32[48]{0:T(128)} %param.10) | copy-start | bytes 580
  10.3 26.4 %all-to-all-start = ((bf16[4,256,640]{2,1,0:T(8,128)(2,1)}), bf16[4,256,640]{2,1,0:T(8,128)(2,1)S(1)}, u32[]{:S(2)}, u32[]{:S(2)}) async-start(bf16[4,256,640]{2,1,0:T(8,128)(2,1)} %pack.1), calls=%async_computation | async-start | bytes 2621440 | tf_op jit(solution)/shard_map/all_to_all | solution.py:202
  15.3 87.7 %all-gather.2.cloned.1.call-start = ((), (), s32[]{:S(2)}) async-start(), calls=%async_computation.4 | async-start | bytes 1392640 | tf_op jit(solution)/shard_map/all_gather | solution.py:199
  15.4 20.7 %collective-permute-start = (bf16[32,1280]{1,0:T(8,128)(2,1)S(1)}, bf16[32,1280]{1,0:T(8,128)(2,1)S(1)}, u32[]{:S(2)}, u32[]{:S(2)}) collective-permute-start(bf16[32,1280]{1,0:T(8,128)(2,1)S(1)} %get-tuple-element.36), channel_id=1, source_target_pairs={{0,752},{16,32},{32,16},{48,64},{64,48},{80,96},{96,80},{112,128},... | collective-permute-start | bytes 245768 | tf_op jit(solution)/shard_map/ppermute | solution.py:206
  20.2 15.8 %collective-permute-start.1 = (bf16[32,1280]{1,0:T(8,128)(2,1)S(1)}, bf16[32,1280]{1,0:T(8,128)(2,1)S(1)}, u32[]{:S(2)}, u32[]{:S(2)}) collective-permute-start(bf16[32,1280]{1,0:T(8,128)(2,1)S(1)} %get-tuple-element.35), channel_id=1, source_target_pairs={{0,16},{16,0},{1,17},{17,1},{2,18},{18,2},{3,19},{19,3},{4,20},{20... | collective-permute-start | bytes 245768 | tf_op jit(solution)/shard_map/ppermute | solution.py:204
  36.1 0.6 copy-start.7
  36.7 10.9 %collective-permute-start.2 = (bf16[4,8,32,640]{3,2,1,0:T(8,128)(2,1)S(1)}, bf16[4,8,32,640]{3,2,1,0:T(8,128)(2,1)S(1)}, u32[]{:S(2)}, u32[]{:S(2)}) collective-permute-start(bf16[4,8,32,640]{3,2,1,0:T(8,128)(2,1)S(1)} %bitcast.56), channel_id=1, source_target_pairs={{0,16},{16,0},{1,17},{17,1},{2,18},{18,2},{3,19},{19,3},{4,20},{20... | collective-permute-start | bytes 3932168 | tf_op jit(solution)/shard_map/ppermute | solution.py:208
  41.7 5.9 %collective-permute-start.3 = (bf16[4,32,384]{2,1,0:T(8,128)(2,1)S(1)}, bf16[4,32,384]{2,1,0:T(8,128)(2,1)S(1)}, u32[]{:S(2)}, u32[]{:S(2)}) collective-permute-start(bf16[4,32,384]{2,1,0:T(8,128)(2,1)S(1)} %fusion), channel_id=1, source_target_pairs={{0,368},{32,16},{64,48},{96,80},{128,112},{160,144},{192,176},{224... | collective-permute-start | bytes 294920 | tf_op jit(solution)/shard_map/ppermute | solution.py:211
  50.2 73.8 %copy-start.6 = (bf16[8,32,640]{2,1,0:T(8,128)(2,1)S(1)}, bf16[8,32,640]{2,1,0:T(8,128)(2,1)}, u32[]{:S(2)}) copy-start(bf16[8,32,640]{2,1,0:T(8,128)(2,1)} %skip_ref.1) | copy-start | bytes 983044
  50.2 73.8 %copy-start.8 = (bf16[32,1280]{1,0:T(8,128)(2,1)S(1)}, bf16[32,1280]{1,0:T(8,128)(2,1)}, u32[]{:S(2)}) copy-start(bf16[32,1280]{1,0:T(8,128)(2,1)} %copy-done.7) | copy-start | bytes 245764
  103.1 20.9 %collective-permute-start.4 = (bf16[640,1024]{1,0:T(8,128)(2,1)}, bf16[640,1024]{1,0:T(8,128)(2,1)S(1)}, u32[]{:S(2)}, u32[]{:S(2)}) collective-permute-start(bf16[640,1024]{1,0:T(8,128)(2,1)} %all-gather.2.cloned.1.call-done.own_ref), channel_id=1, source_target_pairs={{0,16},{16,0},{1,17},{17,1},{2,18},{18,2},{3,19},{19,3},{4,20},{20... | collective-permute-start | bytes 3932168 | tf_op jit(solution)/shard_map/ppermute | solution.py:226
  109.8 28.5 %all-to-all-start.3 = ((f32[24,8,256]{2,1,0:T(8,128)}), f32[24,8,256]{2,1,0:T(8,128)S(1)}, u32[]{:S(2)}, u32[]{:S(2)}) async-start(f32[24,8,256]{2,1,0:T(8,128)} %broadcast_in_dim.2), calls=%async_computation.3 | async-start | bytes 393216 | tf_op jit(solution)/shard_map/all_to_all | solution.py:228
  123.9 1.3 copy-start.5
  138.3 5.1 %collective-permute-start.5 = (f32[24,8,256]{2,1,0:T(8,128)S(1)}, f32[24,8,256]{2,1,0:T(8,128)S(1)}, u32[]{:S(2)}, u32[]{:S(2)}) collective-permute-start(f32[24,8,256]{2,1,0:T(8,128)S(1)} %all-to-all-done.3), channel_id=1, source_target_pairs={{0,16},{16,0},{1,17},{17,1},{2,18},{18,2},{3,19},{19,3},{4,20},{20... | collective-permute-start | bytes 589832 | tf_op jit(solution)/shard_map/ppermute | solution.py:234
Sparse Core Ops, SparseCore 0:
  35.5 61.5 all-gather.1

commit v4 on v3

--- a/solution.py
+++ b/solution.py
@@ -36,12 +36,14 @@
 
 def pack(features, cotangent):
     frames, strip, width = features.shape
-    vmem = pl.BlockSpec(memory_space=pltpu.VMEM)
+    steps = 4
+    block = pl.BlockSpec((frames // steps, strip, width), lambda i: (i, 0, 0))
     return pl.pallas_call(
         pack_kernel,
         out_shape=jax.ShapeDtypeStruct((4, frames * strip, width), jnp.bfloat16),
-        in_specs=[vmem] * 2,
-        out_specs=vmem,
+        grid=(steps,),
+        in_specs=[block] * 2,
+        out_specs=pl.BlockSpec((4, frames * strip // steps, width), lambda i: (0, i, 0)),
         compiler_params=pltpu.CompilerParams(vmem_limit_bytes=48 << 20),
         name="pack",
     )(features, cotangent)
@@ -130,7 +132,7 @@
     )(place, prev_ok, next_ok, own, sib, halo)
 
 
-def out_kernel(place_ref, prev_ref, next_ref, f_ref, g_ref, skip_ref, halo_ref, edge_ref, own_ref, sib_ref, out_ref, back_ref, f_lo, f_hi, g_lo, g_hi):
+def out_kernel(place_ref, prev_ref, next_ref, f_ref, g_ref, skip_ref, halo_ref, edge_ref, weight, out_ref, back_ref, f_lo, f_hi, g_lo, g_hi):
     frames, strip, width = f_ref.shape
     tokens = frames * strip
     core, at = place_ref[0], place_ref[1]
@@ -144,34 +146,23 @@
             put(lo, j, jnp.where(core == 0, halo, edge) if j == 0 else src[j - 1], prev_ref[at + j])
             put(hi, j, jnp.where(core == 0, edge, halo) if j == frames - 1 else src[j + 1], next_ref[at + j])
 
-    def run(low, high):
-        def dot(a, b):
-            return jnp.dot(a, b, preferred_element_type=jnp.float32)
-
-        def dot_t(a, b):
-            return lax.dot_general(a, b, (((1,), (1,)), ((), ())), preferred_element_type=jnp.float32)
-
-        f = f_ref[...].reshape(tokens, width)
-        g = g_ref[...].reshape(tokens, width)
-        for lanes, center in ((slice(0, 384), low[:, 640:1024]), (slice(384, 640), high[:, 128:384])):
-            outer = slice(384 + lanes.start, 384 + lanes.stop)
-            mixed = dot(f_lo[...], low[:, lanes]) + dot(f, center) + dot(f_hi[...], high[:, outer])
-            mixed = mixed.reshape(frames, strip, -1) + skip_ref[:, :, lanes].astype(jnp.float32)
-            out_ref[:, :, lanes] = mixed.astype(jnp.bfloat16)
-        back = dot_t(g_hi[...], low[:, :640]) + dot_t(g[:, :384], low[:, 640:1024])
-        back = back + dot_t(g[:, 384:], high[:, 128:384]) + dot_t(g_lo[...], high[:, 384:])
-        back_ref[...] = back.reshape(frames, strip, width).astype(jnp.bfloat16)
-
-    @pl.when(core == 0)
-    def _():
-        run(own_ref, sib_ref)
-
-    @pl.when(core != 0)
-    def _():
-        run(sib_ref, own_ref)
-
-
-def outputs(place, prev_ok, next_ok, features, cotangent, skip_input, halo, edge, weight_own, weight_sib):
+    def dot(a, b):
+        return jnp.dot(a, b, preferred_element_type=jnp.float32)
+
+    def dot_t(a, b):
+        return lax.dot_general(a, b, (((1,), (1,)), ((), ())), preferred_element_type=jnp.float32)
+
+    f = f_ref[...].reshape(tokens, width)
+    g = g_ref[...].reshape(tokens, width)
+    taps = [weight[:, k * width:(k + 1) * width] for k in range(3)]
+    mixed = dot(f_lo[...], taps[0]) + dot(f, taps[1]) + dot(f_hi[...], taps[2])
+    mixed = mixed.reshape(frames, strip, width) + skip_ref[...].astype(jnp.float32)
+    out_ref[...] = mixed.astype(jnp.bfloat16)
+    back = dot_t(g_hi[...], taps[0]) + dot_t(g, taps[1]) + dot_t(g_lo[...], taps[2])
+    back_ref[...] = back.reshape(frames, strip, width).astype(jnp.bfloat16)
+
+
+def outputs(place, prev_ok, next_ok, features, cotangent, skip_input, halo, edge, weight):
     frames, strip, width = features.shape
     smem = pl.BlockSpec(memory_space=pltpu.SMEM)
     vmem = pl.BlockSpec(memory_space=pltpu.VMEM)
@@ -180,12 +171,12 @@
     return pl.pallas_call(
         out_kernel,
         out_shape=(out, out),
-        in_specs=[smem] * 3 + [vmem] * 7,
+        in_specs=[smem] * 3 + [vmem] * 6,
         out_specs=(vmem, vmem),
         scratch_shapes=[buf] * 4,
         compiler_params=pltpu.CompilerParams(vmem_limit_bytes=48 << 20),
         name="outputs",
-    )(place, prev_ok, next_ok, features, cotangent, skip_input, halo, edge, weight_own, weight_sib)
+    )(place, prev_ok, next_ok, features, cotangent, skip_input, halo, edge, weight)
 
 
 def shards(features, skip_input, cotangent, temporal_weight, clip_lengths, cycle_start):
@@ -195,40 +186,41 @@
     n_dp = lax.axis_size(DP)
     total_frames = frames * n_dp
 
-    weight_half = lax.dynamic_slice_in_dim(temporal_weight, core * 896, 1024, axis=1)
-    weight_half = lax.all_gather(weight_half, FSDP, axis=0, tiled=True)
+    weight_all = lax.all_gather(temporal_weight, FSDP, axis=0, tiled=True)
 
     both = [(0, 1), (1, 0)]
     own = lax.all_to_all(pack(features, cotangent), X, 0, 0, tiled=True).reshape(n_x, frames, strip, width)
+    first = (jnp.arange(2, dtype=jnp.int32) * n_z + z)[:, None] * (2 * frames)
+    chip_frames = (first + jnp.arange(2 * frames, dtype=jnp.int32)).reshape(-1)
+    prev_all, next_all = border_flags(clip_lengths, cycle_start, chip_frames, total_frames)
+    own, prev_all, next_all = lax.optimization_barrier((own, prev_all, next_all))
+    sib = lax.ppermute(own, "c", both)
+    z_next = [(2 * i, (2 * i - 1) % (2 * n_z)) for i in range(n_z)] + [(2 * i + 1, (2 * i + 2) % (2 * n_z)) for i in range(n_z)]
+    edge = jnp.where(core == 0, own[:, 0, :, :384], own[:, -1, :, :384])
+    halo_x = lax.ppermute(edge, ("z", "c"), z_next)
+
+    wrapped = jnp.where(core == 0, z == 0, z == n_z - 1)
+    place = jnp.stack([core, xl, wrapped.astype(jnp.int32)]).astype(jnp.int32)
+    term = x_term(place, prev_all, next_all, own, sib, halo_x)
+
+    _, features, cotangent = lax.optimization_barrier((term, features, cotangent))
     ends = [jnp.concatenate([features[i], cotangent[i]], axis=1) for i in (0, -1)]
     sib_edge = lax.ppermute(jnp.where(core == 0, ends[1], ends[0]), "c", both)
     across = [(d, (d - 1) % n_dp if d % 2 == 0 else (d + 1) % n_dp) for d in range(n_dp)]
     halo = lax.ppermute(jnp.where(core == 0, ends[0], ends[1]), DP, across)
-    own, halo, sib_edge = lax.optimization_barrier((own, halo, sib_edge))
-    sib = lax.ppermute(own, "c", both)
-    z_next = [(2 * i, (2 * i - 1) % (2 * n_z)) for i in range(n_z)] + [(2 * i + 1, (2 * i + 2) % (2 * n_z)) for i in range(n_z)]
-    edge = jnp.where(core == 0, own[:, 0, :, :384], own[:, -1, :, :384])
-    halo_x = lax.ppermute(edge, ("z", "c"), z_next)
-
-    first = (jnp.arange(2, dtype=jnp.int32) * n_z + z)[:, None] * (2 * frames)
-    chip_frames = (first + jnp.arange(2 * frames, dtype=jnp.int32)).reshape(-1)
-    prev_all, next_all = border_flags(clip_lengths, cycle_start, chip_frames, total_frames)
-    wrapped = jnp.where(core == 0, z == 0, z == n_z - 1)
-    place = jnp.stack([core, xl, wrapped.astype(jnp.int32)]).astype(jnp.int32)
-    term = x_term(place, prev_all, next_all, own, sib, halo_x)
-
-    part = lax.all_to_all(term.reshape(n_y, 320 // n_y, 512), "y", 0, 0, tiled=True).sum(0)
+    part = lax.all_to_all(term.reshape(n_y, 320 // n_y, 512), "y", 0, 0, tiled=True)
+    part, halo, sib_edge = lax.optimization_barrier((part, halo, sib_edge))
+    part = part.sum(0)
     local_rows = part.shape[0]
     blocks = jnp.pad(part, ((0, 48 - local_rows), (0, 0))).reshape(6, 8, 2, 256).transpose(0, 2, 1, 3)
     mine = lax.all_to_all(blocks.reshape(n_z, 8, 256), "z", 0, 0, tiled=True).sum(0)
     mine = mine / jnp.sqrt(jnp.float32(total_frames * strip * lax.axis_size(FSDP)))
-    mine, weight_half = lax.optimization_barrier((mine, weight_half))
-    weight_sib = lax.ppermute(weight_half, "c", both)
+    _, weight_all = lax.optimization_barrier((mine, weight_all))
     n_xz = 2 * n_z
     gathered = lax.all_to_all(jnp.broadcast_to(mine[None], (n_xz, 8, 256)), ("xh", "z"), 0, 0, tiled=True)
     place_out = jnp.stack([core, xh * (2 * frames) + core * frames]).astype(jnp.int32)
     block_out, grad_features = outputs(
-        place_out, prev_all, next_all, features, cotangent, skip_input, halo, sib_edge, weight_half, weight_sib
+        place_out, prev_all, next_all, features, cotangent, skip_input, halo, sib_edge, weight_all
     )
     gathered, block_out, grad_features = lax.optimization_barrier((gathered, block_out, grad_features))
     other = lax.ppermute(gathered, "c", both)

time: 152 us -> 138 us (0.908)
  blocking collectives: 52.7 us -> 32.3 us
  waiting for transfers between devices: 14.6 us -> 23.5 us
  local copies, waits for them, and re-layouts: 7.18 us -> 5.63 us
    all_to_all x1 -> x0, blocking collectives: 21.9 us -> none  [shards(): lax.all_to_all(term.reshape(n_y, 320 // n_y, 512), 'y', 0, 0, tiled=True)]
    all_to_all x1, starting transfers between devices: 14.1 us -> 4.02 us  [shards(): lax.all_to_all(jnp.broadcast_to(mine[None], (n_xz, 8, 256)), ('xh', 'z'),...]
    ppermute x1, starting transfers between devices: 2.84 us -> 12.2 us  [shards(): sib = lax.ppermute(own, 'c', both)]
    all_to_all x1, waiting for transfers between devices: 0.01 us -> 8.99 us  [shards(): lax.all_to_all(pack(features, cotangent), X, 0, 0, tiled=True)]
    ppermute x1 -> x0, starting transfers between devices: 6.03 us -> none  [shards(): weight_sib = lax.ppermute(weight_half, 'c', both)]
    all_to_all x0 -> x1, starting transfers between devices: none -> 4.59 us  [shards(): lax.all_to_all(term.reshape(n_y, 320 // n_y, 512), 'y', 0, 0, tiled=True)]
    ppermute x1, starting transfers between devices: 4.09 us -> 5.99 us  [shards(): other = lax.ppermute(gathered, 'c', both)]
    all_to_all x1, waiting for transfers between devices: 9.52 us -> 7.87 us  [shards(): lax.all_to_all(jnp.broadcast_to(mine[None], (n_xz, 8, 256)), ('xh', 'z'),...]
  transfers between devices with their start and end apart: 9 -> 9, of which waited for: 3 -> 5; matrix products, arithmetic and copies ran while one was open for 2% -> 1% of each run, Pallas kernels for 4% -> 5%
where the time goes in v4:
time: 138 us; the launch traced here: 137 us
  starting transfers between devices  51.7 us (37%)
  blocking collectives  32.3 us (23%)
  waiting for transfers between devices  23.5 us (17%)
  between operations  14.9 us (11%)
  Pallas kernels  8.35 us (6%)
  local copies, waits for them, and re-layouts  5.63 us (4%)
    all_to_all x1, blocking collectives, shards(): lax.all_to_all(blocks.reshape(n_z, 8, 256), 'z', 0, 0, tiled=True).sum(0)  32.3 us
    ppermute x1, starting transfers between devices, shards(): sib_edge = lax.ppermute(jnp.where(core == 0, ends[1], ends[0]), 'c', both)  14 us
    ppermute x1, starting transfers between devices, shards(): sib = lax.ppermute(own, 'c', both)  12.2 us
    all_to_all x1, waiting for transfers between devices, shards(): lax.all_to_all(pack(features, cotangent), X, 0, 0, tiled=True)  8.99 us
    all_to_all x1, waiting for transfers between devices, shards(): lax.all_to_all(jnp.broadcast_to(mine[None], (n_xz, 8, 256)), ('xh', 'z'),...  7.87 us
    ppermute x1, starting transfers between devices, shards(): other = lax.ppermute(gathered, 'c', both)  5.99 us
    all_to_all x1, starting transfers between devices, shards(): lax.all_to_all(pack(features, cotangent), X, 0, 0, tiled=True)  4.97 us
    all_to_all x1, starting transfers between devices, shards(): lax.all_to_all(term.reshape(n_y, 320 // n_y, 512), 'y', 0, 0, tiled=True)  4.59 us
  transfers between devices with their start and end apart: 9, of which 5 were waited for; matrix products, arithmetic and copies ran while one was open for 1% of the time, Pallas kernels for 5%

profile of v4, /device:TPU:1, one launch (start us, length us, event | category | flops | bytes accessed | tf_op | source)
XLA Modules:
  0.0 137.2 jit_solution(1273352775037376623)
XLA Ops:
  7.2 1.0 copy-done.1
  8.1 1.0 copy-done.3
  9.1 1.8 %pack.1 = bf16[4,256,640]{2,1,0:T(8,128)(2,1)} custom-call(bf16[8,32,640]{2,1,0:T(8,128)(2,1)S(1)} %copy-done.1, bf16[8,32,640]{2,1,0:T(8,128)(2,1)S(1)} %copy-done.3), custom_call_target="tpu_custom_call" | custom-call | tf_op jit(solution)/shard_map/pack/pallas_call | solution.py:41
  10.9 5.0 %all-to-all-start = ((bf16[4,256,640]{2,1,0:T(8,128)(2,1)}), bf16[4,256,640]{2,1,0:T(8,128)(2,1)S(1)}, u32[]{:S(2)}, u32[]{:S(2)}) async-start(bf16[4,256,640]{2,1,0:T(8,128)(2,1)} %pack.1), calls=%async_computation | async-start | bytes 2621440 | tf_op jit(solution)/shard_map/all_to_all | solution.py:192
  15.8 0.7 all-gather.2.cloned.1.call-update
  17.8 0.2 compare_reduce_fusion
  18.0 9.0 %all-to-all-done = bf16[4,256,640]{2,1,0:T(8,128)(2,1)S(1)} async-done(((bf16[4,256,640]{2,1,0:T(8,128)(2,1)}), bf16[4,256,640]{2,1,0:T(8,128)(2,1)S(1)}, u32[]{:S(2)}, u32[]{:S(2)}) %all-to-all-start) | async-done | bytes 1310752 | tf_op jit(solution)/shard_map/all_to_all | solution.py:192
  27.0 12.2 %collective-permute-start = (bf16[4,8,32,640]{3,2,1,0:T(8,128)(2,1)S(1)}, bf16[4,8,32,640]{3,2,1,0:T(8,128)(2,1)S(1)}, u32[]{:S(2)}, u32[]{:S(2)}) collective-permute-start(bf16[4,8,32,640]{3,2,1,0:T(8,128)(2,1)S(1)} %bitcast.56), channel_id=1, source_target_pairs={{0,16},{16,0},{1,17},{17,1},{2,18},{18,2},{3,19},{19,3},{4,20},{20... | collective-permute-start | bytes 3932168 | tf_op jit(solution)/shard_map/ppermute | solution.py:197
  39.3 1.9 %collective-permute-start.1 = (bf16[4,32,384]{2,1,0:T(8,128)(2,1)S(1)}, bf16[4,32,384]{2,1,0:T(8,128)(2,1)S(1)}, u32[]{:S(2)}, u32[]{:S(2)}) collective-permute-start(bf16[4,32,384]{2,1,0:T(8,128)(2,1)S(1)} %fusion), channel_id=1, source_target_pairs={{0,368},{32,16},{64,48},{96,80},{128,112},{160,144},{192,176},{224... | collective-permute-start | bytes 294920 | tf_op jit(solution)/shard_map/ppermute | solution.py:200
  41.3 3.9 %collective-permute-done.1.halo_ref = bf16[4,32,384]{2,1,0:T(8,128)(2,1)S(1)} collective-permute-done((bf16[4,32,384]{2,1,0:T(8,128)(2,1)S(1)}, bf16[4,32,384]{2,1,0:T(8,128)(2,1)S(1)}, u32[]{:S(2)}, u32[]{:S(2)}) %collective-permute-start.1) | collective-permute-done | bytes 98336 | tf_op jit(solution)/shard_map/ppermute | solution.py:200
  45.2 3.3 %x_term.1 = f32[320,512]{1,0:T(8,128)} custom-call(s32[3]{0:T(128)S(1)} %pad_add_fusion.place_ref, s32[32]{0:T(128)S(1)} %get-tuple-element.16.prev_ref, s32[32]{0:T(128)S(1)} %get-tuple-element.17.next_ref, bf16[4,8,32,640]{3,2,1,0:T(8,128)(2,1)S(1)} %bitcast.58, bf16[4,8,32,640]{3,2,1,0:T(8,128)(2,1)S(1)} %collective-permute-done.sib_ref, ...), custom_call_target="tpu_custom_call" | custom-call | tf_op jit(solution)/shard_map/x_term/pallas_call | solution.py:124
  48.5 4.6 %all-to-all-start.1 = ((f32[8,40,512]{2,1,0:T(8,128)}), f32[8,40,512]{2,1,0:T(8,128)S(1)}, u32[]{:S(2)}, u32[]{:S(2)}) async-start(f32[8,40,512]{2,1,0:T(8,128)} %bitcast.7), calls=%async_computation.1 | async-start | bytes 1310720 | tf_op jit(solution)/shard_map/all_to_all | solution.py:211
  53.2 3.9 %collective-permute-start.2 = (bf16[32,1280]{1,0:T(8,128)(2,1)S(1)}, bf16[32,1280]{1,0:T(8,128)(2,1)S(1)}, u32[]{:S(2)}, u32[]{:S(2)}) collective-permute-start(bf16[32,1280]{1,0:T(8,128)(2,1)S(1)} %get-tuple-element.42), channel_id=1, source_target_pairs={{0,752},{16,32},{32,16},{48,64},{64,48},{80,96},{96,80},{112,128},... | collective-permute-start | bytes 245768 | tf_op jit(solution)/shard_map/ppermute | solution.py:210
  57.2 14.0 %collective-permute-start.3 = (bf16[32,1280]{1,0:T(8,128)(2,1)S(1)}, bf16[32,1280]{1,0:T(8,128)(2,1)S(1)}, u32[]{:S(2)}, u32[]{:S(2)}) collective-permute-start(bf16[32,1280]{1,0:T(8,128)(2,1)S(1)} %get-tuple-element.41), channel_id=1, source_target_pairs={{0,16},{16,0},{1,17},{17,1},{2,18},{18,2},{3,19},{19,3},{4,20},{20... | collective-permute-start | bytes 245768 | tf_op jit(solution)/shard_map/ppermute | solution.py:208
  71.2 0.9 collective-permute-done.3.edge_ref
  72.2 32.3 %all_to_all.20 = f32[12,8,256]{2,1,0:T(8,128)S(1)} all-to-all(f32[12,8,256]{2,1,0:T(8,128)S(1)} %bitcast.68), channel_id=1, replica_groups=mesh['xh'=2,'z'=12,'c'=2,'xl'=2,'y'=8] {'z'}, dimensions={0} | all-to-all | bytes 196608 | tf_op jit(solution)/shard_map/all_to_all | solution.py:216
  104.6 0.7 broadcast_in_dim.2
  105.2 4.0 %all-to-all-start.3 = ((f32[24,8,256]{2,1,0:T(8,128)}), f32[24,8,256]{2,1,0:T(8,128)S(1)}, u32[]{:S(2)}, u32[]{:S(2)}) async-start(f32[24,8,256]{2,1,0:T(8,128)} %broadcast_in_dim.2), calls=%async_computation.3 | async-start | bytes 393216 | tf_op jit(solution)/shard_map/all_to_all | solution.py:220
  109.4 1.7 %copy-done = bf16[640,1920]{1,0:T(8,128)(2,1)S(1)} copy-done((bf16[640,1920]{1,0:T(8,128)(2,1)S(1)}, bf16[640,1920]{1,0:T(8,128)(2,1)}, u32[]{:S(2)}) %copy-start) | copy-done | bytes 2457624
  111.1 3.3 %outputs.1 = (bf16[8,32,640]{2,1,0:T(8,128)(2,1)}, bf16[8,32,640]{2,1,0:T(8,128)(2,1)}) custom-call(s32[2]{0:T(128)S(1)} %pad_add_fusion.1.place_ref, s32[32]{0:T(128)S(1)} %get-tuple-element.16.prev_ref, s32[32]{0:T(128)S(1)} %get-tuple-element.17.next_ref, bf16[8,32,640]{2,1,0:T(8,128)(2,1)S(1)} %copy-done.2, bf16[8,32,640]{2,1,0:T(8,128)(2,1)S(1)} %copy-done.4, ...), custom_call_target="tpu_custom_call" | custom-call | tf_op jit(solution)/shard_map/outputs/pallas_call | solution.py:171
  114.3 7.9 %all-to-all-done.3 = f32[24,8,256]{2,1,0:T(8,128)S(1)} async-done(((f32[24,8,256]{2,1,0:T(8,128)}), f32[24,8,256]{2,1,0:T(8,128)S(1)}, u32[]{:S(2)}, u32[]{:S(2)}) %all-to-all-start.3) | async-done | bytes 196640 | tf_op jit(solution)/shard_map/all_to_all | solution.py:220
  122.2 6.0 %collective-permute-start.4 = (f32[24,8,256]{2,1,0:T(8,128)S(1)}, f32[24,8,256]{2,1,0:T(8,128)S(1)}, u32[]{:S(2)}, u32[]{:S(2)}) collective-permute-start(f32[24,8,256]{2,1,0:T(8,128)S(1)} %all-to-all-done.3), channel_id=1, source_target_pairs={{0,16},{16,0},{1,17},{17,1},{2,18},{18,2},{3,19},{19,3},{4,20},{20... | collective-permute-start | bytes 589832 | tf_op jit(solution)/shard_map/ppermute | solution.py:226
  128.2 1.0 collective-permute-done.4
  129.5 0.8 concatenate.11
  (47 shorter events, 1.1 us)
Async XLA Ops:
  7.2 1.0 copy-start.1
  8.1 1.0 copy-start.3
  10.9 5.7 %copy-start.6 = (s32[48]{0:T(128)S(1)}, s32[48]{0:T(128)}, u32[]{:S(2)}) copy-start(s32[48]{0:T(128)} %param.10) | copy-start | bytes 580
  10.9 16.1 %all-to-all-start = ((bf16[4,256,640]{2,1,0:T(8,128)(2,1)}), bf16[4,256,640]{2,1,0:T(8,128)(2,1)S(1)}, u32[]{:S(2)}, u32[]{:S(2)}) async-start(bf16[4,256,640]{2,1,0:T(8,128)(2,1)} %pack.1), calls=%async_computation | async-start | bytes 2621440 | tf_op jit(solution)/shard_map/all_to_all | solution.py:192
  15.8 93.5 %all-gather.2.cloned.1.call-start = ((), (), s32[]{:S(2)}) async-start(), calls=%async_computation.4 | async-start | bytes 2611200 | tf_op jit(solution)/shard_map/all_gather | solution.py:189
  27.0 18.2 %collective-permute-start = (bf16[4,8,32,640]{3,2,1,0:T(8,128)(2,1)S(1)}, bf16[4,8,32,640]{3,2,1,0:T(8,128)(2,1)S(1)}, u32[]{:S(2)}, u32[]{:S(2)}) collective-permute-start(bf16[4,8,32,640]{3,2,1,0:T(8,128)(2,1)S(1)} %bitcast.56), channel_id=1, source_target_pairs={{0,16},{16,0},{1,17},{17,1},{2,18},{18,2},{3,19},{19,3},{4,20},{20... | collective-permute-start | bytes 3932168 | tf_op jit(solution)/shard_map/ppermute | solution.py:197
  39.3 5.9 %collective-permute-start.1 = (bf16[4,32,384]{2,1,0:T(8,128)(2,1)S(1)}, bf16[4,32,384]{2,1,0:T(8,128)(2,1)S(1)}, u32[]{:S(2)}, u32[]{:S(2)}) collective-permute-start(bf16[4,32,384]{2,1,0:T(8,128)(2,1)S(1)} %fusion), channel_id=1, source_target_pairs={{0,368},{32,16},{64,48},{96,80},{128,112},{160,144},{192,176},{224... | collective-permute-start | bytes 294920 | tf_op jit(solution)/shard_map/ppermute | solution.py:200
  48.5 4.6 %copy-start.4 = (bf16[8,32,640]{2,1,0:T(8,128)(2,1)S(1)}, bf16[8,32,640]{2,1,0:T(8,128)(2,1)}, u32[]{:S(2)}) copy-start(bf16[8,32,640]{2,1,0:T(8,128)(2,1)} %g_ref.2) | copy-start | bytes 983044
  48.5 4.6 %copy-start.2 = (bf16[8,32,640]{2,1,0:T(8,128)(2,1)S(1)}, bf16[8,32,640]{2,1,0:T(8,128)(2,1)}, u32[]{:S(2)}) copy-start(bf16[8,32,640]{2,1,0:T(8,128)(2,1)} %f_ref.2) | copy-start | bytes 983044
  48.5 23.6 %all-to-all-start.1 = ((f32[8,40,512]{2,1,0:T(8,128)}), f32[8,40,512]{2,1,0:T(8,128)S(1)}, u32[]{:S(2)}, u32[]{:S(2)}) async-start(f32[8,40,512]{2,1,0:T(8,128)} %bitcast.7), calls=%async_computation.1 | async-start | bytes 1310720 | tf_op jit(solution)/shard_map/all_to_all | solution.py:211
  53.1 56.2 %copy-start.5 = (bf16[8,32,640]{2,1,0:T(8,128)(2,1)S(1)}, bf16[8,32,640]{2,1,0:T(8,128)(2,1)}, u32[]{:S(2)}) copy-start(bf16[8,32,640]{2,1,0:T(8,128)(2,1)} %skip_ref.1) | copy-start | bytes 983044
  53.2 18.0 %collective-permute-start.2 = (bf16[32,1280]{1,0:T(8,128)(2,1)S(1)}, bf16[32,1280]{1,0:T(8,128)(2,1)S(1)}, u32[]{:S(2)}, u32[]{:S(2)}) collective-permute-start(bf16[32,1280]{1,0:T(8,128)(2,1)S(1)} %get-tuple-element.42), channel_id=1, source_target_pairs={{0,752},{16,32},{32,16},{48,64},{64,48},{80,96},{96,80},{112,128},... | collective-permute-start | bytes 245768 | tf_op jit(solution)/shard_map/ppermute | solution.py:210
  57.2 15.0 %collective-permute-start.3 = (bf16[32,1280]{1,0:T(8,128)(2,1)S(1)}, bf16[32,1280]{1,0:T(8,128)(2,1)S(1)}, u32[]{:S(2)}, u32[]{:S(2)}) collective-permute-start(bf16[32,1280]{1,0:T(8,128)(2,1)S(1)} %get-tuple-element.41), channel_id=1, source_target_pairs={{0,16},{16,0},{1,17},{17,1},{2,18},{18,2},{3,19},{19,3},{4,20},{20... | collective-permute-start | bytes 245768 | tf_op jit(solution)/shard_map/ppermute | solution.py:208
  105.2 17.0 %all-to-all-start.3 = ((f32[24,8,256]{2,1,0:T(8,128)}), f32[24,8,256]{2,1,0:T(8,128)S(1)}, u32[]{:S(2)}, u32[]{:S(2)}) async-start(f32[24,8,256]{2,1,0:T(8,128)} %broadcast_in_dim.2), calls=%async_computation.3 | async-start | bytes 393216 | tf_op jit(solution)/shard_map/all_to_all | solution.py:220
  109.4 1.7 %copy-start = (bf16[640,1920]{1,0:T(8,128)(2,1)S(1)}, bf16[640,1920]{1,0:T(8,128)(2,1)}, u32[]{:S(2)}) copy-start(bf16[640,1920]{1,0:T(8,128)(2,1)} %all-gather.2.cloned.1.call-done.weight) | copy-start | bytes 7372804
  122.2 7.0 %collective-permute-start.4 = (f32[24,8,256]{2,1,0:T(8,128)S(1)}, f32[24,8,256]{2,1,0:T(8,128)S(1)}, u32[]{:S(2)}, u32[]{:S(2)}) collective-permute-start(f32[24,8,256]{2,1,0:T(8,128)S(1)} %all-to-all-done.3), channel_id=1, source_target_pairs={{0,16},{16,0},{1,17},{17,1},{2,18},{18,2},{3,19},{19,3},{4,20},{20... | collective-permute-start | bytes 589832 | tf_op jit(solution)/shard_map/ppermute | solution.py:226
Sparse Core Ops, SparseCore 0:
  19.0 81.7 all-gather.1

commit v5 on v4

--- a/solution.py
+++ b/solution.py
@@ -19,31 +19,56 @@
     return (1 - first_here.astype(jnp.int32), 1 - first_next.astype(jnp.int32))
 
 
-def pack_kernel(f_ref, g_ref, out_ref):
-    frames, strip, width = f_ref.shape
-    f = f_ref[...].reshape(frames * strip, width)
-    g = g_ref[...].reshape(frames * strip, width)
-    f_mid, g_mid = f[:, 256:384], g[:, 256:384]
-    f_rolled, g_rolled = [pltpu.roll(m.astype(jnp.float32), 64, 1).astype(jnp.bfloat16) for m in (f_mid, g_mid)]
-    left = lax.broadcasted_iota(jnp.int32, f_mid.shape, 1) < 64
-    for xh in range(2):
-        for xl in range(2):
-            j = 2 * xh + xl
-            out_ref[j, :, :256] = f[:, 384 * xl:384 * xl + 256]
-            out_ref[j, :, 256:384] = jnp.where(left, f_rolled if xl else f_mid, g_mid if xh else g_rolled)
-            out_ref[j, :, 384:] = g[:, 384 * xh:384 * xh + 256]
+def pack_kernel(f_hbm, g_hbm, out_hbm, f_ref, g_ref, out_ref, in_sems, out_sems):
+    steps = f_ref.shape[0]
+    frames, strip, width = f_ref.shape[1:]
+    rows = frames * strip
+
+    def fetch(i):
+        return [
+            pltpu.make_async_copy(src.at[pl.ds(i * frames, frames)], dst.at[i], in_sems.at[i, k])
+            for k, (src, dst) in enumerate(((f_hbm, f_ref), (g_hbm, g_ref)))
+        ]
+
+    def send(i):
+        return pltpu.make_async_copy(out_ref.at[i], out_hbm.at[:, pl.ds(i * rows, rows), :], out_sems.at[i])
+
+    for i in range(steps):
+        for copy in fetch(i):
+            copy.start()
+    for i in range(steps):
+        for copy in fetch(i):
+            copy.wait()
+        f = f_ref[i].reshape(rows, width)
+        g = g_ref[i].reshape(rows, width)
+        f_mid, g_mid = f[:, 256:384], g[:, 256:384]
+        f_rolled, g_rolled = [pltpu.roll(m.astype(jnp.float32), 64, 1).astype(jnp.bfloat16) for m in (f_mid, g_mid)]
+        left = lax.broadcasted_iota(jnp.int32, f_mid.shape, 1) < 64
+        for xh in range(2):
+            for xl in range(2):
+                j = 2 * xh + xl
+                out_ref[i, j, :, :256] = f[:, 384 * xl:384 * xl + 256]
+                out_ref[i, j, :, 256:384] = jnp.where(left, f_rolled if xl else f_mid, g_mid if xh else g_rolled)
+                out_ref[i, j, :, 384:] = g[:, 384 * xh:384 * xh + 256]
+        send(i).start()
+    for i in range(steps):
+        send(i).wait()
 
 
 def pack(features, cotangent):
     frames, strip, width = features.shape
-    steps = 4
-    block = pl.BlockSpec((frames // steps, strip, width), lambda i: (i, 0, 0))
+    steps = 2
+    hbm = pl.BlockSpec(memory_space=pltpu.HBM)
+    part = pltpu.VMEM((steps, frames // steps, strip, width), jnp.bfloat16)
     return pl.pallas_call(
         pack_kernel,
         out_shape=jax.ShapeDtypeStruct((4, frames * strip, width), jnp.bfloat16),
-        grid=(steps,),
-        in_specs=[block] * 2,
-        out_specs=pl.BlockSpec((4, frames * strip // steps, width), lambda i: (0, i, 0)),
+        in_specs=[hbm] * 2,
+        out_specs=hbm,
+        scratch_shapes=[
+            part, part, pltpu.VMEM((steps, 4, frames * strip // steps, width), jnp.bfloat16),
+            pltpu.SemaphoreType.DMA((steps, 2)), pltpu.SemaphoreType.DMA((steps,)),
+        ],
         compiler_params=pltpu.CompilerParams(vmem_limit_bytes=48 << 20),
         name="pack",
     )(features, cotangent)
@@ -132,10 +157,12 @@
     )(place, prev_ok, next_ok, own, sib, halo)
 
 
-def out_kernel(place_ref, prev_ref, next_ref, f_ref, g_ref, skip_ref, halo_ref, edge_ref, weight, out_ref, back_ref, f_lo, f_hi, g_lo, g_hi):
+def out_kernel(place_ref, prev_ref, next_ref, f_ref, g_ref, skip_ref, halo_ref, edge_ref, *refs):
+    weights, (out_ref, back_ref, f_lo, f_hi, g_lo, g_hi, blocks, weight) = refs[:4], refs[4:]
     frames, strip, width = f_ref.shape
     tokens = frames * strip
-    core, at = place_ref[0], place_ref[1]
+    core, at, xl, y = [place_ref[i] for i in range(4)]
+    count, rows = weights[0].shape[:2]
 
     def put(dst, j, value, ok):
         dst[pl.ds(j * strip, strip), :] = jnp.where(ok != 0, value, jnp.zeros_like(value))
@@ -145,6 +172,15 @@
         for j in range(frames):
             put(lo, j, jnp.where(core == 0, halo, edge) if j == 0 else src[j - 1], prev_ref[at + j])
             put(hi, j, jnp.where(core == 0, edge, halo) if j == frames - 1 else src[j + 1], next_ref[at + j])
+
+    for i in range(count):
+        for half in range(2):
+            blocks[half, core * count + i] = weights[half][i]
+            blocks[half, (1 - core) * count + i] = weights[2 + half][i]
+    for half in range(2):
+        for i in range(2 * count):
+            start = (half * 2 * count + i) * rows
+            weight[start:start + rows, :] = blocks[(half + xl) % 2, (y - i + 2 * count) % (2 * count)]
 
     def dot(a, b):
         return jnp.dot(a, b, preferred_element_type=jnp.float32)
@@ -162,7 +198,7 @@
     back_ref[...] = back.reshape(frames, strip, width).astype(jnp.bfloat16)
 
 
-def outputs(place, prev_ok, next_ok, features, cotangent, skip_input, halo, edge, weight):
+def outputs(place, prev_ok, next_ok, features, cotangent, skip_input, halo, edge, *weights):
     frames, strip, width = features.shape
     smem = pl.BlockSpec(memory_space=pltpu.SMEM)
     vmem = pl.BlockSpec(memory_space=pltpu.VMEM)
@@ -171,34 +207,40 @@
     return pl.pallas_call(
         out_kernel,
         out_shape=(out, out),
-        in_specs=[smem] * 3 + [vmem] * 6,
+        in_specs=[smem] * 3 + [vmem] * 9,
         out_specs=(vmem, vmem),
-        scratch_shapes=[buf] * 4,
+        scratch_shapes=[buf] * 4 + [pltpu.VMEM((2, 8, 40, 3 * width), jnp.bfloat16), pltpu.VMEM((width, 3 * width), jnp.bfloat16)],
         compiler_params=pltpu.CompilerParams(vmem_limit_bytes=48 << 20),
         name="outputs",
-    )(place, prev_ok, next_ok, features, cotangent, skip_input, halo, edge, weight)
+    )(place, prev_ok, next_ok, features, cotangent, skip_input, halo, edge, *weights)
 
 
 def shards(features, skip_input, cotangent, temporal_weight, clip_lengths, cycle_start):
     frames, strip, width = features.shape
-    core, xl, xh, z = [lax.axis_index(a) for a in ("c", "xl", "xh", "z")]
+    core, xl, xh, z, y = [lax.axis_index(a) for a in ("c", "xl", "xh", "z", "y")]
     n_x, n_y, n_z = lax.axis_size(X), lax.axis_size("y"), lax.axis_size("z")
     n_dp = lax.axis_size(DP)
     total_frames = frames * n_dp
 
-    weight_all = lax.all_gather(temporal_weight, FSDP, axis=0, tiled=True)
+    def from_y(k):
+        far = [(n_y + i, n_y + (i - k) % n_y) for i in range(n_y)]
+        near = [(i, (i + k) % n_y) for i in range(n_y)]
+        return lax.ppermute(temporal_weight, ("c", "y"), far if 2 * k == n_y else near + far)
+
+    w_1, w_2, w_3, w_4 = [from_y(k) for k in (1, 2, 3, 4)]
 
     both = [(0, 1), (1, 0)]
     own = lax.all_to_all(pack(features, cotangent), X, 0, 0, tiled=True).reshape(n_x, frames, strip, width)
-    first = (jnp.arange(2, dtype=jnp.int32) * n_z + z)[:, None] * (2 * frames)
-    chip_frames = (first + jnp.arange(2 * frames, dtype=jnp.int32)).reshape(-1)
-    prev_all, next_all = border_flags(clip_lengths, cycle_start, chip_frames, total_frames)
-    own, prev_all, next_all = lax.optimization_barrier((own, prev_all, next_all))
+    own, w_1, w_2, w_3, w_4 = lax.optimization_barrier((own, w_1, w_2, w_3, w_4))
     sib = lax.ppermute(own, "c", both)
     z_next = [(2 * i, (2 * i - 1) % (2 * n_z)) for i in range(n_z)] + [(2 * i + 1, (2 * i + 2) % (2 * n_z)) for i in range(n_z)]
     edge = jnp.where(core == 0, own[:, 0, :, :384], own[:, -1, :, :384])
     halo_x = lax.ppermute(edge, ("z", "c"), z_next)
 
+    _, clip_lengths, cycle_start = lax.optimization_barrier((edge, clip_lengths, cycle_start))
+    first = (jnp.arange(2, dtype=jnp.int32) * n_z + z)[:, None] * (2 * frames)
+    chip_frames = (first + jnp.arange(2 * frames, dtype=jnp.int32)).reshape(-1)
+    prev_all, next_all = border_flags(clip_lengths, cycle_start, chip_frames, total_frames)
     wrapped = jnp.where(core == 0, z == 0, z == n_z - 1)
     place = jnp.stack([core, xl, wrapped.astype(jnp.int32)]).astype(jnp.int32)
     term = x_term(place, prev_all, next_all, own, sib, halo_x)
@@ -208,29 +250,34 @@
     sib_edge = lax.ppermute(jnp.where(core == 0, ends[1], ends[0]), "c", both)
     across = [(d, (d - 1) % n_dp if d % 2 == 0 else (d + 1) % n_dp) for d in range(n_dp)]
     halo = lax.ppermute(jnp.where(core == 0, ends[0], ends[1]), DP, across)
+    blocks = jnp.where(core == 0, jnp.stack([temporal_weight, w_1, w_2, w_3]), jnp.stack([w_4, w_3, w_2, w_1]))
+    _, blocks = lax.optimization_barrier((term, blocks))
+    blocks_far = lax.ppermute(blocks, "xl", both)
+    blocks_sib = lax.ppermute(blocks, "c", both)
+
     part = lax.all_to_all(term.reshape(n_y, 320 // n_y, 512), "y", 0, 0, tiled=True)
-    part, halo, sib_edge = lax.optimization_barrier((part, halo, sib_edge))
+    part, halo, sib_edge, blocks_far, blocks_sib = lax.optimization_barrier((part, halo, sib_edge, blocks_far, blocks_sib))
+    weights = (blocks, blocks_far, blocks_sib, lax.ppermute(blocks_far, "c", both))
     part = part.sum(0)
     local_rows = part.shape[0]
     blocks = jnp.pad(part, ((0, 48 - local_rows), (0, 0))).reshape(6, 8, 2, 256).transpose(0, 2, 1, 3)
     mine = lax.all_to_all(blocks.reshape(n_z, 8, 256), "z", 0, 0, tiled=True).sum(0)
     mine = mine / jnp.sqrt(jnp.float32(total_frames * strip * lax.axis_size(FSDP)))
-    _, weight_all = lax.optimization_barrier((mine, weight_all))
+    _, weights = lax.optimization_barrier((mine, weights))
     n_xz = 2 * n_z
     gathered = lax.all_to_all(jnp.broadcast_to(mine[None], (n_xz, 8, 256)), ("xh", "z"), 0, 0, tiled=True)
-    place_out = jnp.stack([core, xh * (2 * frames) + core * frames]).astype(jnp.int32)
+    place_out = jnp.stack([core, xh * (2 * frames) + core * frames, xl, y]).astype(jnp.int32)
     block_out, grad_features = outputs(
-        place_out, prev_all, next_all, features, cotangent, skip_input, halo, sib_edge, weight_all
+        place_out, prev_all, next_all, features, cotangent, skip_input, halo, sib_edge, *weights
     )
     gathered, block_out, grad_features = lax.optimization_barrier((gathered, block_out, grad_features))
-    other = lax.ppermute(gathered, "c", both)
+    gathered = lax.all_gather(gathered, "c")
 
     def flat(a):
         a = a.reshape(2, 6, 2, 8, 256).transpose(0, 1, 3, 2, 4)
         return a.reshape(2, 48, 512)[:, :local_rows]
 
-    low = flat(jnp.where(core == 0, gathered, other))
-    high = flat(jnp.where(core == 0, other, gathered))
+    low, high = flat(gathered[0]), flat(gathered[1])
 
     def outer_tap(b):
         return [b[0, :, :320], b[1, :, 256:320], b[1, :, :256]]

time: 138 us -> 129 us (0.935)
  blocking collectives: 32.3 us -> 5.76 us
  starting transfers between devices: 51.7 us -> 68 us
  between operations: 14.9 us -> 1.65 us
  waiting for transfers between devices: 23.5 us -> 33.1 us
  other arithmetic: 0.79 us -> 4.27 us
    all_to_all x1 -> x0, blocking collectives: 32.3 us -> none  [shards(): lax.all_to_all(blocks.reshape(n_z, 8, 256), 'z', 0, 0, tiled=True).sum(0)]
    ppermute x1 -> x7, starting transfers between devices: 5.99 us -> 34.9 us  [the longest x4 17.3 us: from_y(): lax.ppermute(temporal_weight, ('c', 'y'), far if 2 * k == n_y else near +...]
    ppermute x1, starting transfers between devices: 14 us -> 2.2 us  [shards(): sib_edge = lax.ppermute(jnp.where(core == 0, ends[1], ends[0]), 'c', both)]
    ppermute x1 -> x7, waiting for transfers between devices: 1.05 us -> 10.9 us  [the longest x1 6.72 us: shards(): blocks_far = lax.ppermute(blocks, 'xl', both)]
    all_to_all x1, waiting for transfers between devices: 8.99 us -> 0.01 us  [shards(): lax.all_to_all(pack(features, cotangent), X, 0, 0, tiled=True)]
    all_to_all x0 -> x1, waiting for transfers between devices: none -> 7.55 us  [shards(): lax.all_to_all(blocks.reshape(n_z, 8, 256), 'z', 0, 0, tiled=True).sum(0)]
    ppermute x1, starting transfers between devices: 12.2 us -> 5.75 us  [shards(): sib = lax.ppermute(own, 'c', both)]
    all_gather x0 -> x1, blocking collectives: none -> 5.76 us  [shards(): gathered = lax.all_gather(gathered, 'c')]
  transfers between devices with their start and end apart: 9 -> 15, of which waited for: 5 -> 6; matrix products, arithmetic and copies ran while one was open for 1% -> 4% of each run, Pallas kernels for 5% -> 3%
where the time goes in v5:
time: 129 us; the launch traced here: 128 us
  starting transfers between devices  68 us (53%)
  waiting for transfers between devices  33.1 us (26%)
  Pallas kernels  8.93 us (7%)
  local copies, waits for them, and re-layouts  6.1 us (5%)
  blocking collectives  5.76 us (4%)
  other arithmetic  4.27 us (3%)
  between operations  1.65 us (1%)
    ppermute x4, starting transfers between devices, from_y(): lax.ppermute(temporal_weight, ('c', 'y'), far if 2 * k == n_y else near +...  17.3 us
    ppermute x1, starting transfers between devices, shards(): blocks_sib = lax.ppermute(blocks, 'c', both)  10.9 us
    all_to_all x1, waiting for transfers between devices, shards(): lax.all_to_all(jnp.broadcast_to(mine[None], (n_xz, 8, 256)), ('xh', 'z'),...  8.41 us
    all_to_all x1, waiting for transfers between devices, shards(): lax.all_to_all(blocks.reshape(n_z, 8, 256), 'z', 0, 0, tiled=True).sum(0)  7.55 us
    all_to_all x1, starting transfers between devices, shards(): lax.all_to_all(jnp.broadcast_to(mine[None], (n_xz, 8, 256)), ('xh', 'z'),...  7.33 us
    ppermute x1, waiting for transfers between devices, shards(): blocks_far = lax.ppermute(blocks, 'xl', both)  6.72 us
    all_gather x1, blocking collectives, shards(): gathered = lax.all_gather(gathered, 'c')  5.76 us
    ppermute x1, starting transfers between devices, shards(): sib = lax.ppermute(own, 'c', both)  5.75 us
  transfers between devices with their start and end apart: 15, of which 6 were waited for; matrix products, arithmetic and copies ran while one was open for 4% of the time, Pallas kernels for 3%

profile of v5, /device:TPU:1, one launch (start us, length us, event | category | flops | bytes accessed | tf_op | source)
XLA Modules:
  0.0 127.8 jit_solution(4941522861331380277)
XLA Ops:
  2.6 2.0 %pack.1 = bf16[4,256,640]{2,1,0:T(8,128)(2,1)} custom-call(bf16[8,32,640]{2,1,0:T(8,128)(2,1)S(1)} %copy-done, bf16[8,32,640]{2,1,0:T(8,128)(2,1)S(1)} %copy-done.2), custom_call_target="tpu_custom_call" | custom-call | tf_op jit(solution)/shard_map/pack/pallas_call | solution.py:63
  4.7 5.0 %all-to-all-start = ((bf16[4,256,640]{2,1,0:T(8,128)(2,1)}), bf16[4,256,640]{2,1,0:T(8,128)(2,1)S(1)}, u32[]{:S(2)}, u32[]{:S(2)}) async-start(bf16[4,256,640]{2,1,0:T(8,128)(2,1)} %pack.1), calls=%async_computation | async-start | bytes 2621440 | tf_op jit(solution)/shard_map/all_to_all | solution.py:233
  9.6 6.7 %collective-permute-start.2 = (bf16[40,1920]{1,0:T(8,128)(2,1)S(1)}, bf16[40,1920]{1,0:T(8,128)(2,1)S(1)}, u32[]{:S(2)}, u32[]{:S(2)}) collective-permute-start(bf16[40,1920]{1,0:T(8,128)(2,1)S(1)} %copy-done.7), channel_id=1, source_target_pairs={{0,3},{1,4},{2,5},{3,6},{4,7},{5,0},{6,1},{7,2},{16,21},{17,22},{1... | collective-permute-start | bytes 460808 | tf_op jit(solution)/shard_map/ppermute | solution.py:228
  16.3 2.9 %collective-permute-start.1 = (bf16[40,1920]{1,0:T(8,128)(2,1)S(1)}, bf16[40,1920]{1,0:T(8,128)(2,1)S(1)}, u32[]{:S(2)}, u32[]{:S(2)}) collective-permute-start(bf16[40,1920]{1,0:T(8,128)(2,1)S(1)} %copy-done.7), channel_id=1, source_target_pairs={{0,2},{1,3},{2,4},{3,5},{4,6},{5,7},{6,0},{7,1},{16,22},{17,23},{1... | collective-permute-start | bytes 460808 | tf_op jit(solution)/shard_map/ppermute | solution.py:228
  19.2 2.1 %collective-permute-start = (bf16[40,1920]{1,0:T(8,128)(2,1)S(1)}, bf16[40,1920]{1,0:T(8,128)(2,1)S(1)}, u32[]{:S(2)}, u32[]{:S(2)}) collective-permute-start(bf16[40,1920]{1,0:T(8,128)(2,1)S(1)} %copy-done.7), channel_id=1, source_target_pairs={{0,1},{1,2},{2,3},{3,4},{4,5},{5,6},{6,7},{7,0},{16,23},{17,16},{1... | collective-permute-start | bytes 460808 | tf_op jit(solution)/shard_map/ppermute | solution.py:228
  21.3 5.7 %collective-permute-start.3 = (bf16[40,1920]{1,0:T(8,128)(2,1)S(1)}, bf16[40,1920]{1,0:T(8,128)(2,1)S(1)}, u32[]{:S(2)}, u32[]{:S(2)}) collective-permute-start(bf16[40,1920]{1,0:T(8,128)(2,1)S(1)} %copy-done.7), channel_id=1, source_target_pairs={{16,20},{17,21},{18,22},{19,23},{20,16},{21,17},{22,18},{23,19},{2... | collective-permute-start | bytes 460808 | tf_op jit(solution)/shard_map/ppermute | solution.py:228
  27.6 4.2 %collective-permute-done.3 = bf16[40,1920]{1,0:T(8,128)(2,1)S(1)} collective-permute-done((bf16[40,1920]{1,0:T(8,128)(2,1)S(1)}, bf16[40,1920]{1,0:T(8,128)(2,1)S(1)}, u32[]{:S(2)}, u32[]{:S(2)}) %collective-permute-start.3) | collective-permute-done | bytes 153632 | tf_op jit(solution)/shard_map/ppermute | solution.py:228
  31.8 5.8 %collective-permute-start.4 = (bf16[4,8,32,640]{3,2,1,0:T(8,128)(2,1)S(1)}, bf16[4,8,32,640]{3,2,1,0:T(8,128)(2,1)S(1)}, u32[]{:S(2)}, u32[]{:S(2)}) collective-permute-start(bf16[4,8,32,640]{3,2,1,0:T(8,128)(2,1)S(1)} %bitcast.62), channel_id=1, source_target_pairs={{0,16},{16,0},{1,17},{17,1},{2,18},{18,2},{3,19},{19,3},{4,20},{20... | collective-permute-start | bytes 3932168 | tf_op jit(solution)/shard_map/ppermute | solution.py:235
  38.6 2.2 %collective-permute-start.5 = (bf16[4,32,384]{2,1,0:T(8,128)(2,1)}, bf16[4,32,384]{2,1,0:T(8,128)(2,1)S(1)}, u32[]{:S(2)}, u32[]{:S(2)}) collective-permute-start(bf16[4,32,384]{2,1,0:T(8,128)(2,1)} %fusion.3), channel_id=1, source_target_pairs={{0,368},{32,16},{64,48},{96,80},{128,112},{160,144},{192,176},{224... | collective-permute-start | bytes 294920 | tf_op jit(solution)/shard_map/ppermute | solution.py:238
  42.6 2.1 %collective-permute-done.5.halo_ref = bf16[4,32,384]{2,1,0:T(8,128)(2,1)S(1)} collective-permute-done((bf16[4,32,384]{2,1,0:T(8,128)(2,1)}, bf16[4,32,384]{2,1,0:T(8,128)(2,1)S(1)}, u32[]{:S(2)}, u32[]{:S(2)}) %collective-permute-start.5) | collective-permute-done | bytes 98336 | tf_op jit(solution)/shard_map/ppermute | solution.py:238
  44.7 3.3 %x_term.1 = f32[320,512]{1,0:T(8,128)} custom-call(s32[3]{0:T(128)S(1)} %pad_add_fusion.place_ref, s32[32]{0:T(128)S(1)} %get-tuple-element.68.prev_ref, s32[32]{0:T(128)S(1)} %get-tuple-element.67.next_ref, bf16[4,8,32,640]{3,2,1,0:T(8,128)(2,1)S(1)} %bitcast.64, bf16[4,8,32,640]{3,2,1,0:T(8,128)(2,1)S(1)} %collective-permute-done.4.sib_ref, ...), custom_call_target="tpu_custom_call" | custom-call | tf_op jit(solution)/shard_map/x_term/pallas_call | solution.py:149
  48.1 4.4 %all-to-all-start.1 = ((f32[8,40,512]{2,1,0:T(8,128)}), f32[8,40,512]{2,1,0:T(8,128)}, u32[]{:S(2)}, u32[]{:S(2)}) async-start(f32[8,40,512]{2,1,0:T(8,128)} %bitcast.7), calls=%async_computation.1 | async-start | bytes 1310720 | tf_op jit(solution)/shard_map/all_to_all | solution.py:258
  52.6 10.9 %collective-permute-start.9 = (bf16[4,40,1920]{2,1,0:T(8,128)(2,1)S(1)}, bf16[4,40,1920]{2,1,0:T(8,128)(2,1)S(1)}, u32[]{:S(2)}, u32[]{:S(2)}) collective-permute-start(bf16[4,40,1920]{2,1,0:T(8,128)(2,1)S(1)} %fusion.1.refs_0_), channel_id=1, source_target_pairs={{0,16},{16,0},{1,17},{17,1},{2,18},{18,2},{3,19},{19,3},{4,20},{20... | collective-permute-start | bytes 1843208 | tf_op jit(solution)/shard_map/ppermute | solution.py:256
  63.5 4.2 %collective-permute-start.8 = (bf16[4,40,1920]{2,1,0:T(8,128)(2,1)S(1)}, bf16[4,40,1920]{2,1,0:T(8,128)(2,1)S(1)}, u32[]{:S(2)}, u32[]{:S(2)}) collective-permute-start(bf16[4,40,1920]{2,1,0:T(8,128)(2,1)S(1)} %fusion.1.refs_0_), channel_id=1, source_target_pairs={{0,8},{8,0},{1,9},{9,1},{2,10},{10,2},{3,11},{11,3},{4,12},{12,4},... | collective-permute-start | bytes 1843208 | tf_op jit(solution)/shard_map/ppermute | solution.py:255
  67.9 2.2 %collective-permute-start.7 = (bf16[32,1280]{1,0:T(8,128)(2,1)S(1)}, bf16[32,1280]{1,0:T(8,128)(2,1)S(1)}, u32[]{:S(2)}, u32[]{:S(2)}) collective-permute-start(bf16[32,1280]{1,0:T(8,128)(2,1)S(1)} %get-tuple-element.63), channel_id=1, source_target_pairs={{0,16},{16,0},{1,17},{17,1},{2,18},{18,2},{3,19},{19,3},{4,20},{20... | collective-permute-start | bytes 245768 | tf_op jit(solution)/shard_map/ppermute | solution.py:250
  72.0 4.1 %collective-permute-done.6.halo_ref = bf16[32,1280]{1,0:T(8,128)(2,1)S(1)} collective-permute-done((bf16[32,1280]{1,0:T(8,128)(2,1)S(1)}, bf16[32,1280]{1,0:T(8,128)(2,1)S(1)}, u32[]{:S(2)}, u32[]{:S(2)}) %collective-permute-start.6) | collective-permute-done | bytes 81952 | tf_op jit(solution)/shard_map/ppermute | solution.py:252
  76.1 6.7 %collective-permute-done.8.refs_1_ = bf16[4,40,1920]{2,1,0:T(8,128)(2,1)S(1)} collective-permute-done((bf16[4,40,1920]{2,1,0:T(8,128)(2,1)S(1)}, bf16[4,40,1920]{2,1,0:T(8,128)(2,1)S(1)}, u32[]{:S(2)}, u32[]{:S(2)}) %collective-permute-start.8) | collective-permute-done | bytes 614432 | tf_op jit(solution)/shard_map/ppermute | solution.py:255
  84.6 4.2 %all-to-all-start.2 = ((f32[12,8,256]{2,1,0:T(8,128)}), f32[12,8,256]{2,1,0:T(8,128)}, u32[]{:S(2)}, u32[]{:S(2)}) async-start(f32[12,8,256]{2,1,0:T(8,128)} %bitcast.19), calls=%async_computation.2 | async-start | bytes 196608 | tf_op jit(solution)/shard_map/all_to_all | solution.py:264
  88.9 2.6 %collective-permute-start.10 = (bf16[4,40,1920]{2,1,0:T(8,128)(2,1)S(1)}, bf16[4,40,1920]{2,1,0:T(8,128)(2,1)S(1)}, u32[]{:S(2)}, u32[]{:S(2)}) collective-permute-start(bf16[4,40,1920]{2,1,0:T(8,128)(2,1)S(1)} %collective-permute-done.8.refs_1_), channel_id=1, source_target_pairs={{0,16},{16,0},{1,17},{17,1},{2,18},{18,2},{3,19},{19,3},{4,20},{20... | collective-permute-start | bytes 1843208 | tf_op jit(solution)/shard_map/ppermute | solution.py:260
  91.5 7.5 %all-to-all-done.2 = f32[12,8,256]{2,1,0:T(8,128)} async-done(((f32[12,8,256]{2,1,0:T(8,128)}), f32[12,8,256]{2,1,0:T(8,128)}, u32[]{:S(2)}, u32[]{:S(2)}) %all-to-all-start.2) | async-done | bytes 98336 | tf_op jit(solution)/shard_map/all_to_all | solution.py:264
  100.6 7.3 %all-to-all-start.3 = ((f32[24,8,256]{2,1,0:T(8,128)}), f32[24,8,256]{2,1,0:T(8,128)}, u32[]{:S(2)}, u32[]{:S(2)}) async-start(f32[24,8,256]{2,1,0:T(8,128)} %broadcast_in_dim.2), calls=%async_computation.3 | async-start | bytes 393216 | tf_op jit(solution)/shard_map/all_to_all | solution.py:268
  109.0 3.5 %outputs.1 = (bf16[8,32,640]{2,1,0:T(8,128)(2,1)}, bf16[8,32,640]{2,1,0:T(8,128)(2,1)}) custom-call(s32[4]{0:T(128)S(1)} %pad_add_fusion.1.place_ref, s32[32]{0:T(128)S(1)} %get-tuple-element.68.prev_ref, s32[32]{0:T(128)S(1)} %get-tuple-element.67.next_ref, bf16[8,32,640]{2,1,0:T(8,128)(2,1)S(1)} %copy-done.1, bf16[8,32,640]{2,1,0:T(8,128)(2,1)S(1)} %copy-done.3, ...), custom_call_target="tpu_custom_call" | custom-call | tf_op jit(solution)/shard_map/outputs/pallas_call | solution.py:207
  112.5 8.4 %all-to-all-done.3 = f32[24,8,256]{2,1,0:T(8,128)} async-done(((f32[24,8,256]{2,1,0:T(8,128)}), f32[24,8,256]{2,1,0:T(8,128)}, u32[]{:S(2)}, u32[]{:S(2)}) %all-to-all-start.3) | async-done | bytes 196640 | tf_op jit(solution)/shard_map/all_to_all | solution.py:268
  120.9 5.8 %all-gather = f32[48,8,256]{2,1,0:T(8,128)S(1)} all-gather(f32[24,8,256]{2,1,0:T(8,128)} %all-to-all-done.3), channel_id=2, replica_groups=mesh['xh'=2,'z'=12,'c'=2,'xl'=2,'y'=8] {'c'}, dimensions={0}, use_global_device_ids=true | all-gather | bytes 589824 | tf_op jit(solution)/shard_map/all_gather | solution.py:274
  (63 shorter events, 12.3 us)
Async XLA Ops:
  0.6 1.0 copy-start
  1.6 1.0 copy-start.2
  4.6 5.0 %copy-start.7 = (bf16[40,1920]{1,0:T(8,128)(2,1)S(1)}, bf16[40,1920]{1,0:T(8,128)(2,1)}, u32[]{:S(2)}) copy-start(bf16[40,1920]{1,0:T(8,128)(2,1)} %param.9) | copy-start | bytes 460804
  4.6 36.1 %copy-start.8 = (s32[48]{0:T(128)S(1)}, s32[48]{0:T(128)}, u32[]{:S(2)}) copy-start(s32[48]{0:T(128)} %param.10) | copy-start | bytes 580
  4.7 27.2 %all-to-all-start = ((bf16[4,256,640]{2,1,0:T(8,128)(2,1)}), bf16[4,256,640]{2,1,0:T(8,128)(2,1)S(1)}, u32[]{:S(2)}, u32[]{:S(2)}) async-start(bf16[4,256,640]{2,1,0:T(8,128)(2,1)} %pack.1), calls=%async_computation | async-start | bytes 2621440 | tf_op jit(solution)/shard_map/all_to_all | solution.py:233
  9.6 18.0 %collective-permute-start.2 = (bf16[40,1920]{1,0:T(8,128)(2,1)S(1)}, bf16[40,1920]{1,0:T(8,128)(2,1)S(1)}, u32[]{:S(2)}, u32[]{:S(2)}) collective-permute-start(bf16[40,1920]{1,0:T(8,128)(2,1)S(1)} %copy-done.7), channel_id=1, source_target_pairs={{0,3},{1,4},{2,5},{3,6},{4,7},{5,0},{6,1},{7,2},{16,21},{17,22},{1... | collective-permute-start | bytes 460808 | tf_op jit(solution)/shard_map/ppermute | solution.py:228
  16.3 11.3 %collective-permute-start.1 = (bf16[40,1920]{1,0:T(8,128)(2,1)S(1)}, bf16[40,1920]{1,0:T(8,128)(2,1)S(1)}, u32[]{:S(2)}, u32[]{:S(2)}) collective-permute-start(bf16[40,1920]{1,0:T(8,128)(2,1)S(1)} %copy-done.7), channel_id=1, source_target_pairs={{0,2},{1,3},{2,4},{3,5},{4,6},{5,7},{6,0},{7,1},{16,22},{17,23},{1... | collective-permute-start | bytes 460808 | tf_op jit(solution)/shard_map/ppermute | solution.py:228
  19.2 8.5 %collective-permute-start = (bf16[40,1920]{1,0:T(8,128)(2,1)S(1)}, bf16[40,1920]{1,0:T(8,128)(2,1)S(1)}, u32[]{:S(2)}, u32[]{:S(2)}) collective-permute-start(bf16[40,1920]{1,0:T(8,128)(2,1)S(1)} %copy-done.7), channel_id=1, source_target_pairs={{0,1},{1,2},{2,3},{3,4},{4,5},{5,6},{6,7},{7,0},{16,23},{17,16},{1... | collective-permute-start | bytes 460808 | tf_op jit(solution)/shard_map/ppermute | solution.py:228
  21.3 10.6 %collective-permute-start.3 = (bf16[40,1920]{1,0:T(8,128)(2,1)S(1)}, bf16[40,1920]{1,0:T(8,128)(2,1)S(1)}, u32[]{:S(2)}, u32[]{:S(2)}) collective-permute-start(bf16[40,1920]{1,0:T(8,128)(2,1)S(1)} %copy-done.7), channel_id=1, source_target_pairs={{16,20},{17,21},{18,22},{19,23},{20,16},{21,17},{22,18},{23,19},{2... | collective-permute-start | bytes 460808 | tf_op jit(solution)/shard_map/ppermute | solution.py:228
  31.8 12.9 %collective-permute-start.4 = (bf16[4,8,32,640]{3,2,1,0:T(8,128)(2,1)S(1)}, bf16[4,8,32,640]{3,2,1,0:T(8,128)(2,1)S(1)}, u32[]{:S(2)}, u32[]{:S(2)}) collective-permute-start(bf16[4,8,32,640]{3,2,1,0:T(8,128)(2,1)S(1)} %bitcast.62), channel_id=1, source_target_pairs={{0,16},{16,0},{1,17},{17,1},{2,18},{18,2},{3,19},{19,3},{4,20},{20... | collective-permute-start | bytes 3932168 | tf_op jit(solution)/shard_map/ppermute | solution.py:235
  38.6 6.1 %collective-permute-start.5 = (bf16[4,32,384]{2,1,0:T(8,128)(2,1)}, bf16[4,32,384]{2,1,0:T(8,128)(2,1)S(1)}, u32[]{:S(2)}, u32[]{:S(2)}) collective-permute-start(bf16[4,32,384]{2,1,0:T(8,128)(2,1)} %fusion.3), channel_id=1, source_target_pairs={{0,368},{32,16},{64,48},{96,80},{128,112},{160,144},{192,176},{224... | collective-permute-start | bytes 294920 | tf_op jit(solution)/shard_map/ppermute | solution.py:238
  48.1 19.7 %copy-start.1 = (bf16[8,32,640]{2,1,0:T(8,128)(2,1)S(1)}, bf16[8,32,640]{2,1,0:T(8,128)(2,1)}, u32[]{:S(2)}) copy-start(bf16[8,32,640]{2,1,0:T(8,128)(2,1)} %f_ref) | copy-start | bytes 983044
  48.1 19.7 %copy-start.3 = (bf16[8,32,640]{2,1,0:T(8,128)(2,1)S(1)}, bf16[8,32,640]{2,1,0:T(8,128)(2,1)}, u32[]{:S(2)}) copy-start(bf16[8,32,640]{2,1,0:T(8,128)(2,1)} %g_ref) | copy-start | bytes 983044
  48.1 34.8 %all-to-all-start.1 = ((f32[8,40,512]{2,1,0:T(8,128)}), f32[8,40,512]{2,1,0:T(8,128)}, u32[]{:S(2)}, u32[]{:S(2)}) async-start(f32[8,40,512]{2,1,0:T(8,128)} %bitcast.7), calls=%async_computation.1 | async-start | bytes 1310720 | tf_op jit(solution)/shard_map/all_to_all | solution.py:258
  52.6 55.4 %copy-start.4 = (bf16[8,32,640]{2,1,0:T(8,128)(2,1)S(1)}, bf16[8,32,640]{2,1,0:T(8,128)(2,1)}, u32[]{:S(2)}) copy-start(bf16[8,32,640]{2,1,0:T(8,128)(2,1)} %skip_ref.1) | copy-start | bytes 983044
  52.6 23.5 %collective-permute-start.9 = (bf16[4,40,1920]{2,1,0:T(8,128)(2,1)S(1)}, bf16[4,40,1920]{2,1,0:T(8,128)(2,1)S(1)}, u32[]{:S(2)}, u32[]{:S(2)}) collective-permute-start(bf16[4,40,1920]{2,1,0:T(8,128)(2,1)S(1)} %fusion.1.refs_0_), channel_id=1, source_target_pairs={{0,16},{16,0},{1,17},{17,1},{2,18},{18,2},{3,19},{19,3},{4,20},{20... | collective-permute-start | bytes 1843208 | tf_op jit(solution)/shard_map/ppermute | solution.py:256
  63.5 19.3 %collective-permute-start.8 = (bf16[4,40,1920]{2,1,0:T(8,128)(2,1)S(1)}, bf16[4,40,1920]{2,1,0:T(8,128)(2,1)S(1)}, u32[]{:S(2)}, u32[]{:S(2)}) collective-permute-start(bf16[4,40,1920]{2,1,0:T(8,128)(2,1)S(1)} %fusion.1.refs_0_), channel_id=1, source_target_pairs={{0,8},{8,0},{1,9},{9,1},{2,10},{10,2},{3,11},{11,3},{4,12},{12,4},... | collective-permute-start | bytes 1843208 | tf_op jit(solution)/shard_map/ppermute | solution.py:255
  67.9 4.1 %collective-permute-start.7 = (bf16[32,1280]{1,0:T(8,128)(2,1)S(1)}, bf16[32,1280]{1,0:T(8,128)(2,1)S(1)}, u32[]{:S(2)}, u32[]{:S(2)}) collective-permute-start(bf16[32,1280]{1,0:T(8,128)(2,1)S(1)} %get-tuple-element.63), channel_id=1, source_target_pairs={{0,16},{16,0},{1,17},{17,1},{2,18},{18,2},{3,19},{19,3},{4,20},{20... | collective-permute-start | bytes 245768 | tf_op jit(solution)/shard_map/ppermute | solution.py:250
  70.1 6.1 %collective-permute-start.6 = (bf16[32,1280]{1,0:T(8,128)(2,1)S(1)}, bf16[32,1280]{1,0:T(8,128)(2,1)S(1)}, u32[]{:S(2)}, u32[]{:S(2)}) collective-permute-start(bf16[32,1280]{1,0:T(8,128)(2,1)S(1)} %get-tuple-element.64), channel_id=1, source_target_pairs={{0,752},{16,32},{32,16},{48,64},{64,48},{80,96},{96,80},{112,128},... | collective-permute-start | bytes 245768 | tf_op jit(solution)/shard_map/ppermute | solution.py:252
  76.1 8.5 %copy-start.5 = (bf16[32,1280]{1,0:T(8,128)(2,1)}, bf16[32,1280]{1,0:T(8,128)(2,1)S(1)}, u32[]{:S(2)}) copy-start(bf16[32,1280]{1,0:T(8,128)(2,1)S(1)} %collective-permute-done.6.halo_ref) | copy-start | bytes 245764
  84.6 14.4 %all-to-all-start.2 = ((f32[12,8,256]{2,1,0:T(8,128)}), f32[12,8,256]{2,1,0:T(8,128)}, u32[]{:S(2)}, u32[]{:S(2)}) async-start(f32[12,8,256]{2,1,0:T(8,128)} %bitcast.19), calls=%async_computation.2 | async-start | bytes 196608 | tf_op jit(solution)/shard_map/all_to_all | solution.py:264
  88.9 19.2 %collective-permute-start.10 = (bf16[4,40,1920]{2,1,0:T(8,128)(2,1)S(1)}, bf16[4,40,1920]{2,1,0:T(8,128)(2,1)S(1)}, u32[]{:S(2)}, u32[]{:S(2)}) collective-permute-start(bf16[4,40,1920]{2,1,0:T(8,128)(2,1)S(1)} %collective-permute-done.8.refs_1_), channel_id=1, source_target_pairs={{0,16},{16,0},{1,17},{17,1},{2,18},{18,2},{3,19},{19,3},{4,20},{20... | collective-permute-start | bytes 1843208 | tf_op jit(solution)/shard_map/ppermute | solution.py:260
  100.6 20.3 %all-to-all-start.3 = ((f32[24,8,256]{2,1,0:T(8,128)}), f32[24,8,256]{2,1,0:T(8,128)}, u32[]{:S(2)}, u32[]{:S(2)}) async-start(f32[24,8,256]{2,1,0:T(8,128)} %broadcast_in_dim.2), calls=%async_computation.3 | async-start | bytes 393216 | tf_op jit(solution)/shard_map/all_to_all | solution.py:268
  108.1 0.9 copy-start.6

commit v6 on v5

--- a/solution.py
+++ b/solution.py
@@ -1,3 +1,5 @@
+import math
+
 import jax
 import jax.numpy as jnp
 from jax import lax
@@ -157,6 +159,22 @@
     )(place, prev_ok, next_ok, own, sib, halo)
 
 
+def y_sum_kernel(part_ref, out_ref):
+    total = part_ref[0]
+    for i in range(1, part_ref.shape[0]):
+        total = total + part_ref[i]
+    rows = total.shape[0]
+    for i in range(out_ref.shape[0]):
+        row, col = i // 2 * 8, i % 2 * 256
+        out_ref[i] = total[row:row + 8, col:col + 256] if row < rows else jnp.zeros((8, 256), jnp.float32)
+
+
+def y_sum(part, pieces):
+    vmem = pl.BlockSpec(memory_space=pltpu.VMEM)
+    shape = jax.ShapeDtypeStruct((pieces, 8, 256), jnp.float32)
+    return pl.pallas_call(y_sum_kernel, out_shape=shape, in_specs=[vmem], out_specs=vmem, name="y_sum")(part)
+
+
 def out_kernel(place_ref, prev_ref, next_ref, f_ref, g_ref, skip_ref, halo_ref, edge_ref, *refs):
     weights, (out_ref, back_ref, f_lo, f_hi, g_lo, g_hi, blocks, weight) = refs[:4], refs[4:]
     frames, strip, width = f_ref.shape
@@ -168,7 +186,7 @@
         dst[pl.ds(j * strip, strip), :] = jnp.where(ok != 0, value, jnp.zeros_like(value))
 
     for src, lo, hi, lanes in ((f_ref, f_lo, f_hi, slice(0, width)), (g_ref, g_lo, g_hi, slice(width, 2 * width))):
-        halo, edge = halo_ref[:, lanes], edge_ref[:, lanes]
+        halo, edge = halo_ref[:, lanes], edge_ref[1 - core, :, lanes]
         for j in range(frames):
             put(lo, j, jnp.where(core == 0, halo, edge) if j == 0 else src[j - 1], prev_ref[at + j])
             put(hi, j, jnp.where(core == 0, edge, halo) if j == frames - 1 else src[j + 1], next_ref[at + j])
@@ -227,11 +245,11 @@
         near = [(i, (i + k) % n_y) for i in range(n_y)]
         return lax.ppermute(temporal_weight, ("c", "y"), far if 2 * k == n_y else near + far)
 
-    w_1, w_2, w_3, w_4 = [from_y(k) for k in (1, 2, 3, 4)]
+    w_4, w_3, w_2, w_1 = [from_y(k) for k in (4, 3, 2, 1)]
 
     both = [(0, 1), (1, 0)]
     own = lax.all_to_all(pack(features, cotangent), X, 0, 0, tiled=True).reshape(n_x, frames, strip, width)
-    own, w_1, w_2, w_3, w_4 = lax.optimization_barrier((own, w_1, w_2, w_3, w_4))
+    own, w_4, w_3, w_2, w_1 = lax.optimization_barrier((own, w_4, w_3, w_2, w_1))
     sib = lax.ppermute(own, "c", both)
     z_next = [(2 * i, (2 * i - 1) % (2 * n_z)) for i in range(n_z)] + [(2 * i + 1, (2 * i + 2) % (2 * n_z)) for i in range(n_z)]
     edge = jnp.where(core == 0, own[:, 0, :, :384], own[:, -1, :, :384])
@@ -247,7 +265,7 @@
 
     _, features, cotangent = lax.optimization_barrier((term, features, cotangent))
     ends = [jnp.concatenate([features[i], cotangent[i]], axis=1) for i in (0, -1)]
-    sib_edge = lax.ppermute(jnp.where(core == 0, ends[1], ends[0]), "c", both)
+    edges = lax.all_gather(jnp.where(core == 0, ends[1], ends[0]), "c")
     across = [(d, (d - 1) % n_dp if d % 2 == 0 else (d + 1) % n_dp) for d in range(n_dp)]
     halo = lax.ppermute(jnp.where(core == 0, ends[0], ends[1]), DP, across)
     blocks = jnp.where(core == 0, jnp.stack([temporal_weight, w_1, w_2, w_3]), jnp.stack([w_4, w_3, w_2, w_1]))
@@ -256,19 +274,20 @@
     blocks_sib = lax.ppermute(blocks, "c", both)
 
     part = lax.all_to_all(term.reshape(n_y, 320 // n_y, 512), "y", 0, 0, tiled=True)
-    part, halo, sib_edge, blocks_far, blocks_sib = lax.optimization_barrier((part, halo, sib_edge, blocks_far, blocks_sib))
+    part, halo, edges, blocks_sib = lax.optimization_barrier((part, halo, edges, blocks_sib))
+    local_rows = part.shape[1]
+    n_xz = 2 * n_z
+    pieces = y_sum(part, n_z)
+    _, blocks_far = lax.optimization_barrier((pieces, blocks_far))
+    mine = lax.all_to_all(pieces, "z", 0, 0, tiled=True)
+    mine = mine.sum(0) * (1.0 / math.sqrt(total_frames * strip * lax.axis_size(FSDP)))
+    mine = jnp.broadcast_to(mine[None], (n_xz, 8, 256))
     weights = (blocks, blocks_far, blocks_sib, lax.ppermute(blocks_far, "c", both))
-    part = part.sum(0)
-    local_rows = part.shape[0]
-    blocks = jnp.pad(part, ((0, 48 - local_rows), (0, 0))).reshape(6, 8, 2, 256).transpose(0, 2, 1, 3)
-    mine = lax.all_to_all(blocks.reshape(n_z, 8, 256), "z", 0, 0, tiled=True).sum(0)
-    mine = mine / jnp.sqrt(jnp.float32(total_frames * strip * lax.axis_size(FSDP)))
     _, weights = lax.optimization_barrier((mine, weights))
-    n_xz = 2 * n_z
-    gathered = lax.all_to_all(jnp.broadcast_to(mine[None], (n_xz, 8, 256)), ("xh", "z"), 0, 0, tiled=True)
+    gathered = lax.all_to_all(mine, ("xh", "z"), 0, 0, tiled=True)
     place_out = jnp.stack([core, xh * (2 * frames) + core * frames, xl, y]).astype(jnp.int32)
     block_out, grad_features = outputs(
-        place_out, prev_all, next_all, features, cotangent, skip_input, halo, sib_edge, *weights
+        place_out, prev_all, next_all, features, cotangent, skip_input, halo, edges, *weights
     )
     gathered, block_out, grad_features = lax.optimization_barrier((gathered, block_out, grad_features))
     gathered = lax.all_gather(gathered, "c")

time: 129 us -> 128 us (level)
  waiting for transfers between devices: 33.1 us -> 22.2 us
  blocking collectives: 5.76 us -> 11.8 us
  starting transfers between devices: 68 us -> 73.4 us
  other arithmetic: 4.27 us -> 2.25 us
  Pallas kernels: 8.93 us -> 10.6 us
    all_to_all x2, starting transfers between devices: 11.6 us -> 18.4 us  [the longest x1 11.6 us: shards(): mine = lax.all_to_all(pieces, 'z', 0, 0, tiled=True)]
    ppermute x1, waiting for transfers between devices: 6.72 us -> 0.01 us  [shards(): blocks_far = lax.ppermute(blocks, 'xl', both)]
    all_gather x0 -> x1, blocking collectives: none -> 6.06 us  [shards(): edges = lax.all_gather(jnp.where(core == 0, ends[1], ends[0]), 'c')]
    ppermute x1, waiting for transfers between devices: 4.12 us -> 0.01 us  [shards(): halo = lax.ppermute(jnp.where(core == 0, ends[0], ends[1]), DP, across)]
    ppermute x1 -> x0, starting transfers between devices: 2.2 us -> none  [shards(): sib_edge = lax.ppermute(jnp.where(core == 0, ends[1], ends[0]), 'c', both)]
    reduce_sum x2 -> x1, other arithmetic: 2.05 us -> 0.01 us  [shards(): mine.sum(0) * (1.0 / math.sqrt(total_frames * strip * lax.axis_size(FSDP)))]
    pallas_call x0 -> x1, Pallas kernels: none -> 1.76 us  [y_sum(): pl.pallas_call(y_sum_kernel, out_shape=shape, in_specs=[vmem], out_specs=...]
    unnamed x18 -> x14, local copies, waits for them, and re-layouts: 2.85 us -> 2.94 us
  transfers between devices with their start and end apart: 15 -> 14, of which waited for: 6 -> 5; matrix products, arithmetic and copies ran while one was open for 4% -> 3% of each run, Pallas kernels for 3% -> 4%
where the time goes in v6:
time: 128 us; the launch traced here: 127 us
  starting transfers between devices  73.4 us (57%)
  waiting for transfers between devices  22.2 us (17%)
  blocking collectives  11.8 us (9%)
  Pallas kernels  10.6 us (8%)
  local copies, waits for them, and re-layouts  5.55 us (4%)
  other arithmetic  2.25 us (2%)
  between operations  1.64 us (1%)
    ppermute x4, starting transfers between devices, from_y(): lax.ppermute(temporal_weight, ('c', 'y'), far if 2 * k == n_y else near +...  17.3 us
    all_to_all x1, starting transfers between devices, shards(): mine = lax.all_to_all(pieces, 'z', 0, 0, tiled=True)  11.6 us
    ppermute x1, starting transfers between devices, shards(): blocks_sib = lax.ppermute(blocks, 'c', both)  11.5 us
    all_to_all x1, waiting for transfers between devices, shards(): gathered = lax.all_to_all(mine, ('xh', 'z'), 0, 0, tiled=True)  8.37 us
    all_to_all x1, waiting for transfers between devices, shards(): mine = lax.all_to_all(pieces, 'z', 0, 0, tiled=True)  7.45 us
    ppermute x1, starting transfers between devices, shards(): sib = lax.ppermute(own, 'c', both)  6.84 us
    all_to_all x1, starting transfers between devices, shards(): gathered = lax.all_to_all(mine, ('xh', 'z'), 0, 0, tiled=True)  6.78 us
    all_gather x1, blocking collectives, shards(): edges = lax.all_gather(jnp.where(core == 0, ends[1], ends[0]), 'c')  6.06 us
  transfers between devices with their start and end apart: 14, of which 5 were waited for; matrix products, arithmetic and copies ran while one was open for 3% of the time, Pallas kernels for 4%

profile of v6, /device:TPU:1, one launch (start us, length us, event | category | flops | bytes accessed | tf_op | source)
XLA Modules:
  0.0 127.4 jit_solution(12748288588734621176)
XLA Ops:
  2.6 2.1 %pack.1 = bf16[4,256,640]{2,1,0:T(8,128)(2,1)} custom-call(bf16[8,32,640]{2,1,0:T(8,128)(2,1)S(1)} %copy-done, bf16[8,32,640]{2,1,0:T(8,128)(2,1)S(1)} %copy-done.2), custom_call_target="tpu_custom_call" | custom-call | tf_op jit(solution)/shard_map/pack/pallas_call | solution.py:65
  4.7 5.0 %all-to-all-start = ((bf16[4,256,640]{2,1,0:T(8,128)(2,1)}), bf16[4,256,640]{2,1,0:T(8,128)(2,1)S(1)}, u32[]{:S(2)}, u32[]{:S(2)}) async-start(bf16[4,256,640]{2,1,0:T(8,128)(2,1)} %pack.1), calls=%async_computation | async-start | bytes 2621440 | tf_op jit(solution)/shard_map/all_to_all | solution.py:251
  9.7 5.9 %collective-permute-start.2 = (bf16[40,1920]{1,0:T(8,128)(2,1)S(1)}, bf16[40,1920]{1,0:T(8,128)(2,1)S(1)}, u32[]{:S(2)}, u32[]{:S(2)}) collective-permute-start(bf16[40,1920]{1,0:T(8,128)(2,1)S(1)} %copy-done.5), channel_id=1, source_target_pairs={{0,2},{1,3},{2,4},{3,5},{4,6},{5,7},{6,0},{7,1},{16,22},{17,23},{1... | collective-permute-start | bytes 460808 | tf_op jit(solution)/shard_map/ppermute | solution.py:246
  15.5 3.6 %collective-permute-start.1 = (bf16[40,1920]{1,0:T(8,128)(2,1)S(1)}, bf16[40,1920]{1,0:T(8,128)(2,1)S(1)}, u32[]{:S(2)}, u32[]{:S(2)}) collective-permute-start(bf16[40,1920]{1,0:T(8,128)(2,1)S(1)} %copy-done.5), channel_id=1, source_target_pairs={{0,3},{1,4},{2,5},{3,6},{4,7},{5,0},{6,1},{7,2},{16,21},{17,22},{1... | collective-permute-start | bytes 460808 | tf_op jit(solution)/shard_map/ppermute | solution.py:246
  19.2 4.8 %collective-permute-start = (bf16[40,1920]{1,0:T(8,128)(2,1)S(1)}, bf16[40,1920]{1,0:T(8,128)(2,1)S(1)}, u32[]{:S(2)}, u32[]{:S(2)}) collective-permute-start(bf16[40,1920]{1,0:T(8,128)(2,1)S(1)} %copy-done.5), channel_id=1, source_target_pairs={{16,20},{17,21},{18,22},{19,23},{20,16},{21,17},{22,18},{23,19},{2... | collective-permute-start | bytes 460808 | tf_op jit(solution)/shard_map/ppermute | solution.py:246
  24.0 3.0 %collective-permute-start.3 = (bf16[40,1920]{1,0:T(8,128)(2,1)S(1)}, bf16[40,1920]{1,0:T(8,128)(2,1)S(1)}, u32[]{:S(2)}, u32[]{:S(2)}) collective-permute-start(bf16[40,1920]{1,0:T(8,128)(2,1)S(1)} %copy-done.5), channel_id=1, source_target_pairs={{0,1},{1,2},{2,3},{3,4},{4,5},{5,6},{6,7},{7,0},{16,23},{17,16},{1... | collective-permute-start | bytes 460808 | tf_op jit(solution)/shard_map/ppermute | solution.py:246
  27.6 3.9 %collective-permute-done = bf16[40,1920]{1,0:T(8,128)(2,1)S(1)} collective-permute-done((bf16[40,1920]{1,0:T(8,128)(2,1)S(1)}, bf16[40,1920]{1,0:T(8,128)(2,1)S(1)}, u32[]{:S(2)}, u32[]{:S(2)}) %collective-permute-start) | collective-permute-done | bytes 153632 | tf_op jit(solution)/shard_map/ppermute | solution.py:246
  31.6 6.8 %collective-permute-start.4 = (bf16[4,8,32,640]{3,2,1,0:T(8,128)(2,1)S(1)}, bf16[4,8,32,640]{3,2,1,0:T(8,128)(2,1)S(1)}, u32[]{:S(2)}, u32[]{:S(2)}) collective-permute-start(bf16[4,8,32,640]{3,2,1,0:T(8,128)(2,1)S(1)} %bitcast.57), channel_id=1, source_target_pairs={{0,16},{16,0},{1,17},{17,1},{2,18},{18,2},{3,19},{19,3},{4,20},{20... | collective-permute-start | bytes 3932168 | tf_op jit(solution)/shard_map/ppermute | solution.py:253
  39.4 1.9 %collective-permute-start.5 = (bf16[4,32,384]{2,1,0:T(8,128)(2,1)}, bf16[4,32,384]{2,1,0:T(8,128)(2,1)S(1)}, u32[]{:S(2)}, u32[]{:S(2)}) collective-permute-start(bf16[4,32,384]{2,1,0:T(8,128)(2,1)} %fusion.3), channel_id=1, source_target_pairs={{0,368},{32,16},{64,48},{96,80},{128,112},{160,144},{192,176},{224... | collective-permute-start | bytes 294920 | tf_op jit(solution)/shard_map/ppermute | solution.py:256
  43.2 2.4 %collective-permute-done.5.halo_ref = bf16[4,32,384]{2,1,0:T(8,128)(2,1)S(1)} collective-permute-done((bf16[4,32,384]{2,1,0:T(8,128)(2,1)}, bf16[4,32,384]{2,1,0:T(8,128)(2,1)S(1)}, u32[]{:S(2)}, u32[]{:S(2)}) %collective-permute-start.5) | collective-permute-done | bytes 98336 | tf_op jit(solution)/shard_map/ppermute | solution.py:256
  45.6 3.3 %x_term.1 = f32[320,512]{1,0:T(8,128)} custom-call(s32[3]{0:T(128)S(1)} %pad_add_fusion.place_ref, s32[32]{0:T(128)S(1)} %get-tuple-element.70.prev_ref, s32[32]{0:T(128)S(1)} %get-tuple-element.69.next_ref, bf16[4,8,32,640]{3,2,1,0:T(8,128)(2,1)S(1)} %bitcast.59, bf16[4,8,32,640]{3,2,1,0:T(8,128)(2,1)S(1)} %collective-permute-done.4.sib_ref, ...), custom_call_target="tpu_custom_call" | custom-call | tf_op jit(solution)/shard_map/x_term/pallas_call | solution.py:151
  48.9 4.3 %all-to-all-start.1 = ((f32[8,40,512]{2,1,0:T(8,128)}), f32[8,40,512]{2,1,0:T(8,128)}, u32[]{:S(2)}, u32[]{:S(2)}) async-start(f32[8,40,512]{2,1,0:T(8,128)} %bitcast.7), calls=%async_computation.1 | async-start | bytes 1310720 | tf_op jit(solution)/shard_map/all_to_all | solution.py:276
  53.4 3.7 %collective-permute-start.8 = (bf16[4,40,1920]{2,1,0:T(8,128)(2,1)S(1)}, bf16[4,40,1920]{2,1,0:T(8,128)(2,1)S(1)}, u32[]{:S(2)}, u32[]{:S(2)}) collective-permute-start(bf16[4,40,1920]{2,1,0:T(8,128)(2,1)S(1)} %fusion.1.refs_0_), channel_id=1, source_target_pairs={{0,8},{8,0},{1,9},{9,1},{2,10},{10,2},{3,11},{11,3},{4,12},{12,4},... | collective-permute-start | bytes 1843208 | tf_op jit(solution)/shard_map/ppermute | solution.py:273
  57.1 11.5 %collective-permute-start.7 = (bf16[4,40,1920]{2,1,0:T(8,128)(2,1)S(1)}, bf16[4,40,1920]{2,1,0:T(8,128)(2,1)S(1)}, u32[]{:S(2)}, u32[]{:S(2)}) collective-permute-start(bf16[4,40,1920]{2,1,0:T(8,128)(2,1)S(1)} %fusion.1.refs_0_), channel_id=1, source_target_pairs={{0,16},{16,0},{1,17},{17,1},{2,18},{18,2},{3,19},{19,3},{4,20},{20... | collective-permute-start | bytes 1843208 | tf_op jit(solution)/shard_map/ppermute | solution.py:274
  68.7 1.9 %collective-permute-start.6 = (bf16[32,1280]{1,0:T(8,128)(2,1)S(1)}, bf16[32,1280]{1,0:T(8,128)(2,1)S(1)}, u32[]{:S(2)}, u32[]{:S(2)}) collective-permute-start(bf16[32,1280]{1,0:T(8,128)(2,1)S(1)} %maximum_select_fusion), channel_id=1, source_target_pairs={{0,752},{16,32},{32,16},{48,64},{64,48},{80,96},{96,80},{112,128},... | collective-permute-start | bytes 245768 | tf_op jit(solution)/shard_map/ppermute | solution.py:270
  70.7 6.1 %all_gather.10.edge_ref = bf16[2,32,1280]{2,1,0:T(8,128)(2,1)S(1)} all-gather(bf16[1,32,1280]{2,1,0:T(8,128)(2,1)S(1)} %maximum_select_fusion.1), channel_id=1, replica_groups=mesh['xh'=2,'z'=12,'c'=2,'xl'=2,'y'=8] {'c'}, dimensions={0}, use_global_device_ids=true | all-gather | bytes 245760 | tf_op jit(solution)/shard_map/all_gather | solution.py:268
  76.8 1.8 %y_sum.1 = f32[12,8,256]{2,1,0:T(8,128)} custom-call(f32[8,40,512]{2,1,0:T(8,128)} %all-to-all-done.1.part_ref), custom_call_target="tpu_custom_call" | custom-call | tf_op jit(solution)/shard_map/y_sum/pallas_call | solution.py:175
  78.5 11.6 %all-to-all-start.2 = ((f32[12,8,256]{2,1,0:T(8,128)}), f32[12,8,256]{2,1,0:T(8,128)S(1)}, u32[]{:S(2)}, u32[]{:S(2)}) async-start(f32[12,8,256]{2,1,0:T(8,128)} %y_sum.1), calls=%async_computation.2 | async-start | bytes 196608 | tf_op jit(solution)/shard_map/all_to_all | solution.py:282
  90.1 2.6 %collective-permute-start.9 = (bf16[4,40,1920]{2,1,0:T(8,128)(2,1)S(1)}, bf16[4,40,1920]{2,1,0:T(8,128)(2,1)S(1)}, u32[]{:S(2)}, u32[]{:S(2)}) collective-permute-start(bf16[4,40,1920]{2,1,0:T(8,128)(2,1)S(1)} %collective-permute-done.8.refs_1_), channel_id=1, source_target_pairs={{0,16},{16,0},{1,17},{17,1},{2,18},{18,2},{3,19},{19,3},{4,20},{20... | collective-permute-start | bytes 1843208 | tf_op jit(solution)/shard_map/ppermute | solution.py:285
  92.7 7.5 %all-to-all-done.2 = f32[12,8,256]{2,1,0:T(8,128)S(1)} async-done(((f32[12,8,256]{2,1,0:T(8,128)}), f32[12,8,256]{2,1,0:T(8,128)S(1)}, u32[]{:S(2)}, u32[]{:S(2)}) %all-to-all-start.2) | async-done | bytes 98336 | tf_op jit(solution)/shard_map/all_to_all | solution.py:282
  100.9 6.8 %all-to-all-start.3 = ((f32[24,8,256]{2,1,0:T(8,128)}), f32[24,8,256]{2,1,0:T(8,128)}, u32[]{:S(2)}, u32[]{:S(2)}) async-start(f32[24,8,256]{2,1,0:T(8,128)} %broadcast_in_dim.2), calls=%async_computation.3 | async-start | bytes 393216 | tf_op jit(solution)/shard_map/all_to_all | solution.py:287
  108.7 3.5 %outputs.1 = (bf16[8,32,640]{2,1,0:T(8,128)(2,1)}, bf16[8,32,640]{2,1,0:T(8,128)(2,1)}) custom-call(s32[4]{0:T(128)S(1)} %pad_add_fusion.1.place_ref, s32[32]{0:T(128)S(1)} %get-tuple-element.70.prev_ref, s32[32]{0:T(128)S(1)} %get-tuple-element.69.next_ref, bf16[8,32,640]{2,1,0:T(8,128)(2,1)S(1)} %copy-done.1, bf16[8,32,640]{2,1,0:T(8,128)(2,1)S(1)} %copy-done.3, ...), custom_call_target="tpu_custom_call" | custom-call | tf_op jit(solution)/shard_map/outputs/pallas_call | solution.py:225
  112.2 8.4 %all-to-all-done.3 = f32[24,8,256]{2,1,0:T(8,128)} async-done(((f32[24,8,256]{2,1,0:T(8,128)}), f32[24,8,256]{2,1,0:T(8,128)}, u32[]{:S(2)}, u32[]{:S(2)}) %all-to-all-start.3) | async-done | bytes 196640 | tf_op jit(solution)/shard_map/all_to_all | solution.py:287
  120.6 5.8 %all-gather = f32[48,8,256]{2,1,0:T(8,128)S(1)} all-gather(f32[24,8,256]{2,1,0:T(8,128)} %all-to-all-done.3), channel_id=2, replica_groups=mesh['xh'=2,'z'=12,'c'=2,'xl'=2,'y'=8] {'c'}, dimensions={0}, use_global_device_ids=true | all-gather | bytes 589824 | tf_op jit(solution)/shard_map/all_gather | solution.py:293
  (58 shorter events, 7.9 us)
Async XLA Ops:
  0.6 1.0 copy-start
  1.6 1.0 copy-start.2
  4.6 5.0 %copy-start.5 = (bf16[40,1920]{1,0:T(8,128)(2,1)S(1)}, bf16[40,1920]{1,0:T(8,128)(2,1)}, u32[]{:S(2)}) copy-start(bf16[40,1920]{1,0:T(8,128)(2,1)} %param.9) | copy-start | bytes 460804
  4.7 36.7 %copy-start.6 = (s32[48]{0:T(128)S(1)}, s32[48]{0:T(128)}, u32[]{:S(2)}) copy-start(s32[48]{0:T(128)} %param.10) | copy-start | bytes 580
  4.7 26.9 %all-to-all-start = ((bf16[4,256,640]{2,1,0:T(8,128)(2,1)}), bf16[4,256,640]{2,1,0:T(8,128)(2,1)S(1)}, u32[]{:S(2)}, u32[]{:S(2)}) async-start(bf16[4,256,640]{2,1,0:T(8,128)(2,1)} %pack.1), calls=%async_computation | async-start | bytes 2621440 | tf_op jit(solution)/shard_map/all_to_all | solution.py:251
  9.7 18.0 %collective-permute-start.2 = (bf16[40,1920]{1,0:T(8,128)(2,1)S(1)}, bf16[40,1920]{1,0:T(8,128)(2,1)S(1)}, u32[]{:S(2)}, u32[]{:S(2)}) collective-permute-start(bf16[40,1920]{1,0:T(8,128)(2,1)S(1)} %copy-done.5), channel_id=1, source_target_pairs={{0,2},{1,3},{2,4},{3,5},{4,6},{5,7},{6,0},{7,1},{16,22},{17,23},{1... | collective-permute-start | bytes 460808 | tf_op jit(solution)/shard_map/ppermute | solution.py:246
  15.5 12.1 %collective-permute-start.1 = (bf16[40,1920]{1,0:T(8,128)(2,1)S(1)}, bf16[40,1920]{1,0:T(8,128)(2,1)S(1)}, u32[]{:S(2)}, u32[]{:S(2)}) collective-permute-start(bf16[40,1920]{1,0:T(8,128)(2,1)S(1)} %copy-done.5), channel_id=1, source_target_pairs={{0,3},{1,4},{2,5},{3,6},{4,7},{5,0},{6,1},{7,2},{16,21},{17,22},{1... | collective-permute-start | bytes 460808 | tf_op jit(solution)/shard_map/ppermute | solution.py:246
  19.2 12.3 %collective-permute-start = (bf16[40,1920]{1,0:T(8,128)(2,1)S(1)}, bf16[40,1920]{1,0:T(8,128)(2,1)S(1)}, u32[]{:S(2)}, u32[]{:S(2)}) collective-permute-start(bf16[40,1920]{1,0:T(8,128)(2,1)S(1)} %copy-done.5), channel_id=1, source_target_pairs={{16,20},{17,21},{18,22},{19,23},{20,16},{21,17},{22,18},{23,19},{2... | collective-permute-start | bytes 460808 | tf_op jit(solution)/shard_map/ppermute | solution.py:246
  24.0 7.6 %collective-permute-start.3 = (bf16[40,1920]{1,0:T(8,128)(2,1)S(1)}, bf16[40,1920]{1,0:T(8,128)(2,1)S(1)}, u32[]{:S(2)}, u32[]{:S(2)}) collective-permute-start(bf16[40,1920]{1,0:T(8,128)(2,1)S(1)} %copy-done.5), channel_id=1, source_target_pairs={{0,1},{1,2},{2,3},{3,4},{4,5},{5,6},{6,7},{7,0},{16,23},{17,16},{1... | collective-permute-start | bytes 460808 | tf_op jit(solution)/shard_map/ppermute | solution.py:246
  31.6 14.0 %collective-permute-start.4 = (bf16[4,8,32,640]{3,2,1,0:T(8,128)(2,1)S(1)}, bf16[4,8,32,640]{3,2,1,0:T(8,128)(2,1)S(1)}, u32[]{:S(2)}, u32[]{:S(2)}) collective-permute-start(bf16[4,8,32,640]{3,2,1,0:T(8,128)(2,1)S(1)} %bitcast.57), channel_id=1, source_target_pairs={{0,16},{16,0},{1,17},{17,1},{2,18},{18,2},{3,19},{19,3},{4,20},{20... | collective-permute-start | bytes 3932168 | tf_op jit(solution)/shard_map/ppermute | solution.py:253
  39.4 6.1 %collective-permute-start.5 = (bf16[4,32,384]{2,1,0:T(8,128)(2,1)}, bf16[4,32,384]{2,1,0:T(8,128)(2,1)S(1)}, u32[]{:S(2)}, u32[]{:S(2)}) collective-permute-start(bf16[4,32,384]{2,1,0:T(8,128)(2,1)} %fusion.3), channel_id=1, source_target_pairs={{0,368},{32,16},{64,48},{96,80},{128,112},{160,144},{192,176},{224... | collective-permute-start | bytes 294920 | tf_op jit(solution)/shard_map/ppermute | solution.py:256
  48.9 19.7 %copy-start.1 = (bf16[8,32,640]{2,1,0:T(8,128)(2,1)S(1)}, bf16[8,32,640]{2,1,0:T(8,128)(2,1)}, u32[]{:S(2)}) copy-start(bf16[8,32,640]{2,1,0:T(8,128)(2,1)} %f_ref) | copy-start | bytes 983044
  48.9 19.8 %copy-start.3 = (bf16[8,32,640]{2,1,0:T(8,128)(2,1)S(1)}, bf16[8,32,640]{2,1,0:T(8,128)(2,1)}, u32[]{:S(2)}) copy-start(bf16[8,32,640]{2,1,0:T(8,128)(2,1)} %g_ref) | copy-start | bytes 983044
  48.9 27.9 %all-to-all-start.1 = ((f32[8,40,512]{2,1,0:T(8,128)}), f32[8,40,512]{2,1,0:T(8,128)}, u32[]{:S(2)}, u32[]{:S(2)}) async-start(f32[8,40,512]{2,1,0:T(8,128)} %bitcast.7), calls=%async_computation.1 | async-start | bytes 1310720 | tf_op jit(solution)/shard_map/all_to_all | solution.py:276
  53.4 36.7 %collective-permute-start.8 = (bf16[4,40,1920]{2,1,0:T(8,128)(2,1)S(1)}, bf16[4,40,1920]{2,1,0:T(8,128)(2,1)S(1)}, u32[]{:S(2)}, u32[]{:S(2)}) collective-permute-start(bf16[4,40,1920]{2,1,0:T(8,128)(2,1)S(1)} %fusion.1.refs_0_), channel_id=1, source_target_pairs={{0,8},{8,0},{1,9},{9,1},{2,10},{10,2},{3,11},{11,3},{4,12},{12,4},... | collective-permute-start | bytes 1843208 | tf_op jit(solution)/shard_map/ppermute | solution.py:273
  57.1 19.7 %collective-permute-start.7 = (bf16[4,40,1920]{2,1,0:T(8,128)(2,1)S(1)}, bf16[4,40,1920]{2,1,0:T(8,128)(2,1)S(1)}, u32[]{:S(2)}, u32[]{:S(2)}) collective-permute-start(bf16[4,40,1920]{2,1,0:T(8,128)(2,1)S(1)} %fusion.1.refs_0_), channel_id=1, source_target_pairs={{0,16},{16,0},{1,17},{17,1},{2,18},{18,2},{3,19},{19,3},{4,20},{20... | collective-permute-start | bytes 1843208 | tf_op jit(solution)/shard_map/ppermute | solution.py:274
  68.7 8.0 %collective-permute-start.6 = (bf16[32,1280]{1,0:T(8,128)(2,1)S(1)}, bf16[32,1280]{1,0:T(8,128)(2,1)S(1)}, u32[]{:S(2)}, u32[]{:S(2)}) collective-permute-start(bf16[32,1280]{1,0:T(8,128)(2,1)S(1)} %maximum_select_fusion), channel_id=1, source_target_pairs={{0,752},{16,32},{32,16},{48,64},{64,48},{80,96},{96,80},{112,128},... | collective-permute-start | bytes 245768 | tf_op jit(solution)/shard_map/ppermute | solution.py:270
  78.5 21.6 %all-to-all-start.2 = ((f32[12,8,256]{2,1,0:T(8,128)}), f32[12,8,256]{2,1,0:T(8,128)S(1)}, u32[]{:S(2)}, u32[]{:S(2)}) async-start(f32[12,8,256]{2,1,0:T(8,128)} %y_sum.1), calls=%async_computation.2 | async-start | bytes 196608 | tf_op jit(solution)/shard_map/all_to_all | solution.py:282
  90.1 17.6 %collective-permute-start.9 = (bf16[4,40,1920]{2,1,0:T(8,128)(2,1)S(1)}, bf16[4,40,1920]{2,1,0:T(8,128)(2,1)S(1)}, u32[]{:S(2)}, u32[]{:S(2)}) collective-permute-start(bf16[4,40,1920]{2,1,0:T(8,128)(2,1)S(1)} %collective-permute-done.8.refs_1_), channel_id=1, source_target_pairs={{0,16},{16,0},{1,17},{17,1},{2,18},{18,2},{3,19},{19,3},{4,20},{20... | collective-permute-start | bytes 1843208 | tf_op jit(solution)/shard_map/ppermute | solution.py:285
  100.9 19.7 %all-to-all-start.3 = ((f32[24,8,256]{2,1,0:T(8,128)}), f32[24,8,256]{2,1,0:T(8,128)}, u32[]{:S(2)}, u32[]{:S(2)}) async-start(f32[24,8,256]{2,1,0:T(8,128)} %broadcast_in_dim.2), calls=%async_computation.3 | async-start | bytes 393216 | tf_op jit(solution)/shard_map/all_to_all | solution.py:287
  107.8 1.0 copy-start.4

commit v7 on v6

--- a/solution.py
+++ b/solution.py
@@ -179,7 +179,7 @@
     weights, (out_ref, back_ref, f_lo, f_hi, g_lo, g_hi, blocks, weight) = refs[:4], refs[4:]
     frames, strip, width = f_ref.shape
     tokens = frames * strip
-    core, at, xl, y = [place_ref[i] for i in range(4)]
+    core, at, xl, y, parity = [place_ref[i] for i in range(5)]
     count, rows = weights[0].shape[:2]
 
     def put(dst, j, value, ok):
@@ -192,9 +192,11 @@
             put(hi, j, jnp.where(core == 0, edge, halo) if j == frames - 1 else src[j + 1], next_ref[at + j])
 
     for i in range(count):
+        odd = parity if i < 2 else 1 - parity
+        low, high = (3 + odd, jnp.where(odd == 0, 5, 0)) if i % 2 == 0 else (1 + odd, 7 - odd)
         for half in range(2):
-            blocks[half, core * count + i] = weights[half][i]
-            blocks[half, (1 - core) * count + i] = weights[2 + half][i]
+            blocks[half, jnp.where(core == 0, low, high)] = weights[half][i]
+            blocks[half, jnp.where(core == 0, high, low)] = weights[2 + half][i]
     for half in range(2):
         for i in range(2 * count):
             start = (half * 2 * count + i) * rows
@@ -240,16 +242,20 @@
     n_dp = lax.axis_size(DP)
     total_frames = frames * n_dp
 
-    def from_y(k):
-        far = [(n_y + i, n_y + (i - k) % n_y) for i in range(n_y)]
-        near = [(i, (i + k) % n_y) for i in range(n_y)]
-        return lax.ppermute(temporal_weight, ("c", "y"), far if 2 * k == n_y else near + far)
-
-    w_4, w_3, w_2, w_1 = [from_y(k) for k in (4, 3, 2, 1)]
+    def from_y(even, odd):
+        pairs = []
+        for plane in range(n_z):
+            distance = (even, odd)[plane % 2]
+            for side in range(2 if 2 * distance < n_y else 1):
+                base = (2 * plane + side) * n_y
+                pairs += [(base + i, base + (i + (1 - 2 * side) * distance) % n_y) for i in range(n_y)]
+        return lax.ppermute(temporal_weight, ("z", "c", "y"), pairs)
+
+    w_far, w_near = from_y(3, 4), from_y(1, 2)
 
     both = [(0, 1), (1, 0)]
     own = lax.all_to_all(pack(features, cotangent), X, 0, 0, tiled=True).reshape(n_x, frames, strip, width)
-    own, w_4, w_3, w_2, w_1 = lax.optimization_barrier((own, w_4, w_3, w_2, w_1))
+    own, w_far, w_near = lax.optimization_barrier((own, w_far, w_near))
     sib = lax.ppermute(own, "c", both)
     z_next = [(2 * i, (2 * i - 1) % (2 * n_z)) for i in range(n_z)] + [(2 * i + 1, (2 * i + 2) % (2 * n_z)) for i in range(n_z)]
     edge = jnp.where(core == 0, own[:, 0, :, :384], own[:, -1, :, :384])
@@ -268,24 +274,27 @@
     edges = lax.all_gather(jnp.where(core == 0, ends[1], ends[0]), "c")
     across = [(d, (d - 1) % n_dp if d % 2 == 0 else (d + 1) % n_dp) for d in range(n_dp)]
     halo = lax.ppermute(jnp.where(core == 0, ends[0], ends[1]), DP, across)
-    blocks = jnp.where(core == 0, jnp.stack([temporal_weight, w_1, w_2, w_3]), jnp.stack([w_4, w_3, w_2, w_1]))
-    _, blocks = lax.optimization_barrier((term, blocks))
+    _, w_far, w_near = lax.optimization_barrier((term, w_far, w_near))
+    parity = z % 2
+    pair = jnp.stack([jnp.where((parity == 1) & (core == 1), temporal_weight, w_far), w_near])
+    pair_far = lax.ppermute(pair, "z", [(i, i ^ 1) for i in range(n_z)])
+    blocks = jnp.concatenate([pair, pair_far])
     blocks_far = lax.ppermute(blocks, "xl", both)
     blocks_sib = lax.ppermute(blocks, "c", both)
 
     part = lax.all_to_all(term.reshape(n_y, 320 // n_y, 512), "y", 0, 0, tiled=True)
-    part, halo, edges, blocks_sib = lax.optimization_barrier((part, halo, edges, blocks_sib))
+    part, halo, edges = lax.optimization_barrier((part, halo, edges))
     local_rows = part.shape[1]
     n_xz = 2 * n_z
     pieces = y_sum(part, n_z)
-    _, blocks_far = lax.optimization_barrier((pieces, blocks_far))
+    _, blocks_far, blocks_sib = lax.optimization_barrier((pieces, blocks_far, blocks_sib))
     mine = lax.all_to_all(pieces, "z", 0, 0, tiled=True)
     mine = mine.sum(0) * (1.0 / math.sqrt(total_frames * strip * lax.axis_size(FSDP)))
     mine = jnp.broadcast_to(mine[None], (n_xz, 8, 256))
     weights = (blocks, blocks_far, blocks_sib, lax.ppermute(blocks_far, "c", both))
     _, weights = lax.optimization_barrier((mine, weights))
     gathered = lax.all_to_all(mine, ("xh", "z"), 0, 0, tiled=True)
-    place_out = jnp.stack([core, xh * (2 * frames) + core * frames, xl, y]).astype(jnp.int32)
+    place_out = jnp.stack([core, xh * (2 * frames) + core * frames, xl, y, parity]).astype(jnp.int32)
     block_out, grad_features = outputs(
         place_out, prev_all, next_all, features, cotangent, skip_input, halo, edges, *weights
     )

time: 128 us -> 125 us (0.977)
  waiting for transfers between devices: 22.2 us -> 31.9 us
  starting transfers between devices: 73.4 us -> 64.2 us
  blocking collectives: 11.8 us -> 10.1 us
  other arithmetic: 2.25 us -> 0.78 us
    all_to_all x1, starting transfers between devices: 11.6 us -> 5.37 us  [shards(): mine = lax.all_to_all(pieces, 'z', 0, 0, tiled=True)]
    ppermute x4 -> x3, starting transfers between devices: 17.3 us -> 13.6 us  [the longest x2 9.63 us: from_y(): return lax.ppermute(temporal_weight, ('z', 'c', 'y'), pairs)]
    ppermute x4 -> x3, waiting for transfers between devices: 3.94 us -> 7.55 us  [the longest x1 4.16 us: shards(): pair_far = lax.ppermute(pair, 'z', [(i, i ^ 1) for i in range(n_z)])]
    all_gather x1, blocking collectives: 5.76 us -> 2.29 us  [shards(): gathered = lax.all_gather(gathered, 'c')]
    all_to_all x1, waiting for transfers between devices: 8.37 us -> 11.6 us  [shards(): gathered = lax.all_to_all(mine, ('xh', 'z'), 0, 0, tiled=True)]
    ppermute x1, starting transfers between devices: 6.84 us -> 9.64 us  [shards(): sib = lax.ppermute(own, 'c', both)]
    all_to_all x1, starting transfers between devices: 6.78 us -> 4.52 us  [shards(): gathered = lax.all_to_all(mine, ('xh', 'z'), 0, 0, tiled=True)]
    ppermute x1, starting transfers between devices: 11.5 us -> 13.5 us  [shards(): blocks_sib = lax.ppermute(blocks, 'c', both)]
  transfers between devices with their start and end apart: 14 -> 13, of which waited for: 5 -> 6; matrix products, arithmetic and copies ran while one was open for 3% -> 1% of each run, Pallas kernels for 4% -> 4%
where the time goes in v7:
time: 125 us; the launch traced here: 124 us
  starting transfers between devices  64.2 us (51%)
  waiting for transfers between devices  31.9 us (26%)
  Pallas kernels  10.7 us (9%)
  blocking collectives  10.1 us (8%)
  local copies, waits for them, and re-layouts  5.02 us (4%)
  between operations  1.64 us (1%)
    ppermute x1, starting transfers between devices, shards(): blocks_sib = lax.ppermute(blocks, 'c', both)  13.5 us
    all_to_all x1, waiting for transfers between devices, shards(): gathered = lax.all_to_all(mine, ('xh', 'z'), 0, 0, tiled=True)  11.6 us
    ppermute x1, starting transfers between devices, shards(): sib = lax.ppermute(own, 'c', both)  9.64 us
    ppermute x2, starting transfers between devices, from_y(): return lax.ppermute(temporal_weight, ('z', 'c', 'y'), pairs)  9.63 us
    all_to_all x1, waiting for transfers between devices, shards(): mine = lax.all_to_all(pieces, 'z', 0, 0, tiled=True)  9.22 us
    all_gather x1, blocking collectives, shards(): edges = lax.all_gather(jnp.where(core == 0, ends[1], ends[0]), 'c')  7.82 us
    all_to_all x1, starting transfers between devices, shards(): mine = lax.all_to_all(pieces, 'z', 0, 0, tiled=True)  5.37 us
    all_to_all x1, starting transfers between devices, shards(): lax.all_to_all(pack(features, cotangent), X, 0, 0, tiled=True)  4.99 us
  transfers between devices with their start and end apart: 13, of which 6 were waited for; matrix products, arithmetic and copies ran while one was open for 1% of the time, Pallas kernels for 4%

profile of v7, /device:TPU:1, one launch (start us, length us, event | category | flops | bytes accessed | tf_op | source)
XLA Modules:
  0.0 124.3 jit_solution(4898662839940800396)
XLA Ops:
  2.6 2.1 %pack.1 = bf16[4,256,640]{2,1,0:T(8,128)(2,1)} custom-call(bf16[8,32,640]{2,1,0:T(8,128)(2,1)S(1)} %copy-done, bf16[8,32,640]{2,1,0:T(8,128)(2,1)S(1)} %copy-done.2), custom_call_target="tpu_custom_call" | custom-call | tf_op jit(solution)/shard_map/pack/pallas_call | solution.py:65
  4.7 5.0 %all-to-all-start = ((bf16[4,256,640]{2,1,0:T(8,128)(2,1)}), bf16[4,256,640]{2,1,0:T(8,128)(2,1)S(1)}, u32[]{:S(2)}, u32[]{:S(2)}) async-start(bf16[4,256,640]{2,1,0:T(8,128)(2,1)} %pack.1), calls=%async_computation | async-start | bytes 2621440 | tf_op jit(solution)/shard_map/all_to_all | solution.py:257
  9.7 6.7 %collective-permute-start = (bf16[40,1920]{1,0:T(8,128)(2,1)S(1)}, bf16[40,1920]{1,0:T(8,128)(2,1)S(1)}, u32[]{:S(2)}, u32[]{:S(2)}) collective-permute-start(bf16[40,1920]{1,0:T(8,128)(2,1)S(1)} %copy-done.5), channel_id=1, source_target_pairs={{0,3},{1,4},{2,5},{3,6},{4,7},{5,0},{6,1},{7,2},{16,21},{17,22},{1... | collective-permute-start | bytes 460808 | tf_op jit(solution)/shard_map/ppermute | solution.py:252
  16.3 3.0 %collective-permute-start.1 = (bf16[40,1920]{1,0:T(8,128)(2,1)S(1)}, bf16[40,1920]{1,0:T(8,128)(2,1)S(1)}, u32[]{:S(2)}, u32[]{:S(2)}) collective-permute-start(bf16[40,1920]{1,0:T(8,128)(2,1)S(1)} %copy-done.5), channel_id=1, source_target_pairs={{0,1},{1,2},{2,3},{3,4},{4,5},{5,6},{6,7},{7,0},{16,23},{17,16},{1... | collective-permute-start | bytes 460808 | tf_op jit(solution)/shard_map/ppermute | solution.py:252
  20.0 1.7 %collective-permute-done = bf16[40,1920]{1,0:T(8,128)(2,1)S(1)} collective-permute-done((bf16[40,1920]{1,0:T(8,128)(2,1)S(1)}, bf16[40,1920]{1,0:T(8,128)(2,1)S(1)}, u32[]{:S(2)}, u32[]{:S(2)}) %collective-permute-start) | collective-permute-done | bytes 153632 | tf_op jit(solution)/shard_map/ppermute | solution.py:252
  23.4 9.6 %collective-permute-start.2 = (bf16[4,8,32,640]{3,2,1,0:T(8,128)(2,1)S(1)}, bf16[4,8,32,640]{3,2,1,0:T(8,128)(2,1)S(1)}, u32[]{:S(2)}, u32[]{:S(2)}) collective-permute-start(bf16[4,8,32,640]{3,2,1,0:T(8,128)(2,1)S(1)} %bitcast.56), channel_id=1, source_target_pairs={{0,16},{16,0},{1,17},{17,1},{2,18},{18,2},{3,19},{19,3},{4,20},{20... | collective-permute-start | bytes 3932168 | tf_op jit(solution)/shard_map/ppermute | solution.py:259
  33.4 1.9 %collective-permute-start.3 = (bf16[4,32,384]{2,1,0:T(8,128)(2,1)S(1)}, bf16[4,32,384]{2,1,0:T(8,128)(2,1)S(1)}, u32[]{:S(2)}, u32[]{:S(2)}) collective-permute-start(bf16[4,32,384]{2,1,0:T(8,128)(2,1)S(1)} %fusion), channel_id=1, source_target_pairs={{0,368},{32,16},{64,48},{96,80},{128,112},{160,144},{192,176},{224... | collective-permute-start | bytes 294920 | tf_op jit(solution)/shard_map/ppermute | solution.py:262
  35.8 3.5 %collective-permute-done.3.halo_ref = bf16[4,32,384]{2,1,0:T(8,128)(2,1)S(1)} collective-permute-done((bf16[4,32,384]{2,1,0:T(8,128)(2,1)S(1)}, bf16[4,32,384]{2,1,0:T(8,128)(2,1)S(1)}, u32[]{:S(2)}, u32[]{:S(2)}) %collective-permute-start.3) | collective-permute-done | bytes 98336 | tf_op jit(solution)/shard_map/ppermute | solution.py:262
  39.4 3.4 %x_term.1 = f32[320,512]{1,0:T(8,128)} custom-call(s32[3]{0:T(128)S(1)} %pad_add_fusion.place_ref, s32[32]{0:T(128)S(1)} %get-tuple-element.68.prev_ref, s32[32]{0:T(128)S(1)} %get-tuple-element.67.next_ref, bf16[4,8,32,640]{3,2,1,0:T(8,128)(2,1)S(1)} %bitcast.58, bf16[4,8,32,640]{3,2,1,0:T(8,128)(2,1)S(1)} %collective-permute-done.2.sib_ref, ...), custom_call_target="tpu_custom_call" | custom-call | tf_op jit(solution)/shard_map/x_term/pallas_call | solution.py:151
  42.7 4.6 %all-to-all-start.1 = ((f32[8,40,512]{2,1,0:T(8,128)}), f32[8,40,512]{2,1,0:T(8,128)}, u32[]{:S(2)}, u32[]{:S(2)}) async-start(f32[8,40,512]{2,1,0:T(8,128)} %bitcast.7), calls=%async_computation.1 | async-start | bytes 1310720 | tf_op jit(solution)/shard_map/all_to_all | solution.py:285
  47.4 4.0 %collective-permute-start.5 = (bf16[2,40,1920]{2,1,0:T(8,128)(2,1)S(1)}, bf16[2,40,1920]{2,1,0:T(8,128)(2,1)S(1)}, u32[]{:S(2)}, u32[]{:S(2)}) collective-permute-start(bf16[2,40,1920]{2,1,0:T(8,128)(2,1)S(1)} %pad_maximum_fusion.1), channel_id=1, source_target_pairs={{0,32},{32,0},{64,96},{96,64},{128,160},{160,128},{192,224},{224,1... | collective-permute-start | bytes 921608 | tf_op jit(solution)/shard_map/ppermute | solution.py:280
  51.4 4.2 %collective-permute-done.5 = bf16[2,40,1920]{2,1,0:T(8,128)(2,1)S(1)} collective-permute-done((bf16[2,40,1920]{2,1,0:T(8,128)(2,1)S(1)}, bf16[2,40,1920]{2,1,0:T(8,128)(2,1)S(1)}, u32[]{:S(2)}, u32[]{:S(2)}) %collective-permute-start.5) | collective-permute-done | bytes 307232 | tf_op jit(solution)/shard_map/ppermute | solution.py:280
  55.7 13.5 %collective-permute-start.7 = (bf16[4,40,1920]{2,1,0:T(8,128)(2,1)S(1)}, bf16[4,40,1920]{2,1,0:T(8,128)(2,1)S(1)}, u32[]{:S(2)}, u32[]{:S(2)}) collective-permute-start(bf16[4,40,1920]{2,1,0:T(8,128)(2,1)S(1)} %pad_maximum_fusion.refs_0_), channel_id=1, source_target_pairs={{0,16},{16,0},{1,17},{17,1},{2,18},{18,2},{3,19},{19,3},{4,20},{20... | collective-permute-start | bytes 1843208 | tf_op jit(solution)/shard_map/ppermute | solution.py:283
  69.2 2.2 %collective-permute-start.6 = (bf16[4,40,1920]{2,1,0:T(8,128)(2,1)S(1)}, bf16[4,40,1920]{2,1,0:T(8,128)(2,1)S(1)}, u32[]{:S(2)}, u32[]{:S(2)}) collective-permute-start(bf16[4,40,1920]{2,1,0:T(8,128)(2,1)S(1)} %pad_maximum_fusion.refs_0_), channel_id=1, source_target_pairs={{0,8},{8,0},{1,9},{9,1},{2,10},{10,2},{3,11},{11,3},{4,12},{12,4},... | collective-permute-start | bytes 1843208 | tf_op jit(solution)/shard_map/ppermute | solution.py:282
  71.4 1.9 %collective-permute-start.4 = (bf16[32,1280]{1,0:T(8,128)(2,1)S(1)}, bf16[32,1280]{1,0:T(8,128)(2,1)S(1)}, u32[]{:S(2)}, u32[]{:S(2)}) collective-permute-start(bf16[32,1280]{1,0:T(8,128)(2,1)S(1)} %maximum_select_fusion), channel_id=1, source_target_pairs={{0,752},{16,32},{32,16},{48,64},{64,48},{80,96},{96,80},{112,128},... | collective-permute-start | bytes 245768 | tf_op jit(solution)/shard_map/ppermute | solution.py:276
  73.4 7.8 %all_gather.10.edge_ref = bf16[2,32,1280]{2,1,0:T(8,128)(2,1)S(1)} all-gather(bf16[1,32,1280]{2,1,0:T(8,128)(2,1)S(1)} %maximum_select_fusion.1), channel_id=1, replica_groups=mesh['xh'=2,'z'=12,'c'=2,'xl'=2,'y'=8] {'c'}, dimensions={0}, use_global_device_ids=true | all-gather | bytes 245760 | tf_op jit(solution)/shard_map/all_gather | solution.py:274
  81.2 1.8 %y_sum.1 = f32[12,8,256]{2,1,0:T(8,128)} custom-call(f32[8,40,512]{2,1,0:T(8,128)} %all-to-all-done.1.part_ref), custom_call_target="tpu_custom_call" | custom-call | tf_op jit(solution)/shard_map/y_sum/pallas_call | solution.py:175
  83.0 5.4 %all-to-all-start.2 = ((f32[12,8,256]{2,1,0:T(8,128)}), f32[12,8,256]{2,1,0:T(8,128)S(1)}, u32[]{:S(2)}, u32[]{:S(2)}) async-start(f32[12,8,256]{2,1,0:T(8,128)} %y_sum.1), calls=%async_computation.2 | async-start | bytes 196608 | tf_op jit(solution)/shard_map/all_to_all | solution.py:291
  88.4 1.9 %collective-permute-start.8 = (bf16[4,40,1920]{2,1,0:T(8,128)(2,1)S(1)}, bf16[4,40,1920]{2,1,0:T(8,128)(2,1)S(1)}, u32[]{:S(2)}, u32[]{:S(2)}) collective-permute-start(bf16[4,40,1920]{2,1,0:T(8,128)(2,1)S(1)} %collective-permute-done.6.refs_1_), channel_id=1, source_target_pairs={{0,16},{16,0},{1,17},{17,1},{2,18},{18,2},{3,19},{19,3},{4,20},{20... | collective-permute-start | bytes 1843208 | tf_op jit(solution)/shard_map/ppermute | solution.py:294
  90.3 9.2 %all-to-all-done.2 = f32[12,8,256]{2,1,0:T(8,128)S(1)} async-done(((f32[12,8,256]{2,1,0:T(8,128)}), f32[12,8,256]{2,1,0:T(8,128)S(1)}, u32[]{:S(2)}, u32[]{:S(2)}) %all-to-all-start.2) | async-done | bytes 98336 | tf_op jit(solution)/shard_map/all_to_all | solution.py:291
  100.3 4.5 %all-to-all-start.3 = ((f32[24,8,256]{2,1,0:T(8,128)}), f32[24,8,256]{2,1,0:T(8,128)}, u32[]{:S(2)}, u32[]{:S(2)}) async-start(f32[24,8,256]{2,1,0:T(8,128)} %broadcast_in_dim.2), calls=%async_computation.3 | async-start | bytes 393216 | tf_op jit(solution)/shard_map/all_to_all | solution.py:296
  105.9 3.5 %outputs.1 = (bf16[8,32,640]{2,1,0:T(8,128)(2,1)}, bf16[8,32,640]{2,1,0:T(8,128)(2,1)}) custom-call(s32[5]{0:T(128)S(1)} %stack.46.place_ref, s32[32]{0:T(128)S(1)} %get-tuple-element.68.prev_ref, s32[32]{0:T(128)S(1)} %get-tuple-element.67.next_ref, bf16[8,32,640]{2,1,0:T(8,128)(2,1)S(1)} %copy-done.1, bf16[8,32,640]{2,1,0:T(8,128)(2,1)S(1)} %copy-done.3, ...), custom_call_target="tpu_custom_call" | custom-call | tf_op jit(solution)/shard_map/outputs/pallas_call | solution.py:227
  109.4 11.6 %all-to-all-done.3 = f32[24,8,256]{2,1,0:T(8,128)} async-done(((f32[24,8,256]{2,1,0:T(8,128)}), f32[24,8,256]{2,1,0:T(8,128)}, u32[]{:S(2)}, u32[]{:S(2)}) %all-to-all-start.3) | async-done | bytes 196640 | tf_op jit(solution)/shard_map/all_to_all | solution.py:296
  121.0 2.3 %all-gather = f32[48,8,256]{2,1,0:T(8,128)S(1)} all-gather(f32[24,8,256]{2,1,0:T(8,128)} %all-to-all-done.3), channel_id=2, replica_groups=mesh['xh'=2,'z'=12,'c'=2,'xl'=2,'y'=8] {'c'}, dimensions={0}, use_global_device_ids=true | all-gather | bytes 589824 | tf_op jit(solution)/shard_map/all_gather | solution.py:302
  (58 shorter events, 7.5 us)
Async XLA Ops:
  0.6 1.0 copy-start
  1.6 1.0 copy-start.2
  4.6 5.0 %copy-start.5 = (bf16[40,1920]{1,0:T(8,128)(2,1)S(1)}, bf16[40,1920]{1,0:T(8,128)(2,1)}, u32[]{:S(2)}) copy-start(bf16[40,1920]{1,0:T(8,128)(2,1)} %param.9) | copy-start | bytes 460804
  4.7 30.7 %copy-start.6 = (s32[48]{0:T(128)S(1)}, s32[48]{0:T(128)}, u32[]{:S(2)}) copy-start(s32[48]{0:T(128)} %param.10) | copy-start | bytes 580
  4.7 18.7 %all-to-all-start = ((bf16[4,256,640]{2,1,0:T(8,128)(2,1)}), bf16[4,256,640]{2,1,0:T(8,128)(2,1)S(1)}, u32[]{:S(2)}, u32[]{:S(2)}) async-start(bf16[4,256,640]{2,1,0:T(8,128)(2,1)} %pack.1), calls=%async_computation | async-start | bytes 2621440 | tf_op jit(solution)/shard_map/all_to_all | solution.py:257
  9.7 12.1 %collective-permute-start = (bf16[40,1920]{1,0:T(8,128)(2,1)S(1)}, bf16[40,1920]{1,0:T(8,128)(2,1)S(1)}, u32[]{:S(2)}, u32[]{:S(2)}) collective-permute-start(bf16[40,1920]{1,0:T(8,128)(2,1)S(1)} %copy-done.5), channel_id=1, source_target_pairs={{0,3},{1,4},{2,5},{3,6},{4,7},{5,0},{6,1},{7,2},{16,21},{17,22},{1... | collective-permute-start | bytes 460808 | tf_op jit(solution)/shard_map/ppermute | solution.py:252
  16.3 7.1 %collective-permute-start.1 = (bf16[40,1920]{1,0:T(8,128)(2,1)S(1)}, bf16[40,1920]{1,0:T(8,128)(2,1)S(1)}, u32[]{:S(2)}, u32[]{:S(2)}) collective-permute-start(bf16[40,1920]{1,0:T(8,128)(2,1)S(1)} %copy-done.5), channel_id=1, source_target_pairs={{0,1},{1,2},{2,3},{3,4},{4,5},{5,6},{6,7},{7,0},{16,23},{17,16},{1... | collective-permute-start | bytes 460808 | tf_op jit(solution)/shard_map/ppermute | solution.py:252
  23.4 16.0 %collective-permute-start.2 = (bf16[4,8,32,640]{3,2,1,0:T(8,128)(2,1)S(1)}, bf16[4,8,32,640]{3,2,1,0:T(8,128)(2,1)S(1)}, u32[]{:S(2)}, u32[]{:S(2)}) collective-permute-start(bf16[4,8,32,640]{3,2,1,0:T(8,128)(2,1)S(1)} %bitcast.56), channel_id=1, source_target_pairs={{0,16},{16,0},{1,17},{17,1},{2,18},{18,2},{3,19},{19,3},{4,20},{20... | collective-permute-start | bytes 3932168 | tf_op jit(solution)/shard_map/ppermute | solution.py:259
  33.4 5.9 %collective-permute-start.3 = (bf16[4,32,384]{2,1,0:T(8,128)(2,1)S(1)}, bf16[4,32,384]{2,1,0:T(8,128)(2,1)S(1)}, u32[]{:S(2)}, u32[]{:S(2)}) collective-permute-start(bf16[4,32,384]{2,1,0:T(8,128)(2,1)S(1)} %fusion), channel_id=1, source_target_pairs={{0,368},{32,16},{64,48},{96,80},{128,112},{160,144},{192,176},{224... | collective-permute-start | bytes 294920 | tf_op jit(solution)/shard_map/ppermute | solution.py:262
  42.7 8.7 %copy-start.1 = (bf16[8,32,640]{2,1,0:T(8,128)(2,1)S(1)}, bf16[8,32,640]{2,1,0:T(8,128)(2,1)}, u32[]{:S(2)}) copy-start(bf16[8,32,640]{2,1,0:T(8,128)(2,1)} %f_ref) | copy-start | bytes 983044
  42.7 8.7 %copy-start.3 = (bf16[8,32,640]{2,1,0:T(8,128)(2,1)S(1)}, bf16[8,32,640]{2,1,0:T(8,128)(2,1)}, u32[]{:S(2)}) copy-start(bf16[8,32,640]{2,1,0:T(8,128)(2,1)} %g_ref) | copy-start | bytes 983044
  42.7 38.5 %all-to-all-start.1 = ((f32[8,40,512]{2,1,0:T(8,128)}), f32[8,40,512]{2,1,0:T(8,128)}, u32[]{:S(2)}, u32[]{:S(2)}) async-start(f32[8,40,512]{2,1,0:T(8,128)} %bitcast.7), calls=%async_computation.1 | async-start | bytes 1310720 | tf_op jit(solution)/shard_map/all_to_all | solution.py:285
  47.4 8.2 %collective-permute-start.5 = (bf16[2,40,1920]{2,1,0:T(8,128)(2,1)S(1)}, bf16[2,40,1920]{2,1,0:T(8,128)(2,1)S(1)}, u32[]{:S(2)}, u32[]{:S(2)}) collective-permute-start(bf16[2,40,1920]{2,1,0:T(8,128)(2,1)S(1)} %pad_maximum_fusion.1), channel_id=1, source_target_pairs={{0,32},{32,0},{64,96},{96,64},{128,160},{160,128},{192,224},{224,1... | collective-permute-start | bytes 921608 | tf_op jit(solution)/shard_map/ppermute | solution.py:280
  55.7 32.7 %collective-permute-start.7 = (bf16[4,40,1920]{2,1,0:T(8,128)(2,1)S(1)}, bf16[4,40,1920]{2,1,0:T(8,128)(2,1)S(1)}, u32[]{:S(2)}, u32[]{:S(2)}) collective-permute-start(bf16[4,40,1920]{2,1,0:T(8,128)(2,1)S(1)} %pad_maximum_fusion.refs_0_), channel_id=1, source_target_pairs={{0,16},{16,0},{1,17},{17,1},{2,18},{18,2},{3,19},{19,3},{4,20},{20... | collective-permute-start | bytes 1843208 | tf_op jit(solution)/shard_map/ppermute | solution.py:283
  69.2 19.2 %collective-permute-start.6 = (bf16[4,40,1920]{2,1,0:T(8,128)(2,1)S(1)}, bf16[4,40,1920]{2,1,0:T(8,128)(2,1)S(1)}, u32[]{:S(2)}, u32[]{:S(2)}) collective-permute-start(bf16[4,40,1920]{2,1,0:T(8,128)(2,1)S(1)} %pad_maximum_fusion.refs_0_), channel_id=1, source_target_pairs={{0,8},{8,0},{1,9},{9,1},{2,10},{10,2},{3,11},{11,3},{4,12},{12,4},... | collective-permute-start | bytes 1843208 | tf_op jit(solution)/shard_map/ppermute | solution.py:282
  71.4 9.8 %collective-permute-start.4 = (bf16[32,1280]{1,0:T(8,128)(2,1)S(1)}, bf16[32,1280]{1,0:T(8,128)(2,1)S(1)}, u32[]{:S(2)}, u32[]{:S(2)}) collective-permute-start(bf16[32,1280]{1,0:T(8,128)(2,1)S(1)} %maximum_select_fusion), channel_id=1, source_target_pairs={{0,752},{16,32},{32,16},{48,64},{64,48},{80,96},{96,80},{112,128},... | collective-permute-start | bytes 245768 | tf_op jit(solution)/shard_map/ppermute | solution.py:276
  83.0 16.5 %all-to-all-start.2 = ((f32[12,8,256]{2,1,0:T(8,128)}), f32[12,8,256]{2,1,0:T(8,128)S(1)}, u32[]{:S(2)}, u32[]{:S(2)}) async-start(f32[12,8,256]{2,1,0:T(8,128)} %y_sum.1), calls=%async_computation.2 | async-start | bytes 196608 | tf_op jit(solution)/shard_map/all_to_all | solution.py:291
  88.4 16.5 %collective-permute-start.8 = (bf16[4,40,1920]{2,1,0:T(8,128)(2,1)S(1)}, bf16[4,40,1920]{2,1,0:T(8,128)(2,1)S(1)}, u32[]{:S(2)}, u32[]{:S(2)}) collective-permute-start(bf16[4,40,1920]{2,1,0:T(8,128)(2,1)S(1)} %collective-permute-done.6.refs_1_), channel_id=1, source_target_pairs={{0,16},{16,0},{1,17},{17,1},{2,18},{18,2},{3,19},{19,3},{4,20},{20... | collective-permute-start | bytes 1843208 | tf_op jit(solution)/shard_map/ppermute | solution.py:294
  100.3 20.7 %all-to-all-start.3 = ((f32[24,8,256]{2,1,0:T(8,128)}), f32[24,8,256]{2,1,0:T(8,128)}, u32[]{:S(2)}, u32[]{:S(2)}) async-start(f32[24,8,256]{2,1,0:T(8,128)} %broadcast_in_dim.2), calls=%async_computation.3 | async-start | bytes 393216 | tf_op jit(solution)/shard_map/all_to_all | solution.py:296
  104.9 1.0 copy-start.4

commit v8 on v7

--- a/solution.py
+++ b/solution.py
@@ -159,22 +159,6 @@
     )(place, prev_ok, next_ok, own, sib, halo)
 
 
-def y_sum_kernel(part_ref, out_ref):
-    total = part_ref[0]
-    for i in range(1, part_ref.shape[0]):
-        total = total + part_ref[i]
-    rows = total.shape[0]
-    for i in range(out_ref.shape[0]):
-        row, col = i // 2 * 8, i % 2 * 256
-        out_ref[i] = total[row:row + 8, col:col + 256] if row < rows else jnp.zeros((8, 256), jnp.float32)
-
-
-def y_sum(part, pieces):
-    vmem = pl.BlockSpec(memory_space=pltpu.VMEM)
-    shape = jax.ShapeDtypeStruct((pieces, 8, 256), jnp.float32)
-    return pl.pallas_call(y_sum_kernel, out_shape=shape, in_specs=[vmem], out_specs=vmem, name="y_sum")(part)
-
-
 def out_kernel(place_ref, prev_ref, next_ref, f_ref, g_ref, skip_ref, halo_ref, edge_ref, *refs):
     weights, (out_ref, back_ref, f_lo, f_hi, g_lo, g_hi, blocks, weight) = refs[:4], refs[4:]
     frames, strip, width = f_ref.shape
@@ -278,16 +262,18 @@
     parity = z % 2
     pair = jnp.stack([jnp.where((parity == 1) & (core == 1), temporal_weight, w_far), w_near])
     pair_far = lax.ppermute(pair, "z", [(i, i ^ 1) for i in range(n_z)])
+    pair_far, halo, edges = lax.optimization_barrier((pair_far, halo, edges))
     blocks = jnp.concatenate([pair, pair_far])
     blocks_far = lax.ppermute(blocks, "xl", both)
+
+    part = lax.all_to_all(term.reshape(n_y, 320 // n_y, 512), "y", 0, 0, tiled=True)
+    part, blocks = lax.optimization_barrier((part, blocks))
+    part = part.sum(0)
+    local_rows = part.shape[0]
+    n_xz = 2 * n_z
+    pieces = jnp.pad(part, ((0, 48 - local_rows), (0, 0))).reshape(6, 8, 2, 256).transpose(0, 2, 1, 3).reshape(n_z, 8, 256)
+    _, blocks, blocks_far = lax.optimization_barrier((pieces, blocks, blocks_far))
     blocks_sib = lax.ppermute(blocks, "c", both)
-
-    part = lax.all_to_all(term.reshape(n_y, 320 // n_y, 512), "y", 0, 0, tiled=True)
-    part, halo, edges = lax.optimization_barrier((part, halo, edges))
-    local_rows = part.shape[1]
-    n_xz = 2 * n_z
-    pieces = y_sum(part, n_z)
-    _, blocks_far, blocks_sib = lax.optimization_barrier((pieces, blocks_far, blocks_sib))
     mine = lax.all_to_all(pieces, "z", 0, 0, tiled=True)
     mine = mine.sum(0) * (1.0 / math.sqrt(total_frames * strip * lax.axis_size(FSDP)))
     mine = jnp.broadcast_to(mine[None], (n_xz, 8, 256))

time: 125 us -> 120 us (0.960)
  waiting for transfers between devices: 31.9 us -> 20.4 us
  starting transfers between devices: 64.2 us -> 73 us
  Pallas kernels: 10.7 us -> 8.88 us
    ppermute x1, starting transfers between devices: 1.92 us -> 12.5 us  [shards(): halo = lax.ppermute(jnp.where(core == 0, ends[0], ends[1]), DP, across)]
    ppermute x1, starting transfers between devices: 13.5 us -> 3.64 us  [shards(): blocks_sib = lax.ppermute(blocks, 'c', both)]
    all_to_all x1, starting transfers between devices: 5.37 us -> 13.4 us  [shards(): mine = lax.all_to_all(pieces, 'z', 0, 0, tiled=True)]
    all_gather x1, blocking collectives: 7.82 us -> 2.96 us  [shards(): edges = lax.all_gather(jnp.where(core == 0, ends[1], ends[0]), 'c')]
    all_to_all x1, waiting for transfers between devices: 9.22 us -> 4.46 us  [shards(): mine = lax.all_to_all(pieces, 'z', 0, 0, tiled=True)]
    ppermute x1, waiting for transfers between devices: 4.16 us -> 0.01 us  [shards(): pair_far = lax.ppermute(pair, 'z', [(i, i ^ 1) for i in range(n_z)])]
    all_gather x1, blocking collectives: 2.29 us -> 6.05 us  [shards(): gathered = lax.all_gather(gathered, 'c')]
    all_to_all x1, waiting for transfers between devices: 11.6 us -> 8.28 us  [shards(): gathered = lax.all_to_all(mine, ('xh', 'z'), 0, 0, tiled=True)]
  transfers between devices with their start and end apart: 13 -> 13, of which waited for: 6 -> 6; matrix products, arithmetic and copies ran while one was open for 1% -> 2% of each run, Pallas kernels for 4% -> 3%
where the time goes in v8:
time: 120 us; the launch traced here: 119 us
  starting transfers between devices  73 us (61%)
  waiting for transfers between devices  20.4 us (17%)
  blocking collectives  9.01 us (8%)
  Pallas kernels  8.88 us (7%)
  local copies, waits for them, and re-layouts  5.66 us (5%)
  between operations  1.66 us (1%)
    all_to_all x1, starting transfers between devices, shards(): mine = lax.all_to_all(pieces, 'z', 0, 0, tiled=True)  13.4 us
    ppermute x1, starting transfers between devices, shards(): halo = lax.ppermute(jnp.where(core == 0, ends[0], ends[1]), DP, across)  12.5 us
    ppermute x1, starting transfers between devices, shards(): sib = lax.ppermute(own, 'c', both)  9.64 us
    ppermute x2, starting transfers between devices, from_y(): return lax.ppermute(temporal_weight, ('z', 'c', 'y'), pairs)  9.63 us
    all_to_all x1, waiting for transfers between devices, shards(): gathered = lax.all_to_all(mine, ('xh', 'z'), 0, 0, tiled=True)  8.28 us
    all_gather x1, blocking collectives, shards(): gathered = lax.all_gather(gathered, 'c')  6.05 us
    all_to_all x1, starting transfers between devices, shards(): lax.all_to_all(pack(features, cotangent), X, 0, 0, tiled=True)  4.99 us
    all_to_all x1, starting transfers between devices, shards(): lax.all_to_all(term.reshape(n_y, 320 // n_y, 512), 'y', 0, 0, tiled=True)  4.59 us
  transfers between devices with their start and end apart: 13, of which 6 were waited for; matrix products, arithmetic and copies ran while one was open for 2% of the time, Pallas kernels for 3%

profile of v8, /device:TPU:1, one launch (start us, length us, event | category | flops | bytes accessed | tf_op | source)
XLA Modules:
  0.0 119.5 jit_solution(10575476393921961816)
XLA Ops:
  1.6 1.0 copy-done.2
  2.6 2.0 %pack.1 = bf16[4,256,640]{2,1,0:T(8,128)(2,1)} custom-call(bf16[8,32,640]{2,1,0:T(8,128)(2,1)S(1)} %copy-done, bf16[8,32,640]{2,1,0:T(8,128)(2,1)S(1)} %copy-done.2), custom_call_target="tpu_custom_call" | custom-call | tf_op jit(solution)/shard_map/pack/pallas_call | solution.py:65
  4.6 5.0 %all-to-all-start = ((bf16[4,256,640]{2,1,0:T(8,128)(2,1)}), bf16[4,256,640]{2,1,0:T(8,128)(2,1)S(1)}, u32[]{:S(2)}, u32[]{:S(2)}) async-start(bf16[4,256,640]{2,1,0:T(8,128)(2,1)} %pack.1), calls=%async_computation | async-start | bytes 2621440 | tf_op jit(solution)/shard_map/all_to_all | solution.py:241
  9.6 6.7 %collective-permute-start = (bf16[40,1920]{1,0:T(8,128)(2,1)S(1)}, bf16[40,1920]{1,0:T(8,128)(2,1)S(1)}, u32[]{:S(2)}, u32[]{:S(2)}) collective-permute-start(bf16[40,1920]{1,0:T(8,128)(2,1)S(1)} %copy-done.5), channel_id=1, source_target_pairs={{0,3},{1,4},{2,5},{3,6},{4,7},{5,0},{6,1},{7,2},{16,21},{17,22},{1... | collective-permute-start | bytes 460808 | tf_op jit(solution)/shard_map/ppermute | solution.py:236
  16.3 3.0 %collective-permute-start.1 = (bf16[40,1920]{1,0:T(8,128)(2,1)S(1)}, bf16[40,1920]{1,0:T(8,128)(2,1)S(1)}, u32[]{:S(2)}, u32[]{:S(2)}) collective-permute-start(bf16[40,1920]{1,0:T(8,128)(2,1)S(1)} %copy-done.5), channel_id=1, source_target_pairs={{0,1},{1,2},{2,3},{3,4},{4,5},{5,6},{6,7},{7,0},{16,23},{17,16},{1... | collective-permute-start | bytes 460808 | tf_op jit(solution)/shard_map/ppermute | solution.py:236
  20.0 1.7 %collective-permute-done = bf16[40,1920]{1,0:T(8,128)(2,1)S(1)} collective-permute-done((bf16[40,1920]{1,0:T(8,128)(2,1)S(1)}, bf16[40,1920]{1,0:T(8,128)(2,1)S(1)}, u32[]{:S(2)}, u32[]{:S(2)}) %collective-permute-start) | collective-permute-done | bytes 153632 | tf_op jit(solution)/shard_map/ppermute | solution.py:236
  21.7 1.6 %collective-permute-done.1 = bf16[40,1920]{1,0:T(8,128)(2,1)S(1)} collective-permute-done((bf16[40,1920]{1,0:T(8,128)(2,1)S(1)}, bf16[40,1920]{1,0:T(8,128)(2,1)S(1)}, u32[]{:S(2)}, u32[]{:S(2)}) %collective-permute-start.1) | collective-permute-done | bytes 153632 | tf_op jit(solution)/shard_map/ppermute | solution.py:236
  23.4 9.6 %collective-permute-start.2 = (bf16[4,8,32,640]{3,2,1,0:T(8,128)(2,1)S(1)}, bf16[4,8,32,640]{3,2,1,0:T(8,128)(2,1)S(1)}, u32[]{:S(2)}, u32[]{:S(2)}) collective-permute-start(bf16[4,8,32,640]{3,2,1,0:T(8,128)(2,1)S(1)} %bitcast.61), channel_id=1, source_target_pairs={{0,16},{16,0},{1,17},{17,1},{2,18},{18,2},{3,19},{19,3},{4,20},{20... | collective-permute-start | bytes 3932168 | tf_op jit(solution)/shard_map/ppermute | solution.py:243
  33.4 1.9 %collective-permute-start.3 = (bf16[4,32,384]{2,1,0:T(8,128)(2,1)S(1)}, bf16[4,32,384]{2,1,0:T(8,128)(2,1)S(1)}, u32[]{:S(2)}, u32[]{:S(2)}) collective-permute-start(bf16[4,32,384]{2,1,0:T(8,128)(2,1)S(1)} %fusion), channel_id=1, source_target_pairs={{0,368},{32,16},{64,48},{96,80},{128,112},{160,144},{192,176},{224... | collective-permute-start | bytes 294920 | tf_op jit(solution)/shard_map/ppermute | solution.py:246
  35.8 3.5 %collective-permute-done.3.halo_ref = bf16[4,32,384]{2,1,0:T(8,128)(2,1)S(1)} collective-permute-done((bf16[4,32,384]{2,1,0:T(8,128)(2,1)S(1)}, bf16[4,32,384]{2,1,0:T(8,128)(2,1)S(1)}, u32[]{:S(2)}, u32[]{:S(2)}) %collective-permute-start.3) | collective-permute-done | bytes 98336 | tf_op jit(solution)/shard_map/ppermute | solution.py:246
  39.3 3.3 %x_term.1 = f32[320,512]{1,0:T(8,128)} custom-call(s32[3]{0:T(128)S(1)} %pad_add_fusion.place_ref, s32[32]{0:T(128)S(1)} %get-tuple-element.72.prev_ref, s32[32]{0:T(128)S(1)} %get-tuple-element.71.next_ref, bf16[4,8,32,640]{3,2,1,0:T(8,128)(2,1)S(1)} %bitcast.63, bf16[4,8,32,640]{3,2,1,0:T(8,128)(2,1)S(1)} %collective-permute-done.2.sib_ref, ...), custom_call_target="tpu_custom_call" | custom-call | tf_op jit(solution)/shard_map/x_term/pallas_call | solution.py:151
  42.6 4.6 %all-to-all-start.1 = ((f32[8,40,512]{2,1,0:T(8,128)}), f32[8,40,512]{2,1,0:T(8,128)S(1)}, u32[]{:S(2)}, u32[]{:S(2)}) async-start(f32[8,40,512]{2,1,0:T(8,128)} %bitcast.7), calls=%async_computation.1 | async-start | bytes 1310720 | tf_op jit(solution)/shard_map/all_to_all | solution.py:269
  47.4 4.0 %collective-permute-start.4 = (bf16[2,40,1920]{2,1,0:T(8,128)(2,1)S(1)}, bf16[2,40,1920]{2,1,0:T(8,128)(2,1)S(1)}, u32[]{:S(2)}, u32[]{:S(2)}) collective-permute-start(bf16[2,40,1920]{2,1,0:T(8,128)(2,1)S(1)} %pad_maximum_fusion.1), channel_id=1, source_target_pairs={{0,32},{32,0},{64,96},{96,64},{128,160},{160,128},{192,224},{224,1... | collective-permute-start | bytes 921608 | tf_op jit(solution)/shard_map/ppermute | solution.py:264
  51.4 12.5 %collective-permute-start.5 = (bf16[32,1280]{1,0:T(8,128)(2,1)S(1)}, bf16[32,1280]{1,0:T(8,128)(2,1)S(1)}, u32[]{:S(2)}, u32[]{:S(2)}) collective-permute-start(bf16[32,1280]{1,0:T(8,128)(2,1)S(1)} %maximum_select_fusion), channel_id=1, source_target_pairs={{0,752},{16,32},{32,16},{48,64},{64,48},{80,96},{96,80},{112,128},... | collective-permute-start | bytes 245768 | tf_op jit(solution)/shard_map/ppermute | solution.py:260
  64.0 3.0 %all_gather.10.edge_ref = bf16[2,32,1280]{2,1,0:T(8,128)(2,1)S(1)} all-gather(bf16[1,32,1280]{2,1,0:T(8,128)(2,1)S(1)} %maximum_select_fusion.1), channel_id=1, replica_groups=mesh['xh'=2,'z'=12,'c'=2,'xl'=2,'y'=8] {'c'}, dimensions={0}, use_global_device_ids=true | all-gather | bytes 245760 | tf_op jit(solution)/shard_map/all_gather | solution.py:258
  67.8 2.2 %collective-permute-start.6 = (bf16[4,40,1920]{2,1,0:T(8,128)(2,1)S(1)}, bf16[4,40,1920]{2,1,0:T(8,128)(2,1)S(1)}, u32[]{:S(2)}, u32[]{:S(2)}) collective-permute-start(bf16[4,40,1920]{2,1,0:T(8,128)(2,1)S(1)} %pad_maximum_fusion.refs_0_), channel_id=1, source_target_pairs={{0,8},{8,0},{1,9},{9,1},{2,10},{10,2},{3,11},{11,3},{4,12},{12,4},... | collective-permute-start | bytes 1843208 | tf_op jit(solution)/shard_map/ppermute | solution.py:267
  70.7 13.4 %all-to-all-start.2 = ((f32[12,8,256]{2,1,0:T(8,128)}), f32[12,8,256]{2,1,0:T(8,128)S(1)}, u32[]{:S(2)}, u32[]{:S(2)}) async-start(f32[12,8,256]{2,1,0:T(8,128)} %bitcast.16), calls=%async_computation.2 | async-start | bytes 196608 | tf_op jit(solution)/shard_map/all_to_all | solution.py:277
  84.2 3.6 %collective-permute-start.7 = (bf16[4,40,1920]{2,1,0:T(8,128)(2,1)S(1)}, bf16[4,40,1920]{2,1,0:T(8,128)(2,1)S(1)}, u32[]{:S(2)}, u32[]{:S(2)}) collective-permute-start(bf16[4,40,1920]{2,1,0:T(8,128)(2,1)S(1)} %pad_maximum_fusion.refs_0_), channel_id=1, source_target_pairs={{0,16},{16,0},{1,17},{17,1},{2,18},{18,2},{3,19},{19,3},{4,20},{20... | collective-permute-start | bytes 1843208 | tf_op jit(solution)/shard_map/ppermute | solution.py:276
  87.8 1.9 %collective-permute-start.8 = (bf16[4,40,1920]{2,1,0:T(8,128)(2,1)S(1)}, bf16[4,40,1920]{2,1,0:T(8,128)(2,1)S(1)}, u32[]{:S(2)}, u32[]{:S(2)}) collective-permute-start(bf16[4,40,1920]{2,1,0:T(8,128)(2,1)S(1)} %collective-permute-done.6.refs_1_), channel_id=1, source_target_pairs={{0,16},{16,0},{1,17},{17,1},{2,18},{18,2},{3,19},{19,3},{4,20},{20... | collective-permute-start | bytes 1843208 | tf_op jit(solution)/shard_map/ppermute | solution.py:280
  89.8 4.5 %all-to-all-done.2 = f32[12,8,256]{2,1,0:T(8,128)S(1)} async-done(((f32[12,8,256]{2,1,0:T(8,128)}), f32[12,8,256]{2,1,0:T(8,128)S(1)}, u32[]{:S(2)}, u32[]{:S(2)}) %all-to-all-start.2) | async-done | bytes 98336 | tf_op jit(solution)/shard_map/all_to_all | solution.py:277
  94.9 4.5 %all-to-all-start.3 = ((f32[24,8,256]{2,1,0:T(8,128)}), f32[24,8,256]{2,1,0:T(8,128)}, u32[]{:S(2)}, u32[]{:S(2)}) async-start(f32[24,8,256]{2,1,0:T(8,128)} %broadcast_in_dim.2), calls=%async_computation.3 | async-start | bytes 393216 | tf_op jit(solution)/shard_map/all_to_all | solution.py:282
  100.5 3.5 %outputs.1 = (bf16[8,32,640]{2,1,0:T(8,128)(2,1)}, bf16[8,32,640]{2,1,0:T(8,128)(2,1)}) custom-call(s32[5]{0:T(128)S(1)} %stack.49.place_ref, s32[32]{0:T(128)S(1)} %get-tuple-element.72.prev_ref, s32[32]{0:T(128)S(1)} %get-tuple-element.71.next_ref, bf16[8,32,640]{2,1,0:T(8,128)(2,1)S(1)} %copy-done.1, bf16[8,32,640]{2,1,0:T(8,128)(2,1)S(1)} %copy-done.3, ...), custom_call_target="tpu_custom_call" | custom-call | tf_op jit(solution)/shard_map/outputs/pallas_call | solution.py:211
  104.1 8.3 %all-to-all-done.3 = f32[24,8,256]{2,1,0:T(8,128)} async-done(((f32[24,8,256]{2,1,0:T(8,128)}), f32[24,8,256]{2,1,0:T(8,128)}, u32[]{:S(2)}, u32[]{:S(2)}) %all-to-all-start.3) | async-done | bytes 196640 | tf_op jit(solution)/shard_map/all_to_all | solution.py:282
  112.4 6.1 %all-gather = f32[48,8,256]{2,1,0:T(8,128)S(1)} all-gather(f32[24,8,256]{2,1,0:T(8,128)} %all-to-all-done.3), channel_id=2, replica_groups=mesh['xh'=2,'z'=12,'c'=2,'xl'=2,'y'=8] {'c'}, dimensions={0}, use_global_device_ids=true | all-gather | bytes 589824 | tf_op jit(solution)/shard_map/all_gather | solution.py:288
  (59 shorter events, 6.3 us)
Async XLA Ops:
  0.6 1.0 copy-start
  1.6 1.0 copy-start.2
  4.6 5.0 %copy-start.5 = (bf16[40,1920]{1,0:T(8,128)(2,1)S(1)}, bf16[40,1920]{1,0:T(8,128)(2,1)}, u32[]{:S(2)}) copy-start(bf16[40,1920]{1,0:T(8,128)(2,1)} %param.9) | copy-start | bytes 460804
  4.6 30.7 %copy-start.6 = (s32[48]{0:T(128)S(1)}, s32[48]{0:T(128)}, u32[]{:S(2)}) copy-start(s32[48]{0:T(128)} %param.10) | copy-start | bytes 580
  4.6 18.7 %all-to-all-start = ((bf16[4,256,640]{2,1,0:T(8,128)(2,1)}), bf16[4,256,640]{2,1,0:T(8,128)(2,1)S(1)}, u32[]{:S(2)}, u32[]{:S(2)}) async-start(bf16[4,256,640]{2,1,0:T(8,128)(2,1)} %pack.1), calls=%async_computation | async-start | bytes 2621440 | tf_op jit(solution)/shard_map/all_to_all | solution.py:241
  9.6 12.1 %collective-permute-start = (bf16[40,1920]{1,0:T(8,128)(2,1)S(1)}, bf16[40,1920]{1,0:T(8,128)(2,1)S(1)}, u32[]{:S(2)}, u32[]{:S(2)}) collective-permute-start(bf16[40,1920]{1,0:T(8,128)(2,1)S(1)} %copy-done.5), channel_id=1, source_target_pairs={{0,3},{1,4},{2,5},{3,6},{4,7},{5,0},{6,1},{7,2},{16,21},{17,22},{1... | collective-permute-start | bytes 460808 | tf_op jit(solution)/shard_map/ppermute | solution.py:236
  16.3 7.1 %collective-permute-start.1 = (bf16[40,1920]{1,0:T(8,128)(2,1)S(1)}, bf16[40,1920]{1,0:T(8,128)(2,1)S(1)}, u32[]{:S(2)}, u32[]{:S(2)}) collective-permute-start(bf16[40,1920]{1,0:T(8,128)(2,1)S(1)} %copy-done.5), channel_id=1, source_target_pairs={{0,1},{1,2},{2,3},{3,4},{4,5},{5,6},{6,7},{7,0},{16,23},{17,16},{1... | collective-permute-start | bytes 460808 | tf_op jit(solution)/shard_map/ppermute | solution.py:236
  23.4 16.0 %collective-permute-start.2 = (bf16[4,8,32,640]{3,2,1,0:T(8,128)(2,1)S(1)}, bf16[4,8,32,640]{3,2,1,0:T(8,128)(2,1)S(1)}, u32[]{:S(2)}, u32[]{:S(2)}) collective-permute-start(bf16[4,8,32,640]{3,2,1,0:T(8,128)(2,1)S(1)} %bitcast.61), channel_id=1, source_target_pairs={{0,16},{16,0},{1,17},{17,1},{2,18},{18,2},{3,19},{19,3},{4,20},{20... | collective-permute-start | bytes 3932168 | tf_op jit(solution)/shard_map/ppermute | solution.py:243
  33.4 5.9 %collective-permute-start.3 = (bf16[4,32,384]{2,1,0:T(8,128)(2,1)S(1)}, bf16[4,32,384]{2,1,0:T(8,128)(2,1)S(1)}, u32[]{:S(2)}, u32[]{:S(2)}) collective-permute-start(bf16[4,32,384]{2,1,0:T(8,128)(2,1)S(1)} %fusion), channel_id=1, source_target_pairs={{0,368},{32,16},{64,48},{96,80},{128,112},{160,144},{192,176},{224... | collective-permute-start | bytes 294920 | tf_op jit(solution)/shard_map/ppermute | solution.py:246
  42.6 4.6 %copy-start.1 = (bf16[8,32,640]{2,1,0:T(8,128)(2,1)S(1)}, bf16[8,32,640]{2,1,0:T(8,128)(2,1)}, u32[]{:S(2)}) copy-start(bf16[8,32,640]{2,1,0:T(8,128)(2,1)} %f_ref) | copy-start | bytes 983044
  42.6 4.7 %copy-start.3 = (bf16[8,32,640]{2,1,0:T(8,128)(2,1)S(1)}, bf16[8,32,640]{2,1,0:T(8,128)(2,1)}, u32[]{:S(2)}) copy-start(bf16[8,32,640]{2,1,0:T(8,128)(2,1)} %g_ref) | copy-start | bytes 983044
  42.6 27.4 %all-to-all-start.1 = ((f32[8,40,512]{2,1,0:T(8,128)}), f32[8,40,512]{2,1,0:T(8,128)S(1)}, u32[]{:S(2)}, u32[]{:S(2)}) async-start(f32[8,40,512]{2,1,0:T(8,128)} %bitcast.7), calls=%async_computation.1 | async-start | bytes 1310720 | tf_op jit(solution)/shard_map/all_to_all | solution.py:269
  47.4 20.3 %collective-permute-start.4 = (bf16[2,40,1920]{2,1,0:T(8,128)(2,1)S(1)}, bf16[2,40,1920]{2,1,0:T(8,128)(2,1)S(1)}, u32[]{:S(2)}, u32[]{:S(2)}) collective-permute-start(bf16[2,40,1920]{2,1,0:T(8,128)(2,1)S(1)} %pad_maximum_fusion.1), channel_id=1, source_target_pairs={{0,32},{32,0},{64,96},{96,64},{128,160},{160,128},{192,224},{224,1... | collective-permute-start | bytes 921608 | tf_op jit(solution)/shard_map/ppermute | solution.py:264
  51.4 16.3 %collective-permute-start.5 = (bf16[32,1280]{1,0:T(8,128)(2,1)S(1)}, bf16[32,1280]{1,0:T(8,128)(2,1)S(1)}, u32[]{:S(2)}, u32[]{:S(2)}) collective-permute-start(bf16[32,1280]{1,0:T(8,128)(2,1)S(1)} %maximum_select_fusion), channel_id=1, source_target_pairs={{0,752},{16,32},{32,16},{48,64},{64,48},{80,96},{96,80},{112,128},... | collective-permute-start | bytes 245768 | tf_op jit(solution)/shard_map/ppermute | solution.py:260
  67.8 16.4 %collective-permute-start.6 = (bf16[4,40,1920]{2,1,0:T(8,128)(2,1)S(1)}, bf16[4,40,1920]{2,1,0:T(8,128)(2,1)S(1)}, u32[]{:S(2)}, u32[]{:S(2)}) collective-permute-start(bf16[4,40,1920]{2,1,0:T(8,128)(2,1)S(1)} %pad_maximum_fusion.refs_0_), channel_id=1, source_target_pairs={{0,8},{8,0},{1,9},{9,1},{2,10},{10,2},{3,11},{11,3},{4,12},{12,4},... | collective-permute-start | bytes 1843208 | tf_op jit(solution)/shard_map/ppermute | solution.py:267
  70.7 23.5 %all-to-all-start.2 = ((f32[12,8,256]{2,1,0:T(8,128)}), f32[12,8,256]{2,1,0:T(8,128)S(1)}, u32[]{:S(2)}, u32[]{:S(2)}) async-start(f32[12,8,256]{2,1,0:T(8,128)} %bitcast.16), calls=%async_computation.2 | async-start | bytes 196608 | tf_op jit(solution)/shard_map/all_to_all | solution.py:277
  84.2 15.4 %collective-permute-start.7 = (bf16[4,40,1920]{2,1,0:T(8,128)(2,1)S(1)}, bf16[4,40,1920]{2,1,0:T(8,128)(2,1)S(1)}, u32[]{:S(2)}, u32[]{:S(2)}) collective-permute-start(bf16[4,40,1920]{2,1,0:T(8,128)(2,1)S(1)} %pad_maximum_fusion.refs_0_), channel_id=1, source_target_pairs={{0,16},{16,0},{1,17},{17,1},{2,18},{18,2},{3,19},{19,3},{4,20},{20... | collective-permute-start | bytes 1843208 | tf_op jit(solution)/shard_map/ppermute | solution.py:276
  87.8 11.7 %collective-permute-start.8 = (bf16[4,40,1920]{2,1,0:T(8,128)(2,1)S(1)}, bf16[4,40,1920]{2,1,0:T(8,128)(2,1)S(1)}, u32[]{:S(2)}, u32[]{:S(2)}) collective-permute-start(bf16[4,40,1920]{2,1,0:T(8,128)(2,1)S(1)} %collective-permute-done.6.refs_1_), channel_id=1, source_target_pairs={{0,16},{16,0},{1,17},{17,1},{2,18},{18,2},{3,19},{19,3},{4,20},{20... | collective-permute-start | bytes 1843208 | tf_op jit(solution)/shard_map/ppermute | solution.py:280
  94.9 17.4 %all-to-all-start.3 = ((f32[24,8,256]{2,1,0:T(8,128)}), f32[24,8,256]{2,1,0:T(8,128)}, u32[]{:S(2)}, u32[]{:S(2)}) async-start(f32[24,8,256]{2,1,0:T(8,128)} %broadcast_in_dim.2), calls=%async_computation.3 | async-start | bytes 393216 | tf_op jit(solution)/shard_map/all_to_all | solution.py:282
  99.6 1.0 copy-start.4

commit v9 on v8

--- a/solution.py
+++ b/solution.py
@@ -71,7 +71,7 @@
             part, part, pltpu.VMEM((steps, 4, frames * strip // steps, width), jnp.bfloat16),
             pltpu.SemaphoreType.DMA((steps, 2)), pltpu.SemaphoreType.DMA((steps,)),
         ],
-        compiler_params=pltpu.CompilerParams(vmem_limit_bytes=48 << 20),
+        compiler_params=pltpu.CompilerParams(vmem_limit_bytes=60 << 20),
         name="pack",
     )(features, cotangent)
 
@@ -264,7 +264,8 @@
     pair_far = lax.ppermute(pair, "z", [(i, i ^ 1) for i in range(n_z)])
     pair_far, halo, edges = lax.optimization_barrier((pair_far, halo, edges))
     blocks = jnp.concatenate([pair, pair_far])
-    blocks_far = lax.ppermute(blocks, "xl", both)
+    pairs = [(i, i ^ (1 if i // 2 % 2 == 0 else 5)) for i in range(8)]
+    blocks_far = lax.ppermute(blocks, ("xh", "c", "xl"), pairs)
 
     part = lax.all_to_all(term.reshape(n_y, 320 // n_y, 512), "y", 0, 0, tiled=True)
     part, blocks = lax.optimization_barrier((part, blocks))

time: 120 us -> 119 us (level)
  local copies, waits for them, and re-layouts: 5.66 us -> 3.72 us
    unnamed x14 -> x10, local copies, waits for them, and re-layouts: 2.93 us -> 0.99 us
where the time goes in v9:
time: 119 us; the launch traced here: 118 us
  starting transfers between devices  72 us (61%)
  waiting for transfers between devices  21.5 us (18%)
  Pallas kernels  9.08 us (8%)
  blocking collectives  9.01 us (8%)
  local copies, waits for them, and re-layouts  3.72 us (3%)
  between operations  1.65 us (1%)
    ppermute x1, starting transfers between devices, shards(): halo = lax.ppermute(jnp.where(core == 0, ends[0], ends[1]), DP, across)  12.5 us
    all_to_all x1, starting transfers between devices, shards(): mine = lax.all_to_all(pieces, 'z', 0, 0, tiled=True)  12.4 us
    ppermute x1, starting transfers between devices, shards(): sib = lax.ppermute(own, 'c', both)  9.64 us
    ppermute x2, starting transfers between devices, from_y(): return lax.ppermute(temporal_weight, ('z', 'c', 'y'), pairs)  9.63 us
    all_to_all x1, waiting for transfers between devices, shards(): gathered = lax.all_to_all(mine, ('xh', 'z'), 0, 0, tiled=True)  8.28 us
    all_gather x1, blocking collectives, shards(): gathered = lax.all_gather(gathered, 'c')  6.05 us
    all_to_all x1, waiting for transfers between devices, shards(): mine = lax.all_to_all(pieces, 'z', 0, 0, tiled=True)  5.52 us
    all_to_all x1, starting transfers between devices, shards(): lax.all_to_all(pack(features, cotangent), X, 0, 0, tiled=True)  4.99 us
  transfers between devices with their start and end apart: 13, of which 6 were waited for; matrix products, arithmetic and copies ran while one was open for 2% of the time, Pallas kernels for 3%

profile of v9, /device:TPU:1, one launch (start us, length us, event | category | flops | bytes accessed | tf_op | source)
XLA Modules:
  0.0 117.8 jit_solution(5758681629402281970)
XLA Ops:
  0.6 2.2 %pack.1 = bf16[4,256,640]{2,1,0:T(8,128)(2,1)} custom-call(bf16[8,32,640]{2,1,0:T(8,128)(2,1)} %f_ref, bf16[8,32,640]{2,1,0:T(8,128)(2,1)} %g_ref), custom_call_target="tpu_custom_call" | custom-call | tf_op jit(solution)/shard_map/pack/pallas_call | solution.py:65
  2.9 5.0 %all-to-all-start = ((bf16[4,256,640]{2,1,0:T(8,128)(2,1)}), bf16[4,256,640]{2,1,0:T(8,128)(2,1)S(1)}, u32[]{:S(2)}, u32[]{:S(2)}) async-start(bf16[4,256,640]{2,1,0:T(8,128)(2,1)} %pack.1), calls=%async_computation | async-start | bytes 2621440 | tf_op jit(solution)/shard_map/all_to_all | solution.py:241
  7.9 6.7 %collective-permute-start = (bf16[40,1920]{1,0:T(8,128)(2,1)S(1)}, bf16[40,1920]{1,0:T(8,128)(2,1)S(1)}, u32[]{:S(2)}, u32[]{:S(2)}) collective-permute-start(bf16[40,1920]{1,0:T(8,128)(2,1)S(1)} %copy-done.3), channel_id=1, source_target_pairs={{0,3},{1,4},{2,5},{3,6},{4,7},{5,0},{6,1},{7,2},{16,21},{17,22},{1... | collective-permute-start | bytes 460808 | tf_op jit(solution)/shard_map/ppermute | solution.py:236
  14.5 3.0 %collective-permute-start.1 = (bf16[40,1920]{1,0:T(8,128)(2,1)S(1)}, bf16[40,1920]{1,0:T(8,128)(2,1)S(1)}, u32[]{:S(2)}, u32[]{:S(2)}) collective-permute-start(bf16[40,1920]{1,0:T(8,128)(2,1)S(1)} %copy-done.3), channel_id=1, source_target_pairs={{0,1},{1,2},{2,3},{3,4},{4,5},{5,6},{6,7},{7,0},{16,23},{17,16},{1... | collective-permute-start | bytes 460808 | tf_op jit(solution)/shard_map/ppermute | solution.py:236
  18.2 1.7 %collective-permute-done = bf16[40,1920]{1,0:T(8,128)(2,1)S(1)} collective-permute-done((bf16[40,1920]{1,0:T(8,128)(2,1)S(1)}, bf16[40,1920]{1,0:T(8,128)(2,1)S(1)}, u32[]{:S(2)}, u32[]{:S(2)}) %collective-permute-start) | collective-permute-done | bytes 153632 | tf_op jit(solution)/shard_map/ppermute | solution.py:236
  20.0 1.6 %collective-permute-done.1 = bf16[40,1920]{1,0:T(8,128)(2,1)S(1)} collective-permute-done((bf16[40,1920]{1,0:T(8,128)(2,1)S(1)}, bf16[40,1920]{1,0:T(8,128)(2,1)S(1)}, u32[]{:S(2)}, u32[]{:S(2)}) %collective-permute-start.1) | collective-permute-done | bytes 153632 | tf_op jit(solution)/shard_map/ppermute | solution.py:236
  21.6 9.6 %collective-permute-start.2 = (bf16[4,8,32,640]{3,2,1,0:T(8,128)(2,1)S(1)}, bf16[4,8,32,640]{3,2,1,0:T(8,128)(2,1)S(1)}, u32[]{:S(2)}, u32[]{:S(2)}) collective-permute-start(bf16[4,8,32,640]{3,2,1,0:T(8,128)(2,1)S(1)} %bitcast.61), channel_id=1, source_target_pairs={{0,16},{16,0},{1,17},{17,1},{2,18},{18,2},{3,19},{19,3},{4,20},{20... | collective-permute-start | bytes 3932168 | tf_op jit(solution)/shard_map/ppermute | solution.py:243
  31.6 1.9 %collective-permute-start.3 = (bf16[4,32,384]{2,1,0:T(8,128)(2,1)S(1)}, bf16[4,32,384]{2,1,0:T(8,128)(2,1)S(1)}, u32[]{:S(2)}, u32[]{:S(2)}) collective-permute-start(bf16[4,32,384]{2,1,0:T(8,128)(2,1)S(1)} %fusion), channel_id=1, source_target_pairs={{0,368},{32,16},{64,48},{96,80},{128,112},{160,144},{192,176},{224... | collective-permute-start | bytes 294920 | tf_op jit(solution)/shard_map/ppermute | solution.py:246
  34.1 3.5 %collective-permute-done.3.halo_ref = bf16[4,32,384]{2,1,0:T(8,128)(2,1)S(1)} collective-permute-done((bf16[4,32,384]{2,1,0:T(8,128)(2,1)S(1)}, bf16[4,32,384]{2,1,0:T(8,128)(2,1)S(1)}, u32[]{:S(2)}, u32[]{:S(2)}) %collective-permute-start.3) | collective-permute-done | bytes 98336 | tf_op jit(solution)/shard_map/ppermute | solution.py:246
  37.6 3.3 %x_term.1 = f32[320,512]{1,0:T(8,128)} custom-call(s32[3]{0:T(128)S(1)} %pad_add_fusion.place_ref, s32[32]{0:T(128)S(1)} %get-tuple-element.72.prev_ref, s32[32]{0:T(128)S(1)} %get-tuple-element.71.next_ref, bf16[4,8,32,640]{3,2,1,0:T(8,128)(2,1)S(1)} %bitcast.63, bf16[4,8,32,640]{3,2,1,0:T(8,128)(2,1)S(1)} %collective-permute-done.2.sib_ref, ...), custom_call_target="tpu_custom_call" | custom-call | tf_op jit(solution)/shard_map/x_term/pallas_call | solution.py:151
  40.9 4.6 %all-to-all-start.1 = ((f32[8,40,512]{2,1,0:T(8,128)}), f32[8,40,512]{2,1,0:T(8,128)S(1)}, u32[]{:S(2)}, u32[]{:S(2)}) async-start(f32[8,40,512]{2,1,0:T(8,128)} %bitcast.7), calls=%async_computation.1 | async-start | bytes 1310720 | tf_op jit(solution)/shard_map/all_to_all | solution.py:270
  45.6 4.0 %collective-permute-start.4 = (bf16[2,40,1920]{2,1,0:T(8,128)(2,1)S(1)}, bf16[2,40,1920]{2,1,0:T(8,128)(2,1)S(1)}, u32[]{:S(2)}, u32[]{:S(2)}) collective-permute-start(bf16[2,40,1920]{2,1,0:T(8,128)(2,1)S(1)} %pad_maximum_fusion.1), channel_id=1, source_target_pairs={{0,32},{32,0},{64,96},{96,64},{128,160},{160,128},{192,224},{224,1... | collective-permute-start | bytes 921608 | tf_op jit(solution)/shard_map/ppermute | solution.py:264
  49.7 12.5 %collective-permute-start.5 = (bf16[32,1280]{1,0:T(8,128)(2,1)S(1)}, bf16[32,1280]{1,0:T(8,128)(2,1)S(1)}, u32[]{:S(2)}, u32[]{:S(2)}) collective-permute-start(bf16[32,1280]{1,0:T(8,128)(2,1)S(1)} %maximum_select_fusion), channel_id=1, source_target_pairs={{0,752},{16,32},{32,16},{48,64},{64,48},{80,96},{96,80},{112,128},... | collective-permute-start | bytes 245768 | tf_op jit(solution)/shard_map/ppermute | solution.py:260
  62.2 3.0 %all_gather.10.edge_ref = bf16[2,32,1280]{2,1,0:T(8,128)(2,1)S(1)} all-gather(bf16[1,32,1280]{2,1,0:T(8,128)(2,1)S(1)} %maximum_select_fusion.1), channel_id=1, replica_groups=mesh['xh'=2,'z'=12,'c'=2,'xl'=2,'y'=8] {'c'}, dimensions={0}, use_global_device_ids=true | all-gather | bytes 245760 | tf_op jit(solution)/shard_map/all_gather | solution.py:258
  66.0 3.3 %collective-permute-start.6 = (bf16[4,40,1920]{2,1,0:T(8,128)(2,1)S(1)}, bf16[4,40,1920]{2,1,0:T(8,128)(2,1)S(1)}, u32[]{:S(2)}, u32[]{:S(2)}) collective-permute-start(bf16[4,40,1920]{2,1,0:T(8,128)(2,1)S(1)} %pad_maximum_fusion.refs_0_), channel_id=1, source_target_pairs={{0,8},{8,0},{16,408},{24,400},{384,392},{392,384},{400,24},{408,16... | collective-permute-start | bytes 1843208 | tf_op jit(solution)/shard_map/ppermute | solution.py:268
  70.0 12.4 %all-to-all-start.2 = ((f32[12,8,256]{2,1,0:T(8,128)}), f32[12,8,256]{2,1,0:T(8,128)S(1)}, u32[]{:S(2)}, u32[]{:S(2)}) async-start(f32[12,8,256]{2,1,0:T(8,128)} %bitcast.16), calls=%async_computation.2 | async-start | bytes 196608 | tf_op jit(solution)/shard_map/all_to_all | solution.py:278
  82.4 2.6 %collective-permute-start.7 = (bf16[4,40,1920]{2,1,0:T(8,128)(2,1)S(1)}, bf16[4,40,1920]{2,1,0:T(8,128)(2,1)S(1)}, u32[]{:S(2)}, u32[]{:S(2)}) collective-permute-start(bf16[4,40,1920]{2,1,0:T(8,128)(2,1)S(1)} %pad_maximum_fusion.refs_0_), channel_id=1, source_target_pairs={{0,16},{16,0},{1,17},{17,1},{2,18},{18,2},{3,19},{19,3},{4,20},{20... | collective-permute-start | bytes 1843208 | tf_op jit(solution)/shard_map/ppermute | solution.py:277
  85.0 1.9 %collective-permute-start.8 = (bf16[4,40,1920]{2,1,0:T(8,128)(2,1)S(1)}, bf16[4,40,1920]{2,1,0:T(8,128)(2,1)S(1)}, u32[]{:S(2)}, u32[]{:S(2)}) collective-permute-start(bf16[4,40,1920]{2,1,0:T(8,128)(2,1)S(1)} %collective-permute-done.6.refs_1_), channel_id=1, source_target_pairs={{0,16},{16,0},{1,17},{17,1},{2,18},{18,2},{3,19},{19,3},{4,20},{20... | collective-permute-start | bytes 1843208 | tf_op jit(solution)/shard_map/ppermute | solution.py:281
  86.9 5.5 %all-to-all-done.2 = f32[12,8,256]{2,1,0:T(8,128)S(1)} async-done(((f32[12,8,256]{2,1,0:T(8,128)}), f32[12,8,256]{2,1,0:T(8,128)S(1)}, u32[]{:S(2)}, u32[]{:S(2)}) %all-to-all-start.2) | async-done | bytes 98336 | tf_op jit(solution)/shard_map/all_to_all | solution.py:278
  93.2 4.5 %all-to-all-start.3 = ((f32[24,8,256]{2,1,0:T(8,128)}), f32[24,8,256]{2,1,0:T(8,128)}, u32[]{:S(2)}, u32[]{:S(2)}) async-start(f32[24,8,256]{2,1,0:T(8,128)} %broadcast_in_dim.2), calls=%async_computation.3 | async-start | bytes 393216 | tf_op jit(solution)/shard_map/all_to_all | solution.py:283
  97.8 1.0 copy-done.2
  98.8 3.5 %outputs.1 = (bf16[8,32,640]{2,1,0:T(8,128)(2,1)}, bf16[8,32,640]{2,1,0:T(8,128)(2,1)}) custom-call(s32[5]{0:T(128)S(1)} %stack.49.place_ref, s32[32]{0:T(128)S(1)} %get-tuple-element.72.prev_ref, s32[32]{0:T(128)S(1)} %get-tuple-element.71.next_ref, bf16[8,32,640]{2,1,0:T(8,128)(2,1)S(1)} %copy-done, bf16[8,32,640]{2,1,0:T(8,128)(2,1)S(1)} %copy-done.1, ...), custom_call_target="tpu_custom_call" | custom-call | tf_op jit(solution)/shard_map/outputs/pallas_call | solution.py:211
  102.3 8.3 %all-to-all-done.3 = f32[24,8,256]{2,1,0:T(8,128)} async-done(((f32[24,8,256]{2,1,0:T(8,128)}), f32[24,8,256]{2,1,0:T(8,128)}, u32[]{:S(2)}, u32[]{:S(2)}) %all-to-all-start.3) | async-done | bytes 196640 | tf_op jit(solution)/shard_map/all_to_all | solution.py:283
  110.6 6.1 %all-gather = f32[48,8,256]{2,1,0:T(8,128)S(1)} all-gather(f32[24,8,256]{2,1,0:T(8,128)} %all-to-all-done.3), channel_id=2, replica_groups=mesh['xh'=2,'z'=12,'c'=2,'xl'=2,'y'=8] {'c'}, dimensions={0}, use_global_device_ids=true | all-gather | bytes 589824 | tf_op jit(solution)/shard_map/all_gather | solution.py:289
  (55 shorter events, 4.4 us)
Async XLA Ops:
  2.9 5.0 %copy-start.3 = (bf16[40,1920]{1,0:T(8,128)(2,1)S(1)}, bf16[40,1920]{1,0:T(8,128)(2,1)}, u32[]{:S(2)}) copy-start(bf16[40,1920]{1,0:T(8,128)(2,1)} %param.9) | copy-start | bytes 460804
  2.9 30.7 %copy-start.4 = (s32[48]{0:T(128)S(1)}, s32[48]{0:T(128)}, u32[]{:S(2)}) copy-start(s32[48]{0:T(128)} %param.10) | copy-start | bytes 580
  2.9 18.7 %all-to-all-start = ((bf16[4,256,640]{2,1,0:T(8,128)(2,1)}), bf16[4,256,640]{2,1,0:T(8,128)(2,1)S(1)}, u32[]{:S(2)}, u32[]{:S(2)}) async-start(bf16[4,256,640]{2,1,0:T(8,128)(2,1)} %pack.1), calls=%async_computation | async-start | bytes 2621440 | tf_op jit(solution)/shard_map/all_to_all | solution.py:241
  7.9 12.1 %collective-permute-start = (bf16[40,1920]{1,0:T(8,128)(2,1)S(1)}, bf16[40,1920]{1,0:T(8,128)(2,1)S(1)}, u32[]{:S(2)}, u32[]{:S(2)}) collective-permute-start(bf16[40,1920]{1,0:T(8,128)(2,1)S(1)} %copy-done.3), channel_id=1, source_target_pairs={{0,3},{1,4},{2,5},{3,6},{4,7},{5,0},{6,1},{7,2},{16,21},{17,22},{1... | collective-permute-start | bytes 460808 | tf_op jit(solution)/shard_map/ppermute | solution.py:236
  14.5 7.1 %collective-permute-start.1 = (bf16[40,1920]{1,0:T(8,128)(2,1)S(1)}, bf16[40,1920]{1,0:T(8,128)(2,1)S(1)}, u32[]{:S(2)}, u32[]{:S(2)}) collective-permute-start(bf16[40,1920]{1,0:T(8,128)(2,1)S(1)} %copy-done.3), channel_id=1, source_target_pairs={{0,1},{1,2},{2,3},{3,4},{4,5},{5,6},{6,7},{7,0},{16,23},{17,16},{1... | collective-permute-start | bytes 460808 | tf_op jit(solution)/shard_map/ppermute | solution.py:236
  21.6 16.0 %collective-permute-start.2 = (bf16[4,8,32,640]{3,2,1,0:T(8,128)(2,1)S(1)}, bf16[4,8,32,640]{3,2,1,0:T(8,128)(2,1)S(1)}, u32[]{:S(2)}, u32[]{:S(2)}) collective-permute-start(bf16[4,8,32,640]{3,2,1,0:T(8,128)(2,1)S(1)} %bitcast.61), channel_id=1, source_target_pairs={{0,16},{16,0},{1,17},{17,1},{2,18},{18,2},{3,19},{19,3},{4,20},{20... | collective-permute-start | bytes 3932168 | tf_op jit(solution)/shard_map/ppermute | solution.py:243
  31.6 5.9 %collective-permute-start.3 = (bf16[4,32,384]{2,1,0:T(8,128)(2,1)S(1)}, bf16[4,32,384]{2,1,0:T(8,128)(2,1)S(1)}, u32[]{:S(2)}, u32[]{:S(2)}) collective-permute-start(bf16[4,32,384]{2,1,0:T(8,128)(2,1)S(1)} %fusion), channel_id=1, source_target_pairs={{0,368},{32,16},{64,48},{96,80},{128,112},{160,144},{192,176},{224... | collective-permute-start | bytes 294920 | tf_op jit(solution)/shard_map/ppermute | solution.py:246
  40.9 4.6 %copy-start = (bf16[8,32,640]{2,1,0:T(8,128)(2,1)S(1)}, bf16[8,32,640]{2,1,0:T(8,128)(2,1)}, u32[]{:S(2)}) copy-start(bf16[8,32,640]{2,1,0:T(8,128)(2,1)} %f_ref) | copy-start | bytes 983044
  40.9 4.7 %copy-start.1 = (bf16[8,32,640]{2,1,0:T(8,128)(2,1)S(1)}, bf16[8,32,640]{2,1,0:T(8,128)(2,1)}, u32[]{:S(2)}) copy-start(bf16[8,32,640]{2,1,0:T(8,128)(2,1)} %g_ref) | copy-start | bytes 983044
  40.9 28.4 %all-to-all-start.1 = ((f32[8,40,512]{2,1,0:T(8,128)}), f32[8,40,512]{2,1,0:T(8,128)S(1)}, u32[]{:S(2)}, u32[]{:S(2)}) async-start(f32[8,40,512]{2,1,0:T(8,128)} %bitcast.7), calls=%async_computation.1 | async-start | bytes 1310720 | tf_op jit(solution)/shard_map/all_to_all | solution.py:270
  45.6 20.3 %collective-permute-start.4 = (bf16[2,40,1920]{2,1,0:T(8,128)(2,1)S(1)}, bf16[2,40,1920]{2,1,0:T(8,128)(2,1)S(1)}, u32[]{:S(2)}, u32[]{:S(2)}) collective-permute-start(bf16[2,40,1920]{2,1,0:T(8,128)(2,1)S(1)} %pad_maximum_fusion.1), channel_id=1, source_target_pairs={{0,32},{32,0},{64,96},{96,64},{128,160},{160,128},{192,224},{224,1... | collective-permute-start | bytes 921608 | tf_op jit(solution)/shard_map/ppermute | solution.py:264
  49.7 16.3 %collective-permute-start.5 = (bf16[32,1280]{1,0:T(8,128)(2,1)S(1)}, bf16[32,1280]{1,0:T(8,128)(2,1)S(1)}, u32[]{:S(2)}, u32[]{:S(2)}) collective-permute-start(bf16[32,1280]{1,0:T(8,128)(2,1)S(1)} %maximum_select_fusion), channel_id=1, source_target_pairs={{0,752},{16,32},{32,16},{48,64},{64,48},{80,96},{96,80},{112,128},... | collective-permute-start | bytes 245768 | tf_op jit(solution)/shard_map/ppermute | solution.py:260
  66.0 16.4 %collective-permute-start.6 = (bf16[4,40,1920]{2,1,0:T(8,128)(2,1)S(1)}, bf16[4,40,1920]{2,1,0:T(8,128)(2,1)S(1)}, u32[]{:S(2)}, u32[]{:S(2)}) collective-permute-start(bf16[4,40,1920]{2,1,0:T(8,128)(2,1)S(1)} %pad_maximum_fusion.refs_0_), channel_id=1, source_target_pairs={{0,8},{8,0},{16,408},{24,400},{384,392},{392,384},{400,24},{408,16... | collective-permute-start | bytes 1843208 | tf_op jit(solution)/shard_map/ppermute | solution.py:268
  70.0 22.5 %all-to-all-start.2 = ((f32[12,8,256]{2,1,0:T(8,128)}), f32[12,8,256]{2,1,0:T(8,128)S(1)}, u32[]{:S(2)}, u32[]{:S(2)}) async-start(f32[12,8,256]{2,1,0:T(8,128)} %bitcast.16), calls=%async_computation.2 | async-start | bytes 196608 | tf_op jit(solution)/shard_map/all_to_all | solution.py:278
  82.4 15.4 %collective-permute-start.7 = (bf16[4,40,1920]{2,1,0:T(8,128)(2,1)S(1)}, bf16[4,40,1920]{2,1,0:T(8,128)(2,1)S(1)}, u32[]{:S(2)}, u32[]{:S(2)}) collective-permute-start(bf16[4,40,1920]{2,1,0:T(8,128)(2,1)S(1)} %pad_maximum_fusion.refs_0_), channel_id=1, source_target_pairs={{0,16},{16,0},{1,17},{17,1},{2,18},{18,2},{3,19},{19,3},{4,20},{20... | collective-permute-start | bytes 1843208 | tf_op jit(solution)/shard_map/ppermute | solution.py:277
  85.0 12.8 %collective-permute-start.8 = (bf16[4,40,1920]{2,1,0:T(8,128)(2,1)S(1)}, bf16[4,40,1920]{2,1,0:T(8,128)(2,1)S(1)}, u32[]{:S(2)}, u32[]{:S(2)}) collective-permute-start(bf16[4,40,1920]{2,1,0:T(8,128)(2,1)S(1)} %collective-permute-done.6.refs_1_), channel_id=1, source_target_pairs={{0,16},{16,0},{1,17},{17,1},{2,18},{18,2},{3,19},{19,3},{4,20},{20... | collective-permute-start | bytes 1843208 | tf_op jit(solution)/shard_map/ppermute | solution.py:281
  93.2 17.4 %all-to-all-start.3 = ((f32[24,8,256]{2,1,0:T(8,128)}), f32[24,8,256]{2,1,0:T(8,128)}, u32[]{:S(2)}, u32[]{:S(2)}) async-start(f32[24,8,256]{2,1,0:T(8,128)} %broadcast_in_dim.2), calls=%async_computation.3 | async-start | bytes 393216 | tf_op jit(solution)/shard_map/all_to_all | solution.py:283
  97.8 1.0 copy-start.2

commit v10 on v9

--- a/solution.py
+++ b/solution.py
@@ -154,7 +154,7 @@
         in_specs=[smem] * 3 + [vmem] * 3,
         out_specs=vmem,
         scratch_shapes=[buf, buf],
-        compiler_params=pltpu.CompilerParams(vmem_limit_bytes=48 << 20),
+        compiler_params=pltpu.CompilerParams(vmem_limit_bytes=20 << 20),
         name="x_term",
     )(place, prev_ok, next_ok, own, sib, halo)
 
@@ -214,7 +214,7 @@
         in_specs=[smem] * 3 + [vmem] * 9,
         out_specs=(vmem, vmem),
         scratch_shapes=[buf] * 4 + [pltpu.VMEM((2, 8, 40, 3 * width), jnp.bfloat16), pltpu.VMEM((width, 3 * width), jnp.bfloat16)],
-        compiler_params=pltpu.CompilerParams(vmem_limit_bytes=48 << 20),
+        compiler_params=pltpu.CompilerParams(vmem_limit_bytes=28 << 20),
         name="outputs",
     )(place, prev_ok, next_ok, features, cotangent, skip_input, halo, edge, *weights)
 
@@ -225,6 +225,9 @@
     n_x, n_y, n_z = lax.axis_size(X), lax.axis_size("y"), lax.axis_size("z")
     n_dp = lax.axis_size(DP)
     total_frames = frames * n_dp
+
+    packed = pack(features, cotangent)
+    _, temporal_weight = lax.optimization_barrier((packed, temporal_weight))
 
     def from_y(even, odd):
         pairs = []
@@ -238,8 +241,12 @@
     w_far, w_near = from_y(3, 4), from_y(1, 2)
 
     both = [(0, 1), (1, 0)]
-    own = lax.all_to_all(pack(features, cotangent), X, 0, 0, tiled=True).reshape(n_x, frames, strip, width)
-    own, w_far, w_near = lax.optimization_barrier((own, w_far, w_near))
+    own = lax.all_to_all(packed, X, 0, 0, tiled=True).reshape(n_x, frames, strip, width)
+    ends = [jnp.concatenate([features[i], cotangent[i]], axis=1) for i in (0, -1)]
+    edges = lax.all_gather(jnp.where(core == 0, ends[1], ends[0]), "c")
+    across = [(d, (d - 1) % n_dp if d % 2 == 0 else (d + 1) % n_dp) for d in range(n_dp)]
+    halo = lax.ppermute(jnp.where(core == 0, ends[0], ends[1]), DP, across)
+    own, w_far, w_near, halo, edges = lax.optimization_barrier((own, w_far, w_near, halo, edges))
     sib = lax.ppermute(own, "c", both)
     z_next = [(2 * i, (2 * i - 1) % (2 * n_z)) for i in range(n_z)] + [(2 * i + 1, (2 * i + 2) % (2 * n_z)) for i in range(n_z)]
     edge = jnp.where(core == 0, own[:, 0, :, :384], own[:, -1, :, :384])
@@ -253,16 +260,10 @@
     place = jnp.stack([core, xl, wrapped.astype(jnp.int32)]).astype(jnp.int32)
     term = x_term(place, prev_all, next_all, own, sib, halo_x)
 
-    _, features, cotangent = lax.optimization_barrier((term, features, cotangent))
-    ends = [jnp.concatenate([features[i], cotangent[i]], axis=1) for i in (0, -1)]
-    edges = lax.all_gather(jnp.where(core == 0, ends[1], ends[0]), "c")
-    across = [(d, (d - 1) % n_dp if d % 2 == 0 else (d + 1) % n_dp) for d in range(n_dp)]
-    halo = lax.ppermute(jnp.where(core == 0, ends[0], ends[1]), DP, across)
     _, w_far, w_near = lax.optimization_barrier((term, w_far, w_near))
     parity = z % 2
     pair = jnp.stack([jnp.where((parity == 1) & (core == 1), temporal_weight, w_far), w_near])
     pair_far = lax.ppermute(pair, "z", [(i, i ^ 1) for i in range(n_z)])
-    pair_far, halo, edges = lax.optimization_barrier((pair_far, halo, edges))
     blocks = jnp.concatenate([pair, pair_far])
     pairs = [(i, i ^ (1 if i // 2 % 2 == 0 else 5)) for i in range(8)]
     blocks_far = lax.ppermute(blocks, ("xh", "c", "xl"), pairs)

time: 119 us -> 120 us (level)
  starting transfers between devices: 72 us -> 61.2 us
  blocking collectives: 9.01 us -> 15.9 us
  other arithmetic: 0.84 us -> 4.66 us
  local copies, waits for them, and re-layouts: 3.72 us -> 5.66 us
    ppermute x1, starting transfers between devices: 9.64 us -> 2.25 us  [shards(): sib = lax.ppermute(own, 'c', both)]
    all_gather x1, blocking collectives: 2.96 us -> 10.2 us  [shards(): edges = lax.all_gather(jnp.where(core == 0, ends[1], ends[0]), 'c')]
    ppermute x1, starting transfers between devices: 12.5 us -> 5.63 us  [shards(): halo = lax.ppermute(jnp.where(core == 0, ends[0], ends[1]), DP, across)]
    ppermute x1, waiting for transfers between devices: 0.01 us -> 5.67 us  [shards(): pair_far = lax.ppermute(pair, 'z', [(i, i ^ 1) for i in range(n_z)])]
    all_to_all x1, starting transfers between devices: 12.4 us -> 16.7 us  [shards(): mine = lax.all_to_all(pieces, 'z', 0, 0, tiled=True)]
    ppermute x1, waiting for transfers between devices: 3.5 us -> 0.01 us  [shards(): halo_x = lax.ppermute(edge, ('z', 'c'), z_next)]
    ppermute x2, waiting for transfers between devices: 3.39 us -> 0.01 us  [from_y(): return lax.ppermute(temporal_weight, ('z', 'c', 'y'), pairs)]
    another operation x2, other arithmetic: 0.19 us -> 2.77 us
  transfers between devices with their start and end apart: 13 -> 13, of which waited for: 6 -> 4; matrix products, arithmetic and copies ran while one was open for 2% -> 6% of each run, Pallas kernels for 3% -> 3%
where the time goes in v10:
time: 120 us; the launch traced here: 119 us
  starting transfers between devices  61.2 us (51%)
  waiting for transfers between devices  20.9 us (17%)
  blocking collectives  15.9 us (13%)
  Pallas kernels  9.1 us (8%)
  local copies, waits for them, and re-layouts  5.66 us (5%)
  other arithmetic  4.66 us (4%)
  between operations  1.69 us (1%)
    all_to_all x1, starting transfers between devices, shards(): mine = lax.all_to_all(pieces, 'z', 0, 0, tiled=True)  16.7 us
    all_gather x1, blocking collectives, shards(): edges = lax.all_gather(jnp.where(core == 0, ends[1], ends[0]), 'c')  10.2 us
    ppermute x2, starting transfers between devices, from_y(): return lax.ppermute(temporal_weight, ('z', 'c', 'y'), pairs)  9.76 us
    all_to_all x1, waiting for transfers between devices, shards(): gathered = lax.all_to_all(mine, ('xh', 'z'), 0, 0, tiled=True)  8.44 us
    ppermute x1, waiting for transfers between devices, shards(): pair_far = lax.ppermute(pair, 'z', [(i, i ^ 1) for i in range(n_z)])  5.67 us
    all_gather x1, blocking collectives, shards(): gathered = lax.all_gather(gathered, 'c')  5.65 us
    ppermute x1, starting transfers between devices, shards(): halo = lax.ppermute(jnp.where(core == 0, ends[0], ends[1]), DP, across)  5.63 us
    all_to_all x1, waiting for transfers between devices, shards(): mine = lax.all_to_all(pieces, 'z', 0, 0, tiled=True)  5.52 us
  transfers between devices with their start and end apart: 13, of which 4 were waited for; matrix products, arithmetic and copies ran while one was open for 6% of the time, Pallas kernels for 3%

profile of v10, /device:TPU:1, one launch (start us, length us, event | category | flops | bytes accessed | tf_op | source)
XLA Modules:
  0.0 119.1 jit_solution(11019379938024759950)
XLA Ops:
  0.6 2.2 %pack.1 = bf16[4,256,640]{2,1,0:T(8,128)(2,1)} custom-call(bf16[8,32,640]{2,1,0:T(8,128)(2,1)} %f_ref.1, bf16[8,32,640]{2,1,0:T(8,128)(2,1)} %g_ref.1), custom_call_target="tpu_custom_call" | custom-call | tf_op jit(solution)/shard_map/pack/pallas_call | solution.py:65
  2.9 5.0 %all-to-all-start = ((bf16[4,256,640]{2,1,0:T(8,128)(2,1)}), bf16[4,256,640]{2,1,0:T(8,128)(2,1)S(1)}, u32[]{:S(2)}, u32[]{:S(2)}) async-start(bf16[4,256,640]{2,1,0:T(8,128)(2,1)} %pack.1), calls=%async_computation | async-start | bytes 2621440 | tf_op jit(solution)/shard_map/all_to_all | solution.py:244
  7.9 5.2 %collective-permute-start.1 = (bf16[40,1920]{1,0:T(8,128)(2,1)S(1)}, bf16[40,1920]{1,0:T(8,128)(2,1)S(1)}, u32[]{:S(2)}, u32[]{:S(2)}) collective-permute-start(bf16[40,1920]{1,0:T(8,128)(2,1)S(1)} %copy-done.7), channel_id=1, source_target_pairs={{0,1},{1,2},{2,3},{3,4},{4,5},{5,6},{6,7},{7,0},{16,23},{17,16},{1... | collective-permute-start | bytes 460808 | tf_op jit(solution)/shard_map/ppermute | solution.py:239
  13.1 4.5 %collective-permute-start = (bf16[40,1920]{1,0:T(8,128)(2,1)S(1)}, bf16[40,1920]{1,0:T(8,128)(2,1)S(1)}, u32[]{:S(2)}, u32[]{:S(2)}) collective-permute-start(bf16[40,1920]{1,0:T(8,128)(2,1)S(1)} %copy-done.7), channel_id=1, source_target_pairs={{0,3},{1,4},{2,5},{3,6},{4,7},{5,0},{6,1},{7,2},{16,21},{17,22},{1... | collective-permute-start | bytes 460808 | tf_op jit(solution)/shard_map/ppermute | solution.py:239
  17.8 5.6 %collective-permute-start.2 = (bf16[32,1280]{1,0:T(8,128)(2,1)S(1)}, bf16[32,1280]{1,0:T(8,128)(2,1)S(1)}, u32[]{:S(2)}, u32[]{:S(2)}) collective-permute-start(bf16[32,1280]{1,0:T(8,128)(2,1)S(1)} %maximum_select_fusion), channel_id=1, source_target_pairs={{0,752},{16,32},{32,16},{48,64},{64,48},{80,96},{96,80},{112,128},... | collective-permute-start | bytes 245768 | tf_op jit(solution)/shard_map/ppermute | solution.py:248
  24.4 10.2 %all_gather.10.edge_ref = bf16[2,32,1280]{2,1,0:T(8,128)(2,1)S(1)} all-gather(bf16[1,32,1280]{2,1,0:T(8,128)(2,1)S(1)} %maximum_select_fusion.1), channel_id=1, replica_groups=mesh['xh'=2,'z'=12,'c'=2,'xl'=2,'y'=8] {'c'}, dimensions={0}, use_global_device_ids=true | all-gather | bytes 245760 | tf_op jit(solution)/shard_map/all_gather | solution.py:246
  35.9 2.3 %collective-permute-start.3 = (bf16[4,8,32,640]{3,2,1,0:T(8,128)(2,1)S(1)}, bf16[4,8,32,640]{3,2,1,0:T(8,128)(2,1)S(1)}, u32[]{:S(2)}, u32[]{:S(2)}) collective-permute-start(bf16[4,8,32,640]{3,2,1,0:T(8,128)(2,1)S(1)} %bitcast.61), channel_id=1, source_target_pairs={{0,16},{16,0},{1,17},{17,1},{2,18},{18,2},{3,19},{19,3},{4,20},{20... | collective-permute-start | bytes 3932168 | tf_op jit(solution)/shard_map/ppermute | solution.py:250
  39.0 1.9 %collective-permute-start.4 = (bf16[4,32,384]{2,1,0:T(8,128)(2,1)}, bf16[4,32,384]{2,1,0:T(8,128)(2,1)S(1)}, u32[]{:S(2)}, u32[]{:S(2)}) collective-permute-start(bf16[4,32,384]{2,1,0:T(8,128)(2,1)} %fusion), channel_id=1, source_target_pairs={{0,368},{32,16},{64,48},{96,80},{128,112},{160,144},{192,176},{224... | collective-permute-start | bytes 294920 | tf_op jit(solution)/shard_map/ppermute | solution.py:253
  41.6 1.4 %reduce-window.9 = s32[48,1]{1,0:T(8,128)} reduce-window(s32[48,1]{1,0:T(8,128)} %copy.20, s32[]{:T(128)} %constant.55.clone.1), window={size=48x1 pad=47_0x0_0}, to_apply=%region_0.1 | reduce-window | flops 2256 | bytes 388 | tf_op jit(solution)/shard_map/reduce-window.4
  43.0 1.4 %reduce = s32[48]{0:T(128)} reduce(s32[48,1]{1,0:T(8,128)} %reduce-window.9, s32[]{:T(128)} %constant.55.clone.1), dimensions={1}, to_apply=%reduce-window.9.reduce_sub_computation | reduce | bytes 388 | tf_op jit(solution)/shard_map/reduce-window.4
  45.2 3.4 %x_term.1 = f32[320,512]{1,0:T(8,128)} custom-call(s32[3]{0:T(128)S(1)} %pad_add_fusion.place_ref, s32[32]{0:T(128)S(1)} %convert_subtract_fusion.1.prev_ref, s32[32]{0:T(128)S(1)} %convert_subtract_fusion.next_ref, bf16[4,8,32,640]{3,2,1,0:T(8,128)(2,1)S(1)} %bitcast.63, bf16[4,8,32,640]{3,2,1,0:T(8,128)(2,1)S(1)} %collective-permute-done.3.sib_ref, ...), custom_call_target="tpu_custom_call" | custom-call | tf_op jit(solution)/shard_map/x_term/pallas_call | solution.py:151
  48.5 3.7 %all-to-all-start.1 = ((f32[8,40,512]{2,1,0:T(8,128)}), f32[8,40,512]{2,1,0:T(8,128)S(1)}, u32[]{:S(2)}, u32[]{:S(2)}) async-start(f32[8,40,512]{2,1,0:T(8,128)} %bitcast.11), calls=%async_computation.1 | async-start | bytes 1310720 | tf_op jit(solution)/shard_map/all_to_all | solution.py:271
  52.3 2.1 %collective-permute-start.5 = (bf16[2,40,1920]{2,1,0:T(8,128)(2,1)S(1)}, bf16[2,40,1920]{2,1,0:T(8,128)(2,1)S(1)}, u32[]{:S(2)}, u32[]{:S(2)}) collective-permute-start(bf16[2,40,1920]{2,1,0:T(8,128)(2,1)S(1)} %pad_maximum_fusion.1), channel_id=1, source_target_pairs={{0,32},{32,0},{64,96},{96,64},{128,160},{160,128},{192,224},{224,1... | collective-permute-start | bytes 921608 | tf_op jit(solution)/shard_map/ppermute | solution.py:266
  54.4 5.7 %collective-permute-done.5 = bf16[2,40,1920]{2,1,0:T(8,128)(2,1)S(1)} collective-permute-done((bf16[2,40,1920]{2,1,0:T(8,128)(2,1)S(1)}, bf16[2,40,1920]{2,1,0:T(8,128)(2,1)S(1)}, u32[]{:S(2)}, u32[]{:S(2)}) %collective-permute-start.5) | collective-permute-done | bytes 307232 | tf_op jit(solution)/shard_map/ppermute | solution.py:266
  60.1 4.4 %collective-permute-start.6 = (bf16[4,40,1920]{2,1,0:T(8,128)(2,1)S(1)}, bf16[4,40,1920]{2,1,0:T(8,128)(2,1)S(1)}, u32[]{:S(2)}, u32[]{:S(2)}) collective-permute-start(bf16[4,40,1920]{2,1,0:T(8,128)(2,1)S(1)} %pad_maximum_fusion.refs_0_), channel_id=1, source_target_pairs={{0,8},{8,0},{16,408},{24,400},{384,392},{392,384},{400,24},{408,16... | collective-permute-start | bytes 1843208 | tf_op jit(solution)/shard_map/ppermute | solution.py:269
  64.5 1.3 %all-to-all-done.1 = f32[8,40,512]{2,1,0:T(8,128)S(1)} async-done(((f32[8,40,512]{2,1,0:T(8,128)}), f32[8,40,512]{2,1,0:T(8,128)S(1)}, u32[]{:S(2)}, u32[]{:S(2)}) %all-to-all-start.1) | async-done | bytes 655392 | tf_op jit(solution)/shard_map/all_to_all | solution.py:271
  66.5 16.7 %all-to-all-start.2 = ((f32[12,8,256]{2,1,0:T(8,128)}), f32[12,8,256]{2,1,0:T(8,128)S(1)}, u32[]{:S(2)}, u32[]{:S(2)}) async-start(f32[12,8,256]{2,1,0:T(8,128)} %bitcast.16), calls=%async_computation.2 | async-start | bytes 196608 | tf_op jit(solution)/shard_map/all_to_all | solution.py:279
  83.2 2.6 %collective-permute-start.7 = (bf16[4,40,1920]{2,1,0:T(8,128)(2,1)S(1)}, bf16[4,40,1920]{2,1,0:T(8,128)(2,1)S(1)}, u32[]{:S(2)}, u32[]{:S(2)}) collective-permute-start(bf16[4,40,1920]{2,1,0:T(8,128)(2,1)S(1)} %pad_maximum_fusion.refs_0_), channel_id=1, source_target_pairs={{0,16},{16,0},{1,17},{17,1},{2,18},{18,2},{3,19},{19,3},{4,20},{20... | collective-permute-start | bytes 1843208 | tf_op jit(solution)/shard_map/ppermute | solution.py:278
  85.8 1.9 %collective-permute-start.8 = (bf16[4,40,1920]{2,1,0:T(8,128)(2,1)S(1)}, bf16[4,40,1920]{2,1,0:T(8,128)(2,1)S(1)}, u32[]{:S(2)}, u32[]{:S(2)}) collective-permute-start(bf16[4,40,1920]{2,1,0:T(8,128)(2,1)S(1)} %collective-permute-done.6.refs_1_), channel_id=1, source_target_pairs={{0,16},{16,0},{1,17},{17,1},{2,18},{18,2},{3,19},{19,3},{4,20},{20... | collective-permute-start | bytes 1843208 | tf_op jit(solution)/shard_map/ppermute | solution.py:282
  87.7 5.5 %all-to-all-done.2 = f32[12,8,256]{2,1,0:T(8,128)S(1)} async-done(((f32[12,8,256]{2,1,0:T(8,128)}), f32[12,8,256]{2,1,0:T(8,128)S(1)}, u32[]{:S(2)}, u32[]{:S(2)}) %all-to-all-start.2) | async-done | bytes 98336 | tf_op jit(solution)/shard_map/all_to_all | solution.py:279
  94.0 5.4 %all-to-all-start.3 = ((f32[24,8,256]{2,1,0:T(8,128)}), f32[24,8,256]{2,1,0:T(8,128)}, u32[]{:S(2)}, u32[]{:S(2)}) async-start(f32[24,8,256]{2,1,0:T(8,128)} %broadcast_in_dim.2), calls=%async_computation.3 | async-start | bytes 393216 | tf_op jit(solution)/shard_map/all_to_all | solution.py:284
  100.5 3.5 %outputs.1 = (bf16[8,32,640]{2,1,0:T(8,128)(2,1)}, bf16[8,32,640]{2,1,0:T(8,128)(2,1)}) custom-call(s32[5]{0:T(128)S(1)} %stack.49.place_ref, s32[32]{0:T(128)S(1)} %convert_subtract_fusion.1.prev_ref, s32[32]{0:T(128)S(1)} %convert_subtract_fusion.next_ref, bf16[8,32,640]{2,1,0:T(8,128)(2,1)S(1)} %copy-done, bf16[8,32,640]{2,1,0:T(8,128)(2,1)S(1)} %copy-done.1, ...), custom_call_target="tpu_custom_call" | custom-call | tf_op jit(solution)/shard_map/outputs/pallas_call | solution.py:211
  104.0 8.4 %all-to-all-done.3 = f32[24,8,256]{2,1,0:T(8,128)} async-done(((f32[24,8,256]{2,1,0:T(8,128)}), f32[24,8,256]{2,1,0:T(8,128)}, u32[]{:S(2)}, u32[]{:S(2)}) %all-to-all-start.3) | async-done | bytes 196640 | tf_op jit(solution)/shard_map/all_to_all | solution.py:284
  112.4 5.6 %all-gather = f32[48,8,256]{2,1,0:T(8,128)S(1)} all-gather(f32[24,8,256]{2,1,0:T(8,128)} %all-to-all-done.3), channel_id=2, replica_groups=mesh['xh'=2,'z'=12,'c'=2,'xl'=2,'y'=8] {'c'}, dimensions={0}, use_global_device_ids=true | all-gather | bytes 589824 | tf_op jit(solution)/shard_map/all_gather | solution.py:290
  (69 shorter events, 7.6 us)
Async XLA Ops:
  2.9 5.0 %copy-start.7 = (bf16[40,1920]{1,0:T(8,128)(2,1)S(1)}, bf16[40,1920]{1,0:T(8,128)(2,1)}, u32[]{:S(2)}) copy-start(bf16[40,1920]{1,0:T(8,128)(2,1)} %param.9) | copy-start | bytes 460804
  2.9 14.8 %copy-start = (bf16[8,32,640]{2,1,0:T(8,128)(2,1)S(1)}, bf16[8,32,640]{2,1,0:T(8,128)(2,1)}, u32[]{:S(2)}) copy-start(bf16[8,32,640]{2,1,0:T(8,128)(2,1)} %f_ref.1) | copy-start | bytes 983044
  2.9 14.8 %copy-start.1 = (bf16[8,32,640]{2,1,0:T(8,128)(2,1)S(1)}, bf16[8,32,640]{2,1,0:T(8,128)(2,1)}, u32[]{:S(2)}) copy-start(bf16[8,32,640]{2,1,0:T(8,128)(2,1)} %g_ref.1) | copy-start | bytes 983044
  2.9 32.3 %all-to-all-start = ((bf16[4,256,640]{2,1,0:T(8,128)(2,1)}), bf16[4,256,640]{2,1,0:T(8,128)(2,1)S(1)}, u32[]{:S(2)}, u32[]{:S(2)}) async-start(bf16[4,256,640]{2,1,0:T(8,128)(2,1)} %pack.1), calls=%async_computation | async-start | bytes 2621440 | tf_op jit(solution)/shard_map/all_to_all | solution.py:244
  7.9 33.0 %copy-start.11 = (s32[48]{0:T(128)S(1)}, s32[48]{0:T(128)}, u32[]{:S(2)}) copy-start(s32[48]{0:T(128)} %param.10) | copy-start | bytes 580
  7.9 27.3 %collective-permute-start.1 = (bf16[40,1920]{1,0:T(8,128)(2,1)S(1)}, bf16[40,1920]{1,0:T(8,128)(2,1)S(1)}, u32[]{:S(2)}, u32[]{:S(2)}) collective-permute-start(bf16[40,1920]{1,0:T(8,128)(2,1)S(1)} %copy-done.7), channel_id=1, source_target_pairs={{0,1},{1,2},{2,3},{3,4},{4,5},{5,6},{6,7},{7,0},{16,23},{17,16},{1... | collective-permute-start | bytes 460808 | tf_op jit(solution)/shard_map/ppermute | solution.py:239
  13.1 22.1 %collective-permute-start = (bf16[40,1920]{1,0:T(8,128)(2,1)S(1)}, bf16[40,1920]{1,0:T(8,128)(2,1)S(1)}, u32[]{:S(2)}, u32[]{:S(2)}) collective-permute-start(bf16[40,1920]{1,0:T(8,128)(2,1)S(1)} %copy-done.7), channel_id=1, source_target_pairs={{0,3},{1,4},{2,5},{3,6},{4,7},{5,0},{6,1},{7,2},{16,21},{17,22},{1... | collective-permute-start | bytes 460808 | tf_op jit(solution)/shard_map/ppermute | solution.py:239
  17.8 16.8 %collective-permute-start.2 = (bf16[32,1280]{1,0:T(8,128)(2,1)S(1)}, bf16[32,1280]{1,0:T(8,128)(2,1)S(1)}, u32[]{:S(2)}, u32[]{:S(2)}) collective-permute-start(bf16[32,1280]{1,0:T(8,128)(2,1)S(1)} %maximum_select_fusion), channel_id=1, source_target_pairs={{0,752},{16,32},{32,16},{48,64},{64,48},{80,96},{96,80},{112,128},... | collective-permute-start | bytes 245768 | tf_op jit(solution)/shard_map/ppermute | solution.py:248
  35.2 0.7 copy-start.5
  35.2 0.7 copy-start.9
  35.9 9.2 %collective-permute-start.3 = (bf16[4,8,32,640]{3,2,1,0:T(8,128)(2,1)S(1)}, bf16[4,8,32,640]{3,2,1,0:T(8,128)(2,1)S(1)}, u32[]{:S(2)}, u32[]{:S(2)}) collective-permute-start(bf16[4,8,32,640]{3,2,1,0:T(8,128)(2,1)S(1)} %bitcast.61), channel_id=1, source_target_pairs={{0,16},{16,0},{1,17},{17,1},{2,18},{18,2},{3,19},{19,3},{4,20},{20... | collective-permute-start | bytes 3932168 | tf_op jit(solution)/shard_map/ppermute | solution.py:250
  39.0 6.2 %collective-permute-start.4 = (bf16[4,32,384]{2,1,0:T(8,128)(2,1)}, bf16[4,32,384]{2,1,0:T(8,128)(2,1)S(1)}, u32[]{:S(2)}, u32[]{:S(2)}) collective-permute-start(bf16[4,32,384]{2,1,0:T(8,128)(2,1)} %fusion), channel_id=1, source_target_pairs={{0,368},{32,16},{64,48},{96,80},{128,112},{160,144},{192,176},{224... | collective-permute-start | bytes 294920 | tf_op jit(solution)/shard_map/ppermute | solution.py:253
  48.5 3.7 %copy-start.8 = (bf16[40,1920]{1,0:T(8,128)(2,1)S(1)}, bf16[40,1920]{1,0:T(8,128)(2,1)}, u32[]{:S(2)}) copy-start(bf16[40,1920]{1,0:T(8,128)(2,1)} %param.9) | copy-start | bytes 460804
  48.5 3.7 %copy-start.10 = (bf16[40,1920]{1,0:T(8,128)(2,1)S(1)}, bf16[40,1920]{1,0:T(8,128)(2,1)}, u32[]{:S(2)}) copy-start(bf16[40,1920]{1,0:T(8,128)(2,1)} %copy-done.9) | copy-start | bytes 460804
  48.5 3.7 %copy-start.6 = (bf16[40,1920]{1,0:T(8,128)(2,1)S(1)}, bf16[40,1920]{1,0:T(8,128)(2,1)}, u32[]{:S(2)}) copy-start(bf16[40,1920]{1,0:T(8,128)(2,1)} %copy-done.5) | copy-start | bytes 460804
  48.5 17.3 %all-to-all-start.1 = ((f32[8,40,512]{2,1,0:T(8,128)}), f32[8,40,512]{2,1,0:T(8,128)S(1)}, u32[]{:S(2)}, u32[]{:S(2)}) async-start(f32[8,40,512]{2,1,0:T(8,128)} %bitcast.11), calls=%async_computation.1 | async-start | bytes 1310720 | tf_op jit(solution)/shard_map/all_to_all | solution.py:271
  52.3 47.2 %copy-start.4 = (bf16[32,1280]{1,0:T(8,128)(2,1)S(1)}, bf16[32,1280]{1,0:T(8,128)(2,1)}, u32[]{:S(2)}) copy-start(bf16[32,1280]{1,0:T(8,128)(2,1)} %copy-done.3) | copy-start | bytes 245764
  52.3 7.7 %collective-permute-start.5 = (bf16[2,40,1920]{2,1,0:T(8,128)(2,1)S(1)}, bf16[2,40,1920]{2,1,0:T(8,128)(2,1)S(1)}, u32[]{:S(2)}, u32[]{:S(2)}) collective-permute-start(bf16[2,40,1920]{2,1,0:T(8,128)(2,1)S(1)} %pad_maximum_fusion.1), channel_id=1, source_target_pairs={{0,32},{32,0},{64,96},{96,64},{128,160},{160,128},{192,224},{224,1... | collective-permute-start | bytes 921608 | tf_op jit(solution)/shard_map/ppermute | solution.py:266
  60.1 23.1 %collective-permute-start.6 = (bf16[4,40,1920]{2,1,0:T(8,128)(2,1)S(1)}, bf16[4,40,1920]{2,1,0:T(8,128)(2,1)S(1)}, u32[]{:S(2)}, u32[]{:S(2)}) collective-permute-start(bf16[4,40,1920]{2,1,0:T(8,128)(2,1)S(1)} %pad_maximum_fusion.refs_0_), channel_id=1, source_target_pairs={{0,8},{8,0},{16,408},{24,400},{384,392},{392,384},{400,24},{408,16... | collective-permute-start | bytes 1843208 | tf_op jit(solution)/shard_map/ppermute | solution.py:269
  66.5 26.7 %all-to-all-start.2 = ((f32[12,8,256]{2,1,0:T(8,128)}), f32[12,8,256]{2,1,0:T(8,128)S(1)}, u32[]{:S(2)}, u32[]{:S(2)}) async-start(f32[12,8,256]{2,1,0:T(8,128)} %bitcast.16), calls=%async_computation.2 | async-start | bytes 196608 | tf_op jit(solution)/shard_map/all_to_all | solution.py:279
  83.2 16.3 %collective-permute-start.7 = (bf16[4,40,1920]{2,1,0:T(8,128)(2,1)S(1)}, bf16[4,40,1920]{2,1,0:T(8,128)(2,1)S(1)}, u32[]{:S(2)}, u32[]{:S(2)}) collective-permute-start(bf16[4,40,1920]{2,1,0:T(8,128)(2,1)S(1)} %pad_maximum_fusion.refs_0_), channel_id=1, source_target_pairs={{0,16},{16,0},{1,17},{17,1},{2,18},{18,2},{3,19},{19,3},{4,20},{20... | collective-permute-start | bytes 1843208 | tf_op jit(solution)/shard_map/ppermute | solution.py:278
  85.8 13.7 %collective-permute-start.8 = (bf16[4,40,1920]{2,1,0:T(8,128)(2,1)S(1)}, bf16[4,40,1920]{2,1,0:T(8,128)(2,1)S(1)}, u32[]{:S(2)}, u32[]{:S(2)}) collective-permute-start(bf16[4,40,1920]{2,1,0:T(8,128)(2,1)S(1)} %collective-permute-done.6.refs_1_), channel_id=1, source_target_pairs={{0,16},{16,0},{1,17},{17,1},{2,18},{18,2},{3,19},{19,3},{4,20},{20... | collective-permute-start | bytes 1843208 | tf_op jit(solution)/shard_map/ppermute | solution.py:282
  94.0 18.4 %all-to-all-start.3 = ((f32[24,8,256]{2,1,0:T(8,128)}), f32[24,8,256]{2,1,0:T(8,128)}, u32[]{:S(2)}, u32[]{:S(2)}) async-start(f32[24,8,256]{2,1,0:T(8,128)} %broadcast_in_dim.2), calls=%async_computation.3 | async-start | bytes 393216 | tf_op jit(solution)/shard_map/all_to_all | solution.py:284
  99.5 1.0 copy-start.2
  (1 other events, 0.6 us)

commit v11 on v10

--- a/solution.py
+++ b/solution.py
@@ -13,11 +13,12 @@
 
 
 def border_flags(clip_lengths, cycle_start, frame_index, total):
-    starts = jnp.cumsum(clip_lengths) - clip_lengths
+    clip = jnp.arange(clip_lengths.shape[0], dtype=jnp.int32)
+    starts = jnp.sum(jnp.where(clip[None, :] < clip[:, None], clip_lengths[None, :], 0), axis=1)
     position = jnp.mod(frame_index - cycle_start[0], total)
     following = jnp.mod(frame_index + 1 - cycle_start[0], total)
-    first_here = jnp.any(position[:, None] == starts[None, :], axis=1)
-    first_next = jnp.any(following[:, None] == starts[None, :], axis=1)
+    first_here = jnp.any(starts[:, None] == position[None, :], axis=0)
+    first_next = jnp.any(starts[:, None] == following[None, :], axis=0)
     return (1 - first_here.astype(jnp.int32), 1 - first_next.astype(jnp.int32))
 
 

time: 120 us -> 118 us (0.983)
  waiting for transfers between devices: 20.9 us -> 24.8 us
  other arithmetic: 4.66 us -> 0.76 us
  local copies, waits for them, and re-layouts: 5.66 us -> 3.63 us
    ppermute x1, waiting for transfers between devices: 0.01 us -> 3.67 us  [shards(): halo_x = lax.ppermute(edge, ('z', 'c'), z_next)]
    another operation x2 -> x0, other arithmetic: 2.77 us -> none
    unnamed x24 -> x10, local copies, waits for them, and re-layouts: 2.32 us -> 0.99 us
  transfers between devices with their start and end apart: 13 -> 13, of which waited for: 4 -> 5; matrix products, arithmetic and copies ran while one was open for 6% -> 2% of each run, Pallas kernels for 3% -> 3%
where the time goes in v11:
time: 118 us; the launch traced here: 117 us
  starting transfers between devices  61.2 us (52%)
  waiting for transfers between devices  24.8 us (21%)
  blocking collectives  16.3 us (14%)
  Pallas kernels  9.05 us (8%)
  local copies, waits for them, and re-layouts  3.63 us (3%)
  between operations  1.67 us (1%)
    all_to_all x1, starting transfers between devices, shards(): mine = lax.all_to_all(pieces, 'z', 0, 0, tiled=True)  17.8 us
    all_gather x1, blocking collectives, shards(): edges = lax.all_gather(jnp.where(core == 0, ends[1], ends[0]), 'c')  10.2 us
    ppermute x2, starting transfers between devices, from_y(): return lax.ppermute(temporal_weight, ('z', 'c', 'y'), pairs)  9.76 us
    all_to_all x1, waiting for transfers between devices, shards(): gathered = lax.all_to_all(mine, ('xh', 'z'), 0, 0, tiled=True)  8.31 us
    all_gather x1, blocking collectives, shards(): gathered = lax.all_gather(gathered, 'c')  6.05 us
    ppermute x1, waiting for transfers between devices, shards(): pair_far = lax.ppermute(pair, 'z', [(i, i ^ 1) for i in range(n_z)])  5.67 us
    ppermute x1, starting transfers between devices, shards(): halo = lax.ppermute(jnp.where(core == 0, ends[0], ends[1]), DP, across)  5.63 us
    all_to_all x1, waiting for transfers between devices, shards(): mine = lax.all_to_all(pieces, 'z', 0, 0, tiled=True)  5.52 us
  transfers between devices with their start and end apart: 13, of which 5 were waited for; matrix products, arithmetic and copies ran while one was open for 2% of the time, Pallas kernels for 3%

profile of v11, /device:TPU:1, one launch (start us, length us, event | category | flops | bytes accessed | tf_op | source)
XLA Modules:
  0.0 117.3 jit_solution(1025185302369759100)
XLA Ops:
  0.6 2.2 %pack.1 = bf16[4,256,640]{2,1,0:T(8,128)(2,1)} custom-call(bf16[8,32,640]{2,1,0:T(8,128)(2,1)} %f_ref.1, bf16[8,32,640]{2,1,0:T(8,128)(2,1)} %g_ref.1), custom_call_target="tpu_custom_call" | custom-call | tf_op jit(solution)/shard_map/pack/pallas_call | solution.py:66
  2.9 5.0 %all-to-all-start = ((bf16[4,256,640]{2,1,0:T(8,128)(2,1)}), bf16[4,256,640]{2,1,0:T(8,128)(2,1)S(1)}, u32[]{:S(2)}, u32[]{:S(2)}) async-start(bf16[4,256,640]{2,1,0:T(8,128)(2,1)} %pack.1), calls=%async_computation | async-start | bytes 2621440 | tf_op jit(solution)/shard_map/all_to_all | solution.py:245
  7.9 5.2 %collective-permute-start.1 = (bf16[40,1920]{1,0:T(8,128)(2,1)S(1)}, bf16[40,1920]{1,0:T(8,128)(2,1)S(1)}, u32[]{:S(2)}, u32[]{:S(2)}) collective-permute-start(bf16[40,1920]{1,0:T(8,128)(2,1)S(1)} %copy-done.3), channel_id=1, source_target_pairs={{0,1},{1,2},{2,3},{3,4},{4,5},{5,6},{6,7},{7,0},{16,23},{17,16},{1... | collective-permute-start | bytes 460808 | tf_op jit(solution)/shard_map/ppermute | solution.py:240
  13.1 4.5 %collective-permute-start = (bf16[40,1920]{1,0:T(8,128)(2,1)S(1)}, bf16[40,1920]{1,0:T(8,128)(2,1)S(1)}, u32[]{:S(2)}, u32[]{:S(2)}) collective-permute-start(bf16[40,1920]{1,0:T(8,128)(2,1)S(1)} %copy-done.3), channel_id=1, source_target_pairs={{0,3},{1,4},{2,5},{3,6},{4,7},{5,0},{6,1},{7,2},{16,21},{17,22},{1... | collective-permute-start | bytes 460808 | tf_op jit(solution)/shard_map/ppermute | solution.py:240
  17.8 5.6 %collective-permute-start.2 = (bf16[32,1280]{1,0:T(8,128)(2,1)S(1)}, bf16[32,1280]{1,0:T(8,128)(2,1)S(1)}, u32[]{:S(2)}, u32[]{:S(2)}) collective-permute-start(bf16[32,1280]{1,0:T(8,128)(2,1)S(1)} %maximum_select_fusion), channel_id=1, source_target_pairs={{0,752},{16,32},{32,16},{48,64},{64,48},{80,96},{96,80},{112,128},... | collective-permute-start | bytes 245768 | tf_op jit(solution)/shard_map/ppermute | solution.py:249
  24.4 10.2 %all_gather.10.edge_ref = bf16[2,32,1280]{2,1,0:T(8,128)(2,1)S(1)} all-gather(bf16[1,32,1280]{2,1,0:T(8,128)(2,1)S(1)} %maximum_select_fusion.1), channel_id=1, replica_groups=mesh['xh'=2,'z'=12,'c'=2,'xl'=2,'y'=8] {'c'}, dimensions={0}, use_global_device_ids=true | all-gather | bytes 245760 | tf_op jit(solution)/shard_map/all_gather | solution.py:247
  34.7 2.3 %collective-permute-start.3 = (bf16[4,8,32,640]{3,2,1,0:T(8,128)(2,1)S(1)}, bf16[4,8,32,640]{3,2,1,0:T(8,128)(2,1)S(1)}, u32[]{:S(2)}, u32[]{:S(2)}) collective-permute-start(bf16[4,8,32,640]{3,2,1,0:T(8,128)(2,1)S(1)} %bitcast.60), channel_id=1, source_target_pairs={{0,16},{16,0},{1,17},{17,1},{2,18},{18,2},{3,19},{19,3},{4,20},{20... | collective-permute-start | bytes 3932168 | tf_op jit(solution)/shard_map/ppermute | solution.py:251
  37.0 1.9 %collective-permute-start.4 = (bf16[4,32,384]{2,1,0:T(8,128)(2,1)S(1)}, bf16[4,32,384]{2,1,0:T(8,128)(2,1)S(1)}, u32[]{:S(2)}, u32[]{:S(2)}) collective-permute-start(bf16[4,32,384]{2,1,0:T(8,128)(2,1)S(1)} %fusion), channel_id=1, source_target_pairs={{0,368},{32,16},{64,48},{96,80},{128,112},{160,144},{192,176},{224... | collective-permute-start | bytes 294920 | tf_op jit(solution)/shard_map/ppermute | solution.py:254
  39.3 3.7 %collective-permute-done.4.halo_ref = bf16[4,32,384]{2,1,0:T(8,128)(2,1)S(1)} collective-permute-done((bf16[4,32,384]{2,1,0:T(8,128)(2,1)S(1)}, bf16[4,32,384]{2,1,0:T(8,128)(2,1)S(1)}, u32[]{:S(2)}, u32[]{:S(2)}) %collective-permute-start.4) | collective-permute-done | bytes 98336 | tf_op jit(solution)/shard_map/ppermute | solution.py:254
  43.0 3.3 %x_term.1 = f32[320,512]{1,0:T(8,128)} custom-call(s32[3]{0:T(128)S(1)} %pad_add_fusion.place_ref, s32[32]{0:T(128)S(1)} %convert_subtract_fusion.1.prev_ref, s32[32]{0:T(128)S(1)} %convert_subtract_fusion.next_ref, bf16[4,8,32,640]{3,2,1,0:T(8,128)(2,1)S(1)} %bitcast.62, bf16[4,8,32,640]{3,2,1,0:T(8,128)(2,1)S(1)} %collective-permute-done.3.sib_ref, ...), custom_call_target="tpu_custom_call" | custom-call | tf_op jit(solution)/shard_map/x_term/pallas_call | solution.py:152
  46.3 3.5 %all-to-all-start.1 = ((f32[8,40,512]{2,1,0:T(8,128)}), f32[8,40,512]{2,1,0:T(8,128)S(1)}, u32[]{:S(2)}, u32[]{:S(2)}) async-start(f32[8,40,512]{2,1,0:T(8,128)} %bitcast.10), calls=%async_computation.1 | async-start | bytes 1310720 | tf_op jit(solution)/shard_map/all_to_all | solution.py:272
  49.9 1.9 %collective-permute-start.5 = (bf16[2,40,1920]{2,1,0:T(8,128)(2,1)S(1)}, bf16[2,40,1920]{2,1,0:T(8,128)(2,1)S(1)}, u32[]{:S(2)}, u32[]{:S(2)}) collective-permute-start(bf16[2,40,1920]{2,1,0:T(8,128)(2,1)S(1)} %pad_maximum_fusion.1), channel_id=1, source_target_pairs={{0,32},{32,0},{64,96},{96,64},{128,160},{160,128},{192,224},{224,1... | collective-permute-start | bytes 921608 | tf_op jit(solution)/shard_map/ppermute | solution.py:267
  51.8 5.7 %collective-permute-done.5 = bf16[2,40,1920]{2,1,0:T(8,128)(2,1)S(1)} collective-permute-done((bf16[2,40,1920]{2,1,0:T(8,128)(2,1)S(1)}, bf16[2,40,1920]{2,1,0:T(8,128)(2,1)S(1)}, u32[]{:S(2)}, u32[]{:S(2)}) %collective-permute-start.5) | collective-permute-done | bytes 307232 | tf_op jit(solution)/shard_map/ppermute | solution.py:267
  57.6 4.3 %collective-permute-start.6 = (bf16[4,40,1920]{2,1,0:T(8,128)(2,1)S(1)}, bf16[4,40,1920]{2,1,0:T(8,128)(2,1)S(1)}, u32[]{:S(2)}, u32[]{:S(2)}) collective-permute-start(bf16[4,40,1920]{2,1,0:T(8,128)(2,1)S(1)} %pad_maximum_fusion.refs_0_), channel_id=1, source_target_pairs={{0,8},{8,0},{16,408},{24,400},{384,392},{392,384},{400,24},{408,16... | collective-permute-start | bytes 1843208 | tf_op jit(solution)/shard_map/ppermute | solution.py:270
  61.9 1.6 %all-to-all-done.1 = f32[8,40,512]{2,1,0:T(8,128)S(1)} async-done(((f32[8,40,512]{2,1,0:T(8,128)}), f32[8,40,512]{2,1,0:T(8,128)S(1)}, u32[]{:S(2)}, u32[]{:S(2)}) %all-to-all-start.1) | async-done | bytes 655392 | tf_op jit(solution)/shard_map/all_to_all | solution.py:272
  64.2 17.8 %all-to-all-start.2 = ((f32[12,8,256]{2,1,0:T(8,128)}), f32[12,8,256]{2,1,0:T(8,128)S(1)}, u32[]{:S(2)}, u32[]{:S(2)}) async-start(f32[12,8,256]{2,1,0:T(8,128)} %bitcast.15), calls=%async_computation.2 | async-start | bytes 196608 | tf_op jit(solution)/shard_map/all_to_all | solution.py:280
  82.0 2.6 %collective-permute-start.7 = (bf16[4,40,1920]{2,1,0:T(8,128)(2,1)S(1)}, bf16[4,40,1920]{2,1,0:T(8,128)(2,1)S(1)}, u32[]{:S(2)}, u32[]{:S(2)}) collective-permute-start(bf16[4,40,1920]{2,1,0:T(8,128)(2,1)S(1)} %pad_maximum_fusion.refs_0_), channel_id=1, source_target_pairs={{0,16},{16,0},{1,17},{17,1},{2,18},{18,2},{3,19},{19,3},{4,20},{20... | collective-permute-start | bytes 1843208 | tf_op jit(solution)/shard_map/ppermute | solution.py:279
  84.6 1.9 %collective-permute-start.8 = (bf16[4,40,1920]{2,1,0:T(8,128)(2,1)S(1)}, bf16[4,40,1920]{2,1,0:T(8,128)(2,1)S(1)}, u32[]{:S(2)}, u32[]{:S(2)}) collective-permute-start(bf16[4,40,1920]{2,1,0:T(8,128)(2,1)S(1)} %collective-permute-done.6.refs_1_), channel_id=1, source_target_pairs={{0,16},{16,0},{1,17},{17,1},{2,18},{18,2},{3,19},{19,3},{4,20},{20... | collective-permute-start | bytes 1843208 | tf_op jit(solution)/shard_map/ppermute | solution.py:283
  86.5 5.5 %all-to-all-done.2 = f32[12,8,256]{2,1,0:T(8,128)S(1)} async-done(((f32[12,8,256]{2,1,0:T(8,128)}), f32[12,8,256]{2,1,0:T(8,128)S(1)}, u32[]{:S(2)}, u32[]{:S(2)}) %all-to-all-start.2) | async-done | bytes 98336 | tf_op jit(solution)/shard_map/all_to_all | solution.py:280
  92.8 4.5 %all-to-all-start.3 = ((f32[24,8,256]{2,1,0:T(8,128)}), f32[24,8,256]{2,1,0:T(8,128)}, u32[]{:S(2)}, u32[]{:S(2)}) async-start(f32[24,8,256]{2,1,0:T(8,128)} %broadcast_in_dim.16), calls=%async_computation.3 | async-start | bytes 393216 | tf_op jit(solution)/shard_map/all_to_all | solution.py:285
  97.4 1.0 copy-done.2
  98.4 3.5 %outputs.1 = (bf16[8,32,640]{2,1,0:T(8,128)(2,1)}, bf16[8,32,640]{2,1,0:T(8,128)(2,1)}) custom-call(s32[5]{0:T(128)S(1)} %stack.49.place_ref, s32[32]{0:T(128)S(1)} %convert_subtract_fusion.1.prev_ref, s32[32]{0:T(128)S(1)} %convert_subtract_fusion.next_ref, bf16[8,32,640]{2,1,0:T(8,128)(2,1)S(1)} %copy-done, bf16[8,32,640]{2,1,0:T(8,128)(2,1)S(1)} %copy-done.1, ...), custom_call_target="tpu_custom_call" | custom-call | tf_op jit(solution)/shard_map/outputs/pallas_call | solution.py:212
  101.9 8.3 %all-to-all-done.3 = f32[24,8,256]{2,1,0:T(8,128)} async-done(((f32[24,8,256]{2,1,0:T(8,128)}), f32[24,8,256]{2,1,0:T(8,128)}, u32[]{:S(2)}, u32[]{:S(2)}) %all-to-all-start.3) | async-done | bytes 196640 | tf_op jit(solution)/shard_map/all_to_all | solution.py:285
  110.2 6.1 %all-gather = f32[48,8,256]{2,1,0:T(8,128)S(1)} all-gather(f32[24,8,256]{2,1,0:T(8,128)} %all-to-all-done.3), channel_id=2, replica_groups=mesh['xh'=2,'z'=12,'c'=2,'xl'=2,'y'=8] {'c'}, dimensions={0}, use_global_device_ids=true | all-gather | bytes 589824 | tf_op jit(solution)/shard_map/all_gather | solution.py:291
  (52 shorter events, 3.4 us)
Async XLA Ops:
  2.9 5.0 %copy-start.3 = (bf16[40,1920]{1,0:T(8,128)(2,1)S(1)}, bf16[40,1920]{1,0:T(8,128)(2,1)}, u32[]{:S(2)}) copy-start(bf16[40,1920]{1,0:T(8,128)(2,1)} %param.9) | copy-start | bytes 460804
  2.9 14.8 %copy-start = (bf16[8,32,640]{2,1,0:T(8,128)(2,1)S(1)}, bf16[8,32,640]{2,1,0:T(8,128)(2,1)}, u32[]{:S(2)}) copy-start(bf16[8,32,640]{2,1,0:T(8,128)(2,1)} %f_ref.1) | copy-start | bytes 983044
  2.9 14.8 %copy-start.1 = (bf16[8,32,640]{2,1,0:T(8,128)(2,1)S(1)}, bf16[8,32,640]{2,1,0:T(8,128)(2,1)}, u32[]{:S(2)}) copy-start(bf16[8,32,640]{2,1,0:T(8,128)(2,1)} %g_ref.1) | copy-start | bytes 983044
  2.9 31.8 %all-to-all-start = ((bf16[4,256,640]{2,1,0:T(8,128)(2,1)}), bf16[4,256,640]{2,1,0:T(8,128)(2,1)S(1)}, u32[]{:S(2)}, u32[]{:S(2)}) async-start(bf16[4,256,640]{2,1,0:T(8,128)(2,1)} %pack.1), calls=%async_computation | async-start | bytes 2621440 | tf_op jit(solution)/shard_map/all_to_all | solution.py:245
  7.9 31.1 %copy-start.4 = (s32[48]{0:T(128)S(1)}, s32[48]{0:T(128)}, u32[]{:S(2)}) copy-start(s32[48]{0:T(128)} %param.10) | copy-start | bytes 580
  7.9 26.8 %collective-permute-start.1 = (bf16[40,1920]{1,0:T(8,128)(2,1)S(1)}, bf16[40,1920]{1,0:T(8,128)(2,1)S(1)}, u32[]{:S(2)}, u32[]{:S(2)}) collective-permute-start(bf16[40,1920]{1,0:T(8,128)(2,1)S(1)} %copy-done.3), channel_id=1, source_target_pairs={{0,1},{1,2},{2,3},{3,4},{4,5},{5,6},{6,7},{7,0},{16,23},{17,16},{1... | collective-permute-start | bytes 460808 | tf_op jit(solution)/shard_map/ppermute | solution.py:240
  13.1 21.6 %collective-permute-start = (bf16[40,1920]{1,0:T(8,128)(2,1)S(1)}, bf16[40,1920]{1,0:T(8,128)(2,1)S(1)}, u32[]{:S(2)}, u32[]{:S(2)}) collective-permute-start(bf16[40,1920]{1,0:T(8,128)(2,1)S(1)} %copy-done.3), channel_id=1, source_target_pairs={{0,3},{1,4},{2,5},{3,6},{4,7},{5,0},{6,1},{7,2},{16,21},{17,22},{1... | collective-permute-start | bytes 460808 | tf_op jit(solution)/shard_map/ppermute | solution.py:240
  17.8 16.9 %collective-permute-start.2 = (bf16[32,1280]{1,0:T(8,128)(2,1)S(1)}, bf16[32,1280]{1,0:T(8,128)(2,1)S(1)}, u32[]{:S(2)}, u32[]{:S(2)}) collective-permute-start(bf16[32,1280]{1,0:T(8,128)(2,1)S(1)} %maximum_select_fusion), channel_id=1, source_target_pairs={{0,752},{16,32},{32,16},{48,64},{64,48},{80,96},{96,80},{112,128},... | collective-permute-start | bytes 245768 | tf_op jit(solution)/shard_map/ppermute | solution.py:249
  34.7 8.3 %collective-permute-start.3 = (bf16[4,8,32,640]{3,2,1,0:T(8,128)(2,1)S(1)}, bf16[4,8,32,640]{3,2,1,0:T(8,128)(2,1)S(1)}, u32[]{:S(2)}, u32[]{:S(2)}) collective-permute-start(bf16[4,8,32,640]{3,2,1,0:T(8,128)(2,1)S(1)} %bitcast.60), channel_id=1, source_target_pairs={{0,16},{16,0},{1,17},{17,1},{2,18},{18,2},{3,19},{19,3},{4,20},{20... | collective-permute-start | bytes 3932168 | tf_op jit(solution)/shard_map/ppermute | solution.py:251
  37.0 5.9 %collective-permute-start.4 = (bf16[4,32,384]{2,1,0:T(8,128)(2,1)S(1)}, bf16[4,32,384]{2,1,0:T(8,128)(2,1)S(1)}, u32[]{:S(2)}, u32[]{:S(2)}) collective-permute-start(bf16[4,32,384]{2,1,0:T(8,128)(2,1)S(1)} %fusion), channel_id=1, source_target_pairs={{0,368},{32,16},{64,48},{96,80},{128,112},{160,144},{192,176},{224... | collective-permute-start | bytes 294920 | tf_op jit(solution)/shard_map/ppermute | solution.py:254
  46.3 17.2 %all-to-all-start.1 = ((f32[8,40,512]{2,1,0:T(8,128)}), f32[8,40,512]{2,1,0:T(8,128)S(1)}, u32[]{:S(2)}, u32[]{:S(2)}) async-start(f32[8,40,512]{2,1,0:T(8,128)} %bitcast.10), calls=%async_computation.1 | async-start | bytes 1310720 | tf_op jit(solution)/shard_map/all_to_all | solution.py:272
  49.9 7.6 %collective-permute-start.5 = (bf16[2,40,1920]{2,1,0:T(8,128)(2,1)S(1)}, bf16[2,40,1920]{2,1,0:T(8,128)(2,1)S(1)}, u32[]{:S(2)}, u32[]{:S(2)}) collective-permute-start(bf16[2,40,1920]{2,1,0:T(8,128)(2,1)S(1)} %pad_maximum_fusion.1), channel_id=1, source_target_pairs={{0,32},{32,0},{64,96},{96,64},{128,160},{160,128},{192,224},{224,1... | collective-permute-start | bytes 921608 | tf_op jit(solution)/shard_map/ppermute | solution.py:267
  57.6 24.4 %collective-permute-start.6 = (bf16[4,40,1920]{2,1,0:T(8,128)(2,1)S(1)}, bf16[4,40,1920]{2,1,0:T(8,128)(2,1)S(1)}, u32[]{:S(2)}, u32[]{:S(2)}) collective-permute-start(bf16[4,40,1920]{2,1,0:T(8,128)(2,1)S(1)} %pad_maximum_fusion.refs_0_), channel_id=1, source_target_pairs={{0,8},{8,0},{16,408},{24,400},{384,392},{392,384},{400,24},{408,16... | collective-permute-start | bytes 1843208 | tf_op jit(solution)/shard_map/ppermute | solution.py:270
  64.2 27.9 %all-to-all-start.2 = ((f32[12,8,256]{2,1,0:T(8,128)}), f32[12,8,256]{2,1,0:T(8,128)S(1)}, u32[]{:S(2)}, u32[]{:S(2)}) async-start(f32[12,8,256]{2,1,0:T(8,128)} %bitcast.15), calls=%async_computation.2 | async-start | bytes 196608 | tf_op jit(solution)/shard_map/all_to_all | solution.py:280
  82.0 15.4 %collective-permute-start.7 = (bf16[4,40,1920]{2,1,0:T(8,128)(2,1)S(1)}, bf16[4,40,1920]{2,1,0:T(8,128)(2,1)S(1)}, u32[]{:S(2)}, u32[]{:S(2)}) collective-permute-start(bf16[4,40,1920]{2,1,0:T(8,128)(2,1)S(1)} %pad_maximum_fusion.refs_0_), channel_id=1, source_target_pairs={{0,16},{16,0},{1,17},{17,1},{2,18},{18,2},{3,19},{19,3},{4,20},{20... | collective-permute-start | bytes 1843208 | tf_op jit(solution)/shard_map/ppermute | solution.py:279
  84.6 12.8 %collective-permute-start.8 = (bf16[4,40,1920]{2,1,0:T(8,128)(2,1)S(1)}, bf16[4,40,1920]{2,1,0:T(8,128)(2,1)S(1)}, u32[]{:S(2)}, u32[]{:S(2)}) collective-permute-start(bf16[4,40,1920]{2,1,0:T(8,128)(2,1)S(1)} %collective-permute-done.6.refs_1_), channel_id=1, source_target_pairs={{0,16},{16,0},{1,17},{17,1},{2,18},{18,2},{3,19},{19,3},{4,20},{20... | collective-permute-start | bytes 1843208 | tf_op jit(solution)/shard_map/ppermute | solution.py:283
  92.8 17.4 %all-to-all-start.3 = ((f32[24,8,256]{2,1,0:T(8,128)}), f32[24,8,256]{2,1,0:T(8,128)}, u32[]{:S(2)}, u32[]{:S(2)}) async-start(f32[24,8,256]{2,1,0:T(8,128)} %broadcast_in_dim.16), calls=%async_computation.3 | async-start | bytes 393216 | tf_op jit(solution)/shard_map/all_to_all | solution.py:285
  97.4 1.0 copy-start.2

commit v12 on v11

--- a/solution.py
+++ b/solution.py
@@ -77,46 +77,90 @@
     )(features, cotangent)
 
 
-def term_kernel(place_ref, prev_ref, next_ref, own_ref, sib_ref, halo_ref, out_ref, fa_own, fa_sib):
+def put(dst, slot, value, ok):
+    rows = value.shape[0]
+    dst[pl.ds(slot * rows, rows), :] = jnp.where(ok != 0, value, jnp.zeros_like(value))
+
+
+def lanes(ref, start, stop):
+    return ref[:, :, :, start:stop].reshape(-1, stop - start)
+
+
+def term_dot(a, b):
+    return lax.dot_general(a, b, (((0,), (0,)), ((), ())), preferred_element_type=jnp.float32)
+
+
+def own_kernel(place_ref, prev_ref, next_ref, own_ref, outer_ref, mid_ref, fa):
     chips, frames, strip, _ = own_ref.shape
-    core, xl, wrapped = place_ref[0], place_ref[1], place_ref[2]
-
-    def put(dst, chip, slot, value, ok):
-        dst[pl.ds((chip * frames + slot) * strip, strip), :] = jnp.where(ok != 0, value, jnp.zeros_like(value))
-
-    def halo(chip):
-        return halo_ref[(chip // 2 + wrapped) % 2 * 2 + chip % 2]
+    core = place_ref[0]
+    nothing = jnp.zeros((strip, 384), jnp.bfloat16)
 
     @pl.when(core == 0)
     def _():
         for chip in range(chips):
             at = chip // 2 * 2 * frames
             for j in range(frames):
-                mine = halo(chip) if j == 0 else own_ref[chip, j - 1, :, :384]
-                its = own_ref[chip, frames - 1, :, :384] if j == 0 else sib_ref[chip, j - 1, :, :384]
-                put(fa_own, chip, j, mine, prev_ref[at + j])
-                put(fa_sib, chip, j, its, prev_ref[at + frames + j])
+                put(fa, chip * frames + j, nothing if j == 0 else own_ref[chip, j - 1, :, :384], prev_ref[at + j])
+        mid_ref[...] = term_dot(lanes(own_ref, 0, 384), lanes(own_ref, 256, 512))
 
     @pl.when(core != 0)
+    def _():
+        for chip in range(chips):
+            at = chip // 2 * 2 * frames + frames
+            for j in range(frames):
+                put(fa, chip * frames + j, nothing if j == frames - 1 else own_ref[chip, j + 1, :, :384], next_ref[at + j])
+        mid_ref[:, :128] = term_dot(lanes(own_ref, 0, 384), lanes(own_ref, 512, 640))
+        mid_ref[:, 128:] = jnp.zeros((384, 128), jnp.float32)
+
+    outer_ref[...] = term_dot(fa[...], lanes(own_ref, 256, 640))
+
+
+def own_term(place, prev_ok, next_ok, own):
+    smem = pl.BlockSpec(memory_space=pltpu.SMEM)
+    vmem = pl.BlockSpec(memory_space=pltpu.VMEM)
+    chips, frames, strip, _ = own.shape
+    return pl.pallas_call(
+        own_kernel,
+        out_shape=(jax.ShapeDtypeStruct((384, 384), jnp.float32), jax.ShapeDtypeStruct((384, 256), jnp.float32)),
+        in_specs=[smem] * 3 + [vmem],
+        out_specs=(vmem, vmem),
+        scratch_shapes=[pltpu.VMEM((chips * frames * strip, 384), jnp.bfloat16)],
+        compiler_params=pltpu.CompilerParams(vmem_limit_bytes=20 << 20),
+        name="own_term",
+    )(place, prev_ok, next_ok, own)
+
+
+def term_kernel(place_ref, prev_ref, next_ref, own_ref, sib_ref, halo_ref, outer_ref, mid_ref, out_ref, fa, fh, gh):
+    chips, frames, strip, _ = own_ref.shape
+    core, xl, wrapped = place_ref[0], place_ref[1], place_ref[2]
+
+    def halo(chip):
+        return halo_ref[(chip // 2 + wrapped) % 2 * 2 + chip % 2]
+
+    @pl.when(core == 0)
     def _():
         for chip in range(chips):
             at = chip // 2 * 2 * frames
+            put(fh, chip, halo(chip), prev_ref[at])
+            gh[pl.ds(chip * strip, strip), :] = own_ref[chip, 0, :, 256:]
             for j in range(frames):
-                mine = halo(chip) if j == frames - 1 else own_ref[chip, j + 1, :, :384]
+                its = own_ref[chip, frames - 1, :, :384] if j == 0 else sib_ref[chip, j - 1, :, :384]
+                put(fa, chip * frames + j, its, prev_ref[at + frames + j])
+
+    @pl.when(core != 0)
+    def _():
+        for chip in range(chips):
+            at = chip // 2 * 2 * frames
+            put(fh, chip, halo(chip), next_ref[at + 2 * frames - 1])
+            gh[pl.ds(chip * strip, strip), :] = own_ref[chip, frames - 1, :, 256:]
+            for j in range(frames):
                 its = own_ref[chip, 0, :, :384] if j == frames - 1 else sib_ref[chip, j + 1, :, :384]
-                put(fa_own, chip, j, mine, next_ref[at + frames + j])
-                put(fa_sib, chip, j, its, next_ref[at + j])
-
-    def flat(ref, start, stop):
-        return ref[:, :, :, start:stop].reshape(chips * frames * strip, stop - start)
-
-    def dot(a, b):
-        return lax.dot_general(a, b, (((0,), (0,)), ((), ())), preferred_element_type=jnp.float32)
+                put(fa, chip * frames + j, its, next_ref[at + j])
 
     def center(start, stop):
-        return dot(flat(own_ref, 0, 384), flat(own_ref, start, stop)) + dot(flat(sib_ref, 0, 384), flat(sib_ref, start, stop))
-
-    outer = dot(fa_own[...], flat(own_ref, 256, 640)) + dot(fa_sib[...], flat(sib_ref, 256, 640))
+        return mid_ref[:, :stop - start] + term_dot(lanes(sib_ref, 0, 384), lanes(sib_ref, start, stop))
+
+    outer = outer_ref[...] + term_dot(fa[...], lanes(sib_ref, 256, 640)) + term_dot(fh[...], gh[...])
     left = lax.broadcasted_iota(jnp.int32, (384, 128), 1) < 64
     rolled = pltpu.roll(outer[:, :128], 64, 1)
 
@@ -144,20 +188,20 @@
         store(384, 512, center(512, 640))
 
 
-def x_term(place, prev_ok, next_ok, own, sib, halo):
+def x_term(place, prev_ok, next_ok, own, sib, halo, outer, mid):
     smem = pl.BlockSpec(memory_space=pltpu.SMEM)
     vmem = pl.BlockSpec(memory_space=pltpu.VMEM)
     chips, frames, strip, _ = own.shape
-    buf = pltpu.VMEM((chips * frames * strip, 384), jnp.bfloat16)
+    few = pltpu.VMEM((chips * strip, 384), jnp.bfloat16)
     return pl.pallas_call(
         term_kernel,
         out_shape=jax.ShapeDtypeStruct((320, 512), jnp.float32),
-        in_specs=[smem] * 3 + [vmem] * 3,
+        in_specs=[smem] * 3 + [vmem] * 5,
         out_specs=vmem,
-        scratch_shapes=[buf, buf],
+        scratch_shapes=[pltpu.VMEM((chips * frames * strip, 384), jnp.bfloat16), few, few],
         compiler_params=pltpu.CompilerParams(vmem_limit_bytes=20 << 20),
         name="x_term",
-    )(place, prev_ok, next_ok, own, sib, halo)
+    )(place, prev_ok, next_ok, own, sib, halo, outer, mid)
 
 
 def out_kernel(place_ref, prev_ref, next_ref, f_ref, g_ref, skip_ref, halo_ref, edge_ref, *refs):
@@ -259,7 +303,8 @@
     prev_all, next_all = border_flags(clip_lengths, cycle_start, chip_frames, total_frames)
     wrapped = jnp.where(core == 0, z == 0, z == n_z - 1)
     place = jnp.stack([core, xl, wrapped.astype(jnp.int32)]).astype(jnp.int32)
-    term = x_term(place, prev_all, next_all, own, sib, halo_x)
+    outer, mid = own_term(place, prev_all, next_all, own)
+    term = x_term(place, prev_all, next_all, own, sib, halo_x, outer, mid)
 
     _, w_far, w_near = lax.optimization_barrier((term, w_far, w_near))
     parity = z % 2

time: 118 us -> 117 us (level)
  waiting for transfers between devices: 24.8 us -> 23.1 us
    ppermute x1, waiting for transfers between devices: 3.67 us -> 2.05 us  [shards(): halo_x = lax.ppermute(edge, ('z', 'c'), z_next)]
    pallas_call x0 -> x1, Pallas kernels: none -> 1.61 us  [own_term(): pl.pallas_call(own_kernel, out_shape=(jax.ShapeDtypeStruct((384, 384), jn...]
  transfers between devices with their start and end apart: 13 -> 13, of which waited for: 5 -> 5; matrix products, arithmetic and copies ran while one was open for 2% -> 2% of each run, Pallas kernels for 3% -> 4%
where the time goes in v12:
time: 117 us
  starting transfers between devices  61.2 us (52%)
  waiting for transfers between devices  23.1 us (20%)
  blocking collectives  16.3 us (14%)
  Pallas kernels  10.1 us (9%)
  local copies, waits for them, and re-layouts  3.63 us (3%)
  between operations  1.68 us (1%)
    all_to_all x1, starting transfers between devices, shards(): mine = lax.all_to_all(pieces, 'z', 0, 0, tiled=True)  17.8 us
    all_gather x1, blocking collectives, shards(): edges = lax.all_gather(jnp.where(core == 0, ends[1], ends[0]), 'c')  10.2 us
    ppermute x2, starting transfers between devices, from_y(): return lax.ppermute(temporal_weight, ('z', 'c', 'y'), pairs)  9.76 us
    all_to_all x1, waiting for transfers between devices, shards(): gathered = lax.all_to_all(mine, ('xh', 'z'), 0, 0, tiled=True)  8.31 us
    all_gather x1, blocking collectives, shards(): gathered = lax.all_gather(gathered, 'c')  6.05 us
    ppermute x1, waiting for transfers between devices, shards(): pair_far = lax.ppermute(pair, 'z', [(i, i ^ 1) for i in range(n_z)])  5.67 us
    ppermute x1, starting transfers between devices, shards(): halo = lax.ppermute(jnp.where(core == 0, ends[0], ends[1]), DP, across)  5.63 us
    all_to_all x1, waiting for transfers between devices, shards(): mine = lax.all_to_all(pieces, 'z', 0, 0, tiled=True)  5.52 us
  transfers between devices with their start and end apart: 13, of which 5 were waited for; matrix products, arithmetic and copies ran while one was open for 2% of the time, Pallas kernels for 4%

profile of v12, /device:TPU:1, one launch (start us, length us, event | category | flops | bytes accessed | tf_op | source)
XLA Modules:
  0.0 116.7 jit_solution(14560508468837432413)
XLA Ops:
  0.6 2.2 %pack.1 = bf16[4,256,640]{2,1,0:T(8,128)(2,1)} custom-call(bf16[8,32,640]{2,1,0:T(8,128)(2,1)} %f_ref.1, bf16[8,32,640]{2,1,0:T(8,128)(2,1)} %g_ref.1), custom_call_target="tpu_custom_call" | custom-call | tf_op jit(solution)/shard_map/pack/pallas_call | solution.py:66
  2.9 5.0 %all-to-all-start = ((bf16[4,256,640]{2,1,0:T(8,128)(2,1)}), bf16[4,256,640]{2,1,0:T(8,128)(2,1)S(1)}, u32[]{:S(2)}, u32[]{:S(2)}) async-start(bf16[4,256,640]{2,1,0:T(8,128)(2,1)} %pack.1), calls=%async_computation | async-start | bytes 2621440 | tf_op jit(solution)/shard_map/all_to_all | solution.py:289
  7.9 5.2 %collective-permute-start.1 = (bf16[40,1920]{1,0:T(8,128)(2,1)S(1)}, bf16[40,1920]{1,0:T(8,128)(2,1)S(1)}, u32[]{:S(2)}, u32[]{:S(2)}) collective-permute-start(bf16[40,1920]{1,0:T(8,128)(2,1)S(1)} %copy-done.3), channel_id=1, source_target_pairs={{0,1},{1,2},{2,3},{3,4},{4,5},{5,6},{6,7},{7,0},{16,23},{17,16},{1... | collective-permute-start | bytes 460808 | tf_op jit(solution)/shard_map/ppermute | solution.py:284
  13.1 4.5 %collective-permute-start = (bf16[40,1920]{1,0:T(8,128)(2,1)S(1)}, bf16[40,1920]{1,0:T(8,128)(2,1)S(1)}, u32[]{:S(2)}, u32[]{:S(2)}) collective-permute-start(bf16[40,1920]{1,0:T(8,128)(2,1)S(1)} %copy-done.3), channel_id=1, source_target_pairs={{0,3},{1,4},{2,5},{3,6},{4,7},{5,0},{6,1},{7,2},{16,21},{17,22},{1... | collective-permute-start | bytes 460808 | tf_op jit(solution)/shard_map/ppermute | solution.py:284
  17.8 5.6 %collective-permute-start.2 = (bf16[32,1280]{1,0:T(8,128)(2,1)S(1)}, bf16[32,1280]{1,0:T(8,128)(2,1)S(1)}, u32[]{:S(2)}, u32[]{:S(2)}) collective-permute-start(bf16[32,1280]{1,0:T(8,128)(2,1)S(1)} %maximum_select_fusion), channel_id=1, source_target_pairs={{0,752},{16,32},{32,16},{48,64},{64,48},{80,96},{96,80},{112,128},... | collective-permute-start | bytes 245768 | tf_op jit(solution)/shard_map/ppermute | solution.py:293
  24.4 10.2 %all_gather.10.edge_ref = bf16[2,32,1280]{2,1,0:T(8,128)(2,1)S(1)} all-gather(bf16[1,32,1280]{2,1,0:T(8,128)(2,1)S(1)} %maximum_select_fusion.1), channel_id=1, replica_groups=mesh['xh'=2,'z'=12,'c'=2,'xl'=2,'y'=8] {'c'}, dimensions={0}, use_global_device_ids=true | all-gather | bytes 245760 | tf_op jit(solution)/shard_map/all_gather | solution.py:291
  34.7 2.3 %collective-permute-start.3 = (bf16[4,8,32,640]{3,2,1,0:T(8,128)(2,1)S(1)}, bf16[4,8,32,640]{3,2,1,0:T(8,128)(2,1)S(1)}, u32[]{:S(2)}, u32[]{:S(2)}) collective-permute-start(bf16[4,8,32,640]{3,2,1,0:T(8,128)(2,1)S(1)} %bitcast.60), channel_id=1, source_target_pairs={{0,16},{16,0},{1,17},{17,1},{2,18},{18,2},{3,19},{19,3},{4,20},{20... | collective-permute-start | bytes 3932168 | tf_op jit(solution)/shard_map/ppermute | solution.py:295
  37.0 1.9 %collective-permute-start.4 = (bf16[4,32,384]{2,1,0:T(8,128)(2,1)S(1)}, bf16[4,32,384]{2,1,0:T(8,128)(2,1)S(1)}, u32[]{:S(2)}, u32[]{:S(2)}) collective-permute-start(bf16[4,32,384]{2,1,0:T(8,128)(2,1)S(1)} %fusion), channel_id=1, source_target_pairs={{0,368},{32,16},{64,48},{96,80},{128,112},{160,144},{192,176},{224... | collective-permute-start | bytes 294920 | tf_op jit(solution)/shard_map/ppermute | solution.py:298
  39.3 1.6 %own_term.1 = (f32[384,384]{1,0:T(8,128)S(1)}, f32[384,256]{1,0:T(8,128)S(1)}) custom-call(s32[3]{0:T(128)S(1)} %pad_add_fusion.place_ref, s32[32]{0:T(128)S(1)} %convert_subtract_fusion.1.prev_ref, s32[32]{0:T(128)S(1)} %convert_subtract_fusion.next_ref, bf16[4,8,32,640]{3,2,1,0:T(8,128)(2,1)S(1)} %bitcast.62), custom_call_target="tpu_custom_call" | custom-call | tf_op jit(solution)/shard_map/own_term/pallas_call | solution.py:122
  40.9 2.1 %collective-permute-done.4.halo_ref = bf16[4,32,384]{2,1,0:T(8,128)(2,1)S(1)} collective-permute-done((bf16[4,32,384]{2,1,0:T(8,128)(2,1)S(1)}, bf16[4,32,384]{2,1,0:T(8,128)(2,1)S(1)}, u32[]{:S(2)}, u32[]{:S(2)}) %collective-permute-start.4) | collective-permute-done | bytes 98336 | tf_op jit(solution)/shard_map/ppermute | solution.py:298
  42.9 2.7 %x_term.1 = f32[320,512]{1,0:T(8,128)} custom-call(s32[3]{0:T(128)S(1)} %pad_add_fusion.place_ref, s32[32]{0:T(128)S(1)} %convert_subtract_fusion.1.prev_ref, s32[32]{0:T(128)S(1)} %convert_subtract_fusion.next_ref, bf16[4,8,32,640]{3,2,1,0:T(8,128)(2,1)S(1)} %bitcast.63, bf16[4,8,32,640]{3,2,1,0:T(8,128)(2,1)S(1)} %collective-permute-done.3.sib_ref, ...), custom_call_target="tpu_custom_call" | custom-call | tf_op jit(solution)/shard_map/x_term/pallas_call | solution.py:196
  45.7 3.5 %all-to-all-start.1 = ((f32[8,40,512]{2,1,0:T(8,128)}), f32[8,40,512]{2,1,0:T(8,128)S(1)}, u32[]{:S(2)}, u32[]{:S(2)}) async-start(f32[8,40,512]{2,1,0:T(8,128)} %bitcast.10), calls=%async_computation.1 | async-start | bytes 1310720 | tf_op jit(solution)/shard_map/all_to_all | solution.py:317
  49.3 1.9 %collective-permute-start.5 = (bf16[2,40,1920]{2,1,0:T(8,128)(2,1)S(1)}, bf16[2,40,1920]{2,1,0:T(8,128)(2,1)S(1)}, u32[]{:S(2)}, u32[]{:S(2)}) collective-permute-start(bf16[2,40,1920]{2,1,0:T(8,128)(2,1)S(1)} %pad_maximum_fusion.1), channel_id=1, source_target_pairs={{0,32},{32,0},{64,96},{96,64},{128,160},{160,128},{192,224},{224,1... | collective-permute-start | bytes 921608 | tf_op jit(solution)/shard_map/ppermute | solution.py:312
  51.2 5.7 %collective-permute-done.5 = bf16[2,40,1920]{2,1,0:T(8,128)(2,1)S(1)} collective-permute-done((bf16[2,40,1920]{2,1,0:T(8,128)(2,1)S(1)}, bf16[2,40,1920]{2,1,0:T(8,128)(2,1)S(1)}, u32[]{:S(2)}, u32[]{:S(2)}) %collective-permute-start.5) | collective-permute-done | bytes 307232 | tf_op jit(solution)/shard_map/ppermute | solution.py:312
  57.0 4.3 %collective-permute-start.6 = (bf16[4,40,1920]{2,1,0:T(8,128)(2,1)S(1)}, bf16[4,40,1920]{2,1,0:T(8,128)(2,1)S(1)}, u32[]{:S(2)}, u32[]{:S(2)}) collective-permute-start(bf16[4,40,1920]{2,1,0:T(8,128)(2,1)S(1)} %pad_maximum_fusion.refs_0_), channel_id=1, source_target_pairs={{0,8},{8,0},{16,408},{24,400},{384,392},{392,384},{400,24},{408,16... | collective-permute-start | bytes 1843208 | tf_op jit(solution)/shard_map/ppermute | solution.py:315
  61.3 1.6 %all-to-all-done.1 = f32[8,40,512]{2,1,0:T(8,128)S(1)} async-done(((f32[8,40,512]{2,1,0:T(8,128)}), f32[8,40,512]{2,1,0:T(8,128)S(1)}, u32[]{:S(2)}, u32[]{:S(2)}) %all-to-all-start.1) | async-done | bytes 655392 | tf_op jit(solution)/shard_map/all_to_all | solution.py:317
  63.5 17.8 %all-to-all-start.2 = ((f32[12,8,256]{2,1,0:T(8,128)}), f32[12,8,256]{2,1,0:T(8,128)S(1)}, u32[]{:S(2)}, u32[]{:S(2)}) async-start(f32[12,8,256]{2,1,0:T(8,128)} %bitcast.15), calls=%async_computation.2 | async-start | bytes 196608 | tf_op jit(solution)/shard_map/all_to_all | solution.py:325
  81.4 2.6 %collective-permute-start.7 = (bf16[4,40,1920]{2,1,0:T(8,128)(2,1)S(1)}, bf16[4,40,1920]{2,1,0:T(8,128)(2,1)S(1)}, u32[]{:S(2)}, u32[]{:S(2)}) collective-permute-start(bf16[4,40,1920]{2,1,0:T(8,128)(2,1)S(1)} %pad_maximum_fusion.refs_0_), channel_id=1, source_target_pairs={{0,16},{16,0},{1,17},{17,1},{2,18},{18,2},{3,19},{19,3},{4,20},{20... | collective-permute-start | bytes 1843208 | tf_op jit(solution)/shard_map/ppermute | solution.py:324
  84.0 1.9 %collective-permute-start.8 = (bf16[4,40,1920]{2,1,0:T(8,128)(2,1)S(1)}, bf16[4,40,1920]{2,1,0:T(8,128)(2,1)S(1)}, u32[]{:S(2)}, u32[]{:S(2)}) collective-permute-start(bf16[4,40,1920]{2,1,0:T(8,128)(2,1)S(1)} %collective-permute-done.6.refs_1_), channel_id=1, source_target_pairs={{0,16},{16,0},{1,17},{17,1},{2,18},{18,2},{3,19},{19,3},{4,20},{20... | collective-permute-start | bytes 1843208 | tf_op jit(solution)/shard_map/ppermute | solution.py:328
  85.9 5.5 %all-to-all-done.2 = f32[12,8,256]{2,1,0:T(8,128)S(1)} async-done(((f32[12,8,256]{2,1,0:T(8,128)}), f32[12,8,256]{2,1,0:T(8,128)S(1)}, u32[]{:S(2)}, u32[]{:S(2)}) %all-to-all-start.2) | async-done | bytes 98336 | tf_op jit(solution)/shard_map/all_to_all | solution.py:325
  92.1 4.5 %all-to-all-start.3 = ((f32[24,8,256]{2,1,0:T(8,128)}), f32[24,8,256]{2,1,0:T(8,128)}, u32[]{:S(2)}, u32[]{:S(2)}) async-start(f32[24,8,256]{2,1,0:T(8,128)} %broadcast_in_dim.16), calls=%async_computation.3 | async-start | bytes 393216 | tf_op jit(solution)/shard_map/all_to_all | solution.py:330
  97.8 3.5 %outputs.1 = (bf16[8,32,640]{2,1,0:T(8,128)(2,1)}, bf16[8,32,640]{2,1,0:T(8,128)(2,1)}) custom-call(s32[5]{0:T(128)S(1)} %stack.49.place_ref, s32[32]{0:T(128)S(1)} %convert_subtract_fusion.1.prev_ref, s32[32]{0:T(128)S(1)} %convert_subtract_fusion.next_ref, bf16[8,32,640]{2,1,0:T(8,128)(2,1)S(1)} %copy-done, bf16[8,32,640]{2,1,0:T(8,128)(2,1)S(1)} %copy-done.1, ...), custom_call_target="tpu_custom_call" | custom-call | tf_op jit(solution)/shard_map/outputs/pallas_call | solution.py:256
  101.3 8.3 %all-to-all-done.3 = f32[24,8,256]{2,1,0:T(8,128)} async-done(((f32[24,8,256]{2,1,0:T(8,128)}), f32[24,8,256]{2,1,0:T(8,128)}, u32[]{:S(2)}, u32[]{:S(2)}) %all-to-all-start.3) | async-done | bytes 196640 | tf_op jit(solution)/shard_map/all_to_all | solution.py:330
  109.6 6.1 %all-gather = f32[48,8,256]{2,1,0:T(8,128)S(1)} all-gather(f32[24,8,256]{2,1,0:T(8,128)} %all-to-all-done.3), channel_id=2, replica_groups=mesh['xh'=2,'z'=12,'c'=2,'xl'=2,'y'=8] {'c'}, dimensions={0}, use_global_device_ids=true | all-gather | bytes 589824 | tf_op jit(solution)/shard_map/all_gather | solution.py:336
  (53 shorter events, 4.4 us)
Async XLA Ops:
  2.8 5.0 %copy-start.3 = (bf16[40,1920]{1,0:T(8,128)(2,1)S(1)}, bf16[40,1920]{1,0:T(8,128)(2,1)}, u32[]{:S(2)}) copy-start(bf16[40,1920]{1,0:T(8,128)(2,1)} %param.9) | copy-start | bytes 460804
  2.9 14.8 %copy-start = (bf16[8,32,640]{2,1,0:T(8,128)(2,1)S(1)}, bf16[8,32,640]{2,1,0:T(8,128)(2,1)}, u32[]{:S(2)}) copy-start(bf16[8,32,640]{2,1,0:T(8,128)(2,1)} %f_ref.1) | copy-start | bytes 983044
  2.9 14.8 %copy-start.1 = (bf16[8,32,640]{2,1,0:T(8,128)(2,1)S(1)}, bf16[8,32,640]{2,1,0:T(8,128)(2,1)}, u32[]{:S(2)}) copy-start(bf16[8,32,640]{2,1,0:T(8,128)(2,1)} %g_ref.1) | copy-start | bytes 983044
  2.9 31.8 %all-to-all-start = ((bf16[4,256,640]{2,1,0:T(8,128)(2,1)}), bf16[4,256,640]{2,1,0:T(8,128)(2,1)S(1)}, u32[]{:S(2)}, u32[]{:S(2)}) async-start(bf16[4,256,640]{2,1,0:T(8,128)(2,1)} %pack.1), calls=%async_computation | async-start | bytes 2621440 | tf_op jit(solution)/shard_map/all_to_all | solution.py:289
  7.9 31.1 %copy-start.4 = (s32[48]{0:T(128)S(1)}, s32[48]{0:T(128)}, u32[]{:S(2)}) copy-start(s32[48]{0:T(128)} %param.10) | copy-start | bytes 580
  7.9 26.8 %collective-permute-start.1 = (bf16[40,1920]{1,0:T(8,128)(2,1)S(1)}, bf16[40,1920]{1,0:T(8,128)(2,1)S(1)}, u32[]{:S(2)}, u32[]{:S(2)}) collective-permute-start(bf16[40,1920]{1,0:T(8,128)(2,1)S(1)} %copy-done.3), channel_id=1, source_target_pairs={{0,1},{1,2},{2,3},{3,4},{4,5},{5,6},{6,7},{7,0},{16,23},{17,16},{1... | collective-permute-start | bytes 460808 | tf_op jit(solution)/shard_map/ppermute | solution.py:284
  13.1 21.6 %collective-permute-start = (bf16[40,1920]{1,0:T(8,128)(2,1)S(1)}, bf16[40,1920]{1,0:T(8,128)(2,1)S(1)}, u32[]{:S(2)}, u32[]{:S(2)}) collective-permute-start(bf16[40,1920]{1,0:T(8,128)(2,1)S(1)} %copy-done.3), channel_id=1, source_target_pairs={{0,3},{1,4},{2,5},{3,6},{4,7},{5,0},{6,1},{7,2},{16,21},{17,22},{1... | collective-permute-start | bytes 460808 | tf_op jit(solution)/shard_map/ppermute | solution.py:284
  17.8 16.9 %collective-permute-start.2 = (bf16[32,1280]{1,0:T(8,128)(2,1)S(1)}, bf16[32,1280]{1,0:T(8,128)(2,1)S(1)}, u32[]{:S(2)}, u32[]{:S(2)}) collective-permute-start(bf16[32,1280]{1,0:T(8,128)(2,1)S(1)} %maximum_select_fusion), channel_id=1, source_target_pairs={{0,752},{16,32},{32,16},{48,64},{64,48},{80,96},{96,80},{112,128},... | collective-permute-start | bytes 245768 | tf_op jit(solution)/shard_map/ppermute | solution.py:293
  34.7 8.3 %collective-permute-start.3 = (bf16[4,8,32,640]{3,2,1,0:T(8,128)(2,1)S(1)}, bf16[4,8,32,640]{3,2,1,0:T(8,128)(2,1)S(1)}, u32[]{:S(2)}, u32[]{:S(2)}) collective-permute-start(bf16[4,8,32,640]{3,2,1,0:T(8,128)(2,1)S(1)} %bitcast.60), channel_id=1, source_target_pairs={{0,16},{16,0},{1,17},{17,1},{2,18},{18,2},{3,19},{19,3},{4,20},{20... | collective-permute-start | bytes 3932168 | tf_op jit(solution)/shard_map/ppermute | solution.py:295
  37.0 5.9 %collective-permute-start.4 = (bf16[4,32,384]{2,1,0:T(8,128)(2,1)S(1)}, bf16[4,32,384]{2,1,0:T(8,128)(2,1)S(1)}, u32[]{:S(2)}, u32[]{:S(2)}) collective-permute-start(bf16[4,32,384]{2,1,0:T(8,128)(2,1)S(1)} %fusion), channel_id=1, source_target_pairs={{0,368},{32,16},{64,48},{96,80},{128,112},{160,144},{192,176},{224... | collective-permute-start | bytes 294920 | tf_op jit(solution)/shard_map/ppermute | solution.py:298
  45.7 17.2 %all-to-all-start.1 = ((f32[8,40,512]{2,1,0:T(8,128)}), f32[8,40,512]{2,1,0:T(8,128)S(1)}, u32[]{:S(2)}, u32[]{:S(2)}) async-start(f32[8,40,512]{2,1,0:T(8,128)} %bitcast.10), calls=%async_computation.1 | async-start | bytes 1310720 | tf_op jit(solution)/shard_map/all_to_all | solution.py:317
  49.3 7.6 %collective-permute-start.5 = (bf16[2,40,1920]{2,1,0:T(8,128)(2,1)S(1)}, bf16[2,40,1920]{2,1,0:T(8,128)(2,1)S(1)}, u32[]{:S(2)}, u32[]{:S(2)}) collective-permute-start(bf16[2,40,1920]{2,1,0:T(8,128)(2,1)S(1)} %pad_maximum_fusion.1), channel_id=1, source_target_pairs={{0,32},{32,0},{64,96},{96,64},{128,160},{160,128},{192,224},{224,1... | collective-permute-start | bytes 921608 | tf_op jit(solution)/shard_map/ppermute | solution.py:312
  57.0 24.4 %collective-permute-start.6 = (bf16[4,40,1920]{2,1,0:T(8,128)(2,1)S(1)}, bf16[4,40,1920]{2,1,0:T(8,128)(2,1)S(1)}, u32[]{:S(2)}, u32[]{:S(2)}) collective-permute-start(bf16[4,40,1920]{2,1,0:T(8,128)(2,1)S(1)} %pad_maximum_fusion.refs_0_), channel_id=1, source_target_pairs={{0,8},{8,0},{16,408},{24,400},{384,392},{392,384},{400,24},{408,16... | collective-permute-start | bytes 1843208 | tf_op jit(solution)/shard_map/ppermute | solution.py:315
  63.5 27.9 %all-to-all-start.2 = ((f32[12,8,256]{2,1,0:T(8,128)}), f32[12,8,256]{2,1,0:T(8,128)S(1)}, u32[]{:S(2)}, u32[]{:S(2)}) async-start(f32[12,8,256]{2,1,0:T(8,128)} %bitcast.15), calls=%async_computation.2 | async-start | bytes 196608 | tf_op jit(solution)/shard_map/all_to_all | solution.py:325
  81.4 15.4 %collective-permute-start.7 = (bf16[4,40,1920]{2,1,0:T(8,128)(2,1)S(1)}, bf16[4,40,1920]{2,1,0:T(8,128)(2,1)S(1)}, u32[]{:S(2)}, u32[]{:S(2)}) collective-permute-start(bf16[4,40,1920]{2,1,0:T(8,128)(2,1)S(1)} %pad_maximum_fusion.refs_0_), channel_id=1, source_target_pairs={{0,16},{16,0},{1,17},{17,1},{2,18},{18,2},{3,19},{19,3},{4,20},{20... | collective-permute-start | bytes 1843208 | tf_op jit(solution)/shard_map/ppermute | solution.py:324
  84.0 12.8 %collective-permute-start.8 = (bf16[4,40,1920]{2,1,0:T(8,128)(2,1)S(1)}, bf16[4,40,1920]{2,1,0:T(8,128)(2,1)S(1)}, u32[]{:S(2)}, u32[]{:S(2)}) collective-permute-start(bf16[4,40,1920]{2,1,0:T(8,128)(2,1)S(1)} %collective-permute-done.6.refs_1_), channel_id=1, source_target_pairs={{0,16},{16,0},{1,17},{17,1},{2,18},{18,2},{3,19},{19,3},{4,20},{20... | collective-permute-start | bytes 1843208 | tf_op jit(solution)/shard_map/ppermute | solution.py:328
  92.1 17.4 %all-to-all-start.3 = ((f32[24,8,256]{2,1,0:T(8,128)}), f32[24,8,256]{2,1,0:T(8,128)}, u32[]{:S(2)}, u32[]{:S(2)}) async-start(f32[24,8,256]{2,1,0:T(8,128)} %broadcast_in_dim.16), calls=%async_computation.3 | async-start | bytes 393216 | tf_op jit(solution)/shard_map/all_to_all | solution.py:330
  96.8 1.0 copy-start.2

commit v13 on v12

--- a/solution.py
+++ b/solution.py
@@ -310,17 +310,24 @@
     parity = z % 2
     pair = jnp.stack([jnp.where((parity == 1) & (core == 1), temporal_weight, w_far), w_near])
     pair_far = lax.ppermute(pair, "z", [(i, i ^ 1) for i in range(n_z)])
-    blocks = jnp.concatenate([pair, pair_far])
-    pairs = [(i, i ^ (1 if i // 2 % 2 == 0 else 5)) for i in range(8)]
-    blocks_far = lax.ppermute(blocks, ("xh", "c", "xl"), pairs)
+    def other_xl(i, planes):
+        xh_z, side, half = i // 4, i // 2 % 2, i % 2
+        far_xh, far_z = (xh_z // n_z + side) % 2, xh_z % n_z ^ planes
+        return ((far_xh * n_z + far_z) * 2 + side) * 2 + 1 - half
+
+    place_x = ("xh", "z", "c", "xl")
+    pair_xl, pair_diag = [
+        lax.ppermute(pair, place_x, [(i, other_xl(i, planes)) for i in range(8 * n_z)]) for planes in (0, 1)
+    ]
 
     part = lax.all_to_all(term.reshape(n_y, 320 // n_y, 512), "y", 0, 0, tiled=True)
-    part, blocks = lax.optimization_barrier((part, blocks))
+    part, pair_far, pair_xl = lax.optimization_barrier((part, pair_far, pair_xl))
     part = part.sum(0)
     local_rows = part.shape[0]
     n_xz = 2 * n_z
     pieces = jnp.pad(part, ((0, 48 - local_rows), (0, 0))).reshape(6, 8, 2, 256).transpose(0, 2, 1, 3).reshape(n_z, 8, 256)
-    _, blocks, blocks_far = lax.optimization_barrier((pieces, blocks, blocks_far))
+    _, pair_far, pair_xl, pair_diag = lax.optimization_barrier((pieces, pair_far, pair_xl, pair_diag))
+    blocks, blocks_far = jnp.concatenate([pair, pair_far]), jnp.concatenate([pair_xl, pair_diag])
     blocks_sib = lax.ppermute(blocks, "c", both)
     mine = lax.all_to_all(pieces, "z", 0, 0, tiled=True)
     mine = mine.sum(0) * (1.0 / math.sqrt(total_frames * strip * lax.axis_size(FSDP)))

time: 117 us -> 118 us (level)
  waiting for transfers between devices: 23.1 us -> 18 us
  starting transfers between devices: 61.2 us -> 65.3 us
  local copies, waits for them, and re-layouts: 3.63 us -> 5.41 us
    ppermute x1, waiting for transfers between devices: 5.67 us -> 2.28 us  [shards(): pair_far = lax.ppermute(pair, 'z', [(i, i ^ 1) for i in range(n_z)])]
    ppermute x1 -> x2, starting transfers between devices: 4.3 us -> 7.66 us  [shards(): lax.ppermute(pair, place_x, [(i, other_xl(i, planes)) for i in range(8 *...]
  transfers between devices with their start and end apart: 13 -> 14, of which waited for: 5 -> 5; matrix products, arithmetic and copies ran while one was open for 2% -> 3% of each run, Pallas kernels for 4% -> 4%
where the time goes in v13:
time: 118 us; the launch traced here: 117 us
  starting transfers between devices  65.3 us (55%)
  waiting for transfers between devices  18 us (15%)
  blocking collectives  16 us (14%)
  Pallas kernels  10.1 us (9%)
  local copies, waits for them, and re-layouts  5.41 us (5%)
  between operations  1.74 us (1%)
    all_to_all x1, starting transfers between devices, shards(): mine = lax.all_to_all(pieces, 'z', 0, 0, tiled=True)  17.8 us
    all_gather x1, blocking collectives, shards(): edges = lax.all_gather(jnp.where(core == 0, ends[1], ends[0]), 'c')  10.2 us
    ppermute x2, starting transfers between devices, from_y(): return lax.ppermute(temporal_weight, ('z', 'c', 'y'), pairs)  9.76 us
    all_to_all x1, waiting for transfers between devices, shards(): gathered = lax.all_to_all(mine, ('xh', 'z'), 0, 0, tiled=True)  8.36 us
    ppermute x2, starting transfers between devices, shards(): lax.ppermute(pair, place_x, [(i, other_xl(i, planes)) for i in range(8 *...  7.66 us
    all_gather x1, blocking collectives, shards(): gathered = lax.all_gather(gathered, 'c')  5.76 us
    ppermute x1, starting transfers between devices, shards(): halo = lax.ppermute(jnp.where(core == 0, ends[0], ends[1]), DP, across)  5.63 us
    all_to_all x1, starting transfers between devices, shards(): gathered = lax.all_to_all(mine, ('xh', 'z'), 0, 0, tiled=True)  5.29 us
  transfers between devices with their start and end apart: 14, of which 5 were waited for; matrix products, arithmetic and copies ran while one was open for 3% of the time, Pallas kernels for 4%

profile of v13, /device:TPU:1, one launch (start us, length us, event | category | flops | bytes accessed | tf_op | source)
XLA Modules:
  0.0 117.3 jit_solution(18221435680371507490)
XLA Ops:
  0.6 2.2 %pack.1 = bf16[4,256,640]{2,1,0:T(8,128)(2,1)} custom-call(bf16[8,32,640]{2,1,0:T(8,128)(2,1)} %f_ref.1, bf16[8,32,640]{2,1,0:T(8,128)(2,1)} %g_ref.1), custom_call_target="tpu_custom_call" | custom-call | tf_op jit(solution)/shard_map/pack/pallas_call | solution.py:66
  2.9 5.0 %all-to-all-start = ((bf16[4,256,640]{2,1,0:T(8,128)(2,1)}), bf16[4,256,640]{2,1,0:T(8,128)(2,1)S(1)}, u32[]{:S(2)}, u32[]{:S(2)}) async-start(bf16[4,256,640]{2,1,0:T(8,128)(2,1)} %pack.1), calls=%async_computation | async-start | bytes 2621440 | tf_op jit(solution)/shard_map/all_to_all | solution.py:289
  7.9 5.2 %collective-permute-start.1 = (bf16[40,1920]{1,0:T(8,128)(2,1)S(1)}, bf16[40,1920]{1,0:T(8,128)(2,1)S(1)}, u32[]{:S(2)}, u32[]{:S(2)}) collective-permute-start(bf16[40,1920]{1,0:T(8,128)(2,1)S(1)} %copy-done.5), channel_id=1, source_target_pairs={{0,1},{1,2},{2,3},{3,4},{4,5},{5,6},{6,7},{7,0},{16,23},{17,16},{1... | collective-permute-start | bytes 460808 | tf_op jit(solution)/shard_map/ppermute | solution.py:284
  13.1 4.5 %collective-permute-start = (bf16[40,1920]{1,0:T(8,128)(2,1)S(1)}, bf16[40,1920]{1,0:T(8,128)(2,1)S(1)}, u32[]{:S(2)}, u32[]{:S(2)}) collective-permute-start(bf16[40,1920]{1,0:T(8,128)(2,1)S(1)} %copy-done.5), channel_id=1, source_target_pairs={{0,3},{1,4},{2,5},{3,6},{4,7},{5,0},{6,1},{7,2},{16,21},{17,22},{1... | collective-permute-start | bytes 460808 | tf_op jit(solution)/shard_map/ppermute | solution.py:284
  17.8 5.6 %collective-permute-start.2 = (bf16[32,1280]{1,0:T(8,128)(2,1)S(1)}, bf16[32,1280]{1,0:T(8,128)(2,1)S(1)}, u32[]{:S(2)}, u32[]{:S(2)}) collective-permute-start(bf16[32,1280]{1,0:T(8,128)(2,1)S(1)} %maximum_select_fusion), channel_id=1, source_target_pairs={{0,752},{16,32},{32,16},{48,64},{64,48},{80,96},{96,80},{112,128},... | collective-permute-start | bytes 245768 | tf_op jit(solution)/shard_map/ppermute | solution.py:293
  24.4 10.2 %all_gather.10.edge_ref = bf16[2,32,1280]{2,1,0:T(8,128)(2,1)S(1)} all-gather(bf16[1,32,1280]{2,1,0:T(8,128)(2,1)S(1)} %maximum_select_fusion.1), channel_id=1, replica_groups=mesh['xh'=2,'z'=12,'c'=2,'xl'=2,'y'=8] {'c'}, dimensions={0}, use_global_device_ids=true | all-gather | bytes 245760 | tf_op jit(solution)/shard_map/all_gather | solution.py:291
  34.7 2.3 %collective-permute-start.3 = (bf16[4,8,32,640]{3,2,1,0:T(8,128)(2,1)S(1)}, bf16[4,8,32,640]{3,2,1,0:T(8,128)(2,1)S(1)}, u32[]{:S(2)}, u32[]{:S(2)}) collective-permute-start(bf16[4,8,32,640]{3,2,1,0:T(8,128)(2,1)S(1)} %bitcast.60), channel_id=1, source_target_pairs={{0,16},{16,0},{1,17},{17,1},{2,18},{18,2},{3,19},{19,3},{4,20},{20... | collective-permute-start | bytes 3932168 | tf_op jit(solution)/shard_map/ppermute | solution.py:295
  37.0 1.9 %collective-permute-start.4 = (bf16[4,32,384]{2,1,0:T(8,128)(2,1)S(1)}, bf16[4,32,384]{2,1,0:T(8,128)(2,1)S(1)}, u32[]{:S(2)}, u32[]{:S(2)}) collective-permute-start(bf16[4,32,384]{2,1,0:T(8,128)(2,1)S(1)} %fusion), channel_id=1, source_target_pairs={{0,368},{32,16},{64,48},{96,80},{128,112},{160,144},{192,176},{224... | collective-permute-start | bytes 294920 | tf_op jit(solution)/shard_map/ppermute | solution.py:298
  39.3 1.6 %own_term.1 = (f32[384,384]{1,0:T(8,128)S(1)}, f32[384,256]{1,0:T(8,128)S(1)}) custom-call(s32[3]{0:T(128)S(1)} %pad_add_fusion.place_ref, s32[32]{0:T(128)S(1)} %convert_subtract_fusion.1.prev_ref, s32[32]{0:T(128)S(1)} %convert_subtract_fusion.next_ref, bf16[4,8,32,640]{3,2,1,0:T(8,128)(2,1)S(1)} %bitcast.62), custom_call_target="tpu_custom_call" | custom-call | tf_op jit(solution)/shard_map/own_term/pallas_call | solution.py:122
  40.9 2.0 %collective-permute-done.4.halo_ref = bf16[4,32,384]{2,1,0:T(8,128)(2,1)S(1)} collective-permute-done((bf16[4,32,384]{2,1,0:T(8,128)(2,1)S(1)}, bf16[4,32,384]{2,1,0:T(8,128)(2,1)S(1)}, u32[]{:S(2)}, u32[]{:S(2)}) %collective-permute-start.4) | collective-permute-done | bytes 98336 | tf_op jit(solution)/shard_map/ppermute | solution.py:298
  43.0 2.7 %x_term.1 = f32[320,512]{1,0:T(8,128)} custom-call(s32[3]{0:T(128)S(1)} %pad_add_fusion.place_ref, s32[32]{0:T(128)S(1)} %convert_subtract_fusion.1.prev_ref, s32[32]{0:T(128)S(1)} %convert_subtract_fusion.next_ref, bf16[4,8,32,640]{3,2,1,0:T(8,128)(2,1)S(1)} %bitcast.63, bf16[4,8,32,640]{3,2,1,0:T(8,128)(2,1)S(1)} %collective-permute-done.3.sib_ref, ...), custom_call_target="tpu_custom_call" | custom-call | tf_op jit(solution)/shard_map/x_term/pallas_call | solution.py:196
  45.7 3.5 %all-to-all-start.1 = ((f32[8,40,512]{2,1,0:T(8,128)}), f32[8,40,512]{2,1,0:T(8,128)S(1)}, u32[]{:S(2)}, u32[]{:S(2)}) async-start(f32[8,40,512]{2,1,0:T(8,128)} %bitcast.10), calls=%async_computation.1 | async-start | bytes 1310720 | tf_op jit(solution)/shard_map/all_to_all | solution.py:323
  49.3 4.3 %collective-permute-start.6 = (bf16[2,40,1920]{2,1,0:T(8,128)(2,1)S(1)}, bf16[2,40,1920]{2,1,0:T(8,128)(2,1)S(1)}, u32[]{:S(2)}, u32[]{:S(2)}) collective-permute-start(bf16[2,40,1920]{2,1,0:T(8,128)(2,1)S(1)} %pad_maximum_fusion.1), channel_id=1, source_target_pairs={{0,8},{8,0},{16,408},{24,400},{32,40},{40,32},{48,440},{56,432},{6... | collective-permute-start | bytes 921608 | tf_op jit(solution)/shard_map/ppermute | solution.py:320
  53.6 1.9 %collective-permute-start.5 = (bf16[2,40,1920]{2,1,0:T(8,128)(2,1)S(1)}, bf16[2,40,1920]{2,1,0:T(8,128)(2,1)S(1)}, u32[]{:S(2)}, u32[]{:S(2)}) collective-permute-start(bf16[2,40,1920]{2,1,0:T(8,128)(2,1)S(1)} %pad_maximum_fusion.1), channel_id=1, source_target_pairs={{0,32},{32,0},{64,96},{96,64},{128,160},{160,128},{192,224},{224,1... | collective-permute-start | bytes 921608 | tf_op jit(solution)/shard_map/ppermute | solution.py:312
  55.6 3.4 %collective-permute-start.7 = (bf16[2,40,1920]{2,1,0:T(8,128)(2,1)S(1)}, bf16[2,40,1920]{2,1,0:T(8,128)(2,1)}, u32[]{:S(2)}, u32[]{:S(2)}) collective-permute-start(bf16[2,40,1920]{2,1,0:T(8,128)(2,1)S(1)} %pad_maximum_fusion.1), channel_id=1, source_target_pairs={{0,40},{8,32},{16,440},{24,432},{32,8},{40,0},{48,408},{56,400},{6... | collective-permute-start | bytes 921608 | tf_op jit(solution)/shard_map/ppermute | solution.py:320
  58.9 2.3 %collective-permute-done.5 = bf16[2,40,1920]{2,1,0:T(8,128)(2,1)S(1)} collective-permute-done((bf16[2,40,1920]{2,1,0:T(8,128)(2,1)S(1)}, bf16[2,40,1920]{2,1,0:T(8,128)(2,1)S(1)}, u32[]{:S(2)}, u32[]{:S(2)}) %collective-permute-start.5) | collective-permute-done | bytes 307232 | tf_op jit(solution)/shard_map/ppermute | solution.py:312
  63.6 17.8 %all-to-all-start.2 = ((f32[12,8,256]{2,1,0:T(8,128)}), f32[12,8,256]{2,1,0:T(8,128)S(1)}, u32[]{:S(2)}, u32[]{:S(2)}) async-start(f32[12,8,256]{2,1,0:T(8,128)} %bitcast.15), calls=%async_computation.2 | async-start | bytes 196608 | tf_op jit(solution)/shard_map/all_to_all | solution.py:332
  82.5 2.6 %collective-permute-start.9 = (bf16[4,40,1920]{2,1,0:T(8,128)(2,1)S(1)}, bf16[4,40,1920]{2,1,0:T(8,128)(2,1)S(1)}, u32[]{:S(2)}, u32[]{:S(2)}) collective-permute-start(bf16[4,40,1920]{2,1,0:T(8,128)(2,1)S(1)} %constant_dynamic-update-slice_fusion.refs_1_), channel_id=1, source_target_pairs={{0,16},{16,0},{1,17},{17,1},{2,18},{18,2},{3,19},{19,3},{4,20},{20... | collective-permute-start | bytes 1843208 | tf_op jit(solution)/shard_map/ppermute | solution.py:335
  85.2 1.9 %collective-permute-start.8 = (bf16[4,40,1920]{2,1,0:T(8,128)(2,1)S(1)}, bf16[4,40,1920]{2,1,0:T(8,128)(2,1)S(1)}, u32[]{:S(2)}, u32[]{:S(2)}) collective-permute-start(bf16[4,40,1920]{2,1,0:T(8,128)(2,1)S(1)} %pad_maximum_fusion.refs_0_), channel_id=1, source_target_pairs={{0,16},{16,0},{1,17},{17,1},{2,18},{18,2},{3,19},{19,3},{4,20},{20... | collective-permute-start | bytes 1843208 | tf_op jit(solution)/shard_map/ppermute | solution.py:331
  87.1 4.3 %all-to-all-done.2 = f32[12,8,256]{2,1,0:T(8,128)S(1)} async-done(((f32[12,8,256]{2,1,0:T(8,128)}), f32[12,8,256]{2,1,0:T(8,128)S(1)}, u32[]{:S(2)}, u32[]{:S(2)}) %all-to-all-start.2) | async-done | bytes 98336 | tf_op jit(solution)/shard_map/all_to_all | solution.py:332
  92.2 5.3 %all-to-all-start.3 = ((f32[24,8,256]{2,1,0:T(8,128)}), f32[24,8,256]{2,1,0:T(8,128)}, u32[]{:S(2)}, u32[]{:S(2)}) async-start(f32[24,8,256]{2,1,0:T(8,128)} %broadcast_in_dim.16), calls=%async_computation.3 | async-start | bytes 393216 | tf_op jit(solution)/shard_map/all_to_all | solution.py:337
  98.5 3.5 %outputs.1 = (bf16[8,32,640]{2,1,0:T(8,128)(2,1)}, bf16[8,32,640]{2,1,0:T(8,128)(2,1)}) custom-call(s32[5]{0:T(128)S(1)} %stack.49.place_ref, s32[32]{0:T(128)S(1)} %convert_subtract_fusion.1.prev_ref, s32[32]{0:T(128)S(1)} %convert_subtract_fusion.next_ref, bf16[8,32,640]{2,1,0:T(8,128)(2,1)S(1)} %copy-done, bf16[8,32,640]{2,1,0:T(8,128)(2,1)S(1)} %copy-done.1, ...), custom_call_target="tpu_custom_call" | custom-call | tf_op jit(solution)/shard_map/outputs/pallas_call | solution.py:256
  102.1 8.4 %all-to-all-done.3 = f32[24,8,256]{2,1,0:T(8,128)} async-done(((f32[24,8,256]{2,1,0:T(8,128)}), f32[24,8,256]{2,1,0:T(8,128)}, u32[]{:S(2)}, u32[]{:S(2)}) %all-to-all-start.3) | async-done | bytes 196640 | tf_op jit(solution)/shard_map/all_to_all | solution.py:337
  110.4 5.8 %all-gather = f32[48,8,256]{2,1,0:T(8,128)S(1)} all-gather(f32[24,8,256]{2,1,0:T(8,128)} %all-to-all-done.3), channel_id=2, replica_groups=mesh['xh'=2,'z'=12,'c'=2,'xl'=2,'y'=8] {'c'}, dimensions={0}, use_global_device_ids=true | all-gather | bytes 589824 | tf_op jit(solution)/shard_map/all_gather | solution.py:343
  (61 shorter events, 7.1 us)
Async XLA Ops:
  2.9 5.0 %copy-start.5 = (bf16[40,1920]{1,0:T(8,128)(2,1)S(1)}, bf16[40,1920]{1,0:T(8,128)(2,1)}, u32[]{:S(2)}) copy-start(bf16[40,1920]{1,0:T(8,128)(2,1)} %param.9) | copy-start | bytes 460804
  2.9 14.8 %copy-start = (bf16[8,32,640]{2,1,0:T(8,128)(2,1)S(1)}, bf16[8,32,640]{2,1,0:T(8,128)(2,1)}, u32[]{:S(2)}) copy-start(bf16[8,32,640]{2,1,0:T(8,128)(2,1)} %f_ref.1) | copy-start | bytes 983044
  2.9 14.8 %copy-start.1 = (bf16[8,32,640]{2,1,0:T(8,128)(2,1)S(1)}, bf16[8,32,640]{2,1,0:T(8,128)(2,1)}, u32[]{:S(2)}) copy-start(bf16[8,32,640]{2,1,0:T(8,128)(2,1)} %g_ref.1) | copy-start | bytes 983044
  2.9 31.8 %all-to-all-start = ((bf16[4,256,640]{2,1,0:T(8,128)(2,1)}), bf16[4,256,640]{2,1,0:T(8,128)(2,1)S(1)}, u32[]{:S(2)}, u32[]{:S(2)}) async-start(bf16[4,256,640]{2,1,0:T(8,128)(2,1)} %pack.1), calls=%async_computation | async-start | bytes 2621440 | tf_op jit(solution)/shard_map/all_to_all | solution.py:289
  7.9 31.1 %copy-start.6 = (s32[48]{0:T(128)S(1)}, s32[48]{0:T(128)}, u32[]{:S(2)}) copy-start(s32[48]{0:T(128)} %param.10) | copy-start | bytes 580
  7.9 26.8 %collective-permute-start.1 = (bf16[40,1920]{1,0:T(8,128)(2,1)S(1)}, bf16[40,1920]{1,0:T(8,128)(2,1)S(1)}, u32[]{:S(2)}, u32[]{:S(2)}) collective-permute-start(bf16[40,1920]{1,0:T(8,128)(2,1)S(1)} %copy-done.5), channel_id=1, source_target_pairs={{0,1},{1,2},{2,3},{3,4},{4,5},{5,6},{6,7},{7,0},{16,23},{17,16},{1... | collective-permute-start | bytes 460808 | tf_op jit(solution)/shard_map/ppermute | solution.py:284
  13.1 21.6 %collective-permute-start = (bf16[40,1920]{1,0:T(8,128)(2,1)S(1)}, bf16[40,1920]{1,0:T(8,128)(2,1)S(1)}, u32[]{:S(2)}, u32[]{:S(2)}) collective-permute-start(bf16[40,1920]{1,0:T(8,128)(2,1)S(1)} %copy-done.5), channel_id=1, source_target_pairs={{0,3},{1,4},{2,5},{3,6},{4,7},{5,0},{6,1},{7,2},{16,21},{17,22},{1... | collective-permute-start | bytes 460808 | tf_op jit(solution)/shard_map/ppermute | solution.py:284
  17.8 16.9 %collective-permute-start.2 = (bf16[32,1280]{1,0:T(8,128)(2,1)S(1)}, bf16[32,1280]{1,0:T(8,128)(2,1)S(1)}, u32[]{:S(2)}, u32[]{:S(2)}) collective-permute-start(bf16[32,1280]{1,0:T(8,128)(2,1)S(1)} %maximum_select_fusion), channel_id=1, source_target_pairs={{0,752},{16,32},{32,16},{48,64},{64,48},{80,96},{96,80},{112,128},... | collective-permute-start | bytes 245768 | tf_op jit(solution)/shard_map/ppermute | solution.py:293
  34.7 8.3 %collective-permute-start.3 = (bf16[4,8,32,640]{3,2,1,0:T(8,128)(2,1)S(1)}, bf16[4,8,32,640]{3,2,1,0:T(8,128)(2,1)S(1)}, u32[]{:S(2)}, u32[]{:S(2)}) collective-permute-start(bf16[4,8,32,640]{3,2,1,0:T(8,128)(2,1)S(1)} %bitcast.60), channel_id=1, source_target_pairs={{0,16},{16,0},{1,17},{17,1},{2,18},{18,2},{3,19},{19,3},{4,20},{20... | collective-permute-start | bytes 3932168 | tf_op jit(solution)/shard_map/ppermute | solution.py:295
  37.0 5.9 %collective-permute-start.4 = (bf16[4,32,384]{2,1,0:T(8,128)(2,1)S(1)}, bf16[4,32,384]{2,1,0:T(8,128)(2,1)S(1)}, u32[]{:S(2)}, u32[]{:S(2)}) collective-permute-start(bf16[4,32,384]{2,1,0:T(8,128)(2,1)S(1)} %fusion), channel_id=1, source_target_pairs={{0,368},{32,16},{64,48},{96,80},{128,112},{160,144},{192,176},{224... | collective-permute-start | bytes 294920 | tf_op jit(solution)/shard_map/ppermute | solution.py:298
  45.7 17.2 %all-to-all-start.1 = ((f32[8,40,512]{2,1,0:T(8,128)}), f32[8,40,512]{2,1,0:T(8,128)S(1)}, u32[]{:S(2)}, u32[]{:S(2)}) async-start(f32[8,40,512]{2,1,0:T(8,128)} %bitcast.10), calls=%async_computation.1 | async-start | bytes 1310720 | tf_op jit(solution)/shard_map/all_to_all | solution.py:323
  49.3 9.6 %collective-permute-start.6 = (bf16[2,40,1920]{2,1,0:T(8,128)(2,1)S(1)}, bf16[2,40,1920]{2,1,0:T(8,128)(2,1)S(1)}, u32[]{:S(2)}, u32[]{:S(2)}) collective-permute-start(bf16[2,40,1920]{2,1,0:T(8,128)(2,1)S(1)} %pad_maximum_fusion.1), channel_id=1, source_target_pairs={{0,8},{8,0},{16,408},{24,400},{32,40},{40,32},{48,440},{56,432},{6... | collective-permute-start | bytes 921608 | tf_op jit(solution)/shard_map/ppermute | solution.py:320
  53.6 7.6 %collective-permute-start.5 = (bf16[2,40,1920]{2,1,0:T(8,128)(2,1)S(1)}, bf16[2,40,1920]{2,1,0:T(8,128)(2,1)S(1)}, u32[]{:S(2)}, u32[]{:S(2)}) collective-permute-start(bf16[2,40,1920]{2,1,0:T(8,128)(2,1)S(1)} %pad_maximum_fusion.1), channel_id=1, source_target_pairs={{0,32},{32,0},{64,96},{96,64},{128,160},{160,128},{192,224},{224,1... | collective-permute-start | bytes 921608 | tf_op jit(solution)/shard_map/ppermute | solution.py:312
  55.6 25.9 %collective-permute-start.7 = (bf16[2,40,1920]{2,1,0:T(8,128)(2,1)S(1)}, bf16[2,40,1920]{2,1,0:T(8,128)(2,1)}, u32[]{:S(2)}, u32[]{:S(2)}) collective-permute-start(bf16[2,40,1920]{2,1,0:T(8,128)(2,1)S(1)} %pad_maximum_fusion.1), channel_id=1, source_target_pairs={{0,40},{8,32},{16,440},{24,432},{32,8},{40,0},{48,408},{56,400},{6... | collective-permute-start | bytes 921608 | tf_op jit(solution)/shard_map/ppermute | solution.py:320
  61.2 0.7 copy-start.3
  63.6 27.9 %all-to-all-start.2 = ((f32[12,8,256]{2,1,0:T(8,128)}), f32[12,8,256]{2,1,0:T(8,128)S(1)}, u32[]{:S(2)}, u32[]{:S(2)}) async-start(f32[12,8,256]{2,1,0:T(8,128)} %bitcast.15), calls=%async_computation.2 | async-start | bytes 196608 | tf_op jit(solution)/shard_map/all_to_all | solution.py:332
  81.4 3.7 %copy-start.4 = (bf16[2,40,1920]{2,1,0:T(8,128)(2,1)S(1)}, bf16[2,40,1920]{2,1,0:T(8,128)(2,1)}, u32[]{:S(2)}) copy-start(bf16[2,40,1920]{2,1,0:T(8,128)(2,1)} %copy-done.3) | copy-start | bytes 921604
  82.5 15.1 %collective-permute-start.9 = (bf16[4,40,1920]{2,1,0:T(8,128)(2,1)S(1)}, bf16[4,40,1920]{2,1,0:T(8,128)(2,1)S(1)}, u32[]{:S(2)}, u32[]{:S(2)}) collective-permute-start(bf16[4,40,1920]{2,1,0:T(8,128)(2,1)S(1)} %constant_dynamic-update-slice_fusion.refs_1_), channel_id=1, source_target_pairs={{0,16},{16,0},{1,17},{17,1},{2,18},{18,2},{3,19},{19,3},{4,20},{20... | collective-permute-start | bytes 1843208 | tf_op jit(solution)/shard_map/ppermute | solution.py:335
  85.2 12.4 %collective-permute-start.8 = (bf16[4,40,1920]{2,1,0:T(8,128)(2,1)S(1)}, bf16[4,40,1920]{2,1,0:T(8,128)(2,1)S(1)}, u32[]{:S(2)}, u32[]{:S(2)}) collective-permute-start(bf16[4,40,1920]{2,1,0:T(8,128)(2,1)S(1)} %pad_maximum_fusion.refs_0_), channel_id=1, source_target_pairs={{0,16},{16,0},{1,17},{17,1},{2,18},{18,2},{3,19},{19,3},{4,20},{20... | collective-permute-start | bytes 1843208 | tf_op jit(solution)/shard_map/ppermute | solution.py:331
  92.2 18.2 %all-to-all-start.3 = ((f32[24,8,256]{2,1,0:T(8,128)}), f32[24,8,256]{2,1,0:T(8,128)}, u32[]{:S(2)}, u32[]{:S(2)}) async-start(f32[24,8,256]{2,1,0:T(8,128)} %broadcast_in_dim.16), calls=%async_computation.3 | async-start | bytes 393216 | tf_op jit(solution)/shard_map/all_to_all | solution.py:337
  97.6 1.0 copy-start.2

commit v14 on v13

--- a/solution.py
+++ b/solution.py
@@ -321,7 +321,7 @@
     ]
 
     part = lax.all_to_all(term.reshape(n_y, 320 // n_y, 512), "y", 0, 0, tiled=True)
-    part, pair_far, pair_xl = lax.optimization_barrier((part, pair_far, pair_xl))
+    part, pair_far = lax.optimization_barrier((part, pair_far))
     part = part.sum(0)
     local_rows = part.shape[0]
     n_xz = 2 * n_z

time: 118 us -> 118 us (level)
    all_to_all x1, waiting for transfers between devices: 0.92 us -> 3.2 us  [shards(): lax.all_to_all(term.reshape(n_y, 320 // n_y, 512), 'y', 0, 0, tiled=True)]
    ppermute x1, waiting for transfers between devices: 2.28 us -> 0.01 us  [shards(): pair_far = lax.ppermute(pair, 'z', [(i, i ^ 1) for i in range(n_z)])]
  transfers between devices with their start and end apart: 14 -> 14, of which waited for: 5 -> 4; matrix products, arithmetic and copies ran while one was open for 3% -> 3% of each run, Pallas kernels for 4% -> 4%
where the time goes in v14:
time: 118 us; the launch traced here: 117 us
  starting transfers between devices  65.3 us (55%)
  waiting for transfers between devices  18 us (15%)
  blocking collectives  16 us (14%)
  Pallas kernels  10.1 us (9%)
  local copies, waits for them, and re-layouts  5.41 us (5%)
  between operations  1.75 us (1%)
    all_to_all x1, starting transfers between devices, shards(): mine = lax.all_to_all(pieces, 'z', 0, 0, tiled=True)  17.8 us
    all_gather x1, blocking collectives, shards(): edges = lax.all_gather(jnp.where(core == 0, ends[1], ends[0]), 'c')  10.2 us
    ppermute x2, starting transfers between devices, from_y(): return lax.ppermute(temporal_weight, ('z', 'c', 'y'), pairs)  9.76 us
    all_to_all x1, waiting for transfers between devices, shards(): gathered = lax.all_to_all(mine, ('xh', 'z'), 0, 0, tiled=True)  8.36 us
    ppermute x2, starting transfers between devices, shards(): lax.ppermute(pair, place_x, [(i, other_xl(i, planes)) for i in range(8 *...  7.66 us
    all_gather x1, blocking collectives, shards(): gathered = lax.all_gather(gathered, 'c')  5.76 us
    ppermute x1, starting transfers between devices, shards(): halo = lax.ppermute(jnp.where(core == 0, ends[0], ends[1]), DP, across)  5.63 us
    all_to_all x1, starting transfers between devices, shards(): gathered = lax.all_to_all(mine, ('xh', 'z'), 0, 0, tiled=True)  5.31 us
  transfers between devices with their start and end apart: 14, of which 4 were waited for; matrix products, arithmetic and copies ran while one was open for 3% of the time, Pallas kernels for 4%

profile of v14, /device:TPU:1, one launch (start us, length us, event | category | flops | bytes accessed | tf_op | source)
XLA Modules:
  0.0 117.3 jit_solution(8373186673416926165)
XLA Ops:
  0.6 2.2 %pack.1 = bf16[4,256,640]{2,1,0:T(8,128)(2,1)} custom-call(bf16[8,32,640]{2,1,0:T(8,128)(2,1)} %f_ref.1, bf16[8,32,640]{2,1,0:T(8,128)(2,1)} %g_ref.1), custom_call_target="tpu_custom_call" | custom-call | tf_op jit(solution)/shard_map/pack/pallas_call | solution.py:66
  2.9 5.0 %all-to-all-start = ((bf16[4,256,640]{2,1,0:T(8,128)(2,1)}), bf16[4,256,640]{2,1,0:T(8,128)(2,1)S(1)}, u32[]{:S(2)}, u32[]{:S(2)}) async-start(bf16[4,256,640]{2,1,0:T(8,128)(2,1)} %pack.1), calls=%async_computation | async-start | bytes 2621440 | tf_op jit(solution)/shard_map/all_to_all | solution.py:289
  7.9 5.2 %collective-permute-start.1 = (bf16[40,1920]{1,0:T(8,128)(2,1)S(1)}, bf16[40,1920]{1,0:T(8,128)(2,1)S(1)}, u32[]{:S(2)}, u32[]{:S(2)}) collective-permute-start(bf16[40,1920]{1,0:T(8,128)(2,1)S(1)} %copy-done.5), channel_id=1, source_target_pairs={{0,1},{1,2},{2,3},{3,4},{4,5},{5,6},{6,7},{7,0},{16,23},{17,16},{1... | collective-permute-start | bytes 460808 | tf_op jit(solution)/shard_map/ppermute | solution.py:284
  13.1 4.5 %collective-permute-start = (bf16[40,1920]{1,0:T(8,128)(2,1)S(1)}, bf16[40,1920]{1,0:T(8,128)(2,1)S(1)}, u32[]{:S(2)}, u32[]{:S(2)}) collective-permute-start(bf16[40,1920]{1,0:T(8,128)(2,1)S(1)} %copy-done.5), channel_id=1, source_target_pairs={{0,3},{1,4},{2,5},{3,6},{4,7},{5,0},{6,1},{7,2},{16,21},{17,22},{1... | collective-permute-start | bytes 460808 | tf_op jit(solution)/shard_map/ppermute | solution.py:284
  17.8 5.6 %collective-permute-start.2 = (bf16[32,1280]{1,0:T(8,128)(2,1)S(1)}, bf16[32,1280]{1,0:T(8,128)(2,1)S(1)}, u32[]{:S(2)}, u32[]{:S(2)}) collective-permute-start(bf16[32,1280]{1,0:T(8,128)(2,1)S(1)} %maximum_select_fusion), channel_id=1, source_target_pairs={{0,752},{16,32},{32,16},{48,64},{64,48},{80,96},{96,80},{112,128},... | collective-permute-start | bytes 245768 | tf_op jit(solution)/shard_map/ppermute | solution.py:293
  24.4 10.2 %all_gather.10.edge_ref = bf16[2,32,1280]{2,1,0:T(8,128)(2,1)S(1)} all-gather(bf16[1,32,1280]{2,1,0:T(8,128)(2,1)S(1)} %maximum_select_fusion.1), channel_id=1, replica_groups=mesh['xh'=2,'z'=12,'c'=2,'xl'=2,'y'=8] {'c'}, dimensions={0}, use_global_device_ids=true | all-gather | bytes 245760 | tf_op jit(solution)/shard_map/all_gather | solution.py:291
  34.7 2.3 %collective-permute-start.3 = (bf16[4,8,32,640]{3,2,1,0:T(8,128)(2,1)S(1)}, bf16[4,8,32,640]{3,2,1,0:T(8,128)(2,1)S(1)}, u32[]{:S(2)}, u32[]{:S(2)}) collective-permute-start(bf16[4,8,32,640]{3,2,1,0:T(8,128)(2,1)S(1)} %bitcast.60), channel_id=1, source_target_pairs={{0,16},{16,0},{1,17},{17,1},{2,18},{18,2},{3,19},{19,3},{4,20},{20... | collective-permute-start | bytes 3932168 | tf_op jit(solution)/shard_map/ppermute | solution.py:295
  37.0 1.9 %collective-permute-start.4 = (bf16[4,32,384]{2,1,0:T(8,128)(2,1)S(1)}, bf16[4,32,384]{2,1,0:T(8,128)(2,1)S(1)}, u32[]{:S(2)}, u32[]{:S(2)}) collective-permute-start(bf16[4,32,384]{2,1,0:T(8,128)(2,1)S(1)} %fusion), channel_id=1, source_target_pairs={{0,368},{32,16},{64,48},{96,80},{128,112},{160,144},{192,176},{224... | collective-permute-start | bytes 294920 | tf_op jit(solution)/shard_map/ppermute | solution.py:298
  39.3 1.6 %own_term.1 = (f32[384,384]{1,0:T(8,128)S(1)}, f32[384,256]{1,0:T(8,128)S(1)}) custom-call(s32[3]{0:T(128)S(1)} %pad_add_fusion.place_ref, s32[32]{0:T(128)S(1)} %convert_subtract_fusion.1.prev_ref, s32[32]{0:T(128)S(1)} %convert_subtract_fusion.next_ref, bf16[4,8,32,640]{3,2,1,0:T(8,128)(2,1)S(1)} %bitcast.62), custom_call_target="tpu_custom_call" | custom-call | tf_op jit(solution)/shard_map/own_term/pallas_call | solution.py:122
  40.9 2.0 %collective-permute-done.4.halo_ref = bf16[4,32,384]{2,1,0:T(8,128)(2,1)S(1)} collective-permute-done((bf16[4,32,384]{2,1,0:T(8,128)(2,1)S(1)}, bf16[4,32,384]{2,1,0:T(8,128)(2,1)S(1)}, u32[]{:S(2)}, u32[]{:S(2)}) %collective-permute-start.4) | collective-permute-done | bytes 98336 | tf_op jit(solution)/shard_map/ppermute | solution.py:298
  43.0 2.7 %x_term.1 = f32[320,512]{1,0:T(8,128)} custom-call(s32[3]{0:T(128)S(1)} %pad_add_fusion.place_ref, s32[32]{0:T(128)S(1)} %convert_subtract_fusion.1.prev_ref, s32[32]{0:T(128)S(1)} %convert_subtract_fusion.next_ref, bf16[4,8,32,640]{3,2,1,0:T(8,128)(2,1)S(1)} %bitcast.63, bf16[4,8,32,640]{3,2,1,0:T(8,128)(2,1)S(1)} %collective-permute-done.3.sib_ref, ...), custom_call_target="tpu_custom_call" | custom-call | tf_op jit(solution)/shard_map/x_term/pallas_call | solution.py:196
  45.7 3.5 %all-to-all-start.1 = ((f32[8,40,512]{2,1,0:T(8,128)}), f32[8,40,512]{2,1,0:T(8,128)S(1)}, u32[]{:S(2)}, u32[]{:S(2)}) async-start(f32[8,40,512]{2,1,0:T(8,128)} %bitcast.10), calls=%async_computation.1 | async-start | bytes 1310720 | tf_op jit(solution)/shard_map/all_to_all | solution.py:323
  49.3 1.9 %collective-permute-start.5 = (bf16[2,40,1920]{2,1,0:T(8,128)(2,1)S(1)}, bf16[2,40,1920]{2,1,0:T(8,128)(2,1)S(1)}, u32[]{:S(2)}, u32[]{:S(2)}) collective-permute-start(bf16[2,40,1920]{2,1,0:T(8,128)(2,1)S(1)} %pad_maximum_fusion.1), channel_id=1, source_target_pairs={{0,32},{32,0},{64,96},{96,64},{128,160},{160,128},{192,224},{224,1... | collective-permute-start | bytes 921608 | tf_op jit(solution)/shard_map/ppermute | solution.py:312
  51.3 5.5 %collective-permute-start.7 = (bf16[2,40,1920]{2,1,0:T(8,128)(2,1)S(1)}, bf16[2,40,1920]{2,1,0:T(8,128)(2,1)S(1)}, u32[]{:S(2)}, u32[]{:S(2)}) collective-permute-start(bf16[2,40,1920]{2,1,0:T(8,128)(2,1)S(1)} %pad_maximum_fusion.1), channel_id=1, source_target_pairs={{0,40},{8,32},{16,440},{24,432},{32,8},{40,0},{48,408},{56,400},{6... | collective-permute-start | bytes 921608 | tf_op jit(solution)/shard_map/ppermute | solution.py:320
  56.7 2.2 %collective-permute-start.6 = (bf16[2,40,1920]{2,1,0:T(8,128)(2,1)S(1)}, bf16[2,40,1920]{2,1,0:T(8,128)(2,1)}, u32[]{:S(2)}, u32[]{:S(2)}) collective-permute-start(bf16[2,40,1920]{2,1,0:T(8,128)(2,1)S(1)} %pad_maximum_fusion.1), channel_id=1, source_target_pairs={{0,8},{8,0},{16,408},{24,400},{32,40},{40,32},{48,440},{56,432},{6... | collective-permute-start | bytes 921608 | tf_op jit(solution)/shard_map/ppermute | solution.py:320
  59.7 3.2 %all-to-all-done.1 = f32[8,40,512]{2,1,0:T(8,128)S(1)} async-done(((f32[8,40,512]{2,1,0:T(8,128)}), f32[8,40,512]{2,1,0:T(8,128)S(1)}, u32[]{:S(2)}, u32[]{:S(2)}) %all-to-all-start.1) | async-done | bytes 655392 | tf_op jit(solution)/shard_map/all_to_all | solution.py:323
  63.6 17.8 %all-to-all-start.2 = ((f32[12,8,256]{2,1,0:T(8,128)}), f32[12,8,256]{2,1,0:T(8,128)S(1)}, u32[]{:S(2)}, u32[]{:S(2)}) async-start(f32[12,8,256]{2,1,0:T(8,128)} %bitcast.15), calls=%async_computation.2 | async-start | bytes 196608 | tf_op jit(solution)/shard_map/all_to_all | solution.py:332
  82.5 2.6 %collective-permute-start.9 = (bf16[4,40,1920]{2,1,0:T(8,128)(2,1)S(1)}, bf16[4,40,1920]{2,1,0:T(8,128)(2,1)S(1)}, u32[]{:S(2)}, u32[]{:S(2)}) collective-permute-start(bf16[4,40,1920]{2,1,0:T(8,128)(2,1)S(1)} %constant_dynamic-update-slice_fusion.refs_1_), channel_id=1, source_target_pairs={{0,16},{16,0},{1,17},{17,1},{2,18},{18,2},{3,19},{19,3},{4,20},{20... | collective-permute-start | bytes 1843208 | tf_op jit(solution)/shard_map/ppermute | solution.py:335
  85.2 1.9 %collective-permute-start.8 = (bf16[4,40,1920]{2,1,0:T(8,128)(2,1)S(1)}, bf16[4,40,1920]{2,1,0:T(8,128)(2,1)S(1)}, u32[]{:S(2)}, u32[]{:S(2)}) collective-permute-start(bf16[4,40,1920]{2,1,0:T(8,128)(2,1)S(1)} %pad_maximum_fusion.refs_0_), channel_id=1, source_target_pairs={{0,16},{16,0},{1,17},{17,1},{2,18},{18,2},{3,19},{19,3},{4,20},{20... | collective-permute-start | bytes 1843208 | tf_op jit(solution)/shard_map/ppermute | solution.py:331
  87.1 4.3 %all-to-all-done.2 = f32[12,8,256]{2,1,0:T(8,128)S(1)} async-done(((f32[12,8,256]{2,1,0:T(8,128)}), f32[12,8,256]{2,1,0:T(8,128)S(1)}, u32[]{:S(2)}, u32[]{:S(2)}) %all-to-all-start.2) | async-done | bytes 98336 | tf_op jit(solution)/shard_map/all_to_all | solution.py:332
  92.2 5.3 %all-to-all-start.3 = ((f32[24,8,256]{2,1,0:T(8,128)}), f32[24,8,256]{2,1,0:T(8,128)}, u32[]{:S(2)}, u32[]{:S(2)}) async-start(f32[24,8,256]{2,1,0:T(8,128)} %broadcast_in_dim.16), calls=%async_computation.3 | async-start | bytes 393216 | tf_op jit(solution)/shard_map/all_to_all | solution.py:337
  98.6 3.5 %outputs.1 = (bf16[8,32,640]{2,1,0:T(8,128)(2,1)}, bf16[8,32,640]{2,1,0:T(8,128)(2,1)}) custom-call(s32[5]{0:T(128)S(1)} %stack.49.place_ref, s32[32]{0:T(128)S(1)} %convert_subtract_fusion.1.prev_ref, s32[32]{0:T(128)S(1)} %convert_subtract_fusion.next_ref, bf16[8,32,640]{2,1,0:T(8,128)(2,1)S(1)} %copy-done, bf16[8,32,640]{2,1,0:T(8,128)(2,1)S(1)} %copy-done.1, ...), custom_call_target="tpu_custom_call" | custom-call | tf_op jit(solution)/shard_map/outputs/pallas_call | solution.py:256
  102.1 8.4 %all-to-all-done.3 = f32[24,8,256]{2,1,0:T(8,128)} async-done(((f32[24,8,256]{2,1,0:T(8,128)}), f32[24,8,256]{2,1,0:T(8,128)}, u32[]{:S(2)}, u32[]{:S(2)}) %all-to-all-start.3) | async-done | bytes 196640 | tf_op jit(solution)/shard_map/all_to_all | solution.py:337
  110.4 5.8 %all-gather = f32[48,8,256]{2,1,0:T(8,128)S(1)} all-gather(f32[24,8,256]{2,1,0:T(8,128)} %all-to-all-done.3), channel_id=2, replica_groups=mesh['xh'=2,'z'=12,'c'=2,'xl'=2,'y'=8] {'c'}, dimensions={0}, use_global_device_ids=true | all-gather | bytes 589824 | tf_op jit(solution)/shard_map/all_gather | solution.py:343
  (61 shorter events, 6.2 us)
Async XLA Ops:
  2.9 5.0 %copy-start.5 = (bf16[40,1920]{1,0:T(8,128)(2,1)S(1)}, bf16[40,1920]{1,0:T(8,128)(2,1)}, u32[]{:S(2)}) copy-start(bf16[40,1920]{1,0:T(8,128)(2,1)} %param.9) | copy-start | bytes 460804
  2.9 14.8 %copy-start = (bf16[8,32,640]{2,1,0:T(8,128)(2,1)S(1)}, bf16[8,32,640]{2,1,0:T(8,128)(2,1)}, u32[]{:S(2)}) copy-start(bf16[8,32,640]{2,1,0:T(8,128)(2,1)} %f_ref.1) | copy-start | bytes 983044
  2.9 14.8 %copy-start.1 = (bf16[8,32,640]{2,1,0:T(8,128)(2,1)S(1)}, bf16[8,32,640]{2,1,0:T(8,128)(2,1)}, u32[]{:S(2)}) copy-start(bf16[8,32,640]{2,1,0:T(8,128)(2,1)} %g_ref.1) | copy-start | bytes 983044
  2.9 31.8 %all-to-all-start = ((bf16[4,256,640]{2,1,0:T(8,128)(2,1)}), bf16[4,256,640]{2,1,0:T(8,128)(2,1)S(1)}, u32[]{:S(2)}, u32[]{:S(2)}) async-start(bf16[4,256,640]{2,1,0:T(8,128)(2,1)} %pack.1), calls=%async_computation | async-start | bytes 2621440 | tf_op jit(solution)/shard_map/all_to_all | solution.py:289
  7.9 31.1 %copy-start.6 = (s32[48]{0:T(128)S(1)}, s32[48]{0:T(128)}, u32[]{:S(2)}) copy-start(s32[48]{0:T(128)} %param.10) | copy-start | bytes 580
  7.9 26.8 %collective-permute-start.1 = (bf16[40,1920]{1,0:T(8,128)(2,1)S(1)}, bf16[40,1920]{1,0:T(8,128)(2,1)S(1)}, u32[]{:S(2)}, u32[]{:S(2)}) collective-permute-start(bf16[40,1920]{1,0:T(8,128)(2,1)S(1)} %copy-done.5), channel_id=1, source_target_pairs={{0,1},{1,2},{2,3},{3,4},{4,5},{5,6},{6,7},{7,0},{16,23},{17,16},{1... | collective-permute-start | bytes 460808 | tf_op jit(solution)/shard_map/ppermute | solution.py:284
  13.1 21.6 %collective-permute-start = (bf16[40,1920]{1,0:T(8,128)(2,1)S(1)}, bf16[40,1920]{1,0:T(8,128)(2,1)S(1)}, u32[]{:S(2)}, u32[]{:S(2)}) collective-permute-start(bf16[40,1920]{1,0:T(8,128)(2,1)S(1)} %copy-done.5), channel_id=1, source_target_pairs={{0,3},{1,4},{2,5},{3,6},{4,7},{5,0},{6,1},{7,2},{16,21},{17,22},{1... | collective-permute-start | bytes 460808 | tf_op jit(solution)/shard_map/ppermute | solution.py:284
  17.8 16.9 %collective-permute-start.2 = (bf16[32,1280]{1,0:T(8,128)(2,1)S(1)}, bf16[32,1280]{1,0:T(8,128)(2,1)S(1)}, u32[]{:S(2)}, u32[]{:S(2)}) collective-permute-start(bf16[32,1280]{1,0:T(8,128)(2,1)S(1)} %maximum_select_fusion), channel_id=1, source_target_pairs={{0,752},{16,32},{32,16},{48,64},{64,48},{80,96},{96,80},{112,128},... | collective-permute-start | bytes 245768 | tf_op jit(solution)/shard_map/ppermute | solution.py:293
  34.7 8.3 %collective-permute-start.3 = (bf16[4,8,32,640]{3,2,1,0:T(8,128)(2,1)S(1)}, bf16[4,8,32,640]{3,2,1,0:T(8,128)(2,1)S(1)}, u32[]{:S(2)}, u32[]{:S(2)}) collective-permute-start(bf16[4,8,32,640]{3,2,1,0:T(8,128)(2,1)S(1)} %bitcast.60), channel_id=1, source_target_pairs={{0,16},{16,0},{1,17},{17,1},{2,18},{18,2},{3,19},{19,3},{4,20},{20... | collective-permute-start | bytes 3932168 | tf_op jit(solution)/shard_map/ppermute | solution.py:295
  37.0 5.9 %collective-permute-start.4 = (bf16[4,32,384]{2,1,0:T(8,128)(2,1)S(1)}, bf16[4,32,384]{2,1,0:T(8,128)(2,1)S(1)}, u32[]{:S(2)}, u32[]{:S(2)}) collective-permute-start(bf16[4,32,384]{2,1,0:T(8,128)(2,1)S(1)} %fusion), channel_id=1, source_target_pairs={{0,368},{32,16},{64,48},{96,80},{128,112},{160,144},{192,176},{224... | collective-permute-start | bytes 294920 | tf_op jit(solution)/shard_map/ppermute | solution.py:298
  45.7 17.2 %all-to-all-start.1 = ((f32[8,40,512]{2,1,0:T(8,128)}), f32[8,40,512]{2,1,0:T(8,128)S(1)}, u32[]{:S(2)}, u32[]{:S(2)}) async-start(f32[8,40,512]{2,1,0:T(8,128)} %bitcast.10), calls=%async_computation.1 | async-start | bytes 1310720 | tf_op jit(solution)/shard_map/all_to_all | solution.py:323
  49.3 9.6 %collective-permute-start.5 = (bf16[2,40,1920]{2,1,0:T(8,128)(2,1)S(1)}, bf16[2,40,1920]{2,1,0:T(8,128)(2,1)S(1)}, u32[]{:S(2)}, u32[]{:S(2)}) collective-permute-start(bf16[2,40,1920]{2,1,0:T(8,128)(2,1)S(1)} %pad_maximum_fusion.1), channel_id=1, source_target_pairs={{0,32},{32,0},{64,96},{96,64},{128,160},{160,128},{192,224},{224,1... | collective-permute-start | bytes 921608 | tf_op jit(solution)/shard_map/ppermute | solution.py:312
  51.3 30.2 %collective-permute-start.7 = (bf16[2,40,1920]{2,1,0:T(8,128)(2,1)S(1)}, bf16[2,40,1920]{2,1,0:T(8,128)(2,1)S(1)}, u32[]{:S(2)}, u32[]{:S(2)}) collective-permute-start(bf16[2,40,1920]{2,1,0:T(8,128)(2,1)S(1)} %pad_maximum_fusion.1), channel_id=1, source_target_pairs={{0,40},{8,32},{16,440},{24,432},{32,8},{40,0},{48,408},{56,400},{6... | collective-permute-start | bytes 921608 | tf_op jit(solution)/shard_map/ppermute | solution.py:320
  56.7 24.7 %collective-permute-start.6 = (bf16[2,40,1920]{2,1,0:T(8,128)(2,1)S(1)}, bf16[2,40,1920]{2,1,0:T(8,128)(2,1)}, u32[]{:S(2)}, u32[]{:S(2)}) collective-permute-start(bf16[2,40,1920]{2,1,0:T(8,128)(2,1)S(1)} %pad_maximum_fusion.1), channel_id=1, source_target_pairs={{0,8},{8,0},{16,408},{24,400},{32,40},{40,32},{48,440},{56,432},{6... | collective-permute-start | bytes 921608 | tf_op jit(solution)/shard_map/ppermute | solution.py:320
  58.9 0.7 copy-start.3
  63.6 27.9 %all-to-all-start.2 = ((f32[12,8,256]{2,1,0:T(8,128)}), f32[12,8,256]{2,1,0:T(8,128)S(1)}, u32[]{:S(2)}, u32[]{:S(2)}) async-start(f32[12,8,256]{2,1,0:T(8,128)} %bitcast.15), calls=%async_computation.2 | async-start | bytes 196608 | tf_op jit(solution)/shard_map/all_to_all | solution.py:332
  81.4 3.7 %copy-start.4 = (bf16[2,40,1920]{2,1,0:T(8,128)(2,1)S(1)}, bf16[2,40,1920]{2,1,0:T(8,128)(2,1)}, u32[]{:S(2)}) copy-start(bf16[2,40,1920]{2,1,0:T(8,128)(2,1)} %copy-done.3) | copy-start | bytes 921604
  82.5 15.1 %collective-permute-start.9 = (bf16[4,40,1920]{2,1,0:T(8,128)(2,1)S(1)}, bf16[4,40,1920]{2,1,0:T(8,128)(2,1)S(1)}, u32[]{:S(2)}, u32[]{:S(2)}) collective-permute-start(bf16[4,40,1920]{2,1,0:T(8,128)(2,1)S(1)} %constant_dynamic-update-slice_fusion.refs_1_), channel_id=1, source_target_pairs={{0,16},{16,0},{1,17},{17,1},{2,18},{18,2},{3,19},{19,3},{4,20},{20... | collective-permute-start | bytes 1843208 | tf_op jit(solution)/shard_map/ppermute | solution.py:335
  85.2 12.4 %collective-permute-start.8 = (bf16[4,40,1920]{2,1,0:T(8,128)(2,1)S(1)}, bf16[4,40,1920]{2,1,0:T(8,128)(2,1)S(1)}, u32[]{:S(2)}, u32[]{:S(2)}) collective-permute-start(bf16[4,40,1920]{2,1,0:T(8,128)(2,1)S(1)} %pad_maximum_fusion.refs_0_), channel_id=1, source_target_pairs={{0,16},{16,0},{1,17},{17,1},{2,18},{18,2},{3,19},{19,3},{4,20},{20... | collective-permute-start | bytes 1843208 | tf_op jit(solution)/shard_map/ppermute | solution.py:331
  92.2 18.3 %all-to-all-start.3 = ((f32[24,8,256]{2,1,0:T(8,128)}), f32[24,8,256]{2,1,0:T(8,128)}, u32[]{:S(2)}, u32[]{:S(2)}) async-start(f32[24,8,256]{2,1,0:T(8,128)} %broadcast_in_dim.16), calls=%async_computation.3 | async-start | bytes 393216 | tf_op jit(solution)/shard_map/all_to_all | solution.py:337
  97.6 1.0 copy-start.2
